TPU v7x, 32 devices: a whole 2x2x4 slice. The times are simulated.
32 devices in a mesh: seq: 8 (over z, y), head: 4 (over x, core).
Axes of the slice: x: 2, y: 2, z: 4, core: 2. Of those that a mesh axis runs over, the one named last changes fastest.
Arguments:
- frames: bfloat16 [8192, 768], P(('seq', 'head')), may hold values from -6 to 6
- condition: bfloat16 [8, 768], P('seq'), may hold values from -6 to 6
- captions: bfloat16 [8, 256, 768], P('seq'), may hold values from -6 to 6
- caption_lengths: int32 [8], P('seq'), may hold values from 5 to 256, as said below
- modulation_weight: bfloat16 [768, 4608], P('seq'), may hold values from -0.21875 to 0.21875
- modulation_bias: bfloat16 [4608], P('seq'), may hold values from -6 to 6
- self_weight: bfloat16 [768, 2304], P('seq'), may hold values from -0.21875 to 0.21875
- self_out: bfloat16 [768, 768], P('seq'), may hold values from -4 to 4
- self_bias: bfloat16 [768], P('seq'), may hold values from -6 to 6
- cross_gain: bfloat16 [768], P('seq'), may hold values from 0.099609375 to 1.8984375
- cross_query: bfloat16 [768, 768], P('seq'), may hold values from -0.21875 to 0.21875
- cross_pair: bfloat16 [768, 1536], P('seq'), may hold values from -0.21875 to 0.21875
- cross_out: bfloat16 [768, 768], P('seq'), may hold values from -0.75 to 0.75
- cross_bias: bfloat16 [768], P('seq'), may hold values from -6 to 6
- up_weight: bfloat16 [768, 3072], P('seq', 'head'), may hold values from -0.21875 to 0.21875
- up_bias: bfloat16 [3072], P('head'), may hold values from -6 to 6
- down_weight: bfloat16 [3072, 768], P('head', 'seq'), may hold values from -0.109375 to 0.109375
- down_bias: bfloat16 [768], P('seq'), may hold values from -6 to 6
- cotangent: bfloat16 [8192, 768], P(('seq', 'head')), may hold values from -6 to 6
Outputs:
- output_frames: bfloat16 [8192, 768], P(('seq', 'head'))
- grad_frames: float32 [8192, 768], P(('seq', 'head'))
- grad_condition: float32 [8, 768], P('seq', 'head')
- grad_captions: float32 [8, 256, 768], P('seq', None, 'head')
- grad_modulation_weight: float32 [768, 4608], P(('seq', 'head'))
- grad_modulation_bias: float32 [4608], P(('seq', 'head'))
- grad_self_weight: float32 [768, 2304], P(('seq', 'head'))
- grad_self_out: float32 [768, 768], P(('seq', 'head'))
- grad_self_bias: float32 [768], P(('seq', 'head'))
- grad_cross_gain: float32 [768], P(('seq', 'head'))
- grad_cross_query: float32 [768, 768], P(('seq', 'head'))
- grad_cross_pair: float32 [768, 1536], P(('seq', 'head'))
- grad_cross_out: float32 [768, 768], P(('seq', 'head'))
- grad_cross_bias: float32 [768], P(('seq', 'head'))
- grad_up_weight: float32 [768, 3072], P('seq', 'head')
- grad_up_bias: float32 [3072], P('head')
- grad_down_weight: float32 [3072, 768], P('head', 'seq')
- grad_down_bias: float32 [768], P(('seq', 'head'))
Inputs may be any that keep to these rules, and one draw needn't show every extreme that they name: `caption_lengths`: every sequence's caption uses between 5 and 256 slots, the first ones; some sequence uses all 256.
All inputs are finite; a program needn't handle non-finite values.
Results may differ from a plain program's by a relative error of at most 0.018.
The roundings to bfloat16 on the way count: a program that leaves them out, or rounds other values in their place, can miss the bound.
Values may be sent and summed in bfloat16 or wider, within the bound.
No kernel may reach another device: no remote copies, remote signals or barrier semaphores. Data moves between devices by JAX's collectives and lax.ppermute only.
A program may use at most 256 MiB of HBM per device.

v0:
```python
import jax
import jax.numpy as jnp
from jax import lax
from jax.sharding import PartitionSpec as P

HD = 64


def split_up(x, dim, peers):
    dims = x.shape
    parts = x.reshape(*dims[:dim], peers, dims[dim] // peers, *dims[dim + 1 :])
    return jnp.moveaxis(parts, dim, 0)


def sum_at_owner(x, axis, dim):
    parts = split_up(x, dim, lax.axis_size(axis))
    arrived = lax.all_to_all(parts, axis, split_axis=0, concat_axis=0, tiled=True)
    return arrived.astype(jnp.float32).sum(axis=0)


def normed(values):
    center = values - jnp.mean(values, axis=-1, keepdims=True)
    spread = jnp.mean(center * center, axis=-1, keepdims=True)
    return center * lax.rsqrt(spread + 1e-06)


def modulate(values, scale, shift):
    return normed(values) * (1.0 + scale) + shift


def gain_norm(values, gain):
    return normed(values) * gain


def gelu_tanh(values):
    return jax.nn.gelu(values, approximate=True)


def to_heads(values):
    return lax.all_to_all(values, "head", split_axis=2, concat_axis=0, tiled=True)


def to_frames(values):
    return lax.all_to_all(values, "head", split_axis=0, concat_axis=2, tiled=True)


def head_rows(values):
    return lax.all_gather(values, "head", axis=0, tiled=True)


def head_sum(function, row_total):
    return lax.psum_scatter(
        function(jnp.int32(0), row_total * lax.axis_size("head")),
        "head",
        scatter_dimension=0,
        tiled=True,
    )


def attend_forward(queries, key_rows, value_rows, visible):
    seq_rows, head_count, head_size = queries.shape
    block_rows = min(512, seq_rows)
    blocks = queries.reshape(seq_rows // block_rows, block_rows, head_count, head_size)

    def one_block(query_block):
        scores = (
            jnp.einsum("qhd,khd->hqk", query_block, key_rows, preferred_element_type=jnp.float32)
            * 0.125
        )
        scores = jnp.where(visible[None, None, :], scores, -1e30)
        largest = jnp.max(scores, axis=-1, keepdims=True)
        weights = jnp.exp(scores - largest)
        totals = jnp.sum(weights, axis=-1, keepdims=True)
        probable = (weights / totals).astype(jnp.bfloat16)
        mixed = jnp.einsum("hqk,khd->qhd", probable, value_rows, preferred_element_type=jnp.float32)
        return (mixed.astype(jnp.bfloat16), (largest + jnp.log(totals))[:, :, 0])

    mixed, log_totals = lax.map(one_block, blocks)
    return (mixed.reshape(seq_rows, head_count * head_size), log_totals)


def attend_backward(queries, key_rows, value_rows, visible, log_totals, grad_mixed):
    seq_rows, head_count, head_size = queries.shape
    block_rows = min(512, seq_rows)
    block_count = seq_rows // block_rows
    query_blocks = queries.reshape(block_count, block_rows, head_count, head_size)
    grad_blocks = grad_mixed.reshape(block_count, block_rows, head_count, head_size)

    def one_block(carried, batch_item):
        grad_keys, grad_values = carried
        query_block, grad_block, log_block = batch_item
        scores = (
            jnp.einsum("qhd,khd->hqk", query_block, key_rows, preferred_element_type=jnp.float32)
            * 0.125
        )
        scores = jnp.where(visible[None, None, :], scores, -1e30)
        weights = jnp.exp(scores - log_block[:, :, None])
        grad_values = grad_values + jnp.einsum(
            "hqk,qhd->khd",
            weights.astype(jnp.bfloat16),
            grad_block,
            preferred_element_type=jnp.float32,
        )
        grad_weights = jnp.einsum(
            "qhd,khd->hqk", grad_block, value_rows, preferred_element_type=jnp.float32
        )
        inner = jnp.sum(weights * grad_weights, axis=-1, keepdims=True)
        grad_scores = (weights * (grad_weights - inner)).astype(jnp.bfloat16)
        grad_query = (
            jnp.einsum("hqk,khd->qhd", grad_scores, key_rows, preferred_element_type=jnp.float32)
            * 0.125
        )
        grad_keys = (
            grad_keys
            + jnp.einsum(
                "hqk,qhd->khd", grad_scores, query_block, preferred_element_type=jnp.float32
            )
            * 0.125
        )
        return ((grad_keys, grad_values), grad_query.astype(jnp.bfloat16))

    zeros = jnp.zeros(key_rows.shape, jnp.float32)
    (grad_keys, grad_values), grad_queries = lax.scan(
        one_block, (zeros, zeros), (query_blocks, grad_blocks, log_totals)
    )
    return (
        grad_queries.reshape(seq_rows, head_count * head_size),
        grad_keys.astype(jnp.bfloat16),
        grad_values.astype(jnp.bfloat16),
    )


def on_device(
    frames,
    condition,
    captions,
    caption_lengths,
    modulation_weight,
    modulation_bias,
    self_weight,
    self_out,
    self_bias,
    cross_gain,
    cross_query,
    cross_pair,
    cross_out,
    cross_bias,
    up_weight,
    up_bias,
    down_weight,
    down_bias,
    cotangent,
):
    heads_dev = lax.axis_size("head")
    my_head = lax.axis_index("head")
    (
        modulation_all,
        modulation_add,
        self_all,
        out_all,
        out_add,
        gain_all,
        query_all,
        pair_all,
        cross_all,
        cross_add,
        up_local,
        down_local,
        down_add,
    ) = (
        lax.all_gather(modulation_weight, "seq", axis=0, tiled=True),
        lax.all_gather(modulation_bias, "seq", axis=0, tiled=True),
        lax.all_gather(self_weight, "seq", axis=0, tiled=True),
        lax.all_gather(self_out, "seq", axis=0, tiled=True),
        lax.all_gather(self_bias, "seq", axis=0, tiled=True),
        lax.all_gather(cross_gain, "seq", axis=0, tiled=True),
        lax.all_gather(cross_query, "seq", axis=0, tiled=True),
        lax.all_gather(cross_pair, "seq", axis=0, tiled=True),
        lax.all_gather(cross_out, "seq", axis=0, tiled=True),
        lax.all_gather(cross_bias, "seq", axis=0, tiled=True),
        lax.all_gather(up_weight, "seq", axis=0, tiled=True),
        lax.all_gather(down_weight, "seq", axis=1, tiled=True),
        lax.all_gather(down_bias, "seq", axis=0, tiled=True),
    )
    frame_rows, model_width = frames.shape
    head_width = model_width // heads_dev
    head_count = head_width // HD
    seq_rows = frame_rows * heads_dev
    state = frames.astype(jnp.float32)
    cond_vector = condition[0].astype(jnp.float32)
    silu_cond = jax.nn.silu(cond_vector).astype(jnp.bfloat16)
    modulation = jnp.dot(silu_cond[None, :], modulation_all, preferred_element_type=jnp.float32)[
        0
    ] + modulation_add.astype(jnp.float32)
    shift_one, scale_one, gate_one, shift_two, scale_two, gate_two = jnp.split(modulation, 6)
    first_in = modulate(state, scale_one, shift_one).astype(jnp.bfloat16)
    joint = jnp.dot(first_in, self_all, preferred_element_type=jnp.float32).astype(jnp.bfloat16)
    joint_heads = to_heads(joint.reshape(frame_rows, 3, model_width))
    self_q = joint_heads[:, 0].reshape(seq_rows, head_count, HD)
    self_k = joint_heads[:, 1].reshape(seq_rows, head_count, HD)
    self_v = joint_heads[:, 2].reshape(seq_rows, head_count, HD)
    everywhere = jnp.ones((seq_rows,), jnp.bool_)
    self_mixed, self_log = attend_forward(self_q, self_k, self_v, everywhere)
    self_frames = to_frames(self_mixed.reshape(seq_rows, 1, head_width)).reshape(
        frame_rows, model_width
    )
    self_proj = jnp.dot(self_frames, out_all, preferred_element_type=jnp.float32) + out_add.astype(
        jnp.float32
    )
    after_self = state + gate_one * self_proj
    gain_values = gain_all.astype(jnp.float32)
    second_in = gain_norm(after_self, gain_values).astype(jnp.bfloat16)
    cross_frames_q = jnp.dot(second_in, query_all, preferred_element_type=jnp.float32).astype(
        jnp.bfloat16
    )
    cross_q = to_heads(cross_frames_q.reshape(frame_rows, 1, model_width)).reshape(
        seq_rows, head_count, HD
    )
    key_cols = lax.dynamic_slice_in_dim(pair_all, my_head * head_width, head_width, 1)
    value_cols = lax.dynamic_slice_in_dim(
        pair_all, model_width + my_head * head_width, head_width, 1
    )
    pair_cols = jnp.concatenate([key_cols, value_cols], axis=1)
    caption = captions[0]
    text_slots = caption.shape[0]
    pair_rows = jnp.dot(caption, pair_cols, preferred_element_type=jnp.float32).astype(jnp.bfloat16)
    cross_k = pair_rows[:, :head_width].reshape(text_slots, head_count, HD)
    cross_v = pair_rows[:, head_width:].reshape(text_slots, head_count, HD)
    visible = jnp.arange(text_slots) < caption_lengths[0]
    cross_mixed, cross_log = attend_forward(cross_q, cross_k, cross_v, visible)
    cross_frames = to_frames(cross_mixed.reshape(seq_rows, 1, head_width)).reshape(
        frame_rows, model_width
    )
    cross_proj = jnp.dot(
        cross_frames, cross_all, preferred_element_type=jnp.float32
    ) + cross_add.astype(jnp.float32)
    after_cross = after_self + cross_proj
    third_in = modulate(after_cross, scale_two, shift_two).astype(jnp.bfloat16)
    down_offset = down_add.astype(jnp.float32)
    row_inputs = head_rows(third_in)
    up_values = jnp.dot(row_inputs, up_local, preferred_element_type=jnp.float32) + up_bias.astype(
        jnp.float32
    )
    hidden = gelu_tanh(up_values).astype(jnp.bfloat16)

    def down_term(first_row, row_count):
        return jnp.dot(hidden, down_local, preferred_element_type=jnp.float32)

    feed = head_sum(down_term, frame_rows) + down_offset
    output_frames = (after_cross + gate_two * feed).astype(jnp.bfloat16)
    grad_out = cotangent.astype(jnp.float32)
    grad_gate_two = jnp.sum(grad_out * feed, axis=0)
    grad_feed = (gate_two * grad_out).astype(jnp.bfloat16)
    grad_down_bias = jnp.sum(grad_feed.astype(jnp.float32), axis=0)
    grad_rows = head_rows(grad_feed)
    grad_hidden = jnp.dot(grad_rows, down_local.T, preferred_element_type=jnp.float32)
    grad_down_part = jnp.dot(hidden.T, grad_rows, preferred_element_type=jnp.float32)
    grad_up = jax.vjp(gelu_tanh, up_values)[1](grad_hidden)[0].astype(jnp.bfloat16)
    grad_up_part = jnp.dot(row_inputs.T, grad_up, preferred_element_type=jnp.float32)
    grad_upbias_part = jnp.sum(grad_up.astype(jnp.float32), axis=0)

    def input_term(first_row, row_count):
        return jnp.dot(grad_up, up_local.T, preferred_element_type=jnp.float32)

    grad_third = head_sum(input_term, frame_rows)
    grad_from_third, grad_scale_two, grad_shift_two = jax.vjp(
        modulate, after_cross, scale_two, shift_two
    )[1](grad_third)
    grad_after_cross = grad_out + grad_from_third
    grad_cross_proj = grad_after_cross.astype(jnp.bfloat16)
    grad_cross_bias = jnp.sum(grad_cross_proj.astype(jnp.float32), axis=0)
    grad_cross_out = jnp.dot(cross_frames.T, grad_cross_proj, preferred_element_type=jnp.float32)
    grad_cross_frames = jnp.dot(
        grad_cross_proj, cross_all.T, preferred_element_type=jnp.float32
    ).astype(jnp.bfloat16)
    grad_cross_heads = to_heads(grad_cross_frames.reshape(frame_rows, 1, model_width)).reshape(
        seq_rows, head_width
    )
    grad_cq, grad_ck, grad_cv = attend_backward(
        cross_q, cross_k, cross_v, visible, cross_log, grad_cross_heads
    )
    grad_cq_frames = to_frames(grad_cq.reshape(seq_rows, 1, head_width)).reshape(
        frame_rows, model_width
    )
    grad_pair_rows = jnp.concatenate(
        [grad_ck.reshape(text_slots, head_width), grad_cv.reshape(text_slots, head_width)], axis=1
    )
    grad_caption = jnp.dot(grad_pair_rows, pair_cols.T, preferred_element_type=jnp.float32)
    grad_pair_local = jnp.dot(caption.T, grad_pair_rows, preferred_element_type=jnp.float32)
    grad_query_weight = jnp.dot(second_in.T, grad_cq_frames, preferred_element_type=jnp.float32)
    grad_second = jnp.dot(grad_cq_frames, query_all.T, preferred_element_type=jnp.float32)
    grad_from_second, grad_gain = jax.vjp(gain_norm, after_self, gain_values)[1](grad_second)
    grad_after_self = grad_after_cross + grad_from_second
    grad_gate_one = jnp.sum(grad_after_self * self_proj, axis=0)
    grad_self_proj = (gate_one * grad_after_self).astype(jnp.bfloat16)
    grad_self_bias = jnp.sum(grad_self_proj.astype(jnp.float32), axis=0)
    grad_self_out = jnp.dot(self_frames.T, grad_self_proj, preferred_element_type=jnp.float32)
    grad_self_frames = jnp.dot(
        grad_self_proj, out_all.T, preferred_element_type=jnp.float32
    ).astype(jnp.bfloat16)
    grad_self_heads = to_heads(grad_self_frames.reshape(frame_rows, 1, model_width)).reshape(
        seq_rows, head_width
    )
    grad_sq, grad_sk, grad_sv = attend_backward(
        self_q, self_k, self_v, everywhere, self_log, grad_self_heads
    )
    grad_joint_heads = jnp.stack(
        [grad_sq, grad_sk.reshape(seq_rows, head_width), grad_sv.reshape(seq_rows, head_width)],
        axis=1,
    )
    grad_joint = to_frames(grad_joint_heads).reshape(frame_rows, 3 * model_width)
    grad_self_weight = jnp.dot(first_in.T, grad_joint, preferred_element_type=jnp.float32)
    grad_first = jnp.dot(grad_joint, self_all.T, preferred_element_type=jnp.float32)
    grad_from_first, grad_scale_one, grad_shift_one = jax.vjp(
        modulate, state, scale_one, shift_one
    )[1](grad_first)
    grad_frames = grad_after_self + grad_from_first
    grad_modulation = jnp.concatenate(
        [
            grad_shift_one,
            grad_scale_one,
            grad_gate_one,
            grad_shift_two,
            grad_scale_two,
            grad_gate_two,
        ]
    )
    grad_silu = jnp.dot(
        modulation_all,
        grad_modulation,
        precision=lax.Precision.HIGHEST,
        preferred_element_type=jnp.float32,
    )
    grad_cond = jax.vjp(jax.nn.silu, cond_vector)[1](grad_silu)[0]
    grad_captions, grad_condition = (
        lax.psum_scatter(
            grad_caption[None].astype(jnp.bfloat16), "head", scatter_dimension=2, tiled=True
        ).astype(jnp.float32),
        lax.psum_scatter(
            grad_cond[None].astype(jnp.bfloat16), "head", scatter_dimension=1, tiled=True
        ).astype(jnp.float32),
    )
    grad_modulation_weight = silu_cond.astype(jnp.float32)[:, None] * grad_modulation[None, :]
    empty_cols = jnp.zeros((caption.shape[1], model_width), jnp.float32)
    grad_pair = jnp.concatenate(
        [
            lax.dynamic_update_slice_in_dim(
                empty_cols, grad_pair_local[:, :head_width], my_head * head_width, 1
            ),
            lax.dynamic_update_slice_in_dim(
                empty_cols, grad_pair_local[:, head_width:], my_head * head_width, 1
            ),
        ],
        axis=1,
    )
    (
        sum_modulation_weight,
        sum_modulation_bias,
        sum_self_weight,
        sum_self_out,
        sum_self_bias,
        sum_gain,
        sum_query,
        sum_pair,
        sum_cross_out,
        sum_cross_bias,
        sum_down_bias,
    ) = (
        lax.psum_scatter(grad_modulation_weight, ("seq", "head"), scatter_dimension=0, tiled=True),
        lax.psum_scatter(grad_modulation, ("seq", "head"), scatter_dimension=0, tiled=True),
        lax.psum_scatter(grad_self_weight, ("seq", "head"), scatter_dimension=0, tiled=True),
        lax.psum_scatter(grad_self_out, ("seq", "head"), scatter_dimension=0, tiled=True),
        lax.psum_scatter(grad_self_bias, ("seq", "head"), scatter_dimension=0, tiled=True),
        lax.psum_scatter(grad_gain, ("seq", "head"), scatter_dimension=0, tiled=True),
        lax.psum_scatter(grad_query_weight, ("seq", "head"), scatter_dimension=0, tiled=True),
        lax.psum_scatter(grad_pair, ("seq", "head"), scatter_dimension=0, tiled=True),
        lax.psum_scatter(grad_cross_out, ("seq", "head"), scatter_dimension=0, tiled=True),
        lax.psum_scatter(grad_cross_bias, ("seq", "head"), scatter_dimension=0, tiled=True),
        lax.psum_scatter(grad_down_bias, ("seq", "head"), scatter_dimension=0, tiled=True),
    )
    sum_up_weight, sum_down_weight = (
        sum_at_owner(grad_up_part.astype(jnp.bfloat16), "seq", 0),
        sum_at_owner(grad_down_part.astype(jnp.bfloat16), "seq", 1),
    )
    sum_up_bias = lax.psum(grad_upbias_part, "seq")
    return (
        output_frames,
        grad_frames,
        grad_condition,
        grad_captions,
        sum_modulation_weight,
        sum_modulation_bias,
        sum_self_weight,
        sum_self_out,
        sum_self_bias,
        sum_gain,
        sum_query,
        sum_pair,
        sum_cross_out,
        sum_cross_bias,
        sum_up_weight,
        sum_up_bias,
        sum_down_weight,
        sum_down_bias,
    )


def solution(mesh):
    return jax.shard_map(
        on_device,
        mesh=mesh,
        in_specs=(
            P(("seq", "head"), None),
            P("seq", None),
            P("seq", None, None),
            P("seq"),
            P("seq", None),
            P("seq"),
            P("seq", None),
            P("seq", None),
            P("seq"),
            P("seq"),
            P("seq", None),
            P("seq", None),
            P("seq", None),
            P("seq"),
            P("seq", "head"),
            P("head"),
            P("head", "seq"),
            P("seq"),
            P(("seq", "head"), None),
        ),
        out_specs=(
            P(("seq", "head"), None),
            P(("seq", "head"), None),
            P("seq", "head"),
            P("seq", None, "head"),
            P(("seq", "head"), None),
            P(("seq", "head")),
            P(("seq", "head"), None),
            P(("seq", "head"), None),
            P(("seq", "head")),
            P(("seq", "head")),
            P(("seq", "head"), None),
            P(("seq", "head"), None),
            P(("seq", "head"), None),
            P(("seq", "head")),
            P("seq", "head"),
            P("head"),
            P("head", "seq"),
            P(("seq", "head")),
        ),
        check_vma=False,
    )
```

profile of v0, /device:TPU:0, one launch (start us, length us, event | category | flops | bytes accessed | tf_op | source)
XLA Modules:
  0.0 1506.1 jit_solution(17954495132779892509)
XLA Ops:
  15.9 40.6 %all-reduce.11 = (bf16[4608]{0:T(1024)(128)(2,1)S(1)}, bf16[768]{0:T(1024)(128)(2,1)}, bf16[768]{0:T(1024)(128)(2,1)}, bf16[768]{0:T(1024)(128)(2,1)}, bf16[768]{0:T(1024)(128)(2,1)}) all-reduce(bf16[4608]{0:T(1024)(128)(2,1)S(1)} %dynamic-update-slice, ...), channel_id=1, replica_groups=mesh['seq'=8,'head'=4] {'seq'}, use_global_device_ids=true, to_apply=%add | all-reduce | flops 7680 | bytes 30720
  56.5 66.0 %all-gather.11.cloned.1.call-done = bf16[768,4608]{1,0:T(8,128)(2,1)} async-done(((bf16[96,4608]{1,0:T(8,128)(2,1)}), bf16[768,4608]{1,0:T(8,128)(2,1)}) %all-gather.11.cloned.1.call-update) | async-done | bytes 7077904 | tf_op jit(solution)/shard_map/all_gather | solution.py:171
  127.1 60.9 %all-gather.13.cloned.1.call-done = bf16[768,2304]{1,0:T(8,128)(2,1)} async-done(((bf16[96,2304]{1,0:T(8,128)(2,1)}), bf16[768,2304]{1,0:T(8,128)(2,1)}) %all-gather.13.cloned.1.call-update) | async-done | bytes 3538960 | tf_op jit(solution)/shard_map/all_gather | solution.py:173
  198.2 19.5 %all-to-all-done = bf16[256,3,768]{0,1,2:T(4,128)(2,1)S(1)} async-done(((bf16[256,3,768]{0,1,2:T(4,128)(2,1)}), bf16[256,3,768]{0,1,2:T(4,128)(2,1)S(1)}, u32[]{:S(2)}, u32[]{:S(2)}) %all-to-all-start) | async-done | bytes 1179680 | tf_op jit(solution)/shard_map/all_to_all | solution.py:40
  218.5 8.6 while.55
  245.0 37.5 %all-gather.15.cloned.1.call-done = bf16[768,768]{1,0:T(8,128)(2,1)} async-done(((bf16[96,768]{1,0:T(8,128)(2,1)}), bf16[768,768]{1,0:T(8,128)(2,1)}) %all-gather.15.cloned.1.call-update) | async-done | bytes 1179664 | tf_op jit(solution)/shard_map/all_gather | solution.py:174
  285.4 38.9 %all-gather.17.cloned.1.call-done = bf16[768,768]{1,0:T(8,128)(2,1)} async-done(((bf16[96,768]{1,0:T(8,128)(2,1)}), bf16[768,768]{1,0:T(8,128)(2,1)}) %all-gather.17.cloned.1.call-update) | async-done | bytes 1179664 | tf_op jit(solution)/shard_map/all_gather | solution.py:177
  353.7 7.4 all-to-all-done.3
  374.3 34.1 %all-gather.25.cloned.1.call-done = bf16[768,768]{1,0:T(8,128)(2,1)} async-done(((bf16[96,768]{1,0:T(8,128)(2,1)}), bf16[768,768]{1,0:T(8,128)(2,1)}) %all-gather.25.cloned.1.call-update) | async-done | bytes 1179664 | tf_op jit(solution)/shard_map/all_gather | solution.py:181
  408.4 20.6 %all-gather.23.cloned.1.call-done = bf16[1024,768]{1,0:T(8,128)(2,1)} async-done(((bf16[256,768]{1,0:T(8,128)(2,1)}), bf16[1024,768]{1,0:T(8,128)(2,1)}) %all-gather.23.cloned.1.call-update) | async-done | bytes 1572880 | tf_op jit(solution)/shard_map/all_gather | solution.py:48
  433.8 38.5 %all-gather.27.cloned.1.call-done = bf16[768,768]{0,1:T(8,128)(2,1)} async-done(((bf16[768,96]{0,1:T(8,128)(2,1)}), bf16[768,768]{0,1:T(8,128)(2,1)}) %all-gather.27.cloned.1.call-update) | async-done | bytes 1179664 | tf_op jit(solution)/shard_map/all_gather | solution.py:182
  472.3 19.9 %all-gather.29.cloned.1.call-done = bf16[1024,768]{1,0:T(8,128)(2,1)} async-done(((bf16[256,768]{1,0:T(8,128)(2,1)}), bf16[1024,768]{1,0:T(8,128)(2,1)}) %all-gather.29.cloned.1.call-update) | async-done | bytes 1572880 | tf_op jit(solution)/shard_map/all_gather | solution.py:48
  492.1 6.4 convert_reduce_fusion
  503.0 5.9 fusion.122
  509.6 31.4 %reduce-scatter.17.cloned.1.call-done = f32[256,768]{1,0:T(8,128)} async-done(((f32[1024,768]{1,0:T(8,128)}), f32[256,768]{1,0:T(8,128)}) %reduce-scatter.17.cloned.1.call-update) | async-done | bytes 786448 | tf_op jit(solution)/shard_map/reduce_scatter | solution.py:52
  543.1 38.5 %reduce-scatter.15.cloned.1.call-done = f32[256,768]{1,0:T(8,128)} async-done(((f32[1024,768]{1,0:T(8,128)}), f32[256,768]{1,0:T(8,128)}) %reduce-scatter.15.cloned.1.call-update) | async-done | bytes 786448 | tf_op jit(solution)/shard_map/reduce_scatter | solution.py:52
  600.1 7.4 all-to-all-done.4
  613.4 8.3 while.57
  627.8 10.9 all_to_all.133
  660.1 7.5 all-to-all-done.6
  677.8 16.3 %while.58 = (s32[]{:T(128)}, f32[1024,3,64]{0,2,1:T(8,128)S(1)}, f32[1024,3,64]{0,2,1:T(8,128)S(1)}, bf16[2,512,3,64]{1,3,2,0:T(8,128)(2,1)}, bf16[2,512,3,64]{1...) while((s32[]{:T(128)}, f32[1024,3,64]{0,2,1:T(8,128)S(1)}, ...), condition=%wide.region_25.26_spmd.clone, body=%wide.region_23.25_spmd.clone.sunk | while | flops 1026685440 | bytes 58833156 | solution.py:123
  705.5 25.6 %all-to-all-done.7 = bf16[1024,3,192]{2,1,0:T(4,128)(2,1)} async-done(((bf16[1024,3,192]{2,1,0:T(4,128)(2,1)}), bf16[1024,3,192]{2,1,0:T(4,128)(2,1)}, u32[]{:S(2)}, u32[]{:S(2)}) %all-to-all-start.7) | async-done | bytes 1179680 | tf_op jit(solution)/shard_map/all_to_all | solution.py:44
  739.9 7.8 convolution_reduce_fusion.1
  785.4 6.8 broadcast_multiply_fusion
  808.0 30.1 %all-to-all-done.8 = bf16[8,96,768]{2,1,0:T(8,128)(2,1)S(1)} async-done(((bf16[8,96,768]{2,1,0:T(8,128)(2,1)}), bf16[8,96,768]{2,1,0:T(8,128)(2,1)S(1)}, u32[]{:S(2)}, u32[]{:S(2)}) %all-to-all-start.8) | async-done | bytes 1179680 | tf_op jit(solution)/shard_map/all_to_all | solution.py:17
  842.3 38.0 %psum.7 = f32[768]{0:T(1024)} all-reduce(f32[768]{0:T(1024)S(1)} %copy-done.81), channel_id=1, replica_groups=mesh['seq'=8,'head'=4] {'seq'}, use_global_device_ids=true, to_apply=%region_51.52 | all-reduce | flops 768 | bytes 6144 | tf_op jit(solution)/shard_map/psum | solution.py:385
  884.0 43.0 %all-reduce.10 = (f32[4608]{0:T(1024)S(1)}, f32[768]{0:T(1024)S(1)}, f32[768]{0:T(1024)S(1)}, f32[768]{0:T(1024)S(1)}, f32[768]{0:T(1024)S(1)}) all-reduce(f32[4608]{0:T(1024)S(1)} %copy-done.42, f32[768]{0:T(1024)S(1)} %copy-done.65, f32[768]{0:T(1024)S(1)} %copy-done.64, ...), channel_id=7, replica_groups=mesh['seq'=8,'head'=4] {'seq','head'}, use_global_device_ids=true, to_apply=%region_37.38.clone | all-reduce | flops 7680 | bytes 61440
  931.4 56.9 %reduce-scatter.25.cloned.1.call-done = f32[24,768]{1,0:T(8,128)} async-done(((f32[768,768]{1,0:T(8,128)}), f32[24,768]{1,0:T(8,128)}) %reduce-scatter.25.cloned.1.call-update) | async-done | bytes 73744 | tf_op jit(solution)/shard_map/reduce_scatter | solution.py:375
  988.3 103.7 %reduce-scatter.23.cloned.1.call-done = f32[24,768]{1,0:T(8,128)} async-done(((f32[768,768]{1,0:T(8,128)}), f32[24,768]{1,0:T(8,128)}) %reduce-scatter.23.cloned.1.call-update) | async-done | bytes 73744 | tf_op jit(solution)/shard_map/reduce_scatter | solution.py:372
  1092.0 112.8 %reduce-scatter.27.cloned.1.call-done = f32[24,1536]{1,0:T(8,128)} async-done(((f32[768,1536]{1,0:T(8,128)}), f32[24,1536]{1,0:T(8,128)}) %reduce-scatter.27.cloned.1.call-update) | async-done | bytes 147472 | tf_op jit(solution)/shard_map/reduce_scatter | solution.py:376
  1204.9 124.5 %reduce-scatter.21.cloned.1.call-done = f32[24,2304]{1,0:T(8,128)} async-done(((f32[768,2304]{1,0:T(8,128)}), f32[24,2304]{1,0:T(8,128)}) %reduce-scatter.21.cloned.1.call-update) | async-done | bytes 221200 | tf_op jit(solution)/shard_map/reduce_scatter | solution.py:371
  1329.4 169.4 %reduce-scatter.19.cloned.1.call-done = f32[24,4608]{1,0:T(8,128)} async-done(((f32[768,4608]{1,0:T(8,128)}), f32[24,4608]{1,0:T(8,128)}) %reduce-scatter.19.cloned.1.call-update) | async-done | bytes 442384 | tf_op jit(solution)/shard_map/reduce_scatter | solution.py:369
  (486 shorter events, 281.0 us)
Async XLA Ops:
  7.2 327.0 %copy-start = (bf16[1,256,768]{2,1,0:T(8,128)(2,1)S(1)}, bf16[1,256,768]{2,1,0:T(8,128)(2,1)}, u32[]{:S(2)}) copy-start(bf16[1,256,768]{2,1,0:T(8,128)(2,1)} %param.29) | copy-start | bytes 1179652
  7.3 115.2 %all-gather.11.cloned.1.call-start = ((), (), s32[]{:S(2)}) async-start(), calls=%async_computation.20 | async-start | bytes 7962624 | tf_op jit(solution)/shard_map/all_gather | solution.py:171
  8.0 180.0 %all-gather.13.cloned.1.call-start = ((), (), s32[]{:S(2)}) async-start(), calls=%async_computation.21 | async-start | bytes 3981312 | tf_op jit(solution)/shard_map/all_gather | solution.py:173
  8.8 232.1 %all-gather.19.cloned.1.call-start = ((), (), s32[]{:S(2)}) async-start(), calls=%async_computation.24 | async-start | bytes 2654208 | tf_op jit(solution)/shard_map/all_gather | solution.py:178
  9.5 273.0 %all-gather.15.cloned.1.call-start = ((), (), s32[]{:S(2)}) async-start(), calls=%async_computation.22 | async-start | bytes 1327104 | tf_op jit(solution)/shard_map/all_gather | solution.py:174
  10.1 314.3 %all-gather.17.cloned.1.call-start = ((), (), s32[]{:S(2)}) async-start(), calls=%async_computation.23 | async-start | bytes 1327104 | tf_op jit(solution)/shard_map/all_gather | solution.py:177
  14.4 173.7 %copy-start.55 = (f32[256]{0:T(256)}, f32[256]{0:T(256)S(1)}, u32[]{:S(2)}) copy-start(f32[256]{0:T(256)S(1)} %broadcast_multiply_fusion.3) | copy-start | bytes 3076
  14.6 173.4 %copy-start.59 = (f32[256]{0:T(256)}, f32[256]{0:T(256)S(1)}, u32[]{:S(2)}) copy-start(f32[256]{0:T(256)S(1)} %fusion.110) | copy-start | bytes 3076
  194.0 23.6 %all-to-all-start = ((bf16[256,3,768]{0,1,2:T(4,128)(2,1)}), bf16[256,3,768]{0,1,2:T(4,128)(2,1)S(1)}, u32[]{:S(2)}, u32[]{:S(2)}) async-start(bf16[256,3,768]{0,1,2:T(4,128)(2,1)} %copy.144), calls=%async_computation | async-start | bytes 3145728 | tf_op jit(solution)/shard_map/all_to_all | solution.py:40
  197.6 169.7 %all-gather.21.cloned.1.call-start = ((), (), s32[]{:S(2)}) async-start(), calls=%async_computation.25 | async-start | bytes 1327104 | tf_op jit(solution)/shard_map/all_gather | solution.py:179
  230.8 12.5 all-to-all-start.1
  234.2 174.2 %all-gather.25.cloned.1.call-start = ((), (), s32[]{:S(2)}) async-start(), calls=%async_computation.27 | async-start | bytes 1327104 | tf_op jit(solution)/shard_map/all_gather | solution.py:181
  330.7 10.9 all-to-all-start.2
  349.5 11.6 all-to-all-start.3
  353.6 75.4 %all-gather.23.cloned.1.call-start = ((), (), s32[]{:S(2)}) async-start(), calls=%async_computation.26 | async-start | bytes 1966080 | tf_op jit(solution)/shard_map/all_gather | solution.py:48
  370.5 101.7 %all-gather.27.cloned.1.call-start = ((), (), s32[]{:S(2)}) async-start(), calls=%async_computation.28 | async-start | bytes 1327104 | tf_op jit(solution)/shard_map/all_gather | solution.py:182
  371.3 120.9 %all-gather.29.cloned.1.call-start = ((), (), s32[]{:S(2)}) async-start(), calls=%async_computation.30 | async-start | bytes 1966080 | tf_op jit(solution)/shard_map/all_gather | solution.py:48
  373.8 167.2 %reduce-scatter.17.cloned.1.call-start = ((), (), s32[]{:S(2)}) async-start(), calls=%async_computation.31 | async-start | bytes 3932160 | tf_op jit(solution)/shard_map/reduce_scatter | solution.py:52
  502.9 78.6 %reduce-scatter.15.cloned.1.call-start = ((), (), s32[]{:S(2)}) async-start(), calls=%async_computation.29 | async-start | bytes 3932160 | tf_op jit(solution)/shard_map/reduce_scatter | solution.py:52
  596.4 11.0 all-to-all-start.4
  655.8 11.8 all-to-all-start.6
  698.6 32.5 %all-to-all-start.7 = ((bf16[1024,3,192]{2,1,0:T(4,128)(2,1)}), bf16[1024,3,192]{2,1,0:T(4,128)(2,1)}, u32[]{:S(2)}, u32[]{:S(2)}) async-start(bf16[1024,3,192]{2,1,0:T(4,128)(2,1)} %copy.172), calls=%async_computation.9 | async-start | bytes 4194304 | tf_op jit(solution)/shard_map/all_to_all | solution.py:44
  703.2 178.9 %reduce-scatter.33.cloned.1.call-start = ((), (), s32[]{:S(2)}) async-start(), calls=%async_computation.39 | async-start | bytes 491520
  705.4 224.5 %reduce-scatter.31.cloned.1.call-start = ((), (), s32[]{:S(2)}) async-start(), calls=%async_computation.38 | async-start | bytes 245760
  749.2 182.2 %reduce-scatter.29.cloned.1.call-start = ((), (), s32[]{:S(2)}) async-start(), calls=%async_computation.37 | async-start | bytes 2433024 | tf_op jit(solution)/shard_map/reduce_scatter | solution.py:377
  752.4 235.9 %reduce-scatter.25.cloned.1.call-start = ((), (), s32[]{:S(2)}) async-start(), calls=%async_computation.35 | async-start | bytes 2433024 | tf_op jit(solution)/shard_map/reduce_scatter | solution.py:375
  755.3 336.7 %reduce-scatter.23.cloned.1.call-start = ((), (), s32[]{:S(2)}) async-start(), calls=%async_computation.34 | async-start | bytes 2433024 | tf_op jit(solution)/shard_map/reduce_scatter | solution.py:372
  758.2 446.7 %reduce-scatter.27.cloned.1.call-start = ((), (), s32[]{:S(2)}) async-start(), calls=%async_computation.36 | async-start | bytes 4866048 | tf_op jit(solution)/shard_map/reduce_scatter | solution.py:376
  779.9 549.5 %reduce-scatter.21.cloned.1.call-start = ((), (), s32[]{:S(2)}) async-start(), calls=%async_computation.33 | async-start | bytes 7299072 | tf_op jit(solution)/shard_map/reduce_scatter | solution.py:371
  784.7 714.1 %reduce-scatter.19.cloned.1.call-start = ((), (), s32[]{:S(2)}) async-start(), calls=%async_computation.32 | async-start | bytes 14598144 | tf_op jit(solution)/shard_map/reduce_scatter | solution.py:369
  797.6 40.5 %all-to-all-start.8 = ((bf16[8,96,768]{2,1,0:T(8,128)(2,1)}), bf16[8,96,768]{2,1,0:T(8,128)(2,1)S(1)}, u32[]{:S(2)}, u32[]{:S(2)}) async-start(bf16[8,96,768]{2,1,0:T(8,128)(2,1)} %bitcast.39), calls=%async_computation.16 | async-start | bytes 2359296 | tf_op jit(solution)/shard_map/all_to_all | solution.py:17
  838.1 43.1 %all-to-all-start.9 = ((bf16[8,768,96]{1,2,0:T(8,128)(2,1)}), bf16[8,768,96]{1,2,0:T(8,128)(2,1)S(1)}, u32[]{:S(2)}, u32[]{:S(2)}) async-start(bf16[8,768,96]{1,2,0:T(8,128)(2,1)} %bitcast.330), calls=%async_computation.17 | async-start | bytes 2359296 | tf_op jit(solution)/shard_map/all_to_all | solution.py:17
  (99 other events, 1313.5 us)
Sparse Core Ops, SparseCore 0:
  10.3 112.0 all-gather.10
  124.6 63.3 all-gather.12
  190.2 50.5 all-gather.18
  242.9 39.5 all-gather.14
  284.5 39.8 all-gather.16
  326.4 39.8 all-gather.20
  368.5 39.8 all-gather.24
  410.5 18.4 all-gather.22
  431.2 41.0 all-gather.26
  473.7 18.4 all-gather.28
  503.0 37.9 reduce-scatter.16
  543.6 37.9 reduce-scatter.14
  706.5 24.4 reduce-scatter.32
  749.3 19.7 reduce-scatter.30
  774.8 109.1 reduce-scatter.28
  890.6 97.6 reduce-scatter.24
  994.0 97.9 reduce-scatter.22
  1098.8 105.9 reduce-scatter.26
  1211.1 118.2 reduce-scatter.20
  1336.8 161.9 reduce-scatter.18
where the time goes:
time: 1520 us; the launch traced here: 1510 us
  waiting for transfers between devices  1070 us (70%)
  blocking collectives  132 us (9%)
  local copies, waits for them, and re-layouts  98.8 us (6%)
  matrix products  96.6 us (6%)
  other arithmetic  53.9 us (4%)
  starting transfers between devices  38.6 us (3%)
  between operations  17.7 us (1%)
    reduce_scatter x1, waiting for transfers between devices, on_device(): lax.psum_scatter(grad_modulation_weight, ('seq', 'head'), scatter_dimensi...  169 us
    reduce_scatter x1, waiting for transfers between devices, on_device(): lax.psum_scatter(grad_self_weight, ('seq', 'head'), scatter_dimension=0,...  125 us
    reduce_scatter x1, waiting for transfers between devices, on_device(): lax.psum_scatter(grad_pair, ('seq', 'head'), scatter_dimension=0, tiled=T...  113 us
    reduce_scatter x1, waiting for transfers between devices, on_device(): lax.psum_scatter(grad_self_out, ('seq', 'head'), scatter_dimension=0, til...  104 us
    unnamed x2, blocking collectives  83.6 us
    reduce_scatter x2, waiting for transfers between devices, head_sum(): lax.psum_scatter(function(jnp.int32(0), row_total * lax.axis_size('head')...  69.9 us
    all_gather x1, waiting for transfers between devices, on_device(): lax.all_gather(modulation_weight, 'seq', axis=0, tiled=True)  66 us
    all_gather x1, waiting for transfers between devices, on_device(): lax.all_gather(self_weight, 'seq', axis=0, tiled=True)  60.9 us
  transfers between devices with their start and end apart: 29, of which 23 were waited for; matrix products, arithmetic and copies ran while one was open for 10% of the time, Pallas kernels for 0%

commit v1 on v0

v1 whole, which is shorter than its diff:
```python
import jax
import jax.numpy as jnp
from jax import lax
from jax.sharding import PartitionSpec as P

HD = 64
BF = jnp.bfloat16
F32 = jnp.float32


def mm(a, b, ca=1, cb=0):
    return lax.dot_general(a, b, (((ca,), (cb,)), ((), ())), preferred_element_type=F32)


def swap(x, bit):
    return lax.ppermute(x, "head", [(i, i ^ bit) for i in range(4)])


def swap_rows(x, bit):
    blocks = jnp.split(swap(x, bit), 4, axis=0)
    return jnp.concatenate([blocks[i ^ bit] for i in range(4)], axis=0)


def head_rel(x, swap=swap):
    near = swap(x, 1)
    far = swap(x, 2)
    return [x, near, far, swap(far, 1)]


def pick(parts, index):
    low, high = (index & 1) == 1, (index & 2) == 2
    return jnp.where(
        high, jnp.where(low, parts[3], parts[2]), jnp.where(low, parts[1], parts[0])
    )


def head_sum(chunks, swap=swap):
    a, b = swap(chunks[1], 1), swap(chunks[3], 1)
    mine = chunks[0].astype(F32) + a.astype(F32)
    other = (chunks[2].astype(F32) + b.astype(F32)).astype(chunks[0].dtype)
    return mine + swap(other, 2).astype(F32)


def seq_gather(x):
    n = lax.axis_size("seq")
    sent = jnp.broadcast_to(x[None], (n, *x.shape))
    return lax.all_to_all(sent, "seq", split_axis=0, concat_axis=0, tiled=True)


def seq_sum(x):
    return lax.all_to_all(x, "seq", split_axis=0, concat_axis=0, tiled=True).astype(F32).sum(0)


def stats(v):
    mean = jnp.mean(v, axis=-1, keepdims=True)
    center = v - mean
    r = lax.rsqrt(jnp.mean(center * center, axis=-1, keepdims=True) + 1e-6)
    return center * r, r


def normback(n, r, e):
    return r * (
        e - jnp.mean(e, axis=-1, keepdims=True) - n * jnp.mean(e * n, axis=-1, keepdims=True)
    )


def attend(q, k, v, visible):
    rows, width = q.shape
    heads = width // HD
    qh, kh, vh = (t.reshape(t.shape[0], heads, HD) for t in (q, k, v))
    s = jnp.einsum("qhd,khd->hqk", qh, kh, preferred_element_type=F32) * 0.125
    if visible is not None:
        s = jnp.where(visible[None, None, :], s, -1e30)
    w = jnp.exp(s - jnp.max(s, axis=-1, keepdims=True))
    p = (w / jnp.sum(w, axis=-1, keepdims=True)).astype(BF)
    o = jnp.einsum("hqk,khd->qhd", p, vh, preferred_element_type=F32)
    return o.astype(BF).reshape(rows, width), p


def attend_back(q, k, v, p, do):
    rows, width = q.shape
    heads = width // HD
    qh, kh, vh, dh = (t.reshape(t.shape[0], heads, HD) for t in (q, k, v, do))
    dv = jnp.einsum("hqk,qhd->khd", p, dh, preferred_element_type=F32)
    dp = jnp.einsum("qhd,khd->hqk", dh, vh, preferred_element_type=F32)
    pf = p.astype(F32)
    inner = jnp.sum(pf * dp, axis=-1, keepdims=True)
    ds = (pf * (dp - inner)).astype(BF)
    dq = jnp.einsum("hqk,khd->qhd", ds, kh, preferred_element_type=F32) * 0.125
    dk = jnp.einsum("hqk,qhd->khd", ds, qh, preferred_element_type=F32) * 0.125
    return (
        dq.astype(BF).reshape(rows, width),
        dk.astype(BF).reshape(-1, width),
        dv.astype(BF).reshape(-1, width),
    )


def on_device(
    frames,
    condition,
    captions,
    caption_lengths,
    modulation_weight,
    modulation_bias,
    self_weight,
    self_out,
    self_bias,
    cross_gain,
    cross_query,
    cross_pair,
    cross_out,
    cross_bias,
    up_weight,
    up_bias,
    down_weight,
    down_bias,
    cotangent,
):
    n = lax.axis_size("seq")
    h = lax.axis_index("head")
    s = lax.axis_index("seq")
    rows, width = frames.shape
    hw = width // 4
    kr = self_weight.shape[0]
    own = kr // 4
    total = rows * 4

    def cols(w, base):
        return lax.dynamic_slice_in_dim(w, base + h * hw, hw, 1)

    small = jnp.concatenate([self_bias, cross_bias, cross_gain, down_bias])[None]
    sent = jnp.concatenate(
        [condition.reshape(n, kr), jnp.broadcast_to(small, (n, 4 * kr))], axis=1
    )
    got = lax.all_to_all(sent, "seq", split_axis=0, concat_axis=0, tiled=True)
    cond_own = jax.nn.silu(got[:, :kr].astype(F32)).astype(BF)
    vectors = got[:, kr:].astype(F32).reshape(n, 4, kr).transpose(1, 0, 2).reshape(4, width)
    out_bias, co_bias, gain, dn_bias = vectors[0], vectors[1], vectors[2], vectors[3]
    mod_part = mm(cond_own, modulation_weight) + lax.dynamic_update_slice(
        jnp.zeros((n * modulation_bias.shape[0],), F32),
        modulation_bias.astype(F32),
        (s * modulation_bias.shape[0],),
    )
    w_self = seq_gather(
        jnp.concatenate([cols(self_weight, 0), cols(self_weight, width), cols(self_weight, 2 * width)], axis=1)
    ).reshape(width, 3 * hw)
    mod = seq_sum(mod_part[:, None])[0]
    two = seq_gather(
        jnp.concatenate(
            [cols(self_out, 0), cols(cross_query, 0), cols(cross_pair, 0), cols(cross_pair, width)], axis=1
        )
    ).reshape(width, 4 * hw)
    three = lax.all_gather(
        jnp.concatenate([cols(cross_out, 0), up_weight, down_weight.T], axis=1), "seq", axis=0, tiled=True
    )
    x = jnp.concatenate(head_rel(frames), axis=0).astype(F32)
    g = jnp.concatenate(head_rel(cotangent), axis=0).astype(F32)
    w_query, w_pair = two[:, hw : 2 * hw], two[:, 2 * hw :]
    out_parts = head_rel(two[:, :hw])
    w_out = jnp.concatenate([pick(out_parts, h ^ a) for a in range(4)], axis=1)
    cross_parts = head_rel(three[:, :hw])
    w_cross = jnp.concatenate([pick(cross_parts, h ^ a) for a in range(4)], axis=1)
    w_up, w_down = three[:, hw : hw + up_weight.shape[1]], three[:, hw + up_weight.shape[1] :]

    shift1, scale1, gate1, shift2, scale2, gate2 = jnp.split(mod, 6)
    n1, r1 = stats(x)
    first = (n1 * (1.0 + scale1) + shift1).astype(BF)
    joint = mm(first, w_self).astype(BF)
    q, k, v = joint[:, :hw], joint[:, hw : 2 * hw], joint[:, 2 * hw :]
    sm_own, probs = attend(q, k, v, None)
    sm_parts = head_rel(sm_own, swap_rows)
    sm = jnp.concatenate([pick(sm_parts, h ^ a) for a in range(4)], axis=1)
    self_proj = mm(sm, w_out) + out_bias
    after_self = x + gate1 * self_proj
    n2, r2 = stats(after_self)
    second = (n2 * gain).astype(BF)
    cq = mm(second, w_query).astype(BF)
    caption = captions[0]
    pair = mm(caption, w_pair).astype(BF)
    ck, cv = pair[:, :hw], pair[:, hw:]
    visible = jnp.arange(caption.shape[0]) < caption_lengths[0]
    cm_own, cprobs = attend(cq, ck, cv, visible)
    cm_parts = head_rel(cm_own, swap_rows)
    cm = jnp.concatenate([pick(cm_parts, h ^ a) for a in range(4)], axis=1)
    after_cross = after_self + mm(cm, w_cross) + co_bias
    n3, r3 = stats(after_cross)
    third = (n3 * (1.0 + scale2) + shift2).astype(BF)
    up_values = mm(third, w_up) + up_bias.astype(F32)

    def gelu(t):
        return jax.nn.gelu(t, approximate=True)

    hidden, gelu_back = jax.vjp(gelu, up_values)
    hidden = hidden.astype(BF)
    g_feed = (gate2 * g).astype(BF)
    g_up = gelu_back(mm(g_feed, w_down))[0].astype(BF)
    g_third = mm(g_up, w_up, 1, 1)
    ga = normback(n3, r3, (1.0 + scale2) * g_third)
    ga = jnp.concatenate([ga[:rows] + cotangent.astype(F32), ga[rows:]], axis=0)
    ga_low = ga.astype(BF)
    g_cm = mm(ga_low, w_cross, 1, 1).astype(BF)
    g_cm_abs = [g_cm[:, a * hw : (a + 1) * hw] for a in range(4)]
    g_cm_own = head_sum([pick(g_cm_abs, h ^ j) for j in range(4)], swap_rows).astype(BF)
    feed_part = mm(hidden, w_down, 1, 1).astype(BF)
    feed = head_sum([feed_part[j * rows : (j + 1) * rows] for j in range(4)]) + dn_bias
    output_frames = (after_cross[:rows] + gate2 * feed).astype(BF)
    cot = cotangent.astype(F32)
    gv_gate2 = jnp.sum(cot * feed, axis=0)
    gv_down = jnp.sum(g_feed[:rows].astype(F32), axis=0)
    gv_upbias = jnp.sum(g_up.astype(F32), axis=0)
    gv_scale2 = jnp.sum(g_third * n3, axis=0)
    gv_shift2 = jnp.sum(g_third, axis=0)
    gv_cross = jnp.sum(ga, axis=0)
    g_updown = jnp.concatenate([mm(third, g_up, 0, 0).astype(BF), mm(g_feed, hidden, 0, 0).astype(BF)], axis=1)
    sum_updown = seq_sum(g_updown.reshape(n, kr, -1))
    g_cross_part = mm(cm, ga_low, 0, 0).astype(BF).reshape(n, 4, own, width)

    dq, dk, dv = attend_back(cq, ck, cv, cprobs, g_cm_own)
    g_second = mm(dq, w_query, 1, 1)
    gas = ga + normback(n2, r2, gain * g_second)
    g_proj = (gate1 * gas).astype(BF)
    g_sm = mm(g_proj, w_out, 1, 1).astype(BF)
    g_sm_abs = [g_sm[:, a * hw : (a + 1) * hw] for a in range(4)]
    g_sm_own = head_sum([pick(g_sm_abs, h ^ j) for j in range(4)], swap_rows).astype(BF)
    g_pair = jnp.concatenate([dk, dv], axis=1)
    g_cap = mm(g_pair, w_pair, 1, 1).astype(BF)
    g_cap_abs = [g_cap[:, a * hw : (a + 1) * hw] for a in range(4)]
    grad_captions = head_sum([pick(g_cap_abs, h ^ j) for j in range(4)])[None]
    gv_gain = jnp.sum(g_second * n2, axis=0)
    gv_gate1 = jnp.sum(gas * self_proj, axis=0)
    gv_self = jnp.sum(g_proj.astype(F32), axis=0)

    def by_head(part):
        return [lax.dynamic_index_in_dim(part, h ^ j, 1, keepdims=False) for j in range(4)]

    g_cross_out = head_sum(by_head(g_cross_part)).astype(BF).reshape(n, -1)
    g_qp = jnp.concatenate([mm(second, dq, 0, 0), mm(caption, g_pair, 0, 0)], axis=1).astype(BF)
    sum_two = seq_sum(jnp.concatenate([g_cross_out, g_qp.reshape(n, -1)], axis=1)[:, None])[0]
    g_out_part = mm(sm, g_proj, 0, 0).astype(BF).reshape(n, 4, own, width)
    g_self_out = head_sum(by_head(g_out_part)).astype(BF).reshape(n, -1)

    dq, dk, dv = attend_back(q, k, v, probs, g_sm_own)
    g_joint = jnp.concatenate([dq, dk, dv], axis=1)
    g_sw = mm(first, g_joint, 0, 0).astype(BF)
    sum_three = seq_sum(jnp.concatenate([g_self_out, g_sw.reshape(n, -1)], axis=1)[:, None])[0]
    g_first = mm(g_joint, w_self, 1, 1)
    gf = (gas + normback(n1, r1, (1.0 + scale1) * g_first)).astype(BF)
    grad_frames = head_sum([gf[j * rows : (j + 1) * rows] for j in range(4)])
    gv_scale1 = jnp.sum(g_first * n1, axis=0)
    gv_shift1 = jnp.sum(g_first, axis=0)

    vec = jnp.concatenate(
        [gv_shift1, gv_scale1, gv_gate1, gv_shift2, gv_scale2, gv_gate2, gv_self, gv_gain, gv_cross, gv_down]
    )[None]
    vec = vec + swap(vec, 1)
    vec = vec + swap(vec, 2)
    every = seq_gather(jnp.concatenate([vec, gv_upbias[None]], axis=1))[:, 0]
    g_mod = every[:, : 6 * width]
    cond_rows = lax.dynamic_slice_in_dim(cond_own, h * own, own, 1).astype(F32)
    grad_mod_weight = lax.dot_general(
        cond_rows, g_mod, (((0,), (0,)), ((), ())), precision=lax.Precision.HIGHEST, preferred_element_type=F32
    )
    sums = every.sum(0)
    place = s * 4 + h
    mb = 6 * width // (4 * n)
    grad_mod_bias = lax.dynamic_slice_in_dim(sums, place * mb, mb, 0)

    def own_vec(i):
        return lax.dynamic_slice_in_dim(sums, (6 + i) * width + place * own, own, 0)

    g_cond_part = lax.dot_general(
        g_mod,
        modulation_weight.astype(F32),
        (((1,), (1,)), ((), ())),
        precision=lax.Precision.HIGHEST,
        preferred_element_type=F32,
    )
    g_silu = lax.all_to_all(g_cond_part[:, None], "seq", split_axis=0, concat_axis=0, tiled=True).reshape(width)
    g_cond = jax.vjp(jax.nn.silu, condition[0].astype(F32))[1](g_silu)[0]
    grad_condition = lax.dynamic_slice_in_dim(g_cond, h * hw, hw, 0)[None]

    cut = own * width
    sum_cross = sum_two[:cut].reshape(own, width)
    sum_out = sum_three[:cut].reshape(own, width)
    cross_cols = jnp.concatenate([sum_two[cut:].reshape(kr, 3 * hw), sum_three[cut:].reshape(kr, 3 * hw)], axis=1)
    spread = lax.all_to_all(
        cross_cols.astype(BF).reshape(4, own, 6 * hw), "head", split_axis=0, concat_axis=0, tiled=True
    ).astype(F32)
    wide = spread.reshape(4, own, 6, hw).transpose(1, 2, 0, 3).reshape(own, 6 * width)
    grad_query, grad_pair, grad_self = wide[:, :width], wide[:, width : 3 * width], wide[:, 3 * width :]
    return (
        output_frames,
        grad_frames,
        grad_condition,
        grad_captions,
        grad_mod_weight,
        grad_mod_bias,
        grad_self,
        sum_out,
        own_vec(0),
        own_vec(1),
        grad_query,
        grad_pair,
        sum_cross,
        own_vec(2),
        sum_updown[:, : up_weight.shape[1]],
        sums[10 * width :],
        sum_updown[:, up_weight.shape[1] :].T,
        own_vec(3),
    )


def solution(mesh):
    both = ("seq", "head")
    return jax.shard_map(
        on_device,
        mesh=mesh,
        in_specs=(
            P(both, None),
            P("seq", None),
            P("seq", None, None),
            P("seq"),
            P("seq", None),
            P("seq"),
            P("seq", None),
            P("seq", None),
            P("seq"),
            P("seq"),
            P("seq", None),
            P("seq", None),
            P("seq", None),
            P("seq"),
            P("seq", "head"),
            P("head"),
            P("head", "seq"),
            P("seq"),
            P(both, None),
        ),
        out_specs=(
            P(both, None),
            P(both, None),
            P("seq", "head"),
            P("seq", None, "head"),
            P(both, None),
            P(both),
            P(both, None),
            P(both, None),
            P(both),
            P(both),
            P(both, None),
            P(both, None),
            P(both, None),
            P(both),
            P("seq", "head"),
            P("head"),
            P("head", "seq"),
            P(both),
        ),
        check_vma=False,
    )
```

time: 1520 us -> 492 us (0.32)
  waiting for transfers between devices: 1070 us -> 162 us
  blocking collectives: 132 us -> 0 us
  other arithmetic: 53.9 us -> 85 us
  starting transfers between devices: 38.6 us -> 66.3 us
  local copies, waits for them, and re-layouts: 98.8 us -> 72.9 us
    reduce_scatter x8 -> x0, waiting for transfers between devices: 637 us -> none  [the longest x1 169 us: on_device(): lax.psum_scatter(grad_modulation_weight, ('seq', 'head'), scatter_dimensi...]
    all_gather x10 -> x1, waiting for transfers between devices: 322 us -> 0.01 us  [on_device(): lax.all_gather(jnp.concatenate([cols(cross_out, 0), up_weight, down_weigh...]
    unnamed x2 -> x0, blocking collectives: 83.6 us -> none
    ppermute x0 -> x41, waiting for transfers between devices: none -> 63.4 us  [swap(): return lax.ppermute(x, 'head', [(i, i ^ bit) for i in range(4)])]
    psum x1 -> x0, blocking collectives: 38 us -> none  [on_device(): sum_up_bias = lax.psum(grad_upbias_part, 'seq')]
    dot_general x51 -> x34, matrix products: 96.6 us -> 70 us  [the longest x22 47.8 us: mm(): lax.dot_general(a, b, (((ca,), (cb,)), ((), ())), preferred_element_type=...]
    convert_element_type x17 -> x19, other arithmetic: 6.26 us -> 31.1 us  [the longest x2 11.5 us: attend(): p = (w / jnp.sum(w, axis=-1, keepdims=True)).astype(BF)]
    ppermute x0 -> x41, starting transfers between devices: none -> 22.8 us  [swap(): return lax.ppermute(x, 'head', [(i, i ^ bit) for i in range(4)])]
  transfers between devices with their start and end apart: 29 -> 52, of which waited for: 23 -> 21; matrix products, arithmetic and copies ran while one was open for 10% -> 33% of each run, Pallas kernels for 0% -> 0%
where the time goes in v1:
time: 492 us; the launch traced here: 486 us
  waiting for transfers between devices  162 us (33%)
  other arithmetic  85 us (17%)
  matrix products  82.6 us (17%)
  local copies, waits for them, and re-layouts  72.9 us (15%)
  starting transfers between devices  66.3 us (13%)
  between operations  17.1 us (3%)
    ppermute x41, waiting for transfers between devices, swap(): return lax.ppermute(x, 'head', [(i, i ^ bit) for i in range(4)])  63.4 us
    all_to_all x4, waiting for transfers between devices, seq_sum(): lax.all_to_all(x, 'seq', split_axis=0, concat_axis=0, tiled=True)  56.1 us
    dot_general x22, matrix products, mm(): lax.dot_general(a, b, (((ca,), (cb,)), ((), ())), preferred_element_type=...  47.8 us
    all_to_all x3, waiting for transfers between devices, seq_gather(): return lax.all_to_all(sent, 'seq', split_axis=0, concat_axis=0, tiled=True)  35.9 us
    unnamed x259, local copies, waits for them, and re-layouts  24.4 us
    ppermute x41, starting transfers between devices, swap(): return lax.ppermute(x, 'head', [(i, i ^ bit) for i in range(4)])  22.8 us
    all_to_all x4, starting transfers between devices, seq_sum(): lax.all_to_all(x, 'seq', split_axis=0, concat_axis=0, tiled=True)  17.5 us
    sub x2, matrix products, attend(): w = jnp.exp(s - jnp.max(s, axis=-1, keepdims=True))  12.7 us
  transfers between devices with their start and end apart: 52, of which 21 were waited for; matrix products, arithmetic and copies ran while one was open for 33% of the time, Pallas kernels for 0%

profile of v1, /device:TPU:0, one launch (start us, length us, event | category | flops | bytes accessed | tf_op | source)
XLA Modules:
  0.0 486.1 jit_solution(13003102243516200275)
XLA Ops:
  10.8 7.3 %all-to-all-start = ((bf16[8,2,240]{2,1,0:T(2,128)(2,1)}), bf16[8,2,240]{2,1,0:T(2,128)(2,1)S(1)}, u32[]{:S(2)}, u32[]{:S(2)}) async-start(bf16[8,2,240]{2,1,0:T(2,128)(2,1)} %reshape.370), calls=%async_computation | async-start | bytes 16384 | tf_op jit(solution)/shard_map/all_to_all | solution.py:135
  18.9 5.7 %all-to-all-done = bf16[8,2,240]{2,1,0:T(2,128)(2,1)S(1)} async-done(((bf16[8,2,240]{2,1,0:T(2,128)(2,1)}), bf16[8,2,240]{2,1,0:T(2,128)(2,1)S(1)}, u32[]{:S(2)}, u32[]{:S(2)}) %all-to-all-start) | async-done | bytes 7712 | tf_op jit(solution)/shard_map/all_to_all | solution.py:135
  31.9 4.6 all-to-all-done.1
  37.5 4.2 all-to-all-start.2
  51.0 24.1 %all-to-all-done.2 = bf16[8,96,576]{2,1,0:T(8,128)(2,1)} async-done(((bf16[8,96,576]{2,1,0:T(8,128)(2,1)}), bf16[8,96,576]{2,1,0:T(8,128)(2,1)}, u32[]{:S(2)}, u32[]{:S(2)}) %all-to-all-start.2) | async-done | bytes 884768 | tf_op jit(solution)/shard_map/all_to_all | solution.py:47
  76.3 4.0 all-to-all-start.3
  84.0 9.8 %fusion.129 = (f32[3,1024]{1,0:T(4,128)S(1)}, f32[3,1024,1024]{1,2,0:T(8,128)}) fusion(bf16[1024,3,64]{0,2,1:T(8,128)(2,1)} %bitcast.181, bf16[1024,3,64]{0,2,1:T(8,128)(2,1)S(1)} %bitcast.179), kind=kOutput, calls=%fused_computation.307 | convolution fusion | flops 412091392 | bytes 13381632 | tf_op jit(solution)/shard_map/sub | solution.py:74
  93.8 9.1 %divide_convert_fusion = bf16[3,1024,1024]{1,2,0:T(8,128)(2,1)} fusion(f32[3,1024,1024]{1,2,0:T(8,128)} %get-tuple-element.259, f32[3,1024]{1,0:T(4,128)S(1)} %get-tuple-element.258), kind=kLoop, calls=%fused_computation.6 | loop fusion | flops 6291456 | bytes 18886656 | tf_op jit(solution)/shard_map/convert_element_type | solution.py:75
  102.9 4.0 convolution_convert_fusion.13
  110.0 4.9 %collective-permute-done.3 = bf16[1024,192]{0,1:T(8,128)(2,1)} collective-permute-done((bf16[1024,192]{0,1:T(8,128)(2,1)S(1)}, bf16[1024,192]{0,1:T(8,128)(2,1)}, u32[]{:S(2)}, u32[]{:S(2)}) %collective-permute-start.3) | collective-permute-done | bytes 393248 | tf_op jit(solution)/shard_map/ppermute | solution.py:16
  118.4 8.0 %all-to-all-done.3 = bf16[8,96,768]{2,1,0:T(8,128)(2,1)S(1)} async-done(((bf16[8,96,768]{2,1,0:T(8,128)(2,1)}), bf16[8,96,768]{2,1,0:T(8,128)(2,1)S(1)}, u32[]{:S(2)}, u32[]{:S(2)}) %all-to-all-start.3) | async-done | bytes 1179680 | tf_op jit(solution)/shard_map/all_to_all | solution.py:47
  131.8 6.3 %collective-permute-done.6 = bf16[768,192]{1,0:T(8,128)(2,1)S(1)} collective-permute-done((bf16[768,192]{1,0:T(8,128)(2,1)S(1)}, bf16[768,192]{1,0:T(8,128)(2,1)S(1)}, u32[]{:S(2)}, u32[]{:S(2)}) %collective-permute-start.6) | collective-permute-done | bytes 294944 | tf_op jit(solution)/shard_map/ppermute | solution.py:16
  158.4 5.4 %collective-permute-done.9 = bf16[1024,192]{0,1:T(8,128)(2,1)} collective-permute-done((bf16[1024,192]{0,1:T(8,128)(2,1)S(1)}, bf16[1024,192]{0,1:T(8,128)(2,1)}, u32[]{:S(2)}, u32[]{:S(2)}) %collective-permute-start.9) | collective-permute-done | bytes 393248 | tf_op jit(solution)/shard_map/ppermute | solution.py:16
  174.9 6.9 %collective-permute-done.12 = bf16[768,192]{1,0:T(8,128)(2,1)S(1)} collective-permute-done((bf16[768,192]{1,0:T(8,128)(2,1)S(1)}, bf16[768,192]{1,0:T(8,128)(2,1)S(1)}, u32[]{:S(2)}, u32[]{:S(2)}) %collective-permute-start.12) | collective-permute-done | bytes 294944 | tf_op jit(solution)/shard_map/ppermute | solution.py:16
  188.4 4.1 convert_reduce_fusion.2
  205.2 7.3 %collective-permute-done.17 = bf16[256,768]{1,0:T(8,128)(2,1)S(1)} collective-permute-done((bf16[256,768]{1,0:T(8,128)(2,1)S(1)}, bf16[256,768]{1,0:T(8,128)(2,1)S(1)}, u32[]{:S(2)}, u32[]{:S(2)}) %collective-permute-start.17) | collective-permute-done | bytes 393248 | tf_op jit(solution)/shard_map/ppermute | solution.py:16
  225.2 7.4 %collective-permute-done.37 = bf16[8,24,768]{2,1,0:T(8,128)(2,1)S(1)} collective-permute-done((bf16[8,24,768]{2,1,0:T(8,128)(2,1)S(1)}, bf16[8,24,768]{2,1,0:T(8,128)(2,1)S(1)}, u32[]{:S(2)}, u32[]{:S(2)}) %collective-permute-start.37) | collective-permute-done | bytes 294944 | tf_op jit(solution)/shard_map/ppermute | solution.py:16
  232.8 7.3 %collective-permute-done.23 = bf16[1024,192]{0,1:T(8,128)(2,1)S(1)} collective-permute-done((bf16[1024,192]{0,1:T(8,128)(2,1)S(1)}, bf16[1024,192]{0,1:T(8,128)(2,1)S(1)}, u32[]{:S(2)}, u32[]{:S(2)}) %collective-permute-start.23) | collective-permute-done | bytes 393248 | tf_op jit(solution)/shard_map/ppermute | solution.py:16
  255.4 9.0 %collective-permute-done.26 = bf16[1024,192]{0,1:T(8,128)(2,1)S(1)} collective-permute-done((bf16[1024,192]{0,1:T(8,128)(2,1)S(1)}, bf16[1024,192]{0,1:T(8,128)(2,1)S(1)}, u32[]{:S(2)}, u32[]{:S(2)}) %collective-permute-start.26) | collective-permute-done | bytes 393248 | tf_op jit(solution)/shard_map/ppermute | solution.py:16
  266.9 6.8 %fusion.2 = (f32[3,1024]{1,0:T(4,128)S(1)}, f32[3,1024,1024]{1,2,0:T(8,128)}) fusion(bf16[3,1024,1024]{1,2,0:T(8,128)(2,1)S(1)} %bitcast.158, bf16[1024,3,64]{0,2,1:T(8,128)(2,1)S(1)} %bitcast.177, bf16[1024,3,64]{0,2,1:T(8,128)(2,1)S(1)} %bitcast.175), kind=kOutput, calls=%fused_computation.4 | convolution fusion | flops 412087296 | bytes 19673088 | tf_op jit(solution)/shard_map/qhd,khd->hqk/dot_general | solution.py:85
  273.7 7.1 %fusion.3 = bf16[3,1024,1024]{1,2,0:T(8,128)(2,1)S(1)} fusion(f32[3,1024,1024]{1,2,0:T(8,128)} %get-tuple-element.272, f32[3,1024]{1,0:T(4,128)S(1)} %get-tuple-element.271, f32[3,1024,1024]{1,2,0:T(8,128)S(1)} %bitcast.160, f32[3,1024]{1,0:T(4,128)S(1)} %copy-done.74), kind=kLoop, calls=%fused_computation.5 | loop fusion | flops 18874368 | bytes 31481856 | tf_op jit(solution)/shard_map/convert_element_type | solution.py:88
  288.2 3.9 multiply_reduce_fusion.3
  303.5 4.3 convolution_convert_fusion.5
  324.2 6.2 %all-to-all-start.6 = ((bf16[8,2,36864]{2,1,0:T(2,128)(2,1)}), bf16[8,2,36864]{2,1,0:T(2,128)(2,1)}, u32[]{:S(2)}, u32[]{:S(2)}) async-start(bf16[8,2,36864]{2,1,0:T(2,128)(2,1)} %reshape.374), calls=%async_computation.6 | async-start | bytes 2359296 | tf_op jit(solution)/shard_map/all_to_all | solution.py:51
  344.6 4.0 convolution_convert_fusion.8
  353.2 6.5 %all-to-all-done.6 = bf16[8,2,36864]{2,1,0:T(2,128)(2,1)} async-done(((bf16[8,2,36864]{2,1,0:T(2,128)(2,1)}), bf16[8,2,36864]{2,1,0:T(2,128)(2,1)}, u32[]{:S(2)}, u32[]{:S(2)}) %all-to-all-start.6) | async-done | bytes 1179680 | tf_op jit(solution)/shard_map/all_to_all | solution.py:51
  372.4 45.0 %all-to-all-done.9 = bf16[8,96,1536]{2,1,0:T(8,128)(2,1)S(1)} async-done(((bf16[8,96,1536]{2,1,0:T(8,128)(2,1)}), bf16[8,96,1536]{2,1,0:T(8,128)(2,1)S(1)}, u32[]{:S(2)}, u32[]{:S(2)}) %all-to-all-start.9) | async-done | bytes 2359328 | tf_op jit(solution)/shard_map/all_to_all | solution.py:51
  417.4 4.3 all-to-all-start.7
  434.8 4.5 collective-permute-done.29
  441.6 5.9 %reshape.375 = bf16[8,1,73728]{2,1,0:T(2,128)(2,1)} reshape(bf16[8,2,36864]{2,1,0:T(2,128)(2,1)} %all-to-all-done.6) | data formatting | bytes 2359296
  447.5 4.8 convert_reduce_fusion.5
  456.3 4.4 reshape.373
  (526 shorter events, 221.9 us)
Async XLA Ops:
  10.8 13.8 %all-to-all-start = ((bf16[8,2,240]{2,1,0:T(2,128)(2,1)}), bf16[8,2,240]{2,1,0:T(2,128)(2,1)S(1)}, u32[]{:S(2)}, u32[]{:S(2)}) async-start(bf16[8,2,240]{2,1,0:T(2,128)(2,1)} %reshape.370), calls=%async_computation | async-start | bytes 16384 | tf_op jit(solution)/shard_map/all_to_all | solution.py:135
  25.7 10.8 %all-to-all-start.1 = ((f32[8,1,4608]{2,1,0:T(1,128)}), f32[8,1,4608]{2,1,0:T(1,128)S(1)}, u32[]{:S(2)}, u32[]{:S(2)}) async-start(f32[8,1,4608]{2,1,0:T(1,128)} %copy.137), calls=%async_computation.1 | async-start | bytes 294912 | tf_op jit(solution)/shard_map/all_to_all | solution.py:51
  29.1 21.0 %collective-permute-start = (bf16[256,768]{1,0:T(8,128)(2,1)}, bf16[256,768]{1,0:T(8,128)(2,1)S(1)}, u32[]{:S(2)}, u32[]{:S(2)}) collective-permute-start(bf16[256,768]{1,0:T(8,128)(2,1)} %param.19), channel_id=1, source_target_pairs={{0,1},{1,0},{2,3},{3,2},{4,5},{5,4},{6,7},{7,6},{8,9},{9,8},{10,11... | collective-permute-start | bytes 1179656 | tf_op jit(solution)/shard_map/ppermute | solution.py:16
  29.2 17.2 %collective-permute-start.1 = (bf16[256,768]{1,0:T(8,128)(2,1)}, bf16[256,768]{1,0:T(8,128)(2,1)S(1)}, u32[]{:S(2)}, u32[]{:S(2)}) collective-permute-start(bf16[256,768]{1,0:T(8,128)(2,1)} %param.19), channel_id=1, source_target_pairs={{0,2},{1,3},{2,0},{3,1},{4,6},{5,7},{6,4},{7,5},{8,10},{9,11},{10,... | collective-permute-start | bytes 1179656 | tf_op jit(solution)/shard_map/ppermute | solution.py:16
  37.5 37.7 %all-to-all-start.2 = ((bf16[8,96,576]{2,1,0:T(8,128)(2,1)}), bf16[8,96,576]{2,1,0:T(8,128)(2,1)}, u32[]{:S(2)}, u32[]{:S(2)}) async-start(bf16[8,96,576]{2,1,0:T(8,128)(2,1)} %broadcast_in_dim.40), calls=%async_computation.2 | async-start | bytes 1966080 | tf_op jit(solution)/shard_map/all_to_all | solution.py:47
  41.8 127.4 %all-gather.2.cloned.1.call-start = ((), (), s32[]{:S(2)}) async-start(), calls=%async_computation.10 | async-start | bytes 3096576 | tf_op jit(solution)/shard_map/all_gather | solution.py:153
  43.8 111.4 %collective-permute-start.19 = (bf16[256,768]{1,0:T(8,128)(2,1)}, bf16[256,768]{1,0:T(8,128)(2,1)}, u32[]{:S(2)}, u32[]{:S(2)}) collective-permute-start(bf16[256,768]{1,0:T(8,128)(2,1)} %param.37), channel_id=1, source_target_pairs={{0,2},{1,3},{2,0},{3,1},{4,6},{5,7},{6,4},{7,5},{8,10},{9,11},{10,... | collective-permute-start | bytes 1179656 | tf_op jit(solution)/shard_map/ppermute | solution.py:16
  76.3 50.2 %all-to-all-start.3 = ((bf16[8,96,768]{2,1,0:T(8,128)(2,1)}), bf16[8,96,768]{2,1,0:T(8,128)(2,1)S(1)}, u32[]{:S(2)}, u32[]{:S(2)}) async-start(bf16[8,96,768]{2,1,0:T(8,128)(2,1)} %broadcast_in_dim.41), calls=%async_computation.3 | async-start | bytes 2359296 | tf_op jit(solution)/shard_map/all_to_all | solution.py:47
  116.7 13.5 %collective-permute-start.4 = (bf16[1024,192]{0,1:T(8,128)(2,1)}, bf16[1024,192]{0,1:T(8,128)(2,1)}, u32[]{:S(2)}, u32[]{:S(2)}) collective-permute-start(bf16[1024,192]{0,1:T(8,128)(2,1)} %pad_maximum_fusion.11), channel_id=1, source_target_pairs={{0,1},{1,0},{2,3},{3,2},{4,5},{5,4},{6,7},{7,6},{8,9},{9,8},{10,11... | collective-permute-start | bytes 1179656 | tf_op jit(solution)/shard_map/ppermute | solution.py:16
  126.5 12.1 %collective-permute-start.8 = (bf16[768,192]{1,0:T(8,128)(2,1)S(1)}, bf16[768,192]{1,0:T(8,128)(2,1)S(1)}, u32[]{:S(2)}, u32[]{:S(2)}) collective-permute-start(bf16[768,192]{1,0:T(8,128)(2,1)S(1)} %slice.236), channel_id=1, source_target_pairs={{0,1},{1,0},{2,3},{3,2},{4,5},{5,4},{6,7},{7,6},{8,9},{9,8},{10,11... | collective-permute-start | bytes 884744 | tf_op jit(solution)/shard_map/ppermute | solution.py:16
  126.6 11.5 %collective-permute-start.6 = (bf16[768,192]{1,0:T(8,128)(2,1)S(1)}, bf16[768,192]{1,0:T(8,128)(2,1)S(1)}, u32[]{:S(2)}, u32[]{:S(2)}) collective-permute-start(bf16[768,192]{1,0:T(8,128)(2,1)S(1)} %slice.236), channel_id=1, source_target_pairs={{0,2},{1,3},{2,0},{3,1},{4,6},{5,7},{6,4},{7,5},{8,10},{9,11},{10,... | collective-permute-start | bytes 884744 | tf_op jit(solution)/shard_map/ppermute | solution.py:16
  152.5 11.3 %collective-permute-start.9 = (bf16[1024,192]{0,1:T(8,128)(2,1)S(1)}, bf16[1024,192]{0,1:T(8,128)(2,1)}, u32[]{:S(2)}, u32[]{:S(2)}) collective-permute-start(bf16[1024,192]{0,1:T(8,128)(2,1)S(1)} %bitcast.163), channel_id=1, source_target_pairs={{0,2},{1,3},{2,0},{3,1},{4,6},{5,7},{6,4},{7,5},{8,10},{9,11},{10,... | collective-permute-start | bytes 1179656 | tf_op jit(solution)/shard_map/ppermute | solution.py:16
  154.0 10.9 %collective-permute-start.18 = (bf16[256,768]{1,0:T(8,128)(2,1)}, bf16[256,768]{1,0:T(8,128)(2,1)}, u32[]{:S(2)}, u32[]{:S(2)}) collective-permute-start(bf16[256,768]{1,0:T(8,128)(2,1)} %param.37), channel_id=1, source_target_pairs={{0,1},{1,0},{2,3},{3,2},{4,5},{5,4},{6,7},{7,6},{8,9},{9,8},{10,11... | collective-permute-start | bytes 1179656 | tf_op jit(solution)/shard_map/ppermute | solution.py:16
  155.2 9.7 %collective-permute-start.20 = (bf16[256,768]{1,0:T(8,128)(2,1)}, bf16[256,768]{1,0:T(8,128)(2,1)}, u32[]{:S(2)}, u32[]{:S(2)}) collective-permute-start(bf16[256,768]{1,0:T(8,128)(2,1)} %collective-permute-done.19), channel_id=1, source_target_pairs={{0,1},{1,0},{2,3},{3,2},{4,5},{5,4},{6,7},{7,6},{8,9},{9,8},{10,11... | collective-permute-start | bytes 1179656 | tf_op jit(solution)/shard_map/ppermute | solution.py:16
  158.4 9.1 %collective-permute-start.11 = (bf16[1024,192]{0,1:T(8,128)(2,1)S(1)}, bf16[1024,192]{0,1:T(8,128)(2,1)S(1)}, u32[]{:S(2)}, u32[]{:S(2)}) collective-permute-start(bf16[1024,192]{0,1:T(8,128)(2,1)S(1)} %bitcast.164), channel_id=1, source_target_pairs={{0,1},{1,0},{2,3},{3,2},{4,5},{5,4},{6,7},{7,6},{8,9},{9,8},{10,11... | collective-permute-start | bytes 1179656 | tf_op jit(solution)/shard_map/ppermute | solution.py:16
  170.3 11.6 %collective-permute-start.12 = (bf16[768,192]{1,0:T(8,128)(2,1)S(1)}, bf16[768,192]{1,0:T(8,128)(2,1)S(1)}, u32[]{:S(2)}, u32[]{:S(2)}) collective-permute-start(bf16[768,192]{1,0:T(8,128)(2,1)S(1)} %slice.244), channel_id=1, source_target_pairs={{0,2},{1,3},{2,0},{3,1},{4,6},{5,7},{6,4},{7,5},{8,10},{9,11},{10,... | collective-permute-start | bytes 884744 | tf_op jit(solution)/shard_map/ppermute | solution.py:16
  201.3 11.2 %collective-permute-start.17 = (bf16[256,768]{1,0:T(8,128)(2,1)S(1)}, bf16[256,768]{1,0:T(8,128)(2,1)S(1)}, u32[]{:S(2)}, u32[]{:S(2)}) collective-permute-start(bf16[256,768]{1,0:T(8,128)(2,1)S(1)} %add_convert_fusion.6), channel_id=1, source_target_pairs={{0,2},{1,3},{2,0},{3,1},{4,6},{5,7},{6,4},{7,5},{8,10},{9,11},{10,... | collective-permute-start | bytes 1179656 | tf_op jit(solution)/shard_map/ppermute | solution.py:16
  222.7 9.9 %collective-permute-start.37 = (bf16[8,24,768]{2,1,0:T(8,128)(2,1)S(1)}, bf16[8,24,768]{2,1,0:T(8,128)(2,1)S(1)}, u32[]{:S(2)}, u32[]{:S(2)}) collective-permute-start(bf16[8,24,768]{2,1,0:T(8,128)(2,1)S(1)} %fusion.60), channel_id=1, source_target_pairs={{0,2},{1,3},{2,0},{3,1},{4,6},{5,7},{6,4},{7,5},{8,10},{9,11},{10,... | collective-permute-start | bytes 884744 | tf_op jit(solution)/shard_map/ppermute | solution.py:16
  224.6 15.5 %collective-permute-start.23 = (bf16[1024,192]{0,1:T(8,128)(2,1)S(1)}, bf16[1024,192]{0,1:T(8,128)(2,1)S(1)}, u32[]{:S(2)}, u32[]{:S(2)}) collective-permute-start(bf16[1024,192]{0,1:T(8,128)(2,1)S(1)} %add_convert_fusion.5), channel_id=1, source_target_pairs={{0,2},{1,3},{2,0},{3,1},{4,6},{5,7},{6,4},{7,5},{8,10},{9,11},{10,... | collective-permute-start | bytes 1179656 | tf_op jit(solution)/shard_map/ppermute | solution.py:16
  253.2 11.2 %collective-permute-start.26 = (bf16[1024,192]{0,1:T(8,128)(2,1)S(1)}, bf16[1024,192]{0,1:T(8,128)(2,1)S(1)}, u32[]{:S(2)}, u32[]{:S(2)}) collective-permute-start(bf16[1024,192]{0,1:T(8,128)(2,1)S(1)} %add_convert_fusion.3), channel_id=1, source_target_pairs={{0,2},{1,3},{2,0},{3,1},{4,6},{5,7},{6,4},{7,5},{8,10},{9,11},{10,... | collective-permute-start | bytes 1179656 | tf_op jit(solution)/shard_map/ppermute | solution.py:16
  298.9 12.7 %all-to-all-start.4 = ((f32[8,1,8448]{2,1,0:T(1,128)}), f32[8,1,8448]{2,1,0:T(1,128)S(1)}, u32[]{:S(2)}, u32[]{:S(2)}) async-start(f32[8,1,8448]{2,1,0:T(1,128)} %broadcast_in_dim.47), calls=%async_computation.4 | async-start | bytes 540672 | tf_op jit(solution)/shard_map/all_to_all | solution.py:47
  313.0 11.1 %all-to-all-start.5 = ((f32[8,1,96]{2,1,0:T(1,128)}), f32[8,1,96]{2,1,0:T(1,128)S(1)}, u32[]{:S(2)}, u32[]{:S(2)}) async-start(f32[8,1,96]{2,1,0:T(1,128)} %bitcast.32), calls=%async_computation.5 | async-start | bytes 8192 | tf_op jit(solution)/shard_map/all_to_all | solution.py:278
  324.2 35.5 %all-to-all-start.6 = ((bf16[8,2,36864]{2,1,0:T(2,128)(2,1)}), bf16[8,2,36864]{2,1,0:T(2,128)(2,1)}, u32[]{:S(2)}, u32[]{:S(2)}) async-start(bf16[8,2,36864]{2,1,0:T(2,128)(2,1)} %reshape.374), calls=%async_computation.6 | async-start | bytes 2359296 | tf_op jit(solution)/shard_map/all_to_all | solution.py:51
  331.9 9.7 %collective-permute-start.38 = (bf16[8,24,768]{2,1,0:T(8,128)(2,1)}, bf16[8,24,768]{2,1,0:T(8,128)(2,1)}, u32[]{:S(2)}, u32[]{:S(2)}) collective-permute-start(bf16[8,24,768]{2,1,0:T(8,128)(2,1)} %get-tuple-element.196), channel_id=1, source_target_pairs={{0,1},{1,0},{2,3},{3,2},{4,5},{5,4},{6,7},{7,6},{8,9},{9,8},{10,11... | collective-permute-start | bytes 884744 | tf_op jit(solution)/shard_map/ppermute | solution.py:16
  333.3 9.3 %collective-permute-start.40 = (bf16[8,24,768]{2,1,0:T(8,128)(2,1)S(1)}, bf16[8,24,768]{2,1,0:T(8,128)(2,1)}, u32[]{:S(2)}, u32[]{:S(2)}) collective-permute-start(bf16[8,24,768]{2,1,0:T(8,128)(2,1)S(1)} %fusion.57), channel_id=1, source_target_pairs={{0,2},{1,3},{2,0},{3,1},{4,6},{5,7},{6,4},{7,5},{8,10},{9,11},{10,... | collective-permute-start | bytes 884744 | tf_op jit(solution)/shard_map/ppermute | solution.py:16
  338.1 83.5 %collective-permute-start.32 = (bf16[256,192]{1,0:T(8,128)(2,1)}, bf16[256,192]{1,0:T(8,128)(2,1)}, u32[]{:S(2)}, u32[]{:S(2)}) collective-permute-start(bf16[256,192]{1,0:T(8,128)(2,1)} %get-tuple-element.206), channel_id=1, source_target_pairs={{0,1},{1,0},{2,3},{3,2},{4,5},{5,4},{6,7},{7,6},{8,9},{9,8},{10,11... | collective-permute-start | bytes 294920 | tf_op jit(solution)/shard_map/ppermute | solution.py:16
  340.1 81.5 %collective-permute-start.34 = (bf16[256,192]{1,0:T(8,128)(2,1)}, bf16[256,192]{1,0:T(8,128)(2,1)}, u32[]{:S(2)}, u32[]{:S(2)}) collective-permute-start(bf16[256,192]{1,0:T(8,128)(2,1)} %add_convert_fusion.7), channel_id=1, source_target_pairs={{0,2},{1,3},{2,0},{3,1},{4,6},{5,7},{6,4},{7,5},{8,10},{9,11},{10,... | collective-permute-start | bytes 294920 | tf_op jit(solution)/shard_map/ppermute | solution.py:16
  353.2 72.4 %collective-permute-start.28 = (bf16[256,768]{1,0:T(8,128)(2,1)}, bf16[256,768]{1,0:T(8,128)(2,1)}, u32[]{:S(2)}, u32[]{:S(2)}) collective-permute-start(bf16[256,768]{1,0:T(8,128)(2,1)} %get-tuple-element.187), channel_id=1, source_target_pairs={{0,1},{1,0},{2,3},{3,2},{4,5},{5,4},{6,7},{7,6},{8,9},{9,8},{10,11... | collective-permute-start | bytes 1179656 | tf_op jit(solution)/shard_map/ppermute | solution.py:16
  359.7 57.7 %all-to-all-start.9 = ((bf16[8,96,1536]{2,1,0:T(8,128)(2,1)}), bf16[8,96,1536]{2,1,0:T(8,128)(2,1)S(1)}, u32[]{:S(2)}, u32[]{:S(2)}) async-start(bf16[8,96,1536]{2,1,0:T(8,128)(2,1)} %bitcast.165), calls=%async_computation.9 | async-start | bytes 4718592 | tf_op jit(solution)/shard_map/all_to_all | solution.py:51
  417.4 38.9 %all-to-all-start.7 = ((bf16[8,2,36864]{2,1,0:T(2,128)(2,1)}), bf16[8,2,36864]{2,1,0:T(2,128)(2,1)}, u32[]{:S(2)}, u32[]{:S(2)}) async-start(bf16[8,2,36864]{2,1,0:T(2,128)(2,1)} %reshape.372), calls=%async_computation.7 | async-start | bytes 2359296 | tf_op jit(solution)/shard_map/all_to_all | solution.py:51
  425.5 9.3 %collective-permute-start.27 = (bf16[256,768]{1,0:T(8,128)(2,1)}, bf16[256,768]{1,0:T(8,128)(2,1)}, u32[]{:S(2)}, u32[]{:S(2)}) collective-permute-start(bf16[256,768]{1,0:T(8,128)(2,1)} %get-tuple-element.186), channel_id=1, source_target_pairs={{0,1},{1,0},{2,3},{3,2},{4,5},{5,4},{6,7},{7,6},{8,9},{9,8},{10,11... | collective-permute-start | bytes 1179656 | tf_op jit(solution)/shard_map/ppermute | solution.py:16
  427.5 11.8 %collective-permute-start.29 = (bf16[256,768]{1,0:T(8,128)(2,1)}, bf16[256,768]{1,0:T(8,128)(2,1)}, u32[]{:S(2)}, u32[]{:S(2)}) collective-permute-start(bf16[256,768]{1,0:T(8,128)(2,1)} %add_convert_fusion.1), channel_id=1, source_target_pairs={{0,2},{1,3},{2,0},{3,1},{4,6},{5,7},{6,4},{7,5},{8,10},{9,11},{10,... | collective-permute-start | bytes 1179656 | tf_op jit(solution)/shard_map/ppermute | solution.py:16
  (140 other events, 1488.6 us)
Sparse Core Ops, SparseCore 0:
  44.8 81.2 all-gather.1

commit v2 on v1

v2 whole, which is shorter than its diff:
```python
import jax
import jax.numpy as jnp
from jax import lax
from jax.experimental import pallas as pl
from jax.experimental.pallas import tpu as pltpu
from jax.sharding import PartitionSpec as P

HD = 64
BF = jnp.bfloat16
F32 = jnp.float32


def mm(a, b, ca=1, cb=0):
    return lax.dot_general(a, b, (((ca,), (cb,)), ((), ())), preferred_element_type=F32)


def swap(x, bit):
    return lax.ppermute(x, "head", [(i, i ^ bit) for i in range(4)])


def swap_rows(x, bit):
    blocks = jnp.split(swap(x, bit), 4, axis=0)
    return jnp.concatenate([blocks[i ^ bit] for i in range(4)], axis=0)


def head_rel(x, swap=swap):
    near = swap(x, 1)
    far = swap(x, 2)
    return [x, near, far, swap(far, 1)]


def pick(parts, index):
    low, high = (index & 1) == 1, (index & 2) == 2
    return jnp.where(
        high, jnp.where(low, parts[3], parts[2]), jnp.where(low, parts[1], parts[0])
    )


def head_sum(chunks, swap=swap):
    a, b = swap(chunks[1], 1), swap(chunks[3], 1)
    mine = chunks[0].astype(F32) + a.astype(F32)
    other = (chunks[2].astype(F32) + b.astype(F32)).astype(chunks[0].dtype)
    return mine + swap(other, 2).astype(F32)


def after(values, ready):
    return lax.optimization_barrier((values, ready))[0]


def seq_swap(x, bit):
    return lax.ppermute(x, "seq", [(i, i ^ bit) for i in range(lax.axis_size("seq"))])


def seq_bits():
    return [1 << b for b in range(lax.axis_size("seq").bit_length() - 1)]


def seq_gather(x):
    for bit in seq_bits():
        x = jnp.concatenate([x, seq_swap(x, bit)], axis=0)
    return x


def seq_scatter_sum(x):
    for bit in reversed(seq_bits()):
        x = x[:bit] + seq_swap(x[bit:], bit)
    return x


def seq_order(x, s):
    n = x.shape[0]
    at = (s ^ jnp.arange(n))[:, None] == jnp.arange(n)[None, :]
    precision = lax.Precision.HIGHEST if x.dtype == F32 else None
    return lax.dot_general(
        at.astype(x.dtype), x, (((1,), (0,)), ((), ())), precision=precision, preferred_element_type=F32
    )


def exchange(x):
    return lax.all_to_all(x, "seq", split_axis=0, concat_axis=0, tiled=True)


def stats(v):
    mean = jnp.mean(v, axis=-1, keepdims=True)
    center = v - mean
    r = lax.rsqrt(jnp.mean(center * center, axis=-1, keepdims=True) + 1e-6)
    return center * r, r


def normback(n, r, e):
    return r * (
        e - jnp.mean(e, axis=-1, keepdims=True) - n * jnp.mean(e * n, axis=-1, keepdims=True)
    )


def whole(x):
    zeros = (0,) * x.ndim
    return pl.BlockSpec(x.shape, lambda i: zeros)


def rows_of(block, width):
    return pl.BlockSpec((block, width), lambda i: (i, 0))


SCALAR = pl.BlockSpec(memory_space=pltpu.SMEM)


def call(kernel, blocks, ins, outs, scratch=()):
    return pl.pallas_call(
        kernel,
        grid=(blocks,),
        in_specs=[spec for _, spec in ins],
        out_specs=[spec for _, spec in outs],
        out_shape=[shape for shape, _ in outs],
        scratch_shapes=list(scratch),
        compiler_params=pltpu.CompilerParams(
            dimension_semantics=("arbitrary",), vmem_limit_bytes=52 * 1024 * 1024
        ),
    )(*[value for value, _ in ins])


def out(shape, dtype, spec=None):
    struct = jax.ShapeDtypeStruct(shape, dtype)
    return struct, whole(struct) if spec is None else spec


def unpack(ref, block, size):
    slab = ref[pl.ds(pl.multiple_of((block // 2) * size, size), size), :]
    half = slab.shape[1] // 2
    return jnp.where(block % 2 == 0, slab[:, :half], slab[:, half:])


def pack(ref, block, size, value):
    half = ref.shape[1] // 2
    place = pl.ds(pl.multiple_of((block // 2) * size, size), size)

    @pl.when(block % 2 == 0)
    def _():
        ref[place, :half] = value

    @pl.when(block % 2 == 1)
    def _():
        ref[place, half:] = value


def take(ref, parts, index):
    for j, part in enumerate(parts):

        @pl.when(index == j)
        def _():
            ref[...] = part[...]


def assemble(ref, parts, head):
    hw = parts[0].shape[-1]
    for a in range(4):
        ref[:, a * hw : (a + 1) * hw] = pick(parts, head ^ a)


def chunks_by_head(value, head):
    hw = value.shape[1] // 4
    blocks = [value[:, a * hw : (a + 1) * hw] for a in range(4)]
    return [pick(blocks, head ^ j) for j in range(4)]


def softmax_columns(keys, queries, values_t, p_ref, inv_ref, visible=None):
    lane = lax.broadcasted_iota(jnp.int32, (1, keys.shape[1]), 1) // HD
    outs = []
    for hd in range(keys.shape[1] // HD):
        st = mm(jnp.where(lane == hd, keys, 0), queries, 1, 1)
        if visible is not None:
            st = jnp.where(visible, st, -1e30)
        e = jnp.exp(st - jnp.max(st, axis=0, keepdims=True))
        inv = 1.0 / jnp.sum(e, axis=0, keepdims=True)
        low = e.astype(BF)
        p_ref[hd] = low
        inv_ref[hd : hd + 1, :] = inv
        outs.append(mm(values_t[hd * HD : (hd + 1) * HD, :], low) * inv)
    return jnp.concatenate(outs, axis=0).T.astype(BF)


def softmax_back(keys, keys_t, values, queries, p_ref, inv_ref, out_low, grad_out, dk_acc, dv_acc):
    width = keys.shape[1]
    lane = lax.broadcasted_iota(jnp.int32, (1, width), 1) // HD
    go_t, o_t = grad_out.T, out_low.astype(F32).T
    heads = width // HD
    scaled, inner = [], []
    for hd in range(heads):
        part = go_t[hd * HD : (hd + 1) * HD, :] * inv_ref[hd : hd + 1, :]
        scaled.append(part)
        inner.append(jnp.sum(part * o_t[hd * HD : (hd + 1) * HD, :], axis=0, keepdims=True))
    go = jnp.concatenate(scaled, axis=0).T.astype(BF)
    grads = []
    dk, dv = 0.0, 0.0
    for hd in range(heads):
        mine = lane == hd
        low = p_ref[hd]
        dp = mm(jnp.where(mine, values, 0), go, 1, 1)
        ds = (low.astype(F32) * (dp - inner[hd])).astype(BF)
        dv = dv + jnp.where(mine, mm(low, go), 0.0)
        dk = dk + jnp.where(mine, mm(ds, queries), 0.0)
        grads.append(mm(keys_t[hd * HD : (hd + 1) * HD, :], ds))
    dk_acc[...] += dk
    dv_acc[...] += dv
    return (jnp.concatenate(grads, axis=0).T * 0.125).astype(BF)


def self_forward(x0, x1, x2, x3, mod, w, first_ref, qkv_ref, sm_ref, p_ref, inv_ref, vt):
    i = pl.program_id(0)
    size, width = x0.shape
    hw = sm_ref.shape[1] // 2

    @pl.when(i == 0)
    def _():
        weights = w[:, : 3 * hw]
        for b, x in enumerate((x0, x1, x2, x3)):
            at = slice(b * size, (b + 1) * size)
            n, _ = stats(x[...].astype(F32))
            first = (n * (1.0 + mod[:, width : 2 * width]) + mod[:, :width]).astype(BF)
            first_ref[at, :] = first
            joint = mm(first, weights)
            qkv_ref[0, at, :] = (joint[:, :hw] * 0.125).astype(BF)
            qkv_ref[1, at, :] = joint[:, hw : 2 * hw].astype(BF)
            qkv_ref[2, at, :] = joint[:, 2 * hw :].astype(BF)
            vt[:, at] = joint[:, 2 * hw :].T.astype(BF)

    queries = qkv_ref[0, pl.ds(pl.multiple_of(i * size, size), size), :]
    pack(sm_ref, i, size, softmax_columns(qkv_ref[1], queries, vt, p_ref, inv_ref))


def cross_forward(
    head, length, x0, x1, x2, x3, sm0, sm1, sm2, sm3, mod, w0, w1, w2, w3, out_bias, gain, w_query, w_pair, caption,
    sm_abs, wout_ref, proj_ref, after_ref, second_ref, cq_ref, pair_ref, cm_ref, p_ref, inv_ref, vt, x,
):
    i, h = pl.program_id(0), head[0]
    size, width = x0.shape
    hw = cq_ref.shape[1]
    take(x, (x0, x1, x2, x3), i)

    @pl.when(i == 0)
    def _():
        assemble(wout_ref, [w[:, :hw] for w in (w0, w1, w2, w3)], h)
        pair = mm(caption[...], w_pair[:, : 2 * hw])
        pair_ref[0] = pair[:, :hw].astype(BF)
        pair_ref[1] = pair[:, hw:].astype(BF)
        vt[...] = pair[:, hw:].T.astype(BF)

    assemble(sm_abs, [unpack(p, i ^ j, size) for j, p in enumerate((sm0, sm1, sm2, sm3))], h)
    proj = mm(sm_abs[...], wout_ref[...]) + out_bias[...]
    proj_ref[...] = proj.astype(BF)
    after = x[...].astype(F32) + mod[:, 2 * width : 3 * width] * proj
    after_ref[...] = after
    n, _ = stats(after)
    second = (n * gain[...]).astype(BF)
    second_ref[...] = second
    queries = (mm(second, w_query[:, 3 * hw :]) * 0.125).astype(BF)
    cq_ref[...] = queries
    slots = lax.broadcasted_iota(jnp.int32, (caption.shape[0], 1), 0)
    pack(cm_ref, i, size, softmax_columns(pair_ref[0], queries, vt, p_ref, inv_ref, slots < length[0]))


def feed_both(
    head, after, cm0, cm1, cm2, cm3, mod, w0, w1, w2, w3, co_bias, w_up, w_down, up_bias, g0, g1, g2, g3,
    cm_abs, wc_ref, across_ref, third_ref, hidden_ref, gup_ref, gfeed_ref, ga_ref, c0, c1, c2, c3, vec_ref, g,
):
    i, h = pl.program_id(0), head[0]
    size, width = after.shape
    hw = width // 4
    take(g, (g0, g1, g2, g3), i)

    @pl.when(i == 0)
    def _():
        assemble(wc_ref, [w[:, hw:] for w in (w0, w1, w2, w3)], h)
        vec_ref[...] = jnp.zeros_like(vec_ref)

    assemble(cm_abs, [unpack(p, i ^ j, size) for j, p in enumerate((cm0, cm1, cm2, cm3))], h)
    across = after[...] + mm(cm_abs[...], wc_ref[...]) + co_bias[...]
    n, r = stats(across)
    scale = 1.0 + mod[:, 4 * width : 5 * width]
    third = (n * scale + mod[:, 3 * width : 4 * width]).astype(BF)
    third_ref[...] = third
    v = mm(third, w_up[...]) + up_bias[...].astype(F32)
    t = jnp.tanh(0.7978845608028654 * (v + 0.044715 * v * v * v))
    hidden_ref[...] = (0.5 * v * (1.0 + t)).astype(BF)
    slope = 0.5 * (1.0 + t) + 0.5 * v * (1.0 - t * t) * (0.7978845608028654 * (1.0 + 0.134145 * v * v))
    grad = g[...].astype(F32)
    gfeed = (mod[:, 5 * width :] * grad).astype(BF)
    gfeed_ref[...] = gfeed
    gup = (mm(gfeed, w_down[...]) * slope).astype(BF)
    gup_ref[...] = gup
    gthird = mm(gup, w_up[...], 1, 1)
    ga = normback(n, r, scale * gthird) + jnp.where(i == 0, grad, 0.0)
    low = ga.astype(BF)
    ga_ref[...] = low
    for j, (ref, chunk) in enumerate(zip((c0, c1, c2, c3), chunks_by_head(mm(low, wc_ref[...], 1, 1).astype(BF), h))):
        pack(ref, i ^ j, size, chunk)

    @pl.when(i == 0)
    def _():
        across_ref[...] = across
        vec_ref[4:5, :] = jnp.sum(gfeed.astype(F32), axis=0, keepdims=True)

    vec_ref[0:1, :] += jnp.sum(gthird, axis=0, keepdims=True)
    vec_ref[1:2, :] += jnp.sum(gthird * n, axis=0, keepdims=True)
    vec_ref[2:3, :] += jnp.sum(ga, axis=0, keepdims=True)
    vec_ref[3:4, :] += jnp.sum(gup.astype(F32), axis=0, keepdims=True)


def cross_back(
    head, a0, a1, a2, cq, p, inv, pair, cm, w_query, ga, after, proj, mod, gain, wout,
    dq_ref, dpair_ref, gas_ref, gproj_ref, c0, c1, c2, c3, vec_ref, kt, dk, dv,
):
    i, h = pl.program_id(0), head[0]
    size, width = after.shape

    @pl.when(i == 0)
    def _():
        vec_ref[...] = jnp.zeros_like(vec_ref)
        dk[...] = jnp.zeros_like(dk)
        dv[...] = jnp.zeros_like(dv)
        kt[...] = pair[0].astype(F32).T.astype(BF)

    grad = sum(unpack(a, i, size).astype(F32) for a in (a0, a1, a2))
    dq = softmax_back(pair[0], kt, pair[1], cq[...], p, inv, unpack(cm, i, size), grad, dk, dv)
    dq_ref[...] = dq
    gsecond = mm(dq, w_query[:, 3 * dq.shape[1] :], 1, 1)
    n, r = stats(after[...])
    gas = ga[...].astype(F32) + normback(n, r, gain[...] * gsecond)
    gas_ref[...] = gas.astype(BF)
    gproj = (mod[:, 2 * width : 3 * width] * gas).astype(BF)
    gproj_ref[...] = gproj
    for j, (ref, chunk) in enumerate(zip((c0, c1, c2, c3), chunks_by_head(mm(gproj, wout[...], 1, 1).astype(BF), h))):
        pack(ref, i ^ j, size, chunk)
    vec_ref[0:1, :] += jnp.sum(gas * proj[...].astype(F32), axis=0, keepdims=True)
    vec_ref[1:2, :] += jnp.sum(gsecond * n, axis=0, keepdims=True)
    vec_ref[2:3, :] += jnp.sum(gproj.astype(F32), axis=0, keepdims=True)

    @pl.when(i == pl.num_programs(0) - 1)
    def _():
        dpair_ref[0] = dk[...].astype(BF)
        dpair_ref[1] = dv[...].astype(BF)


def self_back(a0, a1, a2, qkv, p, inv, sm, grads_ref, kt, dk, dv):
    i = pl.program_id(0)
    size = p.shape[2]
    hw = qkv.shape[2]

    @pl.when(i == 0)
    def _():
        dk[...] = jnp.zeros_like(dk)
        dv[...] = jnp.zeros_like(dv)
        kt[...] = qkv[1].astype(F32).T.astype(BF)

    at = pl.ds(pl.multiple_of(i * size, size), size)
    grad = sum(unpack(a, i, size).astype(F32) for a in (a0, a1, a2))
    grads_ref[at, :hw] = softmax_back(
        qkv[1], kt, qkv[2], qkv[0, at, :], p, inv, unpack(sm, i, size), grad, dk, dv
    )

    @pl.when(i == pl.num_programs(0) - 1)
    def _():
        grads_ref[:, hw : 2 * hw] = dk[...].astype(BF)
        grads_ref[:, 2 * hw :] = dv[...].astype(BF)


def first_back(x0, x1, x2, x3, grads, w, mod, gas, gf_ref, vec_ref, x):
    i = pl.program_id(0)
    width = x0.shape[1]
    take(x, (x0, x1, x2, x3), i)

    @pl.when(i == 0)
    def _():
        vec_ref[...] = jnp.zeros_like(vec_ref)

    gfirst = mm(grads[...], w[:, : grads.shape[1]], 1, 1)
    n, r = stats(x[...].astype(F32))
    scale = 1.0 + mod[:, width : 2 * width]
    gf_ref[...] = (gas[...].astype(F32) + normback(n, r, scale * gfirst)).astype(BF)
    vec_ref[0:1, :] += jnp.sum(gfirst, axis=0, keepdims=True)
    vec_ref[1:2, :] += jnp.sum(gfirst * n, axis=0, keepdims=True)


def own_columns(head, w_self, w_out, w_query, w_pair, w_cross, own_ref):
    h = head[0]
    width = w_out.shape[1]
    hw = width // 4
    places = [(w_self, t * width) for t in range(3)] + [(w_query, 0), (w_pair, 0), (w_pair, width), (w_out, 0), (w_cross, 0)]
    for t, (ref, base) in enumerate(places):
        parts = [ref[:, base + a * hw : base + (a + 1) * hw] for a in range(4)]
        own_ref[:, t * hw : (t + 1) * hw] = pick(parts, h)


def feed_weights(head, third, gup, gfeed, hidden, cm, ga, w_down, both_ref, c0, c1, c2, c3):
    i = pl.program_id(0)
    width = ga.shape[1]
    hw = width // 4
    rows = hidden.shape[0] // 4
    both_ref[:, : gup.shape[1]] = mm(third[...], gup[...], 0, 0).astype(BF)
    both_ref[:, gup.shape[1] :] = mm(gfeed[...], hidden[...], 0, 0).astype(BF)
    chunks = chunks_by_head(mm(cm[...], ga[...], 0, 0).astype(BF), head[0])
    for j, ref in enumerate((c0, c1, c2, c3)):
        for k in range(3):

            @pl.when(i == k)
            def _():
                ref[:, width + k * hw : width + (k + 1) * hw] = chunks[j]

        @pl.when(i == 0)
        def _():
            ref[:, width + 3 * hw :] = jnp.zeros((rows, ref.shape[1] - width - 3 * hw), BF)
            ref[:, :width] = mm(hidden[j * rows : (j + 1) * rows, :], w_down[...], 1, 1).astype(BF)


def mid_weights(head, sm, gproj, second, dq, caption, dpair, w_pair, gcross, mid_ref, c0, c1, c2, c3):
    i = pl.program_id(0)
    hw = dq.shape[1]
    out_chunks = chunks_by_head(mm(sm[...], gproj[...], 0, 0).astype(BF), head[0])
    mid_ref[:, hw : 2 * hw] = mm(second[...], dq[...], 0, 0).astype(BF)
    for t in range(2):
        mid_ref[:, (2 + t) * hw : (3 + t) * hw] = mm(caption[...], dpair[t], 0, 0).astype(BF)
    for k in range(3):

        @pl.when(i == k)
        def _():
            mid_ref[:, :hw] = gcross[:, k * hw : (k + 1) * hw]
            for j, ref in enumerate((c0, c1, c2, c3)):
                ref[:, k * hw : (k + 1) * hw] = out_chunks[j]

    @pl.when(i == 0)
    def _():
        cap = mm(dpair[0], w_pair[:, :hw], 1, 1) + mm(dpair[1], w_pair[:, hw : 2 * hw], 1, 1)
        for ref, chunk in zip((c0, c1, c2, c3), chunks_by_head(cap.astype(BF), head[0])):
            ref[:, 3 * hw :] = chunk


def last_weights(first, gjoint, gout, last_ref):
    i = pl.program_id(0)
    hw = gjoint.shape[1] // 3
    last_ref[:, hw:] = mm(first[...], gjoint[...], 0, 0).astype(BF)
    for k in range(3):

        @pl.when(i == k)
        def _():
            last_ref[:, :hw] = gout[:, k * hw : (k + 1) * hw]


def spread_columns(got, cross_ref, query_ref, pair_ref, out_ref, self_ref):
    hw = got.shape[2] // 8
    for t, (ref, base) in enumerate(
        ((cross_ref, 0), (query_ref, 0), (pair_ref, 0), (pair_ref, 4), (out_ref, 0), (self_ref, 0), (self_ref, 4), (self_ref, 8))
    ):
        for a in range(4):
            ref[:, (base + a) * hw : (base + a + 1) * hw] = got[a, :, t * hw : (t + 1) * hw].astype(F32)


def on_device(
    frames,
    condition,
    captions,
    caption_lengths,
    modulation_weight,
    modulation_bias,
    self_weight,
    self_out,
    self_bias,
    cross_gain,
    cross_query,
    cross_pair,
    cross_out,
    cross_bias,
    up_weight,
    up_bias,
    down_weight,
    down_bias,
    cotangent,
):
    n = lax.axis_size("seq")
    h = lax.axis_index("head")
    s = lax.axis_index("seq")
    rows, width = frames.shape
    hw = width // 4
    kr = self_weight.shape[0]
    own = kr // 4
    total = rows * 4

    ff = up_weight.shape[1]
    head = h.astype(jnp.int32)[None]

    def full(v):
        return v, whole(v)

    (w_own,) = call(
        own_columns,
        1,
        [(head, SCALAR)] + [full(v) for v in (self_weight, self_out, cross_query, cross_pair, cross_out)],
        [out((kr, 8 * hw), BF)],
    )
    w_own = lax.all_gather(w_own, "seq", axis=0, tiled=True)
    small = jnp.concatenate([self_bias, cross_bias, cross_gain, down_bias])[None]
    got = exchange(jnp.concatenate([condition.reshape(n, kr), jnp.broadcast_to(small, (n, 4 * kr))], axis=1))
    cond_own = jax.nn.silu(got[:, :kr].astype(F32)).astype(BF)
    vectors = got[:, kr:].astype(F32).reshape(n, 4, kr).transpose(1, 0, 2).reshape(4, width)
    out_bias, co_bias, gain, dn_bias = vectors[0], vectors[1], vectors[2], vectors[3]
    mod_part = mm(cond_own, modulation_weight) + lax.dynamic_update_slice(
        jnp.zeros((n * modulation_bias.shape[0],), F32),
        modulation_bias.astype(F32),
        (s * modulation_bias.shape[0],),
    )
    mod = exchange(mod_part).sum(0, keepdims=True)
    updown = jnp.concatenate([up_weight, down_weight.T], axis=1)
    updown = jnp.broadcast_to(updown[None], (n, *updown.shape))
    updown = exchange(after(updown, (mod, w_own))).reshape(width, 2 * ff)
    x = head_rel(frames)
    w_parts = head_rel(w_own[:, 6 * hw :])
    g = head_rel(after(cotangent, x[3]))
    two = pl.BlockSpec((width, width), lambda i: (0, 1))
    one = pl.BlockSpec((width, width), lambda i: (0, 0))
    caption = captions[0]
    slots = caption.shape[0]
    heads = hw // HD
    grid, block = 4, rows
    packed = (total // 2, 2 * hw)

    p_spec = pl.BlockSpec((heads, total, block), lambda i: (0, 0, i))
    cp_spec = pl.BlockSpec((heads, slots, block), lambda i: (0, 0, i))
    inv_spec = pl.BlockSpec((heads, block), lambda i: (0, i))
    wide = rows_of(block, width)
    thin = rows_of(block, hw)

    first, qkv, sm_own, probs, inv = call(
        self_forward,
        grid,
        [full(v) for v in (*x, mod)] + [(w_own, one)],
        [
            out((total, width), BF),
            out((3, total, hw), BF),
            out(packed, BF),
            out((heads, total, total), BF, p_spec),
            out((heads, total), F32, inv_spec),
        ],
        [pltpu.VMEM((hw, total), BF)],
    )
    sm_parts = head_rel(sm_own)
    sm, w_out, proj, after_self, second, cq, pair, cm_own, cprobs, cinv = call(
        cross_forward,
        grid,
        [(head, SCALAR), (caption_lengths, SCALAR)]
        + [full(v) for v in (*x, *sm_parts, mod, *w_parts, out_bias[None], gain[None])]
        + [(w_own, one), (w_own, two), full(caption)],
        [
            out((total, width), BF, wide),
            out((width, width), BF),
            out((total, width), BF, wide),
            out((total, width), F32, wide),
            out((total, width), BF, wide),
            out((total, hw), BF, thin),
            out((2, slots, hw), BF),
            out(packed, BF),
            out((heads, slots, total), BF, cp_spec),
            out((heads, total), F32, inv_spec),
        ],
        [pltpu.VMEM((hw, slots), BF), pltpu.VMEM((rows, width), BF)],
    )
    cm_parts = head_rel(cm_own)
    cm, w_cross, across, third, hidden, g_up, g_feed, ga, *chunks, vec_c = call(
        feed_both,
        grid,
        [(head, SCALAR), (after_self, wide)]
        + [full(v) for v in (*cm_parts, mod, *w_parts, co_bias[None])]
        + [(updown, one), (updown, two)]
        + [full(v) for v in (up_bias[None], *g)],
        [
            out((total, width), BF, wide),
            out((width, width), BF),
            out((rows, width), F32),
            out((total, width), BF, wide),
            out((total, ff), BF, rows_of(block, ff)),
            out((total, ff), BF, rows_of(block, ff)),
            out((total, width), BF, wide),
            out((total, width), BF, wide),
            *[out(packed, BF) for _ in range(4)],
            out((8, width), F32),
        ],
        [pltpu.VMEM((rows, width), BF)],
    )

    def near_terms(chunks):
        a, b = swap(chunks[1], 1), swap(chunks[3], 1)
        return chunks[0], a, (chunks[2].astype(F32) + b.astype(F32)).astype(BF)

    mine, near, other = near_terms(chunks)
    far = swap(other, 2)
    third_rows = width // 3
    pad = -3 * hw % 128
    col = pl.BlockSpec((total, third_rows), lambda i: (0, i))
    both, *feed_chunks = call(
        feed_weights,
        3,
        [(head, SCALAR), (after(third, other), col), full(g_up), (g_feed, col), full(hidden), (cm, col), full(ga), (updown, two)],
        [out((width, 2 * ff), BF, rows_of(third_rows, 2 * ff))] + [out((rows, width + 3 * hw + pad), BF) for _ in range(4)],
    )
    both = exchange(both.reshape(n, kr, 2 * ff))
    feed_mine, feed_near, feed_other = near_terms(after(tuple(feed_chunks), far))
    far, feed_other = lax.optimization_barrier((far, feed_other))
    dq, dpair, gas, g_proj, *chunks, vec_d = call(
        cross_back,
        grid,
        [(head, SCALAR)]
        + [full(v) for v in (mine, near, far)]
        + [(cq, thin), (cprobs, cp_spec), (cinv, inv_spec), full(pair), full(cm_own), (w_own, one)]
        + [(ga, wide), (after_self, wide), (proj, wide), full(mod), full(gain[None]), full(w_out)],
        [
            out((total, hw), BF, thin),
            out((2, slots, hw), BF),
            out((total, width), BF, wide),
            out((total, width), BF, wide),
            *[out(packed, BF) for _ in range(4)],
            out((8, width), F32),
        ],
        [pltpu.VMEM((hw, slots), BF), pltpu.VMEM((slots, hw), F32), pltpu.VMEM((slots, hw), F32)],
    )
    feed_sum = feed_mine.astype(F32) + feed_near.astype(F32) + swap(feed_other, 2).astype(F32)
    feed, g_cross = feed_sum[:, :width] + dn_bias, feed_sum[:, width : width + 3 * hw].astype(BF)
    output_frames = (across + mod[:, 5 * width :] * feed).astype(BF)
    gv_gate2 = jnp.sum(cotangent.astype(F32) * feed, axis=0, keepdims=True)
    mine, near, other = near_terms(chunks)
    far = swap(other, 2)
    mid, *out_chunks = call(
        mid_weights,
        3,
        [(head, SCALAR), (after(sm, other), col), full(g_proj), (second, col), full(dq)]
        + [(caption, pl.BlockSpec((slots, third_rows), lambda i: (0, i))), full(dpair), (w_own, two)]
        + [(g_cross, pl.BlockSpec((rows, 3 * hw), lambda i: (0, 0)))],
        [out((width, 4 * hw), BF, rows_of(third_rows, 4 * hw))] + [out((rows, 4 * hw), BF) for _ in range(4)],
    )
    out_mine, out_near, out_other = near_terms(after(tuple(out_chunks), far))
    far, mid, both, out_other = lax.optimization_barrier((far, mid, both, out_other))
    mid = exchange(mid.reshape(n, kr, 4 * hw))
    (g_joint,) = call(
        self_back,
        grid,
        [full(v) for v in (mine, near, far, qkv)]
        + [(probs, p_spec), (inv, inv_spec), full(sm_own)],
        [out((total, 3 * hw), BF)],
        [pltpu.VMEM((hw, total), BF), pltpu.VMEM((total, hw), F32), pltpu.VMEM((total, hw), F32)],
    )
    out_sum = out_mine.astype(F32) + out_near.astype(F32) + swap(out_other, 2).astype(F32)
    grad_captions = out_sum[None, :, 3 * hw :]
    (last,) = call(
        last_weights,
        3,
        [(first, col), full(g_joint), full(out_sum[:, : 3 * hw].astype(BF))],
        [out((width, 4 * hw), BF, rows_of(third_rows, 4 * hw))],
    )
    gas, last = lax.optimization_barrier((gas, last))
    last = exchange(after(last, mid).reshape(n, kr, 4 * hw))
    gf, vec_e = call(
        first_back,
        grid,
        [full(v) for v in x] + [(g_joint, rows_of(block, 3 * hw)), (w_own, one), full(mod), (gas, wide)],
        [out((total, width), BF, wide), out((8, width), F32)],
        [pltpu.VMEM((rows, width), BF)],
    )
    grad_frames = head_sum([gf[j * rows : (j + 1) * rows] for j in range(4)])

    def over_heads(v):
        v = v + swap(v, 1)
        return v + swap(v, 2)

    vec = [vec_e[:2], vec_d[:1], vec_c[:2], gv_gate2, vec_d[2:3], vec_d[1:2], vec_c[2:3], vec_c[4:5]]
    vec = seq_gather(jnp.concatenate([over_heads(jnp.concatenate(vec, axis=0)), vec_c[3:4]], axis=0)[None])
    g_mod = vec[:, :6].reshape(n, 6 * width)
    g_cond = lax.dot_general(
        g_mod,
        modulation_weight.astype(F32),
        (((1,), (1,)), ((), ())),
        precision=lax.Precision.HIGHEST,
        preferred_element_type=F32,
    )
    g_silu = exchange(seq_order(g_cond, s)).reshape(width)
    g_cond = jax.vjp(jax.nn.silu, condition[0].astype(F32))[1](g_silu)[0]
    grad_condition = lax.dynamic_slice_in_dim(g_cond, h * hw, hw, 0)[None]
    cond_rows = seq_order(lax.dynamic_slice_in_dim(cond_own, h * own, own, 1), s)
    grad_mod_weight = lax.dot_general(
        cond_rows, g_mod, (((0,), (0,)), ((), ())), precision=lax.Precision.HIGHEST, preferred_element_type=F32
    )
    sums = vec.sum(0)
    place = s * 4 + h
    mb = 6 * width // (4 * n)
    grad_mod_bias = lax.dynamic_slice_in_dim(sums[:6].reshape(6 * width), place * mb, mb, 0)

    def own_vec(i):
        return lax.dynamic_slice_in_dim(sums[6 + i], place * own, own, 0)

    both = both.astype(F32).sum(0)
    cols = jnp.concatenate([mid.astype(F32).sum(0).astype(BF), last.astype(F32).sum(0).astype(BF)], axis=1)
    cols = lax.all_to_all(cols.reshape(4, own, 8 * hw), "head", split_axis=0, concat_axis=0, tiled=True)
    grad_cross, grad_query, grad_pair, grad_out, grad_self = call(
        spread_columns,
        1,
        [full(cols)],
        [out((own, k * width), F32) for k in (1, 1, 2, 1, 3)],
    )
    return (
        output_frames,
        grad_frames,
        grad_condition,
        grad_captions,
        grad_mod_weight,
        grad_mod_bias,
        grad_self,
        grad_out,
        own_vec(0),
        own_vec(1),
        grad_query,
        grad_pair,
        grad_cross,
        own_vec(2),
        both[:, :ff],
        sums[10],
        both[:, ff:].T,
        own_vec(3),
    )


def solution(mesh):
    both = ("seq", "head")
    return jax.shard_map(
        on_device,
        mesh=mesh,
        in_specs=(
            P(both, None),
            P("seq", None),
            P("seq", None, None),
            P("seq"),
            P("seq", None),
            P("seq"),
            P("seq", None),
            P("seq", None),
            P("seq"),
            P("seq"),
            P("seq", None),
            P("seq", None),
            P("seq", None),
            P("seq"),
            P("seq", "head"),
            P("head"),
            P("head", "seq"),
            P("seq"),
            P(both, None),
        ),
        out_specs=(
            P(both, None),
            P(both, None),
            P("seq", "head"),
            P("seq", None, "head"),
            P(both, None),
            P(both),
            P(both, None),
            P(both, None),
            P(both),
            P(both),
            P(both, None),
            P(both, None),
            P(both, None),
            P(both),
            P("seq", "head"),
            P("head"),
            P("head", "seq"),
            P(both),
        ),
        check_vma=False,
    )
```

time: 492 us -> 361 us (0.73)
  Pallas kernels: 0 us -> 112 us
  matrix products: 82.6 us -> 3.32 us
  other arithmetic: 85 us -> 17.6 us
  local copies, waits for them, and re-layouts: 72.9 us -> 26.2 us
  waiting for transfers between devices: 162 us -> 126 us
  starting transfers between devices: 66.3 us -> 59.6 us
    pallas_call x0 -> x11, Pallas kernels: none -> 112 us  [call(): pl.pallas_call(kernel, grid=(blocks,), in_specs=[spec for _, spec in ins]...]
    all_to_all x10 -> x8, waiting for transfers between devices: 98.8 us -> 34.3 us  [the longest x7 30.1 us: exchange(): return lax.all_to_all(x, 'seq', split_axis=0, concat_axis=0, tiled=True)]
    dot_general x22 -> x1, matrix products: 47.8 us -> 0.23 us  [mm(): lax.dot_general(a, b, (((ca,), (cb,)), ((), ())), preferred_element_type=...]
    all_gather x1, waiting for transfers between devices: 0.01 us -> 28.6 us  [on_device(): w_own = lax.all_gather(w_own, 'seq', axis=0, tiled=True)]
    convert_element_type x10 -> x4, other arithmetic: 23.4 us -> 4.12 us  [near_terms(): return (chunks[0], a, (chunks[2].astype(F32) + b.astype(F32)).astype(BF))]
    dot_general x10 -> x2, matrix products: 18.7 us -> 1 us  [seq_order(): lax.dot_general(at.astype(x.dtype), x, (((1,), (0,)), ((), ())), precisio...]
    reduce_sum x14 -> x8, other arithmetic: 21.4 us -> 6.28 us  [the longest x1 2.48 us: on_device(): gv_gate2 = jnp.sum(cotangent.astype(F32) * feed, axis=0, keepdims=True)]
    unnamed x259 -> x93, local copies, waits for them, and re-layouts: 24.4 us -> 11.5 us
  transfers between devices with their start and end apart: 52 -> 44, of which waited for: 21 -> 22; matrix products, arithmetic and copies ran while one was open for 33% -> 10% of each run, Pallas kernels for 0% -> 21%
where the time goes in v2:
time: 361 us; the launch traced here: 359 us
  waiting for transfers between devices  126 us (35%)
  Pallas kernels  112 us (31%)
  starting transfers between devices  59.6 us (17%)
  local copies, waits for them, and re-layouts  26.2 us (7%)
  other arithmetic  17.6 us (5%)
  between operations  15.4 us (4%)
    pallas_call x11, Pallas kernels, call(): pl.pallas_call(kernel, grid=(blocks,), in_specs=[spec for _, spec in ins]...  112 us
    ppermute x32, waiting for transfers between devices, swap(): return lax.ppermute(x, 'head', [(i, i ^ bit) for i in range(4)])  51.6 us
    all_to_all x7, starting transfers between devices, exchange(): return lax.all_to_all(x, 'seq', split_axis=0, concat_axis=0, tiled=True)  34.1 us
    all_to_all x7, waiting for transfers between devices, exchange(): return lax.all_to_all(x, 'seq', split_axis=0, concat_axis=0, tiled=True)  30.1 us
    all_gather x1, waiting for transfers between devices, on_device(): w_own = lax.all_gather(w_own, 'seq', axis=0, tiled=True)  28.6 us
    ppermute x32, starting transfers between devices, swap(): return lax.ppermute(x, 'head', [(i, i ^ bit) for i in range(4)])  15.1 us
    unnamed x93, local copies, waits for them, and re-layouts  11.5 us
    ppermute x3, waiting for transfers between devices, seq_swap(): lax.ppermute(x, 'seq', [(i, i ^ bit) for i in range(lax.axis_size('seq'))])  11 us
  transfers between devices with their start and end apart: 44, of which 22 were waited for; matrix products, arithmetic and copies ran while one was open for 10% of the time, Pallas kernels for 21%

profile of v2, /device:TPU:0, one launch (start us, length us, event | category | flops | bytes accessed | tf_op | source)
XLA Modules:
  0.0 359.4 jit_solution(14161670792187722944)
XLA Ops:
  15.4 7.3 %all-to-all-start = ((bf16[8,2,240]{2,1,0:T(2,128)(2,1)}), bf16[8,2,240]{2,1,0:T(2,128)(2,1)S(1)}, u32[]{:S(2)}, u32[]{:S(2)}) async-start(bf16[8,2,240]{2,1,0:T(2,128)(2,1)} %reshape.146), calls=%async_computation | async-start | bytes 16384 | tf_op jit(solution)/shard_map/all_to_all | solution.py:80
  22.9 6.5 %all-to-all-done = bf16[8,2,240]{2,1,0:T(2,128)(2,1)S(1)} async-done(((bf16[8,2,240]{2,1,0:T(2,128)(2,1)}), bf16[8,2,240]{2,1,0:T(2,128)(2,1)S(1)}, u32[]{:S(2)}, u32[]{:S(2)}) %all-to-all-start) | async-done | bytes 7712 | tf_op jit(solution)/shard_map/all_to_all | solution.py:80
  30.6 3.4 all-to-all-start.1
  34.0 7.6 %all-to-all-done.1 = f32[8,1,4608]{2,1,0:T(1,128)S(1)} async-done(((f32[8,1,4608]{2,1,0:T(1,128)}), f32[8,1,4608]{2,1,0:T(1,128)S(1)}, u32[]{:S(2)}, u32[]{:S(2)}) %all-to-all-start.1) | async-done | bytes 147488 | tf_op jit(solution)/shard_map/all_to_all | solution.py:80
  41.8 28.6 %all-gather.2.cloned.1.call-done.w.w_query.w_pair = bf16[768,1536]{1,0:T(8,128)(2,1)} async-done(((bf16[96,1536]{1,0:T(8,128)(2,1)}), bf16[768,1536]{1,0:T(8,128)(2,1)}) %all-gather.2.cloned.1.call-update) | async-done | bytes 2359312 | tf_op jit(solution)/shard_map/all_gather | solution.py:499
  72.0 4.5 %all-to-all-start.2 = ((bf16[8,96,1536]{2,1,0:T(8,128)(2,1)}), bf16[8,96,1536]{2,1,0:T(8,128)(2,1)}, u32[]{:S(2)}, u32[]{:S(2)}) async-start(bf16[8,96,1536]{2,1,0:T(8,128)(2,1)} %broadcast_in_dim.42), calls=%async_computation.2 | async-start | bytes 4718592 | tf_op jit(solution)/shard_map/all_to_all | solution.py:80
  78.1 8.2 %collective-permute-done.1.x2 = bf16[256,768]{1,0:T(8,128)(2,1)S(1)} collective-permute-done((bf16[256,768]{1,0:T(8,128)(2,1)S(1)}, bf16[256,768]{1,0:T(8,128)(2,1)S(1)}, u32[]{:S(2)}, u32[]{:S(2)}) %collective-permute-start.1) | collective-permute-done | bytes 393248 | tf_op jit(solution)/shard_map/ppermute | solution.py:18
  89.7 14.6 %shard_map.323 = (bf16[1024,768]{1,0:T(8,128)(2,1)}, bf16[3,1024,192]{2,1,0:T(8,128)(2,1)}, bf16[512,384]{1,0:T(8,128)(2,1)S(1)}, bf16[3,1024,1024]{2,1,0:T(8,128)(2,1)}, f32[3,1024]{1,0:T(4,128)S(1)}) custom-call(bf16[256,768]{1,0:T(8,128)(2,1)S(1)} %copy-done.1, bf16[256,768]{1,0:T(8,128)(2,1)S(1)} %collective-permute-done.x1, ...), custom_call_target="tpu_custom_call" | custom-call | tf_op jit(solution)/shard_map/pallas_call | solution.py:109
  105.3 10.2 %collective-permute-done.4.sm2 = bf16[512,384]{1,0:T(8,128)(2,1)S(1)} collective-permute-done((bf16[512,384]{1,0:T(8,128)(2,1)S(1)}, bf16[512,384]{1,0:T(8,128)(2,1)S(1)}, u32[]{:S(2)}, u32[]{:S(2)}) %collective-permute-start.4) | collective-permute-done | bytes 393248 | tf_op jit(solution)/shard_map/ppermute | solution.py:18
  117.7 15.4 %shard_map.324 = (bf16[1024,768]{1,0:T(8,128)(2,1)}, bf16[768,768]{1,0:T(8,128)(2,1)}, bf16[1024,768]{1,0:T(8,128)(2,1)}, f32[1024,768]{1,0:T(8,128)}, bf16[1024...) custom-call(s32[1]{0:T(128)} %bitcast.head, ...), custom_call_target="tpu_custom_call" | custom-call | tf_op jit(solution)/shard_map/pallas_call | solution.py:109
  135.2 9.3 %collective-permute-done.10.cm2 = bf16[512,384]{1,0:T(8,128)(2,1)S(1)} collective-permute-done((bf16[512,384]{1,0:T(8,128)(2,1)S(1)}, bf16[512,384]{1,0:T(8,128)(2,1)S(1)}, u32[]{:S(2)}, u32[]{:S(2)}) %collective-permute-start.10) | collective-permute-done | bytes 393248 | tf_op jit(solution)/shard_map/ppermute | solution.py:18
  146.4 20.4 %shard_map.325 = (bf16[1024,768]{1,0:T(8,128)(2,1)}, bf16[768,768]{1,0:T(8,128)(2,1)}, f32[256,768]{1,0:T(8,128)}, bf16[1024,768]{1,0:T(8,128)(2,1)}, bf16[1024,...) custom-call(s32[1]{0:T(128)} %bitcast.head, ...), custom_call_target="tpu_custom_call" | custom-call | tf_op jit(solution)/shard_map/pallas_call | solution.py:109
  169.5 12.1 %shard_map.326 = (bf16[768,1536]{1,0:T(8,128)(2,1)}, bf16[256,1408]{1,0:T(8,128)(2,1)S(1)}, bf16[256,1408]{1,0:T(8,128)(2,1)S(1)}, bf16[256,1408]{1,0:T(8,128)(2,1)}, bf16[256,1408]{1,0:T(8,128)(2,1)}) custom-call(s32[1]{0:T(128)} %bitcast.head, bf16[1024,768]{1,0:T(8,128)(2,1)} %get-tuple-element.101.third, bf16[1024,768]{1,0:T(8,128)(2,1)} %get-tuple-element.102.gup, ...), custom_call_target="tpu_custom_call" | custom-call | tf_op jit(solution)/shard_map/pallas_call | solution.py:109
  182.5 5.7 %all-to-all-start.3 = ((bf16[8,96,1536]{2,1,0:T(8,128)(2,1)}), bf16[8,96,1536]{2,1,0:T(8,128)(2,1)}, u32[]{:S(2)}, u32[]{:S(2)}) async-start(bf16[8,96,1536]{2,1,0:T(8,128)(2,1)} %bitcast.49), calls=%async_computation.3 | async-start | bytes 4718592 | tf_op jit(solution)/shard_map/all_to_all | solution.py:80
  189.7 9.6 %collective-permute-done.16.a2 = bf16[512,384]{1,0:T(8,128)(2,1)S(1)} collective-permute-done((bf16[512,384]{1,0:T(8,128)(2,1)}, bf16[512,384]{1,0:T(8,128)(2,1)S(1)}, u32[]{:S(2)}, u32[]{:S(2)}) %collective-permute-start.16) | collective-permute-done | bytes 393248 | tf_op jit(solution)/shard_map/ppermute | solution.py:18
  205.6 16.2 %shard_map.327 = (bf16[1024,192]{1,0:T(8,128)(2,1)}, bf16[2,256,192]{2,1,0:T(8,128)(2,1)S(1)}, bf16[1024,768]{1,0:T(8,128)(2,1)}, bf16[1024,768]{1,0:T(8,128)(2,...) custom-call(s32[1]{0:T(128)} %bitcast.head, ...), custom_call_target="tpu_custom_call" | custom-call | tf_op jit(solution)/shard_map/pallas_call | solution.py:109
  225.9 7.5 %shard_map.328 = (bf16[768,768]{1,0:T(8,128)(2,1)}, bf16[256,768]{1,0:T(8,128)(2,1)S(1)}, bf16[256,768]{1,0:T(8,128)(2,1)S(1)}, bf16[256,768]{1,0:T(8,128)(2,1)S(1)}, bf16[256,768]{1,0:T(8,128)(2,1)}) custom-call(s32[1]{0:T(128)} %bitcast.head, bf16[1024,768]{1,0:T(8,128)(2,1)} %get-tuple-element.130.sm, bf16[1024,768]{1,0:T(8,128)(2,1)} %get-tuple-element.131.gproj, ...), custom_call_target="tpu_custom_call" | custom-call | tf_op jit(solution)/shard_map/pallas_call | solution.py:109
  239.8 2.6 all-to-all-done.3
  244.8 4.5 %all-to-all-start.5 = ((bf16[8,96,768]{2,1,0:T(8,128)(2,1)}), bf16[8,96,768]{2,1,0:T(8,128)(2,1)}, u32[]{:S(2)}, u32[]{:S(2)}) async-start(bf16[8,96,768]{2,1,0:T(8,128)(2,1)} %bitcast.54), calls=%async_computation.5 | async-start | bytes 2359296 | tf_op jit(solution)/shard_map/all_to_all | solution.py:80
  251.8 12.5 %shard_map.329.gjoint.grads = bf16[1024,576]{1,0:T(8,128)(2,1)} custom-call(bf16[512,384]{1,0:T(8,128)(2,1)S(1)} %get-tuple-element.125.a0, bf16[512,384]{1,0:T(8,128)(2,1)} %collective-permute-done.21.a1, bf16[512,384]{1,0:T(8,128)(2,1)S(1)} %copy-done.10, bf16[3,1024,192]{2,1,0:T(8,128)(2,1)} %get-tuple-element.144.qkv, ...), custom_call_target="tpu_custom_call" | custom-call | tf_op jit(solution)/shard_map/pallas_call | solution.py:109
  266.3 4.9 %shard_map.330 = bf16[768,768]{1,0:T(8,128)(2,1)} custom-call(bf16[1024,768]{1,0:T(8,128)(2,1)} %get-tuple-element.148.first, bf16[1024,576]{1,0:T(8,128)(2,1)} %shard_map.329.gjoint.grads, bf16[256,576]{1,0:T(8,128)(2,1)S(1)} %slice.187.gout), custom_call_target="tpu_custom_call" | custom-call | tf_op jit(solution)/shard_map/pallas_call | solution.py:109
  271.2 6.1 %shard_map.331 = (bf16[1024,768]{1,0:T(8,128)(2,1)}, f32[8,768]{1,0:T(8,128)S(1)}) custom-call(bf16[256,768]{1,0:T(8,128)(2,1)S(1)} %copy-done.1, bf16[256,768]{1,0:T(8,128)(2,1)S(1)} %collective-permute-done.x1, bf16[256,768]{1,0:T(8,128)(2,1)S(1)} %collective-permute-done.1.x2, bf16[256,768]{1,0:T(8,128)(2,1)S(1)} %copy-done.3, ...), custom_call_target="tpu_custom_call" | custom-call | tf_op jit(solution)/shard_map/pallas_call | solution.py:109
  279.3 3.5 collective-permute-done.31
  288.7 3.0 collective-permute-done.33
  291.7 3.4 collective-permute-start.34
  295.3 5.6 %collective-permute-done.34 = f32[4,11,768]{2,1,0:T(8,128)S(1)} collective-permute-done((f32[4,11,768]{2,1,0:T(8,128)S(1)}, f32[4,11,768]{2,1,0:T(8,128)S(1)}, u32[]{:S(2)}, u32[]{:S(2)}) %collective-permute-start.34) | collective-permute-done | bytes 135200 | tf_op jit(solution)/shard_map/ppermute | solution.py:51
  302.5 5.3 %all-to-all-start.4 = ((f32[8,1,96]{2,1,0:T(1,128)}), f32[8,1,96]{2,1,0:T(1,128)S(1)}, u32[]{:S(2)}, u32[]{:S(2)}) async-start(f32[8,1,96]{2,1,0:T(1,128)} %bitcast.10), calls=%async_computation.4 | async-start | bytes 8192 | tf_op jit(solution)/shard_map/all_to_all | solution.py:80
  309.8 4.3 %all-to-all-done.4 = f32[8,1,96]{2,1,0:T(1,128)S(1)} async-done(((f32[8,1,96]{2,1,0:T(1,128)}), f32[8,1,96]{2,1,0:T(1,128)S(1)}, u32[]{:S(2)}, u32[]{:S(2)}) %all-to-all-start.4) | async-done | bytes 3104 | tf_op jit(solution)/shard_map/all_to_all | solution.py:80
  314.1 3.6 all-to-all-start.6
  332.0 8.9 %all-to-all-done.6 = bf16[8,96,768]{2,1,0:T(8,128)(2,1)S(1)} async-done(((bf16[8,96,768]{2,1,0:T(8,128)(2,1)}), bf16[8,96,768]{2,1,0:T(8,128)(2,1)S(1)}, u32[]{:S(2)}, u32[]{:S(2)}) %all-to-all-start.6) | async-done | bytes 1179680 | tf_op jit(solution)/shard_map/all_to_all | solution.py:80
  341.8 3.5 all-to-all-start.7
  347.4 4.2 %all-to-all-done.7.got = bf16[4,24,1536]{2,1,0:T(8,128)(2,1)S(1)} async-done(((bf16[4,24,1536]{2,1,0:T(8,128)(2,1)}), bf16[4,24,1536]{2,1,0:T(8,128)(2,1)S(1)}, u32[]{:S(2)}, u32[]{:S(2)}) %all-to-all-start.7) | async-done | bytes 294944 | tf_op jit(solution)/shard_map/all_to_all | solution.py:698
  (236 shorter events, 81.2 us)
Async XLA Ops:
  7.3 63.1 %all-gather.2.cloned.1.call-start = ((), (), s32[]{:S(2)}) async-start(), calls=%async_computation.8 | async-start | bytes 2654208 | tf_op jit(solution)/shard_map/all_gather | solution.py:499
  15.4 14.0 %all-to-all-start = ((bf16[8,2,240]{2,1,0:T(2,128)(2,1)}), bf16[8,2,240]{2,1,0:T(2,128)(2,1)S(1)}, u32[]{:S(2)}, u32[]{:S(2)}) async-start(bf16[8,2,240]{2,1,0:T(2,128)(2,1)} %reshape.146), calls=%async_computation | async-start | bytes 16384 | tf_op jit(solution)/shard_map/all_to_all | solution.py:80
  30.6 11.1 %all-to-all-start.1 = ((f32[8,1,4608]{2,1,0:T(1,128)}), f32[8,1,4608]{2,1,0:T(1,128)S(1)}, u32[]{:S(2)}, u32[]{:S(2)}) async-start(f32[8,1,4608]{2,1,0:T(1,128)} %copy.43), calls=%async_computation.1 | async-start | bytes 294912 | tf_op jit(solution)/shard_map/all_to_all | solution.py:80
  72.0 74.4 %all-to-all-start.2 = ((bf16[8,96,1536]{2,1,0:T(8,128)(2,1)}), bf16[8,96,1536]{2,1,0:T(8,128)(2,1)}, u32[]{:S(2)}, u32[]{:S(2)}) async-start(bf16[8,96,1536]{2,1,0:T(8,128)(2,1)} %broadcast_in_dim.42), calls=%async_computation.2 | async-start | bytes 4718592 | tf_op jit(solution)/shard_map/all_to_all | solution.py:80
  76.5 9.7 %collective-permute-start.1 = (bf16[256,768]{1,0:T(8,128)(2,1)S(1)}, bf16[256,768]{1,0:T(8,128)(2,1)S(1)}, u32[]{:S(2)}, u32[]{:S(2)}) collective-permute-start(bf16[256,768]{1,0:T(8,128)(2,1)S(1)} %copy-done.1), channel_id=1, source_target_pairs={{0,2},{1,3},{2,0},{3,1},{4,6},{5,7},{6,4},{7,5},{8,10},{9,11},{10,... | collective-permute-start | bytes 1179656 | tf_op jit(solution)/shard_map/ppermute | solution.py:18
  78.1 11.6 %collective-permute-start = (bf16[256,768]{1,0:T(8,128)(2,1)S(1)}, bf16[256,768]{1,0:T(8,128)(2,1)S(1)}, u32[]{:S(2)}, u32[]{:S(2)}) collective-permute-start(bf16[256,768]{1,0:T(8,128)(2,1)S(1)} %copy-done.1), channel_id=1, source_target_pairs={{0,1},{1,0},{2,3},{3,2},{4,5},{5,4},{6,7},{7,6},{8,9},{9,8},{10,11... | collective-permute-start | bytes 1179656 | tf_op jit(solution)/shard_map/ppermute | solution.py:18
  88.2 16.6 %collective-permute-start.7 = (bf16[768,384]{1,0:T(8,128)(2,1)}, bf16[768,384]{1,0:T(8,128)(2,1)}, u32[]{:S(2)}, u32[]{:S(2)}) collective-permute-start(bf16[768,384]{1,0:T(8,128)(2,1)} %slice.148.w0), channel_id=1, source_target_pairs={{0,2},{1,3},{2,0},{3,1},{4,6},{5,7},{6,4},{7,5},{8,10},{9,11},{10,... | collective-permute-start | bytes 1769480 | tf_op jit(solution)/shard_map/ppermute | solution.py:18
  104.3 11.2 %collective-permute-start.4 = (bf16[512,384]{1,0:T(8,128)(2,1)S(1)}, bf16[512,384]{1,0:T(8,128)(2,1)S(1)}, u32[]{:S(2)}, u32[]{:S(2)}) collective-permute-start(bf16[512,384]{1,0:T(8,128)(2,1)S(1)} %get-tuple-element.92.sm0.sm), channel_id=1, source_target_pairs={{0,2},{1,3},{2,0},{3,1},{4,6},{5,7},{6,4},{7,5},{8,10},{9,11},{10,... | collective-permute-start | bytes 1179656 | tf_op jit(solution)/shard_map/ppermute | solution.py:18
  104.8 12.9 %collective-permute-start.6 = (bf16[768,384]{1,0:T(8,128)(2,1)}, bf16[768,384]{1,0:T(8,128)(2,1)}, u32[]{:S(2)}, u32[]{:S(2)}) collective-permute-start(bf16[768,384]{1,0:T(8,128)(2,1)} %slice.148.w0), channel_id=1, source_target_pairs={{0,1},{1,0},{2,3},{3,2},{4,5},{5,4},{6,7},{7,6},{8,9},{9,8},{10,11... | collective-permute-start | bytes 1769480 | tf_op jit(solution)/shard_map/ppermute | solution.py:18
  104.8 12.9 %collective-permute-start.8 = (bf16[768,384]{1,0:T(8,128)(2,1)}, bf16[768,384]{1,0:T(8,128)(2,1)}, u32[]{:S(2)}, u32[]{:S(2)}) collective-permute-start(bf16[768,384]{1,0:T(8,128)(2,1)} %collective-permute-done.7.w2), channel_id=1, source_target_pairs={{0,1},{1,0},{2,3},{3,2},{4,5},{5,4},{6,7},{7,6},{8,9},{9,8},{10,11... | collective-permute-start | bytes 1769480 | tf_op jit(solution)/shard_map/ppermute | solution.py:18
  105.3 12.3 %collective-permute-start.3 = (bf16[512,384]{1,0:T(8,128)(2,1)S(1)}, bf16[512,384]{1,0:T(8,128)(2,1)}, u32[]{:S(2)}, u32[]{:S(2)}) collective-permute-start(bf16[512,384]{1,0:T(8,128)(2,1)S(1)} %get-tuple-element.92.sm0.sm), channel_id=1, source_target_pairs={{0,1},{1,0},{2,3},{3,2},{4,5},{5,4},{6,7},{7,6},{8,9},{9,8},{10,11... | collective-permute-start | bytes 1179656 | tf_op jit(solution)/shard_map/ppermute | solution.py:18
  117.1 17.6 %collective-permute-start.13 = (bf16[256,768]{1,0:T(8,128)(2,1)}, bf16[256,768]{1,0:T(8,128)(2,1)}, u32[]{:S(2)}, u32[]{:S(2)}) collective-permute-start(bf16[256,768]{1,0:T(8,128)(2,1)} %g0), channel_id=1, source_target_pairs={{0,2},{1,3},{2,0},{3,1},{4,6},{5,7},{6,4},{7,5},{8,10},{9,11},{10,... | collective-permute-start | bytes 1179656 | tf_op jit(solution)/shard_map/ppermute | solution.py:18
  133.2 11.3 %collective-permute-start.10 = (bf16[512,384]{1,0:T(8,128)(2,1)S(1)}, bf16[512,384]{1,0:T(8,128)(2,1)S(1)}, u32[]{:S(2)}, u32[]{:S(2)}) collective-permute-start(bf16[512,384]{1,0:T(8,128)(2,1)S(1)} %get-tuple-element.94.cm0.cm), channel_id=1, source_target_pairs={{0,2},{1,3},{2,0},{3,1},{4,6},{5,7},{6,4},{7,5},{8,10},{9,11},{10,... | collective-permute-start | bytes 1179656 | tf_op jit(solution)/shard_map/ppermute | solution.py:18
  134.7 9.9 %collective-permute-start.12 = (bf16[256,768]{1,0:T(8,128)(2,1)}, bf16[256,768]{1,0:T(8,128)(2,1)}, u32[]{:S(2)}, u32[]{:S(2)}) collective-permute-start(bf16[256,768]{1,0:T(8,128)(2,1)} %g0), channel_id=1, source_target_pairs={{0,1},{1,0},{2,3},{3,2},{4,5},{5,4},{6,7},{7,6},{8,9},{9,8},{10,11... | collective-permute-start | bytes 1179656 | tf_op jit(solution)/shard_map/ppermute | solution.py:18
  134.7 9.9 %collective-permute-start.14 = (bf16[256,768]{1,0:T(8,128)(2,1)}, bf16[256,768]{1,0:T(8,128)(2,1)}, u32[]{:S(2)}, u32[]{:S(2)}) collective-permute-start(bf16[256,768]{1,0:T(8,128)(2,1)} %collective-permute-done.13.g2), channel_id=1, source_target_pairs={{0,1},{1,0},{2,3},{3,2},{4,5},{5,4},{6,7},{7,6},{8,9},{9,8},{10,11... | collective-permute-start | bytes 1179656 | tf_op jit(solution)/shard_map/ppermute | solution.py:18
  135.2 9.4 %collective-permute-start.9 = (bf16[512,384]{1,0:T(8,128)(2,1)S(1)}, bf16[512,384]{1,0:T(8,128)(2,1)}, u32[]{:S(2)}, u32[]{:S(2)}) collective-permute-start(bf16[512,384]{1,0:T(8,128)(2,1)S(1)} %get-tuple-element.94.cm0.cm), channel_id=1, source_target_pairs={{0,1},{1,0},{2,3},{3,2},{4,5},{5,4},{6,7},{7,6},{8,9},{9,8},{10,11... | collective-permute-start | bytes 1179656 | tf_op jit(solution)/shard_map/ppermute | solution.py:18
  182.5 59.9 %all-to-all-start.3 = ((bf16[8,96,1536]{2,1,0:T(8,128)(2,1)}), bf16[8,96,1536]{2,1,0:T(8,128)(2,1)}, u32[]{:S(2)}, u32[]{:S(2)}) async-start(bf16[8,96,1536]{2,1,0:T(8,128)(2,1)} %bitcast.49), calls=%async_computation.3 | async-start | bytes 4718592 | tf_op jit(solution)/shard_map/all_to_all | solution.py:80
  188.2 11.2 %collective-permute-start.16 = (bf16[512,384]{1,0:T(8,128)(2,1)}, bf16[512,384]{1,0:T(8,128)(2,1)S(1)}, u32[]{:S(2)}, u32[]{:S(2)}) collective-permute-start(bf16[512,384]{1,0:T(8,128)(2,1)} %add_convert_fusion.5), channel_id=1, source_target_pairs={{0,2},{1,3},{2,0},{3,1},{4,6},{5,7},{6,4},{7,5},{8,10},{9,11},{10,... | collective-permute-start | bytes 1179656 | tf_op jit(solution)/shard_map/ppermute | solution.py:18
  199.9 24.6 %collective-permute-start.17 = (bf16[256,1408]{1,0:T(8,128)(2,1)}, bf16[256,1408]{1,0:T(8,128)(2,1)S(1)}, u32[]{:S(2)}, u32[]{:S(2)}) collective-permute-start(bf16[256,1408]{1,0:T(8,128)(2,1)} %copy-done.20), channel_id=1, source_target_pairs={{0,1},{1,0},{2,3},{3,2},{4,5},{5,4},{6,7},{7,6},{8,9},{9,8},{10,11... | collective-permute-start | bytes 2162696 | tf_op jit(solution)/shard_map/ppermute | solution.py:18
  203.3 21.2 %collective-permute-start.19 = (bf16[256,1408]{1,0:T(8,128)(2,1)S(1)}, bf16[256,1408]{1,0:T(8,128)(2,1)S(1)}, u32[]{:S(2)}, u32[]{:S(2)}) collective-permute-start(bf16[256,1408]{1,0:T(8,128)(2,1)S(1)} %add_convert_fusion), channel_id=1, source_target_pairs={{0,2},{1,3},{2,0},{3,1},{4,6},{5,7},{6,4},{7,5},{8,10},{9,11},{10,... | collective-permute-start | bytes 2162696 | tf_op jit(solution)/shard_map/ppermute | solution.py:18
  223.9 11.2 %collective-permute-start.23 = (bf16[512,384]{1,0:T(8,128)(2,1)S(1)}, bf16[512,384]{1,0:T(8,128)(2,1)S(1)}, u32[]{:S(2)}, u32[]{:S(2)}) collective-permute-start(bf16[512,384]{1,0:T(8,128)(2,1)S(1)} %add_convert_fusion.3), channel_id=1, source_target_pairs={{0,2},{1,3},{2,0},{3,1},{4,6},{5,7},{6,4},{7,5},{8,10},{9,11},{10,... | collective-permute-start | bytes 1179656 | tf_op jit(solution)/shard_map/ppermute | solution.py:18
  236.0 15.7 %collective-permute-start.21 = (bf16[512,384]{1,0:T(8,128)(2,1)}, bf16[512,384]{1,0:T(8,128)(2,1)}, u32[]{:S(2)}, u32[]{:S(2)}) collective-permute-start(bf16[512,384]{1,0:T(8,128)(2,1)} %copy-done.21), channel_id=1, source_target_pairs={{0,1},{1,0},{2,3},{3,2},{4,5},{5,4},{6,7},{7,6},{8,9},{9,8},{10,11... | collective-permute-start | bytes 1179656 | tf_op jit(solution)/shard_map/ppermute | solution.py:18
  236.6 27.7 %collective-permute-start.25 = (bf16[256,768]{1,0:T(8,128)(2,1)}, bf16[256,768]{1,0:T(8,128)(2,1)}, u32[]{:S(2)}, u32[]{:S(2)}) collective-permute-start(bf16[256,768]{1,0:T(8,128)(2,1)} %copy-done.22), channel_id=1, source_target_pairs={{0,1},{1,0},{2,3},{3,2},{4,5},{5,4},{6,7},{7,6},{8,9},{9,8},{10,11... | collective-permute-start | bytes 1179656 | tf_op jit(solution)/shard_map/ppermute | solution.py:18
  242.4 21.9 %collective-permute-start.26 = (bf16[256,768]{1,0:T(8,128)(2,1)}, bf16[256,768]{1,0:T(8,128)(2,1)S(1)}, u32[]{:S(2)}, u32[]{:S(2)}) collective-permute-start(bf16[256,768]{1,0:T(8,128)(2,1)} %add_convert_fusion.2), channel_id=1, source_target_pairs={{0,2},{1,3},{2,0},{3,1},{4,6},{5,7},{6,4},{7,5},{8,10},{9,11},{10,... | collective-permute-start | bytes 1179656 | tf_op jit(solution)/shard_map/ppermute | solution.py:18
  244.8 57.7 %all-to-all-start.5 = ((bf16[8,96,768]{2,1,0:T(8,128)(2,1)}), bf16[8,96,768]{2,1,0:T(8,128)(2,1)}, u32[]{:S(2)}, u32[]{:S(2)}) async-start(bf16[8,96,768]{2,1,0:T(8,128)(2,1)} %bitcast.54), calls=%async_computation.5 | async-start | bytes 2359296 | tf_op jit(solution)/shard_map/all_to_all | solution.py:80
  291.7 9.2 %collective-permute-start.34 = (f32[4,11,768]{2,1,0:T(8,128)S(1)}, f32[4,11,768]{2,1,0:T(8,128)S(1)}, u32[]{:S(2)}, u32[]{:S(2)}) collective-permute-start(f32[4,11,768]{2,1,0:T(8,128)S(1)} %pad_maximum_fusion.5), channel_id=1, source_target_pairs={{0,16},{4,20},{8,24},{12,28},{16,0},{20,4},{24,8},{28,12},{1,17},{... | collective-permute-start | bytes 405512 | tf_op jit(solution)/shard_map/ppermute | solution.py:51
  302.5 11.6 %all-to-all-start.4 = ((f32[8,1,96]{2,1,0:T(1,128)}), f32[8,1,96]{2,1,0:T(1,128)S(1)}, u32[]{:S(2)}, u32[]{:S(2)}) async-start(f32[8,1,96]{2,1,0:T(1,128)} %bitcast.10), calls=%async_computation.4 | async-start | bytes 8192 | tf_op jit(solution)/shard_map/all_to_all | solution.py:80
  314.1 26.8 %all-to-all-start.6 = ((bf16[8,96,768]{2,1,0:T(8,128)(2,1)}), bf16[8,96,768]{2,1,0:T(8,128)(2,1)S(1)}, u32[]{:S(2)}, u32[]{:S(2)}) async-start(bf16[8,96,768]{2,1,0:T(8,128)(2,1)} %bitcast.15), calls=%async_computation.6 | async-start | bytes 2359296 | tf_op jit(solution)/shard_map/all_to_all | solution.py:80
  320.6 7.5 %collective-permute-start.28 = (bf16[256,768]{1,0:T(8,128)(2,1)}, bf16[256,768]{1,0:T(8,128)(2,1)}, u32[]{:S(2)}, u32[]{:S(2)}) collective-permute-start(bf16[256,768]{1,0:T(8,128)(2,1)} %get-tuple-element.243), channel_id=1, source_target_pairs={{0,1},{1,0},{2,3},{3,2},{4,5},{5,4},{6,7},{7,6},{8,9},{9,8},{10,11... | collective-permute-start | bytes 1179656 | tf_op jit(solution)/shard_map/ppermute | solution.py:18
  320.6 24.7 %collective-permute-start.27 = (bf16[256,768]{1,0:T(8,128)(2,1)}, bf16[256,768]{1,0:T(8,128)(2,1)}, u32[]{:S(2)}, u32[]{:S(2)}) collective-permute-start(bf16[256,768]{1,0:T(8,128)(2,1)} %get-tuple-element.242), channel_id=1, source_target_pairs={{0,1},{1,0},{2,3},{3,2},{4,5},{5,4},{6,7},{7,6},{8,9},{9,8},{10,11... | collective-permute-start | bytes 1179656 | tf_op jit(solution)/shard_map/ppermute | solution.py:18
  329.3 16.0 %collective-permute-start.29 = (bf16[256,768]{1,0:T(8,128)(2,1)S(1)}, bf16[256,768]{1,0:T(8,128)(2,1)S(1)}, u32[]{:S(2)}, u32[]{:S(2)}) collective-permute-start(bf16[256,768]{1,0:T(8,128)(2,1)S(1)} %add_convert_fusion.1), channel_id=1, source_target_pairs={{0,2},{1,3},{2,0},{3,1},{4,6},{5,7},{6,4},{7,5},{8,10},{9,11},{10,... | collective-permute-start | bytes 1179656 | tf_op jit(solution)/shard_map/ppermute | solution.py:18
  341.8 9.8 %all-to-all-start.7 = ((bf16[4,24,1536]{2,1,0:T(8,128)(2,1)}), bf16[4,24,1536]{2,1,0:T(8,128)(2,1)S(1)}, u32[]{:S(2)}, u32[]{:S(2)}) async-start(bf16[4,24,1536]{2,1,0:T(8,128)(2,1)} %bitcast.16), calls=%async_computation.7 | async-start | bytes 589824 | tf_op jit(solution)/shard_map/all_to_all | solution.py:698
  (56 other events, 455.8 us)
Sparse Core Ops, SparseCore 0:
  13.5 56.8 all-gather.1

commit v3 on v2

--- a/solution.py
+++ b/solution.py
@@ -1,3 +1,5 @@
+from functools import partial
+
 import jax
 import jax.numpy as jnp
 from jax import lax
@@ -78,6 +80,19 @@
 
 def exchange(x):
     return lax.all_to_all(x, "seq", split_axis=0, concat_axis=0, tiled=True)
+
+
+def alike():
+    n = lax.axis_size("seq")
+    return [list(range(odd, n, 2)) for odd in (0, 1)]
+
+
+def half_reduce(near, far):
+    return (near.astype(F32) + seq_swap(far, 1).astype(F32)).astype(BF)
+
+
+def rest_reduce(part):
+    return lax.all_to_all(part, "seq", split_axis=0, concat_axis=0, axis_index_groups=alike(), tiled=True)
 
 
 def stats(v):
@@ -229,7 +244,7 @@
 
 
 def cross_forward(
-    head, length, x0, x1, x2, x3, sm0, sm1, sm2, sm3, mod, w0, w1, w2, w3, out_bias, gain, w_query, w_pair, caption,
+    head, length, x0, x1, x2, x3, sm0, sm1, sm2, sm3, mod, w0, w1, w2, w3, out_bias, gain, w_query, w_rest, caption,
     sm_abs, wout_ref, proj_ref, after_ref, second_ref, cq_ref, pair_ref, cm_ref, p_ref, inv_ref, vt, x,
 ):
     i, h = pl.program_id(0), head[0]
@@ -240,7 +255,7 @@
     @pl.when(i == 0)
     def _():
         assemble(wout_ref, [w[:, :hw] for w in (w0, w1, w2, w3)], h)
-        pair = mm(caption[...], w_pair[:, : 2 * hw])
+        pair = mm(caption[...], w_rest[:, 2 * hw :])
         pair_ref[0] = pair[:, :hw].astype(BF)
         pair_ref[1] = pair[:, hw:].astype(BF)
         vt[...] = pair[:, hw:].T.astype(BF)
@@ -381,18 +396,26 @@
     vec_ref[1:2, :] += jnp.sum(gfirst * n, axis=0, keepdims=True)
 
 
-def own_columns(head, w_self, w_out, w_query, w_pair, w_cross, own_ref):
-    h = head[0]
-    width = w_out.shape[1]
-    hw = width // 4
-    places = [(w_self, t * width) for t in range(3)] + [(w_query, 0), (w_pair, 0), (w_pair, width), (w_out, 0), (w_cross, 0)]
-    for t, (ref, base) in enumerate(places):
-        parts = [ref[:, base + a * hw : base + (a + 1) * hw] for a in range(4)]
-        own_ref[:, t * hw : (t + 1) * hw] = pick(parts, h)
+def own_columns(head, *refs, hw):
+    count = len(refs) // 2 - 1
+    sources, target, held, sems = refs[:count], refs[count], refs[count + 1 : -1], refs[-1]
+    copies = [pltpu.make_async_copy(source, place, sems.at[k]) for k, (source, place) in enumerate(zip(sources, held))]
+    for copy in copies:
+        copy.start()
+    t = 0
+    for copy, ref in zip(copies, held):
+        copy.wait()
+        for base in range(0, ref.shape[1], 4 * hw):
+            part = pick([ref[:, base + a * hw : base + (a + 1) * hw] for a in range(4)], head[0])
+            if len(target.shape) == 2:
+                target[:, t * hw : (t + 1) * hw] = part
+            else:
+                for d in range(target.shape[0]):
+                    target[d, :, t * hw : (t + 1) * hw] = part
+            t += 1
 
 
 def feed_weights(head, third, gup, gfeed, hidden, cm, ga, w_down, both_ref, c0, c1, c2, c3):
-    i = pl.program_id(0)
     width = ga.shape[1]
     hw = width // 4
     rows = hidden.shape[0] // 4
@@ -400,58 +423,63 @@
     both_ref[:, gup.shape[1] :] = mm(gfeed[...], hidden[...], 0, 0).astype(BF)
     chunks = chunks_by_head(mm(cm[...], ga[...], 0, 0).astype(BF), head[0])
     for j, ref in enumerate((c0, c1, c2, c3)):
+        ref[:, :width] = mm(hidden[j * rows : (j + 1) * rows, :], w_down[...], 1, 1).astype(BF)
         for k in range(3):
-
-            @pl.when(i == k)
-            def _():
-                ref[:, width + k * hw : width + (k + 1) * hw] = chunks[j]
-
-        @pl.when(i == 0)
-        def _():
-            ref[:, width + 3 * hw :] = jnp.zeros((rows, ref.shape[1] - width - 3 * hw), BF)
-            ref[:, :width] = mm(hidden[j * rows : (j + 1) * rows, :], w_down[...], 1, 1).astype(BF)
-
-
-def mid_weights(head, sm, gproj, second, dq, caption, dpair, w_pair, gcross, mid_ref, c0, c1, c2, c3):
-    i = pl.program_id(0)
+            ref[:, width + k * hw : width + (k + 1) * hw] = chunks[j][k * rows : (k + 1) * rows]
+        ref[:, width + 3 * hw :] = jnp.zeros((rows, ref.shape[1] - width - 3 * hw), BF)
+
+
+def part_rows(value, odd, near_ref, far_ref, kr):
+    if kr % 16:
+        near_ref[...] = value
+        far_ref[...] = value
+        return
+    for z in range(value.shape[0] // (2 * kr)):
+        even_rows = value[2 * z * kr : (2 * z + 1) * kr]
+        odd_rows = value[(2 * z + 1) * kr : (2 * z + 2) * kr]
+        near_ref[z] = jnp.where(odd == 1, odd_rows, even_rows)
+        far_ref[z] = jnp.where(odd == 1, even_rows, odd_rows)
+
+
+def mid_weights(place, sm, gproj, second, dq, caption, dpair, w_rest, gcross, near_ref, far_ref, c0, c1, c2, c3, *, kr):
     hw = dq.shape[1]
-    out_chunks = chunks_by_head(mm(sm[...], gproj[...], 0, 0).astype(BF), head[0])
-    mid_ref[:, hw : 2 * hw] = mm(second[...], dq[...], 0, 0).astype(BF)
-    for t in range(2):
-        mid_ref[:, (2 + t) * hw : (3 + t) * hw] = mm(caption[...], dpair[t], 0, 0).astype(BF)
-    for k in range(3):
-
-        @pl.when(i == k)
-        def _():
-            mid_ref[:, :hw] = gcross[:, k * hw : (k + 1) * hw]
-            for j, ref in enumerate((c0, c1, c2, c3)):
-                ref[:, k * hw : (k + 1) * hw] = out_chunks[j]
-
-    @pl.when(i == 0)
-    def _():
-        cap = mm(dpair[0], w_pair[:, :hw], 1, 1) + mm(dpair[1], w_pair[:, hw : 2 * hw], 1, 1)
-        for ref, chunk in zip((c0, c1, c2, c3), chunks_by_head(cap.astype(BF), head[0])):
-            ref[:, 3 * hw :] = chunk
-
-
-def last_weights(first, gjoint, gout, last_ref):
-    i = pl.program_id(0)
+    rows = gcross.shape[0]
+    out_chunks = chunks_by_head(mm(sm[...], gproj[...], 0, 0).astype(BF), place[0])
+    cap = mm(dpair[0], w_rest[:, 2 * hw : 3 * hw], 1, 1) + mm(dpair[1], w_rest[:, 3 * hw :], 1, 1)
+    cap_chunks = chunks_by_head(cap.astype(BF), place[0])
+    for ref, out_chunk, cap_chunk in zip((c0, c1, c2, c3), out_chunks, cap_chunks):
+        for k in range(3):
+            ref[:, k * hw : (k + 1) * hw] = out_chunk[k * rows : (k + 1) * rows]
+        ref[:, 3 * hw :] = cap_chunk
+    cross = jnp.concatenate([gcross[:, k * hw : (k + 1) * hw] for k in range(3)], axis=0)
+    parts = [mm(second[...], dq[...], 0, 0)] + [mm(caption[...], dpair[t], 0, 0) for t in range(2)]
+    part_rows(jnp.concatenate([cross] + [p.astype(BF) for p in parts], axis=1), place[1], near_ref, far_ref, kr)
+
+
+def last_weights(place, first, gjoint, gout, near_ref, far_ref, *, kr):
     hw = gjoint.shape[1] // 3
-    last_ref[:, hw:] = mm(first[...], gjoint[...], 0, 0).astype(BF)
-    for k in range(3):
-
-        @pl.when(i == k)
-        def _():
-            last_ref[:, :hw] = gout[:, k * hw : (k + 1) * hw]
-
-
-def spread_columns(got, cross_ref, query_ref, pair_ref, out_ref, self_ref):
-    hw = got.shape[2] // 8
-    for t, (ref, base) in enumerate(
-        ((cross_ref, 0), (query_ref, 0), (pair_ref, 0), (pair_ref, 4), (out_ref, 0), (self_ref, 0), (self_ref, 4), (self_ref, 8))
-    ):
-        for a in range(4):
-            ref[:, (base + a) * hw : (base + a + 1) * hw] = got[a, :, t * hw : (t + 1) * hw].astype(F32)
+    rows = gout.shape[0]
+    cross = jnp.concatenate([gout[:, k * hw : (k + 1) * hw] for k in range(3)], axis=0)
+    value = jnp.concatenate([cross, mm(first[...], gjoint[...], 0, 0).astype(BF)], axis=1)
+    part_rows(value, place[1], near_ref, far_ref, kr)
+
+
+def column_chunks(head, mid, last, *refs):
+    own = refs[0].shape[0]
+    value = jnp.concatenate([jnp.sum(v[...].astype(F32), axis=0) for v in (mid, last)], axis=1)
+    for j, ref in enumerate(refs):
+        ref[...] = pick([value[a * own : (a + 1) * own] for a in range(4)], head[0] ^ j).astype(BF)
+
+
+def spread_columns(head, p0, p1, p2, p3, cross_ref, query_ref, pair_ref, out_ref, self_ref):
+    hw = p0.shape[1] // 8
+    got = [p[...].astype(F32) for p in (p0, p1, p2, p3)]
+    for a in range(4):
+        rows = pick(got, head[0] ^ a)
+        for t, (ref, base) in enumerate(
+            ((cross_ref, 0), (query_ref, 0), (pair_ref, 0), (pair_ref, 4), (out_ref, 0), (self_ref, 0), (self_ref, 4), (self_ref, 8))
+        ):
+            ref[:, (base + a) * hw : (base + a + 1) * hw] = rows[:, t * hw : (t + 1) * hw]
 
 
 def on_device(
@@ -490,15 +518,25 @@
     def full(v):
         return v, whole(v)
 
-    (w_own,) = call(
-        own_columns,
-        1,
-        [(head, SCALAR)] + [full(v) for v in (self_weight, self_out, cross_query, cross_pair, cross_out)],
-        [out((kr, 8 * hw), BF)],
-    )
+    def columns(weights, shape):
+        (own_cols,) = call(
+            partial(own_columns, hw=hw),
+            1,
+            [(head, SCALAR)] + [(v, pl.BlockSpec(memory_space=pltpu.HBM)) for v in weights],
+            [out(shape, BF)],
+            [pltpu.VMEM(v.shape, BF) for v in weights] + [pltpu.SemaphoreType.DMA((len(weights),))],
+        )
+        return own_cols
+
+    w_own = columns((self_weight, cross_query, self_out, cross_out, cross_pair), (kr, 8 * hw))
+    updown = jnp.concatenate([up_weight, down_weight.T], axis=1)
+    condition, updown, w_own = lax.optimization_barrier((condition, updown, w_own))
     w_own = lax.all_gather(w_own, "seq", axis=0, tiled=True)
-    small = jnp.concatenate([self_bias, cross_bias, cross_gain, down_bias])[None]
-    got = exchange(jnp.concatenate([condition.reshape(n, kr), jnp.broadcast_to(small, (n, 4 * kr))], axis=1))
+    one = pl.BlockSpec((width, width), lambda i: (0, 0))
+    two = pl.BlockSpec((width, width), lambda i: (0, 1))
+    x = head_rel(frames)
+    biases = jnp.concatenate([self_bias, cross_bias, cross_gain, down_bias])[None]
+    got = exchange(jnp.concatenate([condition.reshape(n, kr), jnp.broadcast_to(biases, (n, 4 * kr))], axis=1))
     cond_own = jax.nn.silu(got[:, :kr].astype(F32)).astype(BF)
     vectors = got[:, kr:].astype(F32).reshape(n, 4, kr).transpose(1, 0, 2).reshape(4, width)
     out_bias, co_bias, gain, dn_bias = vectors[0], vectors[1], vectors[2], vectors[3]
@@ -507,15 +545,14 @@
         modulation_bias.astype(F32),
         (s * modulation_bias.shape[0],),
     )
+    g = head_rel(cotangent)
+    mod_part, x, g = lax.optimization_barrier((mod_part, x, g))
     mod = exchange(mod_part).sum(0, keepdims=True)
-    updown = jnp.concatenate([up_weight, down_weight.T], axis=1)
-    updown = jnp.broadcast_to(updown[None], (n, *updown.shape))
-    updown = exchange(after(updown, (mod, w_own))).reshape(width, 2 * ff)
-    x = head_rel(frames)
-    w_parts = head_rel(w_own[:, 6 * hw :])
-    g = head_rel(after(cotangent, x[3]))
-    two = pl.BlockSpec((width, width), lambda i: (0, 1))
-    one = pl.BlockSpec((width, width), lambda i: (0, 0))
+    updown, w_own = after((updown, w_own), mod)
+    updown = lax.all_gather(updown, "seq", axis=0, tiled=True)
+    w_parts = w_own[:, 4 * hw : 6 * hw]
+    mod, w_parts = lax.optimization_barrier((mod, w_parts))
+    w_parts = head_rel(w_parts)
     caption = captions[0]
     slots = caption.shape[0]
     heads = hw // HD
@@ -527,6 +564,8 @@
     inv_spec = pl.BlockSpec((heads, block), lambda i: (0, i))
     wide = rows_of(block, width)
     thin = rows_of(block, hw)
+    up_spec = pl.BlockSpec((width, ff), lambda i: (0, 0))
+    down_spec = pl.BlockSpec((width, ff), lambda i: (0, 1))
 
     first, qkv, sm_own, probs, inv = call(
         self_forward,
@@ -568,7 +607,7 @@
         grid,
         [(head, SCALAR), (after_self, wide)]
         + [full(v) for v in (*cm_parts, mod, *w_parts, co_bias[None])]
-        + [(updown, one), (updown, two)]
+        + [(updown, up_spec), (updown, down_spec)]
         + [full(v) for v in (up_bias[None], *g)],
         [
             out((total, width), BF, wide),
@@ -591,16 +630,31 @@
 
     mine, near, other = near_terms(chunks)
     far = swap(other, 2)
-    third_rows = width // 3
     pad = -3 * hw % 128
-    col = pl.BlockSpec((total, third_rows), lambda i: (0, i))
+    place = jnp.stack([h, s & 1]).astype(jnp.int32)
+
+    def halves(columns):
+        shape = (width, columns) if kr % 16 else (n // 2, kr, columns)
+        return [out(shape, BF) for _ in range(2)]
+
+    def parted(near_rows, far_rows):
+        if kr % 16 == 0:
+            return near_rows, far_rows
+        near_rows, far_rows = (v.reshape(n // 2, 2, kr, -1) for v in (near_rows, far_rows))
+        return (
+            lax.dynamic_index_in_dim(near_rows, s & 1, 1, keepdims=False),
+            lax.dynamic_index_in_dim(far_rows, 1 - (s & 1), 1, keepdims=False),
+        )
+
     both, *feed_chunks = call(
         feed_weights,
-        3,
-        [(head, SCALAR), (after(third, other), col), full(g_up), (g_feed, col), full(hidden), (cm, col), full(ga), (updown, two)],
-        [out((width, 2 * ff), BF, rows_of(third_rows, 2 * ff))] + [out((rows, width + 3 * hw + pad), BF) for _ in range(4)],
-    )
-    both = exchange(both.reshape(n, kr, 2 * ff))
+        1,
+        [(head, SCALAR)]
+        + [full(v) for v in (after(third, other), g_up, g_feed, hidden, cm, ga)]
+        + [(updown, down_spec)],
+        [out((width, 2 * ff), BF)] + [out((rows, width + 3 * hw + pad), BF) for _ in range(4)],
+    )
+    both = exchange(after(both, far).reshape(n, kr, 2 * ff))
     feed_mine, feed_near, feed_other = near_terms(after(tuple(feed_chunks), far))
     far, feed_other = lax.optimization_barrier((far, feed_other))
     dq, dpair, gas, g_proj, *chunks, vec_d = call(
@@ -621,22 +675,22 @@
         [pltpu.VMEM((hw, slots), BF), pltpu.VMEM((slots, hw), F32), pltpu.VMEM((slots, hw), F32)],
     )
     feed_sum = feed_mine.astype(F32) + feed_near.astype(F32) + swap(feed_other, 2).astype(F32)
-    feed, g_cross = feed_sum[:, :width] + dn_bias, feed_sum[:, width : width + 3 * hw].astype(BF)
-    output_frames = (across + mod[:, 5 * width :] * feed).astype(BF)
-    gv_gate2 = jnp.sum(cotangent.astype(F32) * feed, axis=0, keepdims=True)
+    chunks, feed_sum = lax.optimization_barrier((chunks, feed_sum))
+    g_cross = feed_sum[:, width : width + 3 * hw].astype(BF)
     mine, near, other = near_terms(chunks)
     far = swap(other, 2)
-    mid, *out_chunks = call(
-        mid_weights,
-        3,
-        [(head, SCALAR), (after(sm, other), col), full(g_proj), (second, col), full(dq)]
-        + [(caption, pl.BlockSpec((slots, third_rows), lambda i: (0, i))), full(dpair), (w_own, two)]
-        + [(g_cross, pl.BlockSpec((rows, 3 * hw), lambda i: (0, 0)))],
-        [out((width, 4 * hw), BF, rows_of(third_rows, 4 * hw))] + [out((rows, 4 * hw), BF) for _ in range(4)],
-    )
+    *mid, out0, out1, out2, out3 = call(
+        partial(mid_weights, kr=kr),
+        1,
+        [(place, SCALAR)]
+        + [full(v) for v in (after(sm, other), g_proj, second, dq, caption, dpair)]
+        + [(w_own, two), full(g_cross)],
+        halves(4 * hw) + [out((rows, 4 * hw), BF) for _ in range(4)],
+    )
+    out_chunks = (out0, out1, out2, out3)
     out_mine, out_near, out_other = near_terms(after(tuple(out_chunks), far))
-    far, mid, both, out_other = lax.optimization_barrier((far, mid, both, out_other))
-    mid = exchange(mid.reshape(n, kr, 4 * hw))
+    far, mid, out_other = lax.optimization_barrier((far, mid, out_other))
+    mid = half_reduce(*parted(*mid))
     (g_joint,) = call(
         self_back,
         grid,
@@ -645,16 +699,21 @@
         [out((total, 3 * hw), BF)],
         [pltpu.VMEM((hw, total), BF), pltpu.VMEM((total, hw), F32), pltpu.VMEM((total, hw), F32)],
     )
+    feed_sum = after(feed_sum, g_joint)
+    feed = feed_sum[:, :width] + dn_bias
+    output_frames = (across + mod[:, 5 * width :] * feed).astype(BF)
+    gv_gate2 = jnp.sum(cotangent.astype(F32) * feed, axis=0, keepdims=True)
     out_sum = out_mine.astype(F32) + out_near.astype(F32) + swap(out_other, 2).astype(F32)
     grad_captions = out_sum[None, :, 3 * hw :]
-    (last,) = call(
-        last_weights,
-        3,
-        [(first, col), full(g_joint), full(out_sum[:, : 3 * hw].astype(BF))],
-        [out((width, 4 * hw), BF, rows_of(third_rows, 4 * hw))],
-    )
-    gas, last = lax.optimization_barrier((gas, last))
-    last = exchange(after(last, mid).reshape(n, kr, 4 * hw))
+    last = call(
+        partial(last_weights, kr=kr),
+        1,
+        [(place, SCALAR)] + [full(v) for v in (first, after(g_joint, mid), out_sum[:, : 3 * hw].astype(BF))],
+        halves(4 * hw),
+    )
+    gas, last, both = lax.optimization_barrier((gas, last, both))
+    last = half_reduce(*parted(*last))
+    mid = rest_reduce(after(mid, both))
     gf, vec_e = call(
         first_back,
         grid,
@@ -662,6 +721,8 @@
         [out((total, width), BF, wide), out((8, width), F32)],
         [pltpu.VMEM((rows, width), BF)],
     )
+    vec_e, gf, last = lax.optimization_barrier((vec_e, gf, last))
+    last = rest_reduce(after(last, mid))
     grad_frames = head_sum([gf[j * rows : (j + 1) * rows] for j in range(4)])
 
     def over_heads(v):
@@ -678,7 +739,7 @@
         precision=lax.Precision.HIGHEST,
         preferred_element_type=F32,
     )
-    g_silu = exchange(seq_order(g_cond, s)).reshape(width)
+    g_silu = exchange(after(seq_order(g_cond, s), last)).reshape(width)
     g_cond = jax.vjp(jax.nn.silu, condition[0].astype(F32))[1](g_silu)[0]
     grad_condition = lax.dynamic_slice_in_dim(g_cond, h * hw, hw, 0)[None]
     cond_rows = seq_order(lax.dynamic_slice_in_dim(cond_own, h * own, own, 1), s)
@@ -686,20 +747,24 @@
         cond_rows, g_mod, (((0,), (0,)), ((), ())), precision=lax.Precision.HIGHEST, preferred_element_type=F32
     )
     sums = vec.sum(0)
-    place = s * 4 + h
+    index = s * 4 + h
     mb = 6 * width // (4 * n)
-    grad_mod_bias = lax.dynamic_slice_in_dim(sums[:6].reshape(6 * width), place * mb, mb, 0)
+    grad_mod_bias = lax.dynamic_slice_in_dim(sums[:6].reshape(6 * width), index * mb, mb, 0)
 
     def own_vec(i):
-        return lax.dynamic_slice_in_dim(sums[6 + i], place * own, own, 0)
+        return lax.dynamic_slice_in_dim(sums[6 + i], index * own, own, 0)
 
     both = both.astype(F32).sum(0)
-    cols = jnp.concatenate([mid.astype(F32).sum(0).astype(BF), last.astype(F32).sum(0).astype(BF)], axis=1)
-    cols = lax.all_to_all(cols.reshape(4, own, 8 * hw), "head", split_axis=0, concat_axis=0, tiled=True)
+    cols = call(
+        column_chunks, 1, [(head, SCALAR), full(mid), full(last)], [out((own, 8 * hw), BF) for _ in range(4)]
+    )
+    cols = [cols[0]] + [
+        lax.ppermute(cols[j], "head", [(i, i ^ j) for i in range(4)]) for j in range(1, 4)
+    ]
     grad_cross, grad_query, grad_pair, grad_out, grad_self = call(
         spread_columns,
         1,
-        [full(cols)],
+        [(head, SCALAR)] + [full(v) for v in cols],
         [out((own, k * width), F32) for k in (1, 1, 2, 1, 3)],
     )
     return (

time: 361 us -> 319 us (0.88)
  waiting for transfers between devices: 126 us -> 83.8 us
  blocking collectives: 0 us -> 16 us
  starting transfers between devices: 59.6 us -> 51.1 us
  local copies, waits for them, and re-layouts: 26.2 us -> 20.8 us
    all_to_all x7 -> x3, waiting for transfers between devices: 30.1 us -> 1.97 us  [exchange(): return lax.all_to_all(x, 'seq', split_axis=0, concat_axis=0, tiled=True)]
    all_to_all x7 -> x3, starting transfers between devices: 34.1 us -> 15 us  [exchange(): return lax.all_to_all(x, 'seq', split_axis=0, concat_axis=0, tiled=True)]
    all_to_all x0 -> x1, blocking collectives: none -> 16 us  [exchange(): return lax.all_to_all(x, 'seq', split_axis=0, concat_axis=0, tiled=True)]
    all_gather x1, waiting for transfers between devices: 28.6 us -> 17.9 us  [on_device(): w_own = lax.all_gather(w_own, 'seq', axis=0, tiled=True)]
    ppermute x32, waiting for transfers between devices: 51.6 us -> 42.6 us  [swap(): return lax.ppermute(x, 'head', [(i, i ^ bit) for i in range(4)])]
    ppermute x3 -> x5, starting transfers between devices: 6.83 us -> 12.4 us  [seq_swap(): lax.ppermute(x, 'seq', [(i, i ^ bit) for i in range(lax.axis_size('seq'))])]
    ppermute x3 -> x5, waiting for transfers between devices: 11 us -> 16 us  [seq_swap(): lax.ppermute(x, 'seq', [(i, i ^ bit) for i in range(lax.axis_size('seq'))])]
    pallas_call x11 -> x12, Pallas kernels: 112 us -> 109 us  [call(): pl.pallas_call(kernel, grid=(blocks,), in_specs=[spec for _, spec in ins]...]
  transfers between devices with their start and end apart: 44 -> 47, of which waited for: 22 -> 22; matrix products, arithmetic and copies ran while one was open for 10% -> 10% of each run, Pallas kernels for 21% -> 27%
where the time goes in v3:
time: 319 us; the launch traced here: 318 us
  Pallas kernels  109 us (34%)
  waiting for transfers between devices  83.8 us (26%)
  starting transfers between devices  51.1 us (16%)
  local copies, waits for them, and re-layouts  20.8 us (7%)
  other arithmetic  18.7 us (6%)
  blocking collectives  16 us (5%)
  between operations  15.4 us (5%)
  matrix products  3.28 us (1%)
    pallas_call x12, Pallas kernels, call(): pl.pallas_call(kernel, grid=(blocks,), in_specs=[spec for _, spec in ins]...  109 us
    ppermute x32, waiting for transfers between devices, swap(): return lax.ppermute(x, 'head', [(i, i ^ bit) for i in range(4)])  42.6 us
    all_gather x1, waiting for transfers between devices, on_device(): w_own = lax.all_gather(w_own, 'seq', axis=0, tiled=True)  17.9 us
    ppermute x5, waiting for transfers between devices, seq_swap(): lax.ppermute(x, 'seq', [(i, i ^ bit) for i in range(lax.axis_size('seq'))])  16 us
    all_to_all x1, blocking collectives, exchange(): return lax.all_to_all(x, 'seq', split_axis=0, concat_axis=0, tiled=True)  16 us
    all_to_all x3, starting transfers between devices, exchange(): return lax.all_to_all(x, 'seq', split_axis=0, concat_axis=0, tiled=True)  15 us
    ppermute x32, starting transfers between devices, swap(): return lax.ppermute(x, 'head', [(i, i ^ bit) for i in range(4)])  14.6 us
    ppermute x5, starting transfers between devices, seq_swap(): lax.ppermute(x, 'seq', [(i, i ^ bit) for i in range(lax.axis_size('seq'))])  12.4 us
  transfers between devices with their start and end apart: 47, of which 22 were waited for; matrix products, arithmetic and copies ran while one was open for 10% of the time, Pallas kernels for 27%

profile of v3, /device:TPU:0, one launch (start us, length us, event | category | flops | bytes accessed | tf_op | source)
XLA Modules:
  0.0 318.0 jit_solution(1938648830493389949)
XLA Ops:
  13.8 2.3 shard_map.322
  16.2 3.0 collective-permute-start.1
  21.9 6.3 %all-to-all-start = ((bf16[8,2,240]{2,1,0:T(2,128)(2,1)}), bf16[8,2,240]{2,1,0:T(2,128)(2,1)S(1)}, u32[]{:S(2)}, u32[]{:S(2)}) async-start(bf16[8,2,240]{2,1,0:T(2,128)(2,1)} %reshape.129), calls=%async_computation | async-start | bytes 16384 | tf_op jit(solution)/shard_map/all_to_all | solution.py:82
  29.2 7.6 %collective-permute-done.4.g2 = bf16[256,768]{1,0:T(8,128)(2,1)S(1)} collective-permute-done((bf16[256,768]{1,0:T(8,128)(2,1)S(1)}, bf16[256,768]{1,0:T(8,128)(2,1)S(1)}, u32[]{:S(2)}, u32[]{:S(2)}) %collective-permute-start.4) | collective-permute-done | bytes 393248 | tf_op jit(solution)/shard_map/ppermute | solution.py:20
  38.8 16.0 %all_to_all.45 = f32[8,1,4608]{2,1,0:T(1,128)S(1)} all-to-all(f32[8,1,4608]{2,1,0:T(1,128)S(1)} %copy.43), channel_id=1, replica_groups=mesh['seq'=8,'head'=4] {'seq'}, dimensions={0} | all-to-all | bytes 294912 | tf_op jit(solution)/shard_map/all_to_all | solution.py:82
  54.9 17.9 %all-gather.3.cloned.1.call-done.w.w_query.w_rest = bf16[768,1536]{1,0:T(8,128)(2,1)} async-done(((bf16[96,1536]{1,0:T(8,128)(2,1)}), bf16[768,1536]{1,0:T(8,128)(2,1)}) %all-gather.3.cloned.1.call-update) | async-done | bytes 2359312 | tf_op jit(solution)/shard_map/all_gather | solution.py:534
  75.4 14.4 %shard_map.323 = (bf16[1024,768]{1,0:T(8,128)(2,1)}, bf16[3,1024,192]{2,1,0:T(8,128)(2,1)}, bf16[512,384]{1,0:T(8,128)(2,1)S(1)}, bf16[3,1024,1024]{2,1,0:T(8,128)(2,1)}, f32[3,1024]{1,0:T(4,128)S(1)}) custom-call(bf16[256,768]{1,0:T(8,128)(2,1)S(1)} %copy-done.1, bf16[256,768]{1,0:T(8,128)(2,1)S(1)} %collective-permute-done.x1, ...), custom_call_target="tpu_custom_call" | custom-call | tf_op jit(solution)/shard_map/pallas_call | solution.py:124
  91.1 9.0 %collective-permute-done.7.sm2 = bf16[512,384]{1,0:T(8,128)(2,1)} collective-permute-done((bf16[512,384]{1,0:T(8,128)(2,1)S(1)}, bf16[512,384]{1,0:T(8,128)(2,1)}, u32[]{:S(2)}, u32[]{:S(2)}) %collective-permute-start.7) | collective-permute-done | bytes 393248 | tf_op jit(solution)/shard_map/ppermute | solution.py:20
  102.2 15.4 %shard_map.324 = (bf16[1024,768]{1,0:T(8,128)(2,1)}, bf16[768,768]{1,0:T(8,128)(2,1)}, bf16[1024,768]{1,0:T(8,128)(2,1)}, f32[1024,768]{1,0:T(8,128)}, bf16[1024...) custom-call(s32[1]{0:T(128)} %bitcast.head, ...), custom_call_target="tpu_custom_call" | custom-call | tf_op jit(solution)/shard_map/pallas_call | solution.py:124
  118.3 10.6 %collective-permute-done.13.cm2 = bf16[512,384]{1,0:T(8,128)(2,1)S(1)} collective-permute-done((bf16[512,384]{1,0:T(8,128)(2,1)S(1)}, bf16[512,384]{1,0:T(8,128)(2,1)S(1)}, u32[]{:S(2)}, u32[]{:S(2)}) %collective-permute-start.13) | collective-permute-done | bytes 393248 | tf_op jit(solution)/shard_map/ppermute | solution.py:20
  130.7 20.4 %shard_map.325 = (bf16[1024,768]{1,0:T(8,128)(2,1)}, bf16[768,768]{1,0:T(8,128)(2,1)}, f32[256,768]{1,0:T(8,128)}, bf16[1024,768]{1,0:T(8,128)(2,1)}, bf16[1024,...) custom-call(s32[1]{0:T(128)} %bitcast.head, ...), custom_call_target="tpu_custom_call" | custom-call | tf_op jit(solution)/shard_map/pallas_call | solution.py:124
  153.7 10.0 %shard_map.326 = (bf16[768,1536]{1,0:T(8,128)(2,1)}, bf16[256,1408]{1,0:T(8,128)(2,1)S(1)}, bf16[256,1408]{1,0:T(8,128)(2,1)S(1)}, bf16[256,1408]{1,0:T(8,128)(2,1)}, bf16[256,1408]{1,0:T(8,128)(2,1)}) custom-call(s32[1]{0:T(128)} %bitcast.head, bf16[1024,768]{1,0:T(8,128)(2,1)} %get-tuple-element.153.third, bf16[1024,768]{1,0:T(8,128)(2,1)} %get-tuple-element.154.gup, ...), custom_call_target="tpu_custom_call" | custom-call | tf_op jit(solution)/shard_map/pallas_call | solution.py:124
  165.4 4.4 %all-to-all-start.2 = ((bf16[8,96,1536]{2,1,0:T(8,128)(2,1)}), bf16[8,96,1536]{2,1,0:T(8,128)(2,1)}, u32[]{:S(2)}, u32[]{:S(2)}) async-start(bf16[8,96,1536]{2,1,0:T(8,128)(2,1)} %bitcast.45), calls=%async_computation.2 | async-start | bytes 4718592 | tf_op jit(solution)/shard_map/all_to_all | solution.py:82
  175.8 16.4 %shard_map.327 = (bf16[1024,192]{1,0:T(8,128)(2,1)}, bf16[2,256,192]{2,1,0:T(8,128)(2,1)S(1)}, bf16[1024,768]{1,0:T(8,128)(2,1)}, bf16[1024,768]{1,0:T(8,128)(2,...) custom-call(s32[1]{0:T(128)} %bitcast.head, ...), custom_call_target="tpu_custom_call" | custom-call | tf_op jit(solution)/shard_map/pallas_call | solution.py:124
  198.0 6.6 %shard_map.328 = (bf16[4,96,768]{2,1,0:T(8,128)(2,1)}, bf16[4,96,768]{2,1,0:T(8,128)(2,1)}, bf16[256,768]{1,0:T(8,128)(2,1)S(1)}, bf16[256,768]{1,0:T(8,128)(2,1...) custom-call(s32[2]{0:T(128)S(1)} %pad_add_fusion.place, bf16[1024,768]{1,0:T(8,128)(2,1)} %get-tuple-element.185.sm, ...), custom_call_target="tpu_custom_call" | custom-call | tf_op jit(solution)/shard_map/pallas_call | solution.py:124
  204.7 3.1 collective-permute-done.23.a2
  213.1 12.6 %shard_map.329.gjoint.grads = bf16[1024,576]{1,0:T(8,128)(2,1)} custom-call(bf16[512,384]{1,0:T(8,128)(2,1)S(1)} %copy-done.9, bf16[512,384]{1,0:T(8,128)(2,1)} %collective-permute-done.21.a1, bf16[512,384]{1,0:T(8,128)(2,1)} %collective-permute-done.23.a2, bf16[3,1024,192]{2,1,0:T(8,128)(2,1)} %get-tuple-element.199.qkv, ...), custom_call_target="tpu_custom_call" | custom-call | tf_op jit(solution)/shard_map/pallas_call | solution.py:124
  227.1 2.8 collective-permute-done.25
  230.8 3.3 %shard_map.330 = (bf16[4,96,768]{2,1,0:T(8,128)(2,1)S(1)}, bf16[4,96,768]{2,1,0:T(8,128)(2,1)S(1)}) custom-call(s32[2]{0:T(128)S(1)} %pad_add_fusion.place, bf16[1024,768]{1,0:T(8,128)(2,1)} %get-tuple-element.204.first, bf16[1024,576]{1,0:T(8,128)(2,1)} %shard_map.329.gjoint.grads, bf16[256,576]{1,0:T(8,128)(2,1)S(1)} %slice.184.gout), custom_call_target="tpu_custom_call" | custom-call | tf_op jit(solution)/shard_map/pallas_call | solution.py:124
  235.0 2.4 collective-permute-start.28
  238.3 2.3 multiply_reduce_fusion
  240.6 6.3 %shard_map.331 = (bf16[1024,768]{1,0:T(8,128)(2,1)}, f32[8,768]{1,0:T(8,128)S(1)}) custom-call(bf16[256,768]{1,0:T(8,128)(2,1)S(1)} %copy-done.1, bf16[256,768]{1,0:T(8,128)(2,1)S(1)} %collective-permute-done.x1, bf16[256,768]{1,0:T(8,128)(2,1)S(1)} %collective-permute-done.1.x2, bf16[256,768]{1,0:T(8,128)(2,1)S(1)} %copy-done.3, ...), custom_call_target="tpu_custom_call" | custom-call | tf_op jit(solution)/shard_map/pallas_call | solution.py:124
  246.9 4.3 %collective-permute-done.28 = bf16[4,96,768]{2,1,0:T(8,128)(2,1)S(1)} collective-permute-done((bf16[4,96,768]{2,1,0:T(8,128)(2,1)}, bf16[4,96,768]{2,1,0:T(8,128)(2,1)S(1)}, u32[]{:S(2)}, u32[]{:S(2)}) %collective-permute-start.28) | collective-permute-done | bytes 589856 | tf_op jit(solution)/shard_map/ppermute | solution.py:53
  256.9 3.6 %all-to-all-start.3 = ((bf16[4,96,768]{2,1,0:T(8,128)(2,1)}), bf16[4,96,768]{2,1,0:T(8,128)(2,1)S(1)}, u32[]{:S(2)}, u32[]{:S(2)}) async-start(bf16[4,96,768]{2,1,0:T(8,128)(2,1)} %add_convert_fusion.2), calls=%async_computation.3 | async-start | bytes 1179648 | tf_op jit(solution)/shard_map/all_to_all | solution.py:95
  264.6 2.1 collective-permute-start.35
  267.6 4.8 %collective-permute-done.35 = f32[2,11,768]{2,1,0:T(8,128)S(1)} collective-permute-done((f32[2,11,768]{2,1,0:T(8,128)S(1)}, f32[2,11,768]{2,1,0:T(8,128)S(1)}, u32[]{:S(2)}, u32[]{:S(2)}) %collective-permute-start.35) | collective-permute-done | bytes 67616 | tf_op jit(solution)/shard_map/ppermute | solution.py:53
  272.4 4.6 %collective-permute-start.36 = (f32[4,11,768]{2,1,0:T(8,128)S(1)}, f32[4,11,768]{2,1,0:T(8,128)S(1)}, u32[]{:S(2)}, u32[]{:S(2)}) collective-permute-start(f32[4,11,768]{2,1,0:T(8,128)S(1)} %pad_maximum_fusion.4), channel_id=1, source_target_pairs={{0,16},{4,20},{8,24},{12,28},{16,0},{20,4},{24,8},{28,12},{1,17},{... | collective-permute-start | bytes 405512 | tf_op jit(solution)/shard_map/ppermute | solution.py:53
  277.7 3.5 %all-to-all-start.4 = ((bf16[4,96,768]{2,1,0:T(8,128)(2,1)}), bf16[4,96,768]{2,1,0:T(8,128)(2,1)S(1)}, u32[]{:S(2)}, u32[]{:S(2)}) async-start(bf16[4,96,768]{2,1,0:T(8,128)(2,1)} %add_convert_fusion.1), calls=%async_computation.4 | async-start | bytes 1179648 | tf_op jit(solution)/shard_map/all_to_all | solution.py:95
  281.2 3.8 %collective-permute-done.36 = f32[4,11,768]{2,1,0:T(8,128)S(1)} collective-permute-done((f32[4,11,768]{2,1,0:T(8,128)S(1)}, f32[4,11,768]{2,1,0:T(8,128)S(1)}, u32[]{:S(2)}, u32[]{:S(2)}) %collective-permute-start.36) | collective-permute-done | bytes 135200 | tf_op jit(solution)/shard_map/ppermute | solution.py:53
  292.3 5.3 %all-to-all-done.4.last = bf16[4,96,768]{2,1,0:T(8,128)(2,1)S(1)} async-done(((bf16[4,96,768]{2,1,0:T(8,128)(2,1)}), bf16[4,96,768]{2,1,0:T(8,128)(2,1)S(1)}, u32[]{:S(2)}, u32[]{:S(2)}) %all-to-all-start.4) | async-done | bytes 589856 | tf_op jit(solution)/shard_map/all_to_all | solution.py:95
  297.5 4.3 %all-to-all-start.5 = ((f32[8,1,96]{2,1,0:T(1,128)}), f32[8,1,96]{2,1,0:T(1,128)S(1)}, u32[]{:S(2)}, u32[]{:S(2)}) async-start(f32[8,1,96]{2,1,0:T(1,128)} %bitcast.10), calls=%async_computation.5 | async-start | bytes 8192 | tf_op jit(solution)/shard_map/all_to_all | solution.py:82
  301.9 2.2 convert_add_fusion.1
  (236 shorter events, 71.1 us)
Async XLA Ops:
  7.3 65.5 %all-gather.3.cloned.1.call-start = ((), (), s32[]{:S(2)}) async-start(), calls=%async_computation.6 | async-start | bytes 2654208 | tf_op jit(solution)/shard_map/all_gather | solution.py:534
  16.2 12.9 %collective-permute-start.1 = (bf16[256,768]{1,0:T(8,128)(2,1)S(1)}, bf16[256,768]{1,0:T(8,128)(2,1)S(1)}, u32[]{:S(2)}, u32[]{:S(2)}) collective-permute-start(bf16[256,768]{1,0:T(8,128)(2,1)S(1)} %copy-done.1), channel_id=1, source_target_pairs={{0,2},{1,3},{2,0},{3,1},{4,6},{5,7},{6,4},{7,5},{8,10},{9,11},{10,... | collective-permute-start | bytes 1179656 | tf_op jit(solution)/shard_map/ppermute | solution.py:20
  19.2 17.5 %collective-permute-start.4 = (bf16[256,768]{1,0:T(8,128)(2,1)S(1)}, bf16[256,768]{1,0:T(8,128)(2,1)S(1)}, u32[]{:S(2)}, u32[]{:S(2)}) collective-permute-start(bf16[256,768]{1,0:T(8,128)(2,1)S(1)} %copy-done.24), channel_id=1, source_target_pairs={{0,2},{1,3},{2,0},{3,1},{4,6},{5,7},{6,4},{7,5},{8,10},{9,11},{10,... | collective-permute-start | bytes 1179656 | tf_op jit(solution)/shard_map/ppermute | solution.py:20
  19.3 17.9 %collective-permute-start = (bf16[256,768]{1,0:T(8,128)(2,1)S(1)}, bf16[256,768]{1,0:T(8,128)(2,1)S(1)}, u32[]{:S(2)}, u32[]{:S(2)}) collective-permute-start(bf16[256,768]{1,0:T(8,128)(2,1)S(1)} %copy-done.1), channel_id=1, source_target_pairs={{0,1},{1,0},{2,3},{3,2},{4,5},{5,4},{6,7},{7,6},{8,9},{9,8},{10,11... | collective-permute-start | bytes 1179656 | tf_op jit(solution)/shard_map/ppermute | solution.py:20
  19.3 17.9 %collective-permute-start.3 = (bf16[256,768]{1,0:T(8,128)(2,1)S(1)}, bf16[256,768]{1,0:T(8,128)(2,1)}, u32[]{:S(2)}, u32[]{:S(2)}) collective-permute-start(bf16[256,768]{1,0:T(8,128)(2,1)S(1)} %copy-done.24), channel_id=1, source_target_pairs={{0,1},{1,0},{2,3},{3,2},{4,5},{5,4},{6,7},{7,6},{8,9},{9,8},{10,11... | collective-permute-start | bytes 1179656 | tf_op jit(solution)/shard_map/ppermute | solution.py:20
  21.9 15.0 %all-to-all-start = ((bf16[8,2,240]{2,1,0:T(2,128)(2,1)}), bf16[8,2,240]{2,1,0:T(2,128)(2,1)S(1)}, u32[]{:S(2)}, u32[]{:S(2)}) async-start(bf16[8,2,240]{2,1,0:T(2,128)(2,1)} %reshape.129), calls=%async_computation | async-start | bytes 16384 | tf_op jit(solution)/shard_map/all_to_all | solution.py:82
  28.2 102.5 %all-gather.5.cloned.1.call-start = ((), (), s32[]{:S(2)}) async-start(), calls=%async_computation.7 | async-start | bytes 2654208 | tf_op jit(solution)/shard_map/all_gather | solution.py:552
  29.2 8.1 %collective-permute-start.2 = (bf16[256,768]{1,0:T(8,128)(2,1)S(1)}, bf16[256,768]{1,0:T(8,128)(2,1)S(1)}, u32[]{:S(2)}, u32[]{:S(2)}) collective-permute-start(bf16[256,768]{1,0:T(8,128)(2,1)S(1)} %collective-permute-done.1.x2), channel_id=1, source_target_pairs={{0,1},{1,0},{2,3},{3,2},{4,5},{5,4},{6,7},{7,6},{8,9},{9,8},{10,11... | collective-permute-start | bytes 1179656 | tf_op jit(solution)/shard_map/ppermute | solution.py:20
  74.0 16.6 %collective-permute-start.10 = (bf16[768,384]{1,0:T(8,128)(2,1)S(1)}, bf16[768,384]{1,0:T(8,128)(2,1)}, u32[]{:S(2)}, u32[]{:S(2)}) collective-permute-start(bf16[768,384]{1,0:T(8,128)(2,1)S(1)} %slice.112.w0), channel_id=1, source_target_pairs={{0,2},{1,3},{2,0},{3,1},{4,6},{5,7},{6,4},{7,5},{8,10},{9,11},{10,... | collective-permute-start | bytes 1769480 | tf_op jit(solution)/shard_map/ppermute | solution.py:20
  89.8 10.3 %collective-permute-start.7 = (bf16[512,384]{1,0:T(8,128)(2,1)S(1)}, bf16[512,384]{1,0:T(8,128)(2,1)}, u32[]{:S(2)}, u32[]{:S(2)}) collective-permute-start(bf16[512,384]{1,0:T(8,128)(2,1)S(1)} %get-tuple-element.138.sm0.sm), channel_id=1, source_target_pairs={{0,2},{1,3},{2,0},{3,1},{4,6},{5,7},{6,4},{7,5},{8,10},{9,11},{10,... | collective-permute-start | bytes 1179656 | tf_op jit(solution)/shard_map/ppermute | solution.py:20
  90.5 10.7 %collective-permute-start.9 = (bf16[768,384]{1,0:T(8,128)(2,1)S(1)}, bf16[768,384]{1,0:T(8,128)(2,1)}, u32[]{:S(2)}, u32[]{:S(2)}) collective-permute-start(bf16[768,384]{1,0:T(8,128)(2,1)S(1)} %slice.112.w0), channel_id=1, source_target_pairs={{0,1},{1,0},{2,3},{3,2},{4,5},{5,4},{6,7},{7,6},{8,9},{9,8},{10,11... | collective-permute-start | bytes 1769480 | tf_op jit(solution)/shard_map/ppermute | solution.py:20
  90.5 11.7 %collective-permute-start.11 = (bf16[768,384]{1,0:T(8,128)(2,1)}, bf16[768,384]{1,0:T(8,128)(2,1)}, u32[]{:S(2)}, u32[]{:S(2)}) collective-permute-start(bf16[768,384]{1,0:T(8,128)(2,1)} %collective-permute-done.10.w2), channel_id=1, source_target_pairs={{0,1},{1,0},{2,3},{3,2},{4,5},{5,4},{6,7},{7,6},{8,9},{9,8},{10,11... | collective-permute-start | bytes 1769480 | tf_op jit(solution)/shard_map/ppermute | solution.py:20
  91.0 10.2 %collective-permute-start.6 = (bf16[512,384]{1,0:T(8,128)(2,1)S(1)}, bf16[512,384]{1,0:T(8,128)(2,1)}, u32[]{:S(2)}, u32[]{:S(2)}) collective-permute-start(bf16[512,384]{1,0:T(8,128)(2,1)S(1)} %get-tuple-element.138.sm0.sm), channel_id=1, source_target_pairs={{0,1},{1,0},{2,3},{3,2},{4,5},{5,4},{6,7},{7,6},{8,9},{9,8},{10,11... | collective-permute-start | bytes 1179656 | tf_op jit(solution)/shard_map/ppermute | solution.py:20
  117.7 11.2 %collective-permute-start.13 = (bf16[512,384]{1,0:T(8,128)(2,1)S(1)}, bf16[512,384]{1,0:T(8,128)(2,1)S(1)}, u32[]{:S(2)}, u32[]{:S(2)}) collective-permute-start(bf16[512,384]{1,0:T(8,128)(2,1)S(1)} %get-tuple-element.141.cm0.cm), channel_id=1, source_target_pairs={{0,2},{1,3},{2,0},{3,1},{4,6},{5,7},{6,4},{7,5},{8,10},{9,11},{10,... | collective-permute-start | bytes 1179656 | tf_op jit(solution)/shard_map/ppermute | solution.py:20
  118.3 10.7 %collective-permute-start.12 = (bf16[512,384]{1,0:T(8,128)(2,1)S(1)}, bf16[512,384]{1,0:T(8,128)(2,1)}, u32[]{:S(2)}, u32[]{:S(2)}) collective-permute-start(bf16[512,384]{1,0:T(8,128)(2,1)S(1)} %get-tuple-element.141.cm0.cm), channel_id=1, source_target_pairs={{0,1},{1,0},{2,3},{3,2},{4,5},{5,4},{6,7},{7,6},{8,9},{9,8},{10,11... | collective-permute-start | bytes 1179656 | tf_op jit(solution)/shard_map/ppermute | solution.py:20
  153.1 11.6 %collective-permute-start.17 = (bf16[512,384]{1,0:T(8,128)(2,1)S(1)}, bf16[512,384]{1,0:T(8,128)(2,1)S(1)}, u32[]{:S(2)}, u32[]{:S(2)}) collective-permute-start(bf16[512,384]{1,0:T(8,128)(2,1)S(1)} %add_convert_fusion.7), channel_id=1, source_target_pairs={{0,2},{1,3},{2,0},{3,1},{4,6},{5,7},{6,4},{7,5},{8,10},{9,11},{10,... | collective-permute-start | bytes 1179656 | tf_op jit(solution)/shard_map/ppermute | solution.py:20
  165.4 69.6 %all-to-all-start.2 = ((bf16[8,96,1536]{2,1,0:T(8,128)(2,1)}), bf16[8,96,1536]{2,1,0:T(8,128)(2,1)}, u32[]{:S(2)}, u32[]{:S(2)}) async-start(bf16[8,96,1536]{2,1,0:T(8,128)(2,1)} %bitcast.45), calls=%async_computation.2 | async-start | bytes 4718592 | tf_op jit(solution)/shard_map/all_to_all | solution.py:82
  169.8 22.5 %collective-permute-start.19 = (bf16[256,1408]{1,0:T(8,128)(2,1)}, bf16[256,1408]{1,0:T(8,128)(2,1)S(1)}, u32[]{:S(2)}, u32[]{:S(2)}) collective-permute-start(bf16[256,1408]{1,0:T(8,128)(2,1)} %copy-done.18), channel_id=1, source_target_pairs={{0,1},{1,0},{2,3},{3,2},{4,5},{5,4},{6,7},{7,6},{8,9},{9,8},{10,11... | collective-permute-start | bytes 2162696 | tf_op jit(solution)/shard_map/ppermute | solution.py:20
  171.8 20.4 %collective-permute-start.20 = (bf16[256,1408]{1,0:T(8,128)(2,1)S(1)}, bf16[256,1408]{1,0:T(8,128)(2,1)S(1)}, u32[]{:S(2)}, u32[]{:S(2)}) collective-permute-start(bf16[256,1408]{1,0:T(8,128)(2,1)S(1)} %add_convert_fusion), channel_id=1, source_target_pairs={{0,2},{1,3},{2,0},{3,1},{4,6},{5,7},{6,4},{7,5},{8,10},{9,11},{10,... | collective-permute-start | bytes 2162696 | tf_op jit(solution)/shard_map/ppermute | solution.py:20
  196.3 11.5 %collective-permute-start.23 = (bf16[512,384]{1,0:T(8,128)(2,1)}, bf16[512,384]{1,0:T(8,128)(2,1)}, u32[]{:S(2)}, u32[]{:S(2)}) collective-permute-start(bf16[512,384]{1,0:T(8,128)(2,1)} %add_convert_fusion.6), channel_id=1, source_target_pairs={{0,2},{1,3},{2,0},{3,1},{4,6},{5,7},{6,4},{7,5},{8,10},{9,11},{10,... | collective-permute-start | bytes 1179656 | tf_op jit(solution)/shard_map/ppermute | solution.py:20
  208.3 17.3 %collective-permute-start.26 = (bf16[256,768]{1,0:T(8,128)(2,1)}, bf16[256,768]{1,0:T(8,128)(2,1)}, u32[]{:S(2)}, u32[]{:S(2)}) collective-permute-start(bf16[256,768]{1,0:T(8,128)(2,1)} %get-tuple-element.209), channel_id=1, source_target_pairs={{0,1},{1,0},{2,3},{3,2},{4,5},{5,4},{6,7},{7,6},{8,9},{9,8},{10,11... | collective-permute-start | bytes 1179656 | tf_op jit(solution)/shard_map/ppermute | solution.py:20
  209.8 15.9 %collective-permute-start.27 = (bf16[256,768]{1,0:T(8,128)(2,1)S(1)}, bf16[256,768]{1,0:T(8,128)(2,1)}, u32[]{:S(2)}, u32[]{:S(2)}) collective-permute-start(bf16[256,768]{1,0:T(8,128)(2,1)S(1)} %add_convert_fusion.5), channel_id=1, source_target_pairs={{0,2},{1,3},{2,0},{3,1},{4,6},{5,7},{6,4},{7,5},{8,10},{9,11},{10,... | collective-permute-start | bytes 1179656 | tf_op jit(solution)/shard_map/ppermute | solution.py:20
  210.5 19.4 %collective-permute-start.25 = (bf16[4,96,768]{2,1,0:T(8,128)(2,1)}, bf16[4,96,768]{2,1,0:T(8,128)(2,1)S(1)}, u32[]{:S(2)}, u32[]{:S(2)}) collective-permute-start(bf16[4,96,768]{2,1,0:T(8,128)(2,1)} %get-tuple-element.206), channel_id=1, source_target_pairs={{0,4},{4,0},{8,12},{12,8},{16,20},{20,16},{24,28},{28,24},{1,5},{5... | collective-permute-start | bytes 1769480 | tf_op jit(solution)/shard_map/ppermute | solution.py:53
  235.0 16.1 %collective-permute-start.28 = (bf16[4,96,768]{2,1,0:T(8,128)(2,1)}, bf16[4,96,768]{2,1,0:T(8,128)(2,1)S(1)}, u32[]{:S(2)}, u32[]{:S(2)}) collective-permute-start(bf16[4,96,768]{2,1,0:T(8,128)(2,1)} %copy-done.19), channel_id=1, source_target_pairs={{0,4},{4,0},{8,12},{12,8},{16,20},{20,16},{24,28},{28,24},{1,5},{5... | collective-permute-start | bytes 1769480 | tf_op jit(solution)/shard_map/ppermute | solution.py:53
  256.9 20.8 %all-to-all-start.3 = ((bf16[4,96,768]{2,1,0:T(8,128)(2,1)}), bf16[4,96,768]{2,1,0:T(8,128)(2,1)S(1)}, u32[]{:S(2)}, u32[]{:S(2)}) async-start(bf16[4,96,768]{2,1,0:T(8,128)(2,1)} %add_convert_fusion.2), calls=%async_computation.3 | async-start | bytes 1179648 | tf_op jit(solution)/shard_map/all_to_all | solution.py:95
  264.6 7.8 %collective-permute-start.35 = (f32[2,11,768]{2,1,0:T(8,128)S(1)}, f32[2,11,768]{2,1,0:T(8,128)S(1)}, u32[]{:S(2)}, u32[]{:S(2)}) collective-permute-start(f32[2,11,768]{2,1,0:T(8,128)S(1)} %pad_maximum_fusion.5), channel_id=1, source_target_pairs={{0,8},{4,12},{8,0},{12,4},{16,24},{20,28},{24,16},{28,20},{1,9},{5... | collective-permute-start | bytes 202760 | tf_op jit(solution)/shard_map/ppermute | solution.py:53
  272.4 12.6 %collective-permute-start.36 = (f32[4,11,768]{2,1,0:T(8,128)S(1)}, f32[4,11,768]{2,1,0:T(8,128)S(1)}, u32[]{:S(2)}, u32[]{:S(2)}) collective-permute-start(f32[4,11,768]{2,1,0:T(8,128)S(1)} %pad_maximum_fusion.4), channel_id=1, source_target_pairs={{0,16},{4,20},{8,24},{12,28},{16,0},{20,4},{24,8},{28,12},{1,17},{... | collective-permute-start | bytes 405512 | tf_op jit(solution)/shard_map/ppermute | solution.py:53
  277.1 10.2 %collective-permute-start.30 = (bf16[256,768]{1,0:T(8,128)(2,1)S(1)}, bf16[256,768]{1,0:T(8,128)(2,1)}, u32[]{:S(2)}, u32[]{:S(2)}) collective-permute-start(bf16[256,768]{1,0:T(8,128)(2,1)S(1)} %get-tuple-element.315), channel_id=1, source_target_pairs={{0,1},{1,0},{2,3},{3,2},{4,5},{5,4},{6,7},{7,6},{8,9},{9,8},{10,11... | collective-permute-start | bytes 1179656 | tf_op jit(solution)/shard_map/ppermute | solution.py:20
  277.1 24.7 %collective-permute-start.29 = (bf16[256,768]{1,0:T(8,128)(2,1)S(1)}, bf16[256,768]{1,0:T(8,128)(2,1)}, u32[]{:S(2)}, u32[]{:S(2)}) collective-permute-start(bf16[256,768]{1,0:T(8,128)(2,1)S(1)} %get-tuple-element.314), channel_id=1, source_target_pairs={{0,1},{1,0},{2,3},{3,2},{4,5},{5,4},{6,7},{7,6},{8,9},{9,8},{10,11... | collective-permute-start | bytes 1179656 | tf_op jit(solution)/shard_map/ppermute | solution.py:20
  277.7 19.9 %all-to-all-start.4 = ((bf16[4,96,768]{2,1,0:T(8,128)(2,1)}), bf16[4,96,768]{2,1,0:T(8,128)(2,1)S(1)}, u32[]{:S(2)}, u32[]{:S(2)}) async-start(bf16[4,96,768]{2,1,0:T(8,128)(2,1)} %add_convert_fusion.1), calls=%async_computation.4 | async-start | bytes 1179648 | tf_op jit(solution)/shard_map/all_to_all | solution.py:95
  288.5 13.4 %collective-permute-start.31 = (bf16[256,768]{1,0:T(8,128)(2,1)S(1)}, bf16[256,768]{1,0:T(8,128)(2,1)}, u32[]{:S(2)}, u32[]{:S(2)}) collective-permute-start(bf16[256,768]{1,0:T(8,128)(2,1)S(1)} %add_convert_fusion.3), channel_id=1, source_target_pairs={{0,2},{1,3},{2,0},{3,1},{4,6},{5,7},{6,4},{7,5},{8,10},{9,11},{10,... | collective-permute-start | bytes 1179656 | tf_op jit(solution)/shard_map/ppermute | solution.py:20
  297.5 10.7 %all-to-all-start.5 = ((f32[8,1,96]{2,1,0:T(1,128)}), f32[8,1,96]{2,1,0:T(1,128)S(1)}, u32[]{:S(2)}, u32[]{:S(2)}) async-start(f32[8,1,96]{2,1,0:T(1,128)} %bitcast.10), calls=%async_computation.5 | async-start | bytes 8192 | tf_op jit(solution)/shard_map/all_to_all | solution.py:82
  (55 other events, 457.0 us)
Sparse Core Ops, SparseCore 0:
  16.3 56.4 all-gather.2
  75.6 50.1 all-gather.4

commit v4 on v1

v4 whole, which is shorter than its diff:
```python
from functools import partial

import jax
import jax.numpy as jnp
from jax import lax
from jax.experimental import pallas as pl
from jax.experimental.pallas import tpu as pltpu
from jax.sharding import PartitionSpec as P

HD = 64
BF = jnp.bfloat16
F32 = jnp.float32


def mm(a, b, ca=1, cb=0):
    return lax.dot_general(a, b, (((ca,), (cb,)), ((), ())), preferred_element_type=F32)


def swap(x, bit):
    return lax.ppermute(x, "head", [(i, i ^ bit) for i in range(4)])


def swap_rows(x, bit):
    blocks = jnp.split(swap(x, bit), 4, axis=0)
    return jnp.concatenate([blocks[i ^ bit] for i in range(4)], axis=0)


def head_rel(x, swap=swap):
    near = swap(x, 1)
    far = swap(x, 2)
    return [x, near, far, swap(far, 1)]


def pick(parts, index):
    low, high = (index & 1) == 1, (index & 2) == 2
    return jnp.where(
        high, jnp.where(low, parts[3], parts[2]), jnp.where(low, parts[1], parts[0])
    )


def head_sum(chunks, swap=swap):
    a, b = swap(chunks[1], 1), swap(chunks[3], 1)
    mine = chunks[0].astype(F32) + a.astype(F32)
    other = (chunks[2].astype(F32) + b.astype(F32)).astype(chunks[0].dtype)
    return mine + swap(other, 2).astype(F32)


def after(values, ready):
    return lax.optimization_barrier((values, ready))[0]


def seq_swap(x, bit):
    return lax.ppermute(x, "seq", [(i, i ^ bit) for i in range(lax.axis_size("seq"))])


def seq_bits():
    return [1 << b for b in range(lax.axis_size("seq").bit_length() - 1)]


def seq_gather(x):
    for bit in seq_bits():
        x = jnp.concatenate([x, seq_swap(x, bit)], axis=0)
    return x


def seq_scatter_sum(x):
    for bit in reversed(seq_bits()):
        x = x[:bit] + seq_swap(x[bit:], bit)
    return x


def seq_order(x, s):
    n = x.shape[0]
    at = (s ^ jnp.arange(n))[:, None] == jnp.arange(n)[None, :]
    precision = lax.Precision.HIGHEST if x.dtype == F32 else None
    return lax.dot_general(
        at.astype(x.dtype), x, (((1,), (0,)), ((), ())), precision=precision, preferred_element_type=F32
    )


def exchange(x):
    return lax.all_to_all(x, "seq", split_axis=0, concat_axis=0, tiled=True)


def alike():
    n = lax.axis_size("seq")
    return [list(range(odd, n, 2)) for odd in (0, 1)]


def half_reduce(near, far):
    return (near.astype(F32) + seq_swap(far, 1).astype(F32)).astype(BF)


def rest_reduce(part):
    return lax.all_to_all(part, "seq", split_axis=0, concat_axis=0, axis_index_groups=alike(), tiled=True)


def stats(v):
    mean = jnp.mean(v, axis=-1, keepdims=True)
    center = v - mean
    r = lax.rsqrt(jnp.mean(center * center, axis=-1, keepdims=True) + 1e-6)
    return center * r, r


def normback(n, r, e):
    return r * (
        e - jnp.mean(e, axis=-1, keepdims=True) - n * jnp.mean(e * n, axis=-1, keepdims=True)
    )


class Held:
    def __init__(self, outside, inside, sems, count):
        self.outside, self.inside, self.sems, self.count = outside, inside, sems, count
        self.pending = []
        self.shape, self.dtype = inside.shape, inside.dtype

    def copy(self, source, target):
        copy = pltpu.make_async_copy(source, target, self.sems.at[self.count[0]])
        self.count[0] += 1
        copy.start()
        self.pending.append(copy)

    def send(self, at=...):
        if self.outside is not None:
            self.copy(self.inside.at[at], self.outside.at[at])

    def wait(self):
        for copy in self.pending:
            copy.wait()
        self.pending = []

    def __getitem__(self, at):
        self.wait()
        return self.inside[at]

    def __setitem__(self, at, value):
        self.inside[at] = value


class Result(Held):
    def __getitem__(self, at):
        return self.inside[at]


def call(kernel, scalars, ins, outs, scratch=(), sends=0, small=0, limit=58):
    ins = [v if isinstance(v, tuple) else (v, ...) for v in ins]
    parts = [v if at is ... else jax.eval_shape(lambda x, at=at: x[at], v) for v, at in ins]

    def is_small(v):
        return v.size * v.dtype.itemsize <= small

    plain = [is_small(v) and at is ... for v, at in ins] + [is_small(v) for v in outs]
    kept = [v for v, p in zip((*parts, *outs), plain) if not p]

    def body(*refs):
        refs = list(refs)
        numbers = [refs.pop(0) for _ in scalars]
        outside = [refs.pop(0) for _ in plain]
        inside = [refs.pop(0) for _ in kept]
        sems, rest, count = refs[-1], refs[:-1], [0]
        arrays = []
        for k, (ref, p) in enumerate(zip(outside, plain)):
            kind = Held if k < len(ins) else Result
            arrays.append(kind(None, ref, sems, count) if p else kind(ref, inside.pop(0), sems, count))
        held, results = arrays[: len(ins)], arrays[len(ins) :]
        for v, (_, at) in zip(held, ins):
            if v.outside is not None:
                v.copy(v.outside.at[at], v.inside)
        kernel(*numbers, *held, *results, *rest)
        for v in results:
            if not v.pending:
                v.send()
        for v in arrays:
            v.wait()

    specs = [pl.BlockSpec(memory_space=pltpu.VMEM if p else pl.ANY) for p in plain]
    return pl.pallas_call(
        body,
        in_specs=[pl.BlockSpec(memory_space=pltpu.SMEM)] * len(scalars) + specs[: len(ins)],
        out_specs=specs[len(ins) :],
        out_shape=list(outs),
        scratch_shapes=[pltpu.VMEM(v.shape, v.dtype) for v in kept]
        + list(scratch)
        + [pltpu.SemaphoreType.DMA((len(kept) + sends + 1,))],
        compiler_params=pltpu.CompilerParams(vmem_limit_bytes=limit * 1024 * 1024),
    )(*scalars, *[v for v, _ in ins])


def out(shape, dtype):
    return jax.ShapeDtypeStruct(shape, dtype)


def block(b, size=256):
    return slice(b * size, (b + 1) * size)


def packed_at(shape, b):
    size, half = shape[0] // 2, shape[1] // 2
    return (block(b // 2, size), slice(half * (b % 2), half * (b % 2 + 1)))


def unpack(ref, b):
    return ref[packed_at(ref.shape, b)]


def pack(ref, b, value):
    ref[packed_at(ref.shape, b)] = value


def by_head(parts, head):
    return jnp.concatenate([pick(parts, head ^ a) for a in range(4)], axis=1)


def chunks_by_head(value, head):
    hw = value.shape[1] // 4
    blocks = [value[:, a * hw : (a + 1) * hw] for a in range(4)]
    return [pick(blocks, head ^ j) for j in range(4)]


def staggered(stages, tasks):
    done = [None] * len(tasks)
    for t in range(len(tasks) + len(stages) - 1):
        for k, stage in enumerate(stages):
            if 0 <= t - k < len(tasks):
                done[t - k] = stage(*tasks[t - k]) if k == 0 else stage(*tasks[t - k], done[t - k])
    return done


def of_head(values, hd):
    lane = lax.broadcasted_iota(jnp.int32, (1, values.shape[1]), 1) // HD
    return jnp.where(lane == hd, values, 0)


def softmax_columns(keys, queries, values_t, p_ref, inv_ref, visible=None):
    heads = keys.shape[1] // HD
    own_keys = [of_head(keys, hd) for hd in range(heads)]

    def scores(b, hd):
        return mm(own_keys[hd], queries[b], 1, 1)

    def weights(b, hd, st):
        if visible is not None:
            st = jnp.where(visible, st, -1e30)
        e = jnp.exp(st - jnp.max(st, axis=0, keepdims=True))
        inv = 1.0 / jnp.sum(e, axis=0, keepdims=True)
        low = e.astype(BF)
        p_ref[hd, :, block(b)] = low
        inv_ref[hd : hd + 1, block(b)] = inv
        return low, inv

    def mixed(b, hd, done):
        result = mm(values_t[hd * HD : (hd + 1) * HD, :], done[0]) * done[1]
        if hd == heads - 1:
            p_ref.send((slice(None), slice(None), block(b)))
        return result

    parts = staggered((scores, weights, mixed), [(b, hd) for b in range(len(queries)) for hd in range(heads)])
    return [
        jnp.concatenate(parts[b * heads : (b + 1) * heads], axis=0).T.astype(BF) for b in range(len(queries))
    ]


def softmax_back(keys, values, queries, p_ref, inv_ref, results, grads, ds_ref):
    heads = keys.shape[1] // HD
    keys_t = keys.astype(F32).T.astype(BF)
    own_values = [of_head(values, hd) for hd in range(heads)]
    count = len(grads)
    scaled, inner = [], []
    for b in range(count):
        go_t, o_t = grads[b].T, results[b].astype(F32).T
        parts = []
        for hd in range(heads):
            at = slice(hd * HD, (hd + 1) * HD)
            parts.append(go_t[at, :] * inv_ref[hd : hd + 1, block(b)])
            inner.append(jnp.sum(parts[-1] * o_t[at, :], axis=0, keepdims=True))
        scaled.append(jnp.concatenate(parts, axis=0).T.astype(BF))

    def dprob(b, hd):
        return mm(own_values[hd], scaled[b], 1, 1)

    def dscore(b, hd, dp):
        ds = (p_ref[hd, :, block(b)].astype(F32) * (dp - inner[b * heads + hd])).astype(BF)
        ds_ref[hd, :, block(b)] = ds
        return ds

    def dquery(b, hd, ds):
        return mm(keys_t[hd * HD : (hd + 1) * HD, :], ds)

    parts = staggered((dprob, dscore, dquery), [(b, hd) for b in range(count) for hd in range(heads)])
    dq = [
        (jnp.concatenate(parts[b * heads : (b + 1) * heads], axis=0).T * 0.125).astype(BF) for b in range(count)
    ]
    everything = jnp.concatenate(scaled, axis=0)
    dk = sum(of_head(mm(ds_ref[hd], queries), hd) for hd in range(heads))
    dv = sum(of_head(mm(p_ref[hd], everything), hd) for hd in range(heads))
    return dq, dk.astype(BF), dv.astype(BF)


BLOCKS = range(4)


def self_forward(x0, x1, x2, x3, mod, w, n_ref, qkv_ref, sm_ref, p_ref, inv_ref):
    width = x0.shape[1]
    hw = sm_ref.shape[1] // 2
    norms = [stats(x[...].astype(F32))[0] for x in (x0, x1, x2, x3)]
    scale, shift = 1.0 + mod[:, width : 2 * width], mod[:, :width]
    firsts = [(n * scale + shift).astype(BF) for n in norms]
    weights = w[:, 2 * hw :]
    joints = [mm(first, weights) for first in firsts]
    for b in BLOCKS:
        n_ref[block(b), :] = norms[b].astype(BF)
    n_ref.send()
    queries = [(joint[:, :hw] * 0.125).astype(BF) for joint in joints]
    keys = jnp.concatenate([joint[:, hw : 2 * hw].astype(BF) for joint in joints], axis=0)
    for b in BLOCKS:
        qkv_ref[0, block(b), :] = queries[b]
        qkv_ref[2, block(b), :] = joints[b][:, 2 * hw :].astype(BF)
    qkv_ref[1] = keys
    qkv_ref.send()
    values_t = jnp.concatenate([joint[:, 2 * hw :].T.astype(BF) for joint in joints], axis=1)
    for b, result in enumerate(softmax_columns(keys, queries, values_t, p_ref, inv_ref)):
        pack(sm_ref, b, result)


def cross_forward(
    head, length, x0, x1, x2, x3, w0, w1, w2, w3, sm0, sm1, sm2, sm3, mod, out_bias, gain, w_later, caption,
    sm_ref, wout_ref, proj_ref, after_ref, second_ref, cq_ref, pair_ref, cm_ref, p_ref, inv_ref,
):
    h = head[0]
    width = x0.shape[1]
    hw = cq_ref.shape[1]
    w_out = by_head([w[:, :hw] for w in (w0, w1, w2, w3)], h)
    wout_ref[...] = w_out
    wout_ref.send()
    mixed = [by_head([unpack(p, b ^ j) for j, p in enumerate((sm0, sm1, sm2, sm3))], h) for b in BLOCKS]
    projs = [mm(m, w_out) + out_bias[...] for m in mixed]
    pair = mm(caption[...], w_later[:, hw:])
    keys, values = pair[:, :hw].astype(BF), pair[:, hw:]
    pair_ref[0] = keys
    pair_ref[1] = values.astype(BF)
    afters, seconds = [], []
    for b, x in enumerate((x0, x1, x2, x3)):
        sm_ref[block(b), :] = mixed[b]
        proj_ref[block(b), :] = projs[b].astype(BF)
        after = x[...].astype(F32) + mod[:, 2 * width : 3 * width] * projs[b]
        after_ref[block(b), :] = after
        seconds.append((stats(after)[0] * gain[...]).astype(BF))
        second_ref[block(b), :] = seconds[b]
    for ref in (sm_ref, proj_ref, after_ref, second_ref):
        ref.send()
    queries = [(mm(second, w_later[:, :hw]) * 0.125).astype(BF) for second in seconds]
    for b in BLOCKS:
        cq_ref[block(b), :] = queries[b]
    slots = lax.broadcasted_iota(jnp.int32, (caption.shape[0], 1), 0)
    results = softmax_columns(keys, queries, values.T.astype(BF), p_ref, inv_ref, slots < length[0])
    for b, result in enumerate(results):
        pack(cm_ref, b, result)


def feed_both(
    head, cm0, w0, w1, w2, w3, cm1, cm2, cm3, after, co_bias, mod, w_up, up_bias, w_down, g0, g1, g2, g3,
    cm_ref, wc_ref, across_ref, third_ref, hidden_ref, gup_ref, gfeed_ref, ga_ref, c0, c1, c2, c3, vec_ref,
):
    h = head[0]
    width = after.shape[1]
    hw = width // 4
    ff = w_up.shape[1]
    w_cross = by_head([w[:, hw:] for w in (w0, w1, w2, w3)], h)
    wc_ref[...] = w_cross
    wc_ref.send()
    mixed = [by_head([unpack(p, b ^ j) for j, p in enumerate((cm0, cm1, cm2, cm3))], h) for b in BLOCKS]
    across = [after[block(b), :] + mm(mixed[b], w_cross) + co_bias[...] for b in BLOCKS]
    across_ref[...] = across[0]
    across_ref.send()
    scale, shift = 1.0 + mod[:, 4 * width : 5 * width], mod[:, 3 * width : 4 * width]
    norms = [stats(v) for v in across]
    thirds = [(n * scale + shift).astype(BF) for n, _ in norms]
    for b in BLOCKS:
        cm_ref[block(b), :] = mixed[b]
        third_ref[block(b), :] = thirds[b]
    cm_ref.send()
    third_ref.send()
    ups = [mm(third, w_up[...]) + up_bias[...].astype(F32) for third in thirds]
    cots = [g[...].astype(F32) for g in (g0, g1, g2, g3)]
    feeds = [(mod[:, 5 * width :] * cot).astype(BF) for cot in cots]
    hiddens = [mm(feed, w_down[...]) for feed in feeds]
    gups = []
    for b in BLOCKS:
        v = ups[b]
        t = jnp.tanh(0.7978845608028654 * (v + 0.044715 * v * v * v))
        hidden_ref[block(b), :] = (0.5 * v * (1.0 + t)).astype(BF)
        slope = 0.5 * (1.0 + t) + 0.5 * v * (1.0 - t * t) * (0.7978845608028654 * (1.0 + 0.134145 * v * v))
        gups.append((hiddens[b] * slope).astype(BF))
        gup_ref[block(b), :] = gups[b]
        gfeed_ref[block(b), :] = feeds[b]
    for ref in (hidden_ref, gup_ref, gfeed_ref):
        ref.send()
    gthirds = [mm(gup, w_up[...], 1, 1) for gup in gups]
    gas = [normback(*norms[b], scale * gthirds[b]) for b in BLOCKS]
    gas[0] = gas[0] + cots[0]
    lows = [ga.astype(BF) for ga in gas]
    for b in BLOCKS:
        ga_ref[block(b), :] = lows[b]
    ga_ref.send()
    for b in BLOCKS:
        chunks = chunks_by_head(mm(lows[b], w_cross, 1, 1).astype(BF), h)
        for j, (ref, chunk) in enumerate(zip((c0, c1, c2, c3), chunks)):
            pack(ref, b ^ j, chunk)

    def over_rows(values):
        return sum(jnp.sum(v, axis=0, keepdims=True) for v in values)

    vec_ref[...] = jnp.concatenate(
        [
            over_rows(gthirds),
            over_rows([gthirds[b] * norms[b][0] for b in BLOCKS]),
            over_rows(gas),
            over_rows([gup.astype(F32) for gup in gups]),
            over_rows([feeds[0].astype(F32)]),
            jnp.zeros((3, width), F32),
        ],
        axis=0,
    )


def cross_back(
    head, a0, a1, a2, cm, inv, pair, cq, p, w_later, ga, after, gain, mod, proj, wout,
    dq_ref, dpair_ref, gas_ref, gproj_ref, c0, c1, c2, c3, vec_ref, ds_ref,
):
    h = head[0]
    width = after.shape[1]
    hw = cq.shape[1]
    grads = [sum(unpack(a, b).astype(F32) for a in (a0, a1, a2)) for b in BLOCKS]
    results = [unpack(cm, b) for b in BLOCKS]
    dqs, dk, dv = softmax_back(pair[0], pair[1], cq[...], p, inv, results, grads, ds_ref)
    dpair_ref[0] = dk
    dpair_ref[1] = dv
    for b in BLOCKS:
        dq_ref[block(b), :] = dqs[b]
    gseconds = [mm(dq, w_later[:, :hw], 1, 1) for dq in dqs]
    norms = [stats(after[block(b), :]) for b in BLOCKS]
    gas = [ga[block(b), :].astype(F32) + normback(*norms[b], gain[...] * gseconds[b]) for b in BLOCKS]
    gprojs = [(mod[:, 2 * width : 3 * width] * v).astype(BF) for v in gas]
    for b in BLOCKS:
        gas_ref[block(b), :] = gas[b].astype(BF)
        gproj_ref[block(b), :] = gprojs[b]
    gas_ref.send()
    gproj_ref.send()
    for b in BLOCKS:
        chunks = chunks_by_head(mm(gprojs[b], wout[...], 1, 1).astype(BF), h)
        for j, (ref, chunk) in enumerate(zip((c0, c1, c2, c3), chunks)):
            pack(ref, b ^ j, chunk)

    def over_rows(values):
        return sum(jnp.sum(v, axis=0, keepdims=True) for v in values)

    vec_ref[...] = jnp.concatenate(
        [
            over_rows([gas[b] * proj[block(b), :].astype(F32) for b in BLOCKS]),
            over_rows([gseconds[b] * norms[b][0] for b in BLOCKS]),
            over_rows([gproj.astype(F32) for gproj in gprojs]),
            jnp.zeros((5, width), F32),
        ],
        axis=0,
    )


def self_back(a0, a1, a2, sm, inv, qkv, p, grads_ref, ds_ref):
    hw = qkv.shape[2]
    grads = [sum(unpack(a, b).astype(F32) for a in (a0, a1, a2)) for b in BLOCKS]
    results = [unpack(sm, b) for b in BLOCKS]
    dqs, dk, dv = softmax_back(qkv[1], qkv[2], qkv[0], p, inv, results, grads, ds_ref)
    for b in BLOCKS:
        grads_ref[block(b), :hw] = dqs[b]
    grads_ref[:, hw : 2 * hw] = dk
    grads_ref[:, 2 * hw :] = dv


def first_back(x0, x1, x2, x3, grads, w, mod, gas, gf_ref):
    width = x0.shape[1]
    weights = w[:, w.shape[1] - grads.shape[1] :]
    gfirsts = [mm(grads[block(b), :], weights, 1, 1) for b in BLOCKS]
    scale = 1.0 + mod[:, width : 2 * width]
    for b, x in enumerate((x0, x1, x2, x3)):
        ga = normback(*stats(x[...].astype(F32)), scale * gfirsts[b])
        gf_ref[block(b), :] = (gas[block(b), :].astype(F32) + ga).astype(BF)


def own_columns(head, *refs, hw):
    sources, target = refs[:-1], refs[-1]
    t = 0
    for ref in sources:
        for base in range(0, ref.shape[1], 4 * hw):
            part = pick([ref[:, base + a * hw : base + (a + 1) * hw] for a in range(4)], head[0])
            if len(target.shape) == 2:
                target[:, t * hw : (t + 1) * hw] = part
            else:
                for d in range(target.shape[0]):
                    target[d, :, t * hw : (t + 1) * hw] = part
            t += 1


def feed_weights(head, cm, ga, hidden, w_down, third, gup, gfeed, c0, c1, c2, c3, both_ref):
    width = ga.shape[1]
    hw = width // 4
    rows = hidden.shape[0] // 4
    chunks = chunks_by_head(mm(cm[...], ga[...], 0, 0).astype(BF), head[0])
    for j, ref in enumerate((c0, c1, c2, c3)):
        ref[:, :width] = mm(hidden[block(j, rows), :], w_down[...], 1, 1).astype(BF)
        for k in range(3):
            ref[:, width + k * hw : width + (k + 1) * hw] = chunks[j][k * rows : (k + 1) * rows]
        ref[:, width + 3 * hw :] = jnp.zeros((rows, ref.shape[1] - width - 3 * hw), BF)
        ref.send()
    both_ref[:, : gup.shape[1]] = mm(third[...], gup[...], 0, 0).astype(BF)
    both_ref[:, gup.shape[1] :] = mm(gfeed[...], hidden[...], 0, 0).astype(BF)


def part_rows(value, odd, near_ref, far_ref, kr):
    if kr % 16:
        near_ref[...] = value
        far_ref[...] = value
        return
    for z in range(value.shape[0] // (2 * kr)):
        even_rows = value[2 * z * kr : (2 * z + 1) * kr]
        odd_rows = value[(2 * z + 1) * kr : (2 * z + 2) * kr]
        near_ref[z] = jnp.where(odd == 1, odd_rows, even_rows)
        far_ref[z] = jnp.where(odd == 1, even_rows, odd_rows)


def mid_weights(
    place, f0, f1, f2, across, cot, mod, dn_bias, sm, gproj, caption, dpair, w_later, second, dq,
    near_ref, far_ref, c0, c1, c2, c3, output_ref, gate_ref, *, kr,
):
    hw, width = dq.shape[1], sm.shape[1]
    rows = f0.shape[0]
    total = sum(f[...].astype(F32) for f in (f0, f1, f2))
    feed = total[:, :width] + dn_bias[...]
    output_ref[...] = (across[...] + mod[:, 5 * width :] * feed).astype(BF)
    gate_ref[...] = jnp.sum(cot[...].astype(F32) * feed, axis=0, keepdims=True)
    out_chunks = chunks_by_head(mm(sm[...], gproj[...], 0, 0).astype(BF), place[0])
    cap = mm(dpair[0], w_later[:, hw : 2 * hw], 1, 1) + mm(dpair[1], w_later[:, 2 * hw :], 1, 1)
    cap_chunks = chunks_by_head(cap.astype(BF), place[0])
    for ref, out_chunk, cap_chunk in zip((c0, c1, c2, c3), out_chunks, cap_chunks):
        for k in range(3):
            ref[:, k * hw : (k + 1) * hw] = out_chunk[k * rows : (k + 1) * rows]
        ref[:, 3 * hw :] = cap_chunk
    low = total[:, width:].astype(BF)
    cross = jnp.concatenate([low[:, k * hw : (k + 1) * hw] for k in range(3)], axis=0)
    parts = [mm(second[...], dq[...], 0, 0)] + [mm(caption[...], dpair[t], 0, 0) for t in range(2)]
    part_rows(jnp.concatenate([cross] + [p.astype(BF) for p in parts], axis=1), place[1], near_ref, far_ref, kr)


def last_weights(place, n_one, gjoint, mod, w, o0, o1, o2, vec_c, vec_d, gate, near_ref, far_ref, cap_ref, vec_ref, *, kr):
    hw = gjoint.shape[1] // 3
    rows, width = o0.shape[0], w.shape[0]
    product = mm(n_one[...], gjoint[...], 0, 0)
    sums = jnp.sum(gjoint[...].astype(F32), axis=0, keepdims=True)
    weights = w[:, 2 * hw :].astype(F32)
    vec_ref[0:1, :] = jnp.sum(weights * sums, axis=1, keepdims=True).T
    vec_ref[1:2, :] = jnp.sum(weights * product, axis=1, keepdims=True).T
    grad = (1.0 + mod[:, width : 2 * width]).T * product + mod[:, :width].T * sums
    total = sum(o[...].astype(F32) for o in (o0, o1, o2))
    cap_ref[0] = total[:, 3 * hw :]
    low = total[:, : 3 * hw].astype(BF)
    cross = jnp.concatenate([low[:, k * hw : (k + 1) * hw] for k in range(3)], axis=0)
    part_rows(jnp.concatenate([cross, grad.astype(BF)], axis=1), place[1], near_ref, far_ref, kr)
    rest = (vec_d[0:1], vec_c[0:1], vec_c[1:2], gate[...], vec_d[2:3], vec_d[1:2], vec_c[2:3], vec_c[4:5], vec_c[3:4])
    for t, row in enumerate(rest):
        vec_ref[2 + t : 3 + t, :] = row
    vec_ref[2 + len(rest) :, :] = jnp.zeros((vec_ref.shape[0] - 2 - len(rest), width), F32)


def column_chunks(head, mid, last, *refs):
    own = refs[0].shape[0]
    parts = mid[...], last[:, : mid.shape[1], :]
    value = jnp.concatenate([jnp.sum(v.astype(F32), axis=0) for v in parts], axis=1)
    for j, ref in enumerate(refs):
        ref[...] = pick([value[a * own : (a + 1) * own] for a in range(4)], head[0] ^ j).astype(BF)


def spread_columns(head, p0, p1, p2, p3, cross_ref, query_ref, pair_ref, out_ref, self_ref):
    hw = p0.shape[1] // 8
    got = [p[...].astype(F32) for p in (p0, p1, p2, p3)]
    for a in range(4):
        rows = pick(got, head[0] ^ a)
        for t, (ref, base) in enumerate(
            ((cross_ref, 0), (query_ref, 0), (pair_ref, 0), (pair_ref, 4), (out_ref, 0), (self_ref, 0), (self_ref, 4), (self_ref, 8))
        ):
            ref[:, (base + a) * hw : (base + a + 1) * hw] = rows[:, t * hw : (t + 1) * hw]


def on_device(
    frames,
    condition,
    captions,
    caption_lengths,
    modulation_weight,
    modulation_bias,
    self_weight,
    self_out,
    self_bias,
    cross_gain,
    cross_query,
    cross_pair,
    cross_out,
    cross_bias,
    up_weight,
    up_bias,
    down_weight,
    down_bias,
    cotangent,
):
    n = lax.axis_size("seq")
    h = lax.axis_index("head")
    s = lax.axis_index("seq")
    rows, width = frames.shape
    hw = width // 4
    kr = self_weight.shape[0]
    own = kr // 4
    total = rows * 4

    ff = up_weight.shape[1]
    head = h.astype(jnp.int32)[None]

    def columns(weights, shape):
        return call(partial(own_columns, hw=hw), [head], weights, [out(shape, BF)])[0]

    w_own = columns((self_out, cross_out, self_weight), (kr, 5 * hw))
    condition, w_own, later = lax.optimization_barrier((condition, w_own, (cross_query, cross_pair)))
    w_later = columns(later, (n, kr, 3 * hw))
    w_own = lax.all_gather(w_own, "seq", axis=0, tiled=True)
    x = head_rel(frames)
    biases = jnp.concatenate([self_bias, cross_bias, cross_gain, down_bias])[None]
    got = exchange(jnp.concatenate([condition.reshape(n, kr), jnp.broadcast_to(biases, (n, 4 * kr))], axis=1))
    cond_own = jax.nn.silu(got[:, :kr].astype(F32)).astype(BF)
    vectors = got[:, kr:].astype(F32).reshape(n, 4, kr).transpose(1, 0, 2).reshape(4, width)
    out_bias, co_bias, gain, dn_bias = vectors[0], vectors[1], vectors[2], vectors[3]
    mod_part = mm(cond_own, modulation_weight) + lax.dynamic_update_slice(
        jnp.zeros((n * modulation_bias.shape[0],), F32),
        modulation_bias.astype(F32),
        (s * modulation_bias.shape[0],),
    )
    g = head_rel(cotangent)
    mod_part, x = lax.optimization_barrier((mod_part, x))
    mod = exchange(mod_part).sum(0, keepdims=True)
    w_own = after(w_own, (mod, w_later, g))
    updown = after((up_weight, down_weight), (mod, g))
    updown = jnp.concatenate([updown[0], updown[1].T], axis=1)
    updown = lax.all_gather(updown, "seq", axis=0, tiled=True)
    w_up = (updown, (slice(None), slice(0, ff)))
    w_down = (updown, (slice(None), slice(ff, 2 * ff)))
    w_later = exchange(after(w_later, mod)).reshape(width, 3 * hw)
    w_parts = w_own[:, : 2 * hw]
    mod, w_parts = lax.optimization_barrier((mod, w_parts))
    w_parts = head_rel(w_parts)
    caption = captions[0]
    slots = caption.shape[0]
    heads = hw // HD
    packed = (total // 2, 2 * hw)
    pad = -3 * hw % 128
    deep = out((total, width), BF)
    n_one, qkv, sm_own, probs, inv = call(
        self_forward,
        [],
        [*x, mod, w_own],
        [deep, out((3, total, hw), BF), out(packed, BF), out((heads, total, total), BF), out((heads, total), F32)],
        sends=4,
    )
    sm_parts = head_rel(sm_own)
    sm, w_out, proj, after_self, second, cq, pair, cm_own, cprobs, cinv = call(
        cross_forward,
        [head, caption_lengths],
        [*x, *w_parts, *sm_parts, mod, out_bias[None], gain[None], w_later, caption],
        [
            deep,
            out((width, width), BF),
            deep,
            out((total, width), F32),
            deep,
            out((total, hw), BF),
            out((2, slots, hw), BF),
            out(packed, BF),
            out((heads, slots, total), BF),
            out((heads, total), F32),
        ],
        sends=4,
    )
    cm_parts = head_rel(cm_own)
    cm, w_cross, across, third, hidden, g_up, g_feed, ga, *chunks, vec_c = call(
        feed_both,
        [head],
        [cm_parts[0], *w_parts, *cm_parts[1:], after_self, co_bias[None], mod]
        + [w_up, up_bias[None], w_down, *g],
        [deep, out((width, width), BF), out((rows, width), F32), deep]
        + [out((total, ff), BF), out((total, ff), BF), deep, deep]
        + [out(packed, BF) for _ in range(4)]
        + [out((8, width), F32)],
    )

    def near_terms(chunks):
        a, b = swap(chunks[1], 1), swap(chunks[3], 1)
        return chunks[0], a, (chunks[2].astype(F32) + b.astype(F32)).astype(BF)

    mine, near, other = near_terms(chunks)
    far = swap(other, 2)
    place = jnp.stack([h, s & 1]).astype(jnp.int32)

    def halves(columns):
        shape = (width, columns) if kr % 16 else (n // 2, kr, columns)
        return [out(shape, BF) for _ in range(2)]

    def parted(near_rows, far_rows):
        if kr % 16 == 0:
            return near_rows, far_rows
        near_rows, far_rows = (v.reshape(n // 2, 2, kr, -1) for v in (near_rows, far_rows))
        return (
            lax.dynamic_index_in_dim(near_rows, s & 1, 1, keepdims=False),
            lax.dynamic_index_in_dim(far_rows, 1 - (s & 1), 1, keepdims=False),
        )

    *feed_chunks, both = call(
        feed_weights,
        [head],
        [after(cm, other), ga, hidden, w_down, third, g_up, g_feed],
        [out((rows, width + 3 * hw + pad), BF) for _ in range(4)] + [out((width, 2 * ff), BF)],
    )
    both = exchange(after(both, far).reshape(n, kr, 2 * ff))
    feed_mine, feed_near, feed_other = near_terms(after(tuple(feed_chunks), far))
    far, feed_other = lax.optimization_barrier((far, feed_other))
    feed_far = swap(feed_other, 2)
    dq, dpair, gas, g_proj, *chunks, vec_d = call(
        cross_back,
        [head],
        [mine, near, far, cm_own, cinv, pair, cq, cprobs, w_later, ga, after_self, gain[None], mod, proj, w_out],
        [out((total, hw), BF), out((2, slots, hw), BF), deep, deep]
        + [out(packed, BF) for _ in range(4)]
        + [out((8, width), F32)],
        [pltpu.VMEM((heads, slots, total), BF)],
    )
    mine, near, other = near_terms(chunks)
    other, feed_far = lax.optimization_barrier((other, feed_far))
    far = swap(other, 2)
    *mid, out0, out1, out2, out3, output_frames, gv_gate2 = call(
        partial(mid_weights, kr=kr),
        [place],
        [feed_mine, feed_near, feed_far, across, cotangent, mod, dn_bias[None]]
        + [after(sm, other), g_proj, caption, dpair, w_later, second, dq],
        halves(4 * hw)
        + [out((rows, 4 * hw), BF) for _ in range(4)]
        + [out((rows, width), BF), out((1, width), F32)],
    )
    out_mine, out_near, out_other = near_terms(after((out0, out1, out2, out3), far))
    far, mid, out_other = lax.optimization_barrier((far, mid, out_other))
    mid = half_reduce(*parted(*mid))
    out_far = swap(out_other, 2)
    (g_joint,) = call(
        self_back,
        [],
        [mine, near, far, sm_own, inv, qkv, probs],
        [out((total, 3 * hw), BF)],
        [pltpu.VMEM((heads, total, total), BF)],
    )
    n_one, out_far, mid, both = after((n_one, out_far, mid, both), g_joint)
    *last, grad_captions, vec = call(
        partial(last_weights, kr=kr),
        [place],
        [n_one, g_joint, mod, w_own, out_mine, out_near, out_far, vec_c, vec_d, gv_gate2],
        halves(4 * hw) + [out((1, slots, hw), F32), out((16, width), F32)],
    )
    mid = rest_reduce(after(mid, both))
    gas, last, vec = lax.optimization_barrier((gas, last, vec))
    shared = vec + swap(vec, 1)
    shared = shared + swap(shared, 2)
    vec = jnp.where(jnp.arange(16)[:, None] == 10, vec, shared).astype(BF)
    last = half_reduce(*parted(*last))
    vec = jnp.concatenate([vec, seq_swap(vec, 1)], axis=0)
    (gf,) = call(first_back, [], [*x, g_joint, w_own, mod, gas], [deep])
    gf, last, vec, mid = lax.optimization_barrier((gf, last, vec, mid))
    last = jnp.concatenate([last, jnp.broadcast_to(vec[None], (n // 2, *vec.shape))], axis=1)
    last = rest_reduce(last)
    vec = last[:, kr:].reshape(n, 16, width).astype(F32)
    if kr % 16:
        last = last[:, :kr]
    grad_frames = head_sum([gf[j * rows : (j + 1) * rows] for j in range(4)])

    def pairs(v):
        v = v.reshape(n // 2, 2, -1)
        return jnp.where((s & 1) == 1, v[:, ::-1], v).reshape(n, -1)

    g_mod = vec[:, :6].reshape(n, 6 * width)
    g_cond = lax.dot_general(
        g_mod,
        modulation_weight.astype(F32),
        (((1,), (1,)), ((), ())),
        precision=lax.Precision.HIGHEST,
        preferred_element_type=F32,
    )
    g_silu = exchange(pairs(g_cond)).reshape(width)
    g_cond = jax.vjp(jax.nn.silu, condition[0].astype(F32))[1](g_silu)[0]
    grad_condition = lax.dynamic_slice_in_dim(g_cond, h * hw, hw, 0)[None]
    cond_rows = pairs(lax.dynamic_slice_in_dim(cond_own, h * own, own, 1).astype(F32))
    grad_mod_weight = lax.dot_general(
        cond_rows, g_mod, (((0,), (0,)), ((), ())), precision=lax.Precision.HIGHEST, preferred_element_type=F32
    )
    sums = vec.sum(0)
    index = s * 4 + h
    mb = 6 * width // (4 * n)
    grad_mod_bias = lax.dynamic_slice_in_dim(sums[:6].reshape(6 * width), index * mb, mb, 0)

    def own_vec(i):
        return lax.dynamic_slice_in_dim(sums[6 + i], index * own, own, 0)

    both = both.astype(F32).sum(0)
    tiny = dict(small=1 << 20, limit=8)
    cols = call(column_chunks, [head], [mid, last], [out((own, 8 * hw), BF) for _ in range(4)], **tiny)
    cols = [cols[0]] + [
        lax.ppermute(cols[j], "head", [(i, i ^ j) for i in range(4)]) for j in range(1, 4)
    ]
    grad_cross, grad_query, grad_pair, grad_out, grad_self = call(
        spread_columns, [head], cols, [out((own, k * width), F32) for k in (1, 1, 2, 1, 3)], **tiny
    )
    return (
        output_frames,
        grad_frames,
        grad_condition,
        grad_captions,
        grad_mod_weight,
        grad_mod_bias,
        grad_self,
        grad_out,
        own_vec(0),
        own_vec(1),
        grad_query,
        grad_pair,
        grad_cross,
        own_vec(2),
        both[:, :ff],
        sums[10],
        both[:, ff:].T,
        own_vec(3),
    )


def solution(mesh):
    both = ("seq", "head")
    return jax.shard_map(
        on_device,
        mesh=mesh,
        in_specs=(
            P(both, None),
            P("seq", None),
            P("seq", None, None),
            P("seq"),
            P("seq", None),
            P("seq"),
            P("seq", None),
            P("seq", None),
            P("seq"),
            P("seq"),
            P("seq", None),
            P("seq", None),
            P("seq", None),
            P("seq"),
            P("seq", "head"),
            P("head"),
            P("head", "seq"),
            P("seq"),
            P(both, None),
        ),
        out_specs=(
            P(both, None),
            P(both, None),
            P("seq", "head"),
            P("seq", None, "head"),
            P(both, None),
            P(both),
            P(both, None),
            P(both, None),
            P(both),
            P(both),
            P(both, None),
            P(both, None),
            P(both, None),
            P(both),
            P("seq", "head"),
            P("head"),
            P("head", "seq"),
            P(both),
        ),
        check_vma=False,
    )
```

time: 492 us -> 301 us (0.61)
  Pallas kernels: 0 us -> 102 us
  waiting for transfers between devices: 162 us -> 74 us
  matrix products: 82.6 us -> 1.73 us
  other arithmetic: 85 us -> 23.1 us
  local copies, waits for them, and re-layouts: 72.9 us -> 16.4 us
  starting transfers between devices: 66.3 us -> 50.3 us
  blocking collectives: 0 us -> 14.5 us
    pallas_call x0 -> x13, Pallas kernels: none -> 102 us  [call(): pl.pallas_call(body, in_specs=[pl.BlockSpec(memory_space=pltpu.SMEM)] * l...]
    all_to_all x10 -> x6, waiting for transfers between devices: 98.8 us -> 18.3 us  [the longest x4 13 us: exchange(): return lax.all_to_all(x, 'seq', split_axis=0, concat_axis=0, tiled=True)]
    dot_general x22 -> x1, matrix products: 47.8 us -> 0.23 us  [mm(): lax.dot_general(a, b, (((ca,), (cb,)), ((), ())), preferred_element_type=...]
    ppermute x41 -> x32, waiting for transfers between devices: 63.4 us -> 37.9 us  [swap(): return lax.ppermute(x, 'head', [(i, i ^ bit) for i in range(4)])]
    unnamed x259 -> x57, local copies, waits for them, and re-layouts: 24.4 us -> 4.97 us
    reduce_sum x14 -> x3, other arithmetic: 21.4 us -> 2.19 us  [the longest x1 2.05 us: on_device(): both = both.astype(F32).sum(0)]
    dot_general x10 -> x0, matrix products: 18.7 us -> none  [the longest x2 7.42 us: attend_back(): dp = jnp.einsum('qhd,khd->hqk', dh, vh, preferred_element_type=F32)]
    all_to_all x0 -> x1, blocking collectives: none -> 14.5 us  [exchange(): return lax.all_to_all(x, 'seq', split_axis=0, concat_axis=0, tiled=True)]
  transfers between devices with their start and end apart: 52 -> 46, of which waited for: 21 -> 21; matrix products, arithmetic and copies ran while one was open for 33% -> 12% of each run, Pallas kernels for 0% -> 25%
where the time goes in v4:
time: 301 us; the launch traced here: 297 us
  Pallas kernels  102 us (34%)
  waiting for transfers between devices  74 us (25%)
  starting transfers between devices  50.3 us (17%)
  other arithmetic  23.1 us (8%)
  local copies, waits for them, and re-layouts  16.4 us (5%)
  between operations  15.6 us (5%)
  blocking collectives  14.5 us (5%)
    pallas_call x13, Pallas kernels, call(): pl.pallas_call(body, in_specs=[pl.BlockSpec(memory_space=pltpu.SMEM)] * l...  102 us
    ppermute x32, waiting for transfers between devices, swap(): return lax.ppermute(x, 'head', [(i, i ^ bit) for i in range(4)])  37.9 us
    all_to_all x4, starting transfers between devices, exchange(): return lax.all_to_all(x, 'seq', split_axis=0, concat_axis=0, tiled=True)  19.4 us
    ppermute x32, starting transfers between devices, swap(): return lax.ppermute(x, 'head', [(i, i ^ bit) for i in range(4)])  14.8 us
    all_to_all x1, blocking collectives, exchange(): return lax.all_to_all(x, 'seq', split_axis=0, concat_axis=0, tiled=True)  14.5 us
    all_to_all x4, waiting for transfers between devices, exchange(): return lax.all_to_all(x, 'seq', split_axis=0, concat_axis=0, tiled=True)  13 us
    all_to_all x2, starting transfers between devices, rest_reduce(): lax.all_to_all(part, 'seq', split_axis=0, concat_axis=0, axis_index_group...  9.78 us
    all_gather x1, waiting for transfers between devices, on_device(): updown = lax.all_gather(updown, 'seq', axis=0, tiled=True)  7.43 us
  transfers between devices with their start and end apart: 46, of which 21 were waited for; matrix products, arithmetic and copies ran while one was open for 12% of the time, Pallas kernels for 25%

profile of v4, /device:TPU:0, one launch (start us, length us, event | category | flops | bytes accessed | tf_op | source)
XLA Modules:
  0.0 297.3 jit_solution(7636093964756830850)
XLA Ops:
  7.3 2.2 shard_map.322
  9.5 3.0 %collective-permute-start.1 = (bf16[256,768]{1,0:T(8,128)(2,1)}, bf16[256,768]{1,0:T(8,128)(2,1)S(1)}, u32[]{:S(2)}, u32[]{:S(2)}) collective-permute-start(bf16[256,768]{1,0:T(8,128)(2,1)} %refs_0_.1), channel_id=1, source_target_pairs={{0,2},{1,3},{2,0},{3,1},{4,6},{5,7},{6,4},{7,5},{8,10},{9,11},{10,... | collective-permute-start | bytes 1179656 | tf_op jit(solution)/shard_map/ppermute | solution.py:20
  16.4 6.1 %all-to-all-start = ((bf16[8,2,240]{2,1,0:T(2,128)(2,1)}), bf16[8,2,240]{2,1,0:T(2,128)(2,1)S(1)}, u32[]{:S(2)}, u32[]{:S(2)}) async-start(bf16[8,2,240]{2,1,0:T(2,128)(2,1)} %reshape.154), calls=%async_computation | async-start | bytes 16384 | tf_op jit(solution)/shard_map/all_to_all | solution.py:82
  23.5 5.6 %all-to-all-done = bf16[8,2,240]{2,1,0:T(2,128)(2,1)S(1)} async-done(((bf16[8,2,240]{2,1,0:T(2,128)(2,1)}), bf16[8,2,240]{2,1,0:T(2,128)(2,1)S(1)}, u32[]{:S(2)}, u32[]{:S(2)}) %all-to-all-start) | async-done | bytes 7712 | tf_op jit(solution)/shard_map/all_to_all | solution.py:82
  30.7 14.5 %all_to_all.50 = f32[8,1,4608]{2,1,0:T(1,128)S(1)} all-to-all(f32[8,1,4608]{2,1,0:T(1,128)S(1)} %copy.49), channel_id=1, replica_groups=mesh['seq'=8,'head'=4] {'seq'}, dimensions={0} | all-to-all | bytes 294912 | tf_op jit(solution)/shard_map/all_to_all | solution.py:82
  46.7 2.3 shard_map.323
  49.1 5.6 %all-to-all-start.2 = ((bf16[8,96,576]{2,1,0:T(8,128)(2,1)}), bf16[8,96,576]{2,1,0:T(8,128)(2,1)S(1)}, u32[]{:S(2)}, u32[]{:S(2)}) async-start(bf16[8,96,576]{2,1,0:T(8,128)(2,1)} %shard_map.323), calls=%async_computation.2 | async-start | bytes 1966080 | tf_op jit(solution)/shard_map/all_to_all | solution.py:82
  54.7 4.1 %all-gather.3.cloned.1.call-done.refs_5_.refs_4_ = bf16[768,960]{1,0:T(8,128)(2,1)} async-done(((bf16[96,960]{1,0:T(8,128)(2,1)}), bf16[768,960]{1,0:T(8,128)(2,1)}) %all-gather.3.cloned.1.call-update) | async-done | bytes 1474576 | tf_op jit(solution)/shard_map/all_gather | solution.py:631
  61.3 10.6 %shard_map.324 = (bf16[1024,768]{1,0:T(8,128)(2,1)}, bf16[3,1024,192]{2,1,0:T(8,128)(2,1)}, bf16[512,384]{1,0:T(8,128)(2,1)}, bf16[3,1024,1024]{2,1,0:T(8,128)(2,1)}, f32[3,1024]{1,0:T(4,128)}) custom-call(bf16[256,768]{1,0:T(8,128)(2,1)} %refs_0_.1, bf16[256,768]{1,0:T(8,128)(2,1)} %copy-done.6, bf16[256,768]{1,0:T(8,128)(2,1)} %copy-done.5, ...), custom_call_target="tpu_custom_call" | custom-call | tf_op jit(solution)/shard_map/pallas_call | solution.py:177
  75.0 7.4 %collective-permute-done.10.refs_12_ = bf16[512,384]{1,0:T(8,128)(2,1)S(1)} collective-permute-done((bf16[512,384]{1,0:T(8,128)(2,1)}, bf16[512,384]{1,0:T(8,128)(2,1)S(1)}, u32[]{:S(2)}, u32[]{:S(2)}) %collective-permute-start.10) | collective-permute-done | bytes 393248 | tf_op jit(solution)/shard_map/ppermute | solution.py:20
  84.6 4.0 %all-to-all-done.2 = bf16[8,96,576]{2,1,0:T(8,128)(2,1)S(1)} async-done(((bf16[8,96,576]{2,1,0:T(8,128)(2,1)}), bf16[8,96,576]{2,1,0:T(8,128)(2,1)S(1)}, u32[]{:S(2)}, u32[]{:S(2)}) %all-to-all-start.2) | async-done | bytes 884768 | tf_op jit(solution)/shard_map/all_to_all | solution.py:82
  89.6 11.1 %shard_map.325 = (bf16[1024,768]{1,0:T(8,128)(2,1)}, bf16[768,768]{1,0:T(8,128)(2,1)}, bf16[1024,768]{1,0:T(8,128)(2,1)}, f32[1024,768]{1,0:T(8,128)}, bf16[1024...) custom-call(s32[1]{0:T(128)} %bitcast.refs_0_, ...), custom_call_target="tpu_custom_call" | custom-call | tf_op jit(solution)/shard_map/pallas_call | solution.py:177
  102.1 6.7 %collective-permute-done.13.refs_7_ = bf16[512,384]{1,0:T(8,128)(2,1)S(1)} collective-permute-done((bf16[512,384]{1,0:T(8,128)(2,1)}, bf16[512,384]{1,0:T(8,128)(2,1)S(1)}, u32[]{:S(2)}, u32[]{:S(2)}) %collective-permute-start.13) | collective-permute-done | bytes 393248 | tf_op jit(solution)/shard_map/ppermute | solution.py:20
  110.5 7.4 %all-gather.5.cloned.1.call-done.refs_12_.refs_14_.refs_4_ = bf16[768,1536]{1,0:T(8,128)(2,1)} async-done(((bf16[96,1536]{1,0:T(8,128)(2,1)}), bf16[768,1536]{1,0:T(8,128)(2,1)}) %all-gather.5.cloned.1.call-update) | async-done | bytes 2359312 | tf_op jit(solution)/shard_map/all_gather | solution.py:649
  118.0 16.9 %shard_map.326 = (bf16[1024,768]{1,0:T(8,128)(2,1)}, bf16[768,768]{1,0:T(8,128)(2,1)}, f32[256,768]{1,0:T(8,128)}, bf16[1024,768]{1,0:T(8,128)(2,1)}, bf16[1024,...) custom-call(s32[1]{0:T(128)} %bitcast.refs_0_, ...), custom_call_target="tpu_custom_call" | custom-call | tf_op jit(solution)/shard_map/pallas_call | solution.py:177
  139.5 10.9 %shard_map.327 = (bf16[256,1408]{1,0:T(8,128)(2,1)}, bf16[256,1408]{1,0:T(8,128)(2,1)}, bf16[256,1408]{1,0:T(8,128)(2,1)}, bf16[256,1408]{1,0:T(8,128)(2,1)}, bf16[768,1536]{1,0:T(8,128)(2,1)}) custom-call(s32[1]{0:T(128)} %bitcast.refs_0_, bf16[1024,768]{1,0:T(8,128)(2,1)} %get-tuple-element.148.refs_1_, ...), custom_call_target="tpu_custom_call" | custom-call | tf_op jit(solution)/shard_map/pallas_call | solution.py:177
  150.4 3.8 %all-to-all-start.3 = ((bf16[8,96,1536]{2,1,0:T(8,128)(2,1)}), bf16[8,96,1536]{2,1,0:T(8,128)(2,1)S(1)}, u32[]{:S(2)}, u32[]{:S(2)}) async-start(bf16[8,96,1536]{2,1,0:T(8,128)(2,1)} %bitcast.48), calls=%async_computation.3 | async-start | bytes 4718592 | tf_op jit(solution)/shard_map/all_to_all | solution.py:82
  159.3 11.2 %shard_map.328 = (bf16[1024,192]{1,0:T(8,128)(2,1)}, bf16[2,256,192]{2,1,0:T(8,128)(2,1)}, bf16[1024,768]{1,0:T(8,128)(2,1)}, bf16[1024,768]{1,0:T(8,128)(2,1)},...) custom-call(s32[1]{0:T(128)} %bitcast.refs_0_, ...), custom_call_target="tpu_custom_call" | custom-call | tf_op jit(solution)/shard_map/pallas_call | solution.py:177
  178.8 10.1 %shard_map.329 = (bf16[4,96,768]{2,1,0:T(8,128)(2,1)}, bf16[4,96,768]{2,1,0:T(8,128)(2,1)}, bf16[256,768]{1,0:T(8,128)(2,1)}, bf16[256,768]{1,0:T(8,128)(2,1)}, ...) custom-call(s32[2]{0:T(128)} %pad_add_fusion.refs_0_, ...), custom_call_target="tpu_custom_call" | custom-call | tf_op jit(solution)/shard_map/pallas_call | solution.py:177
  196.5 11.1 %shard_map.330.refs_2_.refs_4_ = bf16[1024,576]{1,0:T(8,128)(2,1)} custom-call(bf16[512,384]{1,0:T(8,128)(2,1)} %get-tuple-element.184.refs_0_, bf16[512,384]{1,0:T(8,128)(2,1)} %copy-done.19, bf16[512,384]{1,0:T(8,128)(2,1)} %collective-permute-done.23.refs_2_, bf16[512,384]{1,0:T(8,128)(2,1)} %get-tuple-element.139.refs_10_.refs_3_, ...), custom_call_target="tpu_custom_call" | custom-call | tf_op jit(solution)/shard_map/pallas_call | solution.py:177
  207.5 4.9 %collective-permute-done.26 = bf16[4,96,768]{2,1,0:T(8,128)(2,1)S(1)} collective-permute-done((bf16[4,96,768]{2,1,0:T(8,128)(2,1)}, bf16[4,96,768]{2,1,0:T(8,128)(2,1)S(1)}, u32[]{:S(2)}, u32[]{:S(2)}) %collective-permute-start.26) | collective-permute-done | bytes 589856 | tf_op jit(solution)/shard_map/ppermute | solution.py:53
  213.4 7.1 %shard_map.331 = (bf16[4,96,768]{2,1,0:T(8,128)(2,1)}, bf16[4,96,768]{2,1,0:T(8,128)(2,1)}, f32[1,256,192]{2,1,0:T(8,128)}, f32[16,768]{1,0:T(8,128)}) custom-call(s32[2]{0:T(128)} %pad_add_fusion.refs_0_, bf16[1024,768]{1,0:T(8,128)(2,1)} %get-tuple-element.205.refs_1_, bf16[1024,576]{1,0:T(8,128)(2,1)} %shard_map.330.refs_2_.refs_4_, ...), custom_call_target="tpu_custom_call" | custom-call | tf_op jit(solution)/shard_map/pallas_call | solution.py:177
  220.7 5.0 %all-to-all-start.4 = ((bf16[4,96,768]{2,1,0:T(8,128)(2,1)}), bf16[4,96,768]{2,1,0:T(8,128)(2,1)S(1)}, u32[]{:S(2)}, u32[]{:S(2)}) async-start(bf16[4,96,768]{2,1,0:T(8,128)(2,1)} %add_convert_fusion.2), calls=%async_computation.4 | async-start | bytes 1179648 | tf_op jit(solution)/shard_map/all_to_all | solution.py:95
  225.6 2.3 collective-permute-start.28
  229.3 3.5 %collective-permute-done.30 = f32[16,768]{1,0:T(8,128)S(1)} collective-permute-done((f32[16,768]{1,0:T(8,128)S(1)}, f32[16,768]{1,0:T(8,128)S(1)}, u32[]{:S(2)}, u32[]{:S(2)}) %collective-permute-start.30) | collective-permute-done | bytes 49184 | tf_op jit(solution)/shard_map/ppermute | solution.py:20
  233.8 7.1 %shard_map.332 = bf16[1024,768]{1,0:T(8,128)(2,1)} custom-call(bf16[256,768]{1,0:T(8,128)(2,1)} %refs_0_.1, bf16[256,768]{1,0:T(8,128)(2,1)} %copy-done.6, bf16[256,768]{1,0:T(8,128)(2,1)} %copy-done.5, bf16[256,768]{1,0:T(8,128)(2,1)} %copy-done.7, bf16[1024,576]{1,0:T(8,128)(2,1)} %shard_map.330.refs_2_.refs_4_, ...), custom_call_target="tpu_custom_call" | custom-call | tf_op jit(solution)/shard_map/pallas_call | solution.py:177
  245.3 2.1 pad_maximum_fusion
  247.4 4.8 %all-to-all-start.5 = ((bf16[4,128,768]{2,1,0:T(8,128)(2,1)}), bf16[4,128,768]{2,1,0:T(8,128)(2,1)S(1)}, u32[]{:S(2)}, u32[]{:S(2)}) async-start(bf16[4,128,768]{2,1,0:T(8,128)(2,1)} %pad_maximum_fusion), calls=%async_computation.5 | async-start | bytes 1572864 | tf_op jit(solution)/shard_map/all_to_all | solution.py:95
  257.9 7.8 %collective-permute-done.34 = bf16[256,768]{1,0:T(8,128)(2,1)S(1)} collective-permute-done((bf16[256,768]{1,0:T(8,128)(2,1)S(1)}, bf16[256,768]{1,0:T(8,128)(2,1)S(1)}, u32[]{:S(2)}, u32[]{:S(2)}) %collective-permute-start.34) | collective-permute-done | bytes 393248 | tf_op jit(solution)/shard_map/ppermute | solution.py:20
  267.7 5.3 %all-to-all-done.5.refs_2_ = bf16[4,128,768]{2,1,0:T(8,128)(2,1)S(1)} async-done(((bf16[4,128,768]{2,1,0:T(8,128)(2,1)}), bf16[4,128,768]{2,1,0:T(8,128)(2,1)S(1)}, u32[]{:S(2)}, u32[]{:S(2)}) %all-to-all-start.5) | async-done | bytes 786464 | tf_op jit(solution)/shard_map/all_to_all | solution.py:95
  276.9 3.9 %all-to-all-start.6 = ((f32[8,1,96]{2,1,0:T(1,128)}), f32[8,1,96]{2,1,0:T(1,128)S(1)}, u32[]{:S(2)}, u32[]{:S(2)}) async-start(f32[8,1,96]{2,1,0:T(1,128)} %bitcast.12), calls=%async_computation.6 | async-start | bytes 8192 | tf_op jit(solution)/shard_map/all_to_all | solution.py:82
  283.8 3.4 %all-to-all-done.6 = f32[8,1,96]{2,1,0:T(1,128)S(1)} async-done(((f32[8,1,96]{2,1,0:T(1,128)}), f32[8,1,96]{2,1,0:T(1,128)S(1)}, u32[]{:S(2)}, u32[]{:S(2)}) %all-to-all-start.6) | async-done | bytes 3104 | tf_op jit(solution)/shard_map/all_to_all | solution.py:82
  (197 shorter events, 70.1 us)
Async XLA Ops:
  7.2 51.5 %all-gather.3.cloned.1.call-start = ((), (), s32[]{:S(2)}) async-start(), calls=%async_computation.7 | async-start | bytes 1769472 | tf_op jit(solution)/shard_map/all_gather | solution.py:631
  9.5 13.2 %collective-permute-start.1 = (bf16[256,768]{1,0:T(8,128)(2,1)}, bf16[256,768]{1,0:T(8,128)(2,1)S(1)}, u32[]{:S(2)}, u32[]{:S(2)}) collective-permute-start(bf16[256,768]{1,0:T(8,128)(2,1)} %refs_0_.1), channel_id=1, source_target_pairs={{0,2},{1,3},{2,0},{3,1},{4,6},{5,7},{6,4},{7,5},{8,10},{9,11},{10,... | collective-permute-start | bytes 1179656 | tf_op jit(solution)/shard_map/ppermute | solution.py:20
  12.5 18.0 %collective-permute-start = (bf16[256,768]{1,0:T(8,128)(2,1)}, bf16[256,768]{1,0:T(8,128)(2,1)S(1)}, u32[]{:S(2)}, u32[]{:S(2)}) collective-permute-start(bf16[256,768]{1,0:T(8,128)(2,1)} %refs_0_.1), channel_id=1, source_target_pairs={{0,1},{1,0},{2,3},{3,2},{4,5},{5,4},{6,7},{7,6},{8,9},{9,8},{10,11... | collective-permute-start | bytes 1179656 | tf_op jit(solution)/shard_map/ppermute | solution.py:20
  12.5 17.8 %collective-permute-start.4 = (bf16[256,768]{1,0:T(8,128)(2,1)}, bf16[256,768]{1,0:T(8,128)(2,1)S(1)}, u32[]{:S(2)}, u32[]{:S(2)}) collective-permute-start(bf16[256,768]{1,0:T(8,128)(2,1)} %refs_5_.1), channel_id=1, source_target_pairs={{0,2},{1,3},{2,0},{3,1},{4,6},{5,7},{6,4},{7,5},{8,10},{9,11},{10,... | collective-permute-start | bytes 1179656 | tf_op jit(solution)/shard_map/ppermute | solution.py:20
  12.6 33.3 %collective-permute-start.3 = (bf16[256,768]{1,0:T(8,128)(2,1)}, bf16[256,768]{1,0:T(8,128)(2,1)S(1)}, u32[]{:S(2)}, u32[]{:S(2)}) collective-permute-start(bf16[256,768]{1,0:T(8,128)(2,1)} %refs_5_.1), channel_id=1, source_target_pairs={{0,1},{1,0},{2,3},{3,2},{4,5},{5,4},{6,7},{7,6},{8,9},{9,8},{10,11... | collective-permute-start | bytes 1179656 | tf_op jit(solution)/shard_map/ppermute | solution.py:20
  16.4 12.7 %all-to-all-start = ((bf16[8,2,240]{2,1,0:T(2,128)(2,1)}), bf16[8,2,240]{2,1,0:T(2,128)(2,1)S(1)}, u32[]{:S(2)}, u32[]{:S(2)}) async-start(bf16[8,2,240]{2,1,0:T(2,128)(2,1)} %reshape.154), calls=%async_computation | async-start | bytes 16384 | tf_op jit(solution)/shard_map/all_to_all | solution.py:82
  22.5 95.4 %all-gather.5.cloned.1.call-start = ((), (), s32[]{:S(2)}) async-start(), calls=%async_computation.8 | async-start | bytes 2654208 | tf_op jit(solution)/shard_map/all_gather | solution.py:649
  30.2 15.7 %collective-permute-start.5 = (bf16[256,768]{1,0:T(8,128)(2,1)S(1)}, bf16[256,768]{1,0:T(8,128)(2,1)}, u32[]{:S(2)}, u32[]{:S(2)}) collective-permute-start(bf16[256,768]{1,0:T(8,128)(2,1)S(1)} %collective-permute-done.4.refs_17_), channel_id=1, source_target_pairs={{0,1},{1,0},{2,3},{3,2},{4,5},{5,4},{6,7},{7,6},{8,9},{9,8},{10,11... | collective-permute-start | bytes 1179656 | tf_op jit(solution)/shard_map/ppermute | solution.py:20
  49.1 39.6 %all-to-all-start.2 = ((bf16[8,96,576]{2,1,0:T(8,128)(2,1)}), bf16[8,96,576]{2,1,0:T(8,128)(2,1)S(1)}, u32[]{:S(2)}, u32[]{:S(2)}) async-start(bf16[8,96,576]{2,1,0:T(8,128)(2,1)} %shard_map.323), calls=%async_computation.2 | async-start | bytes 1966080 | tf_op jit(solution)/shard_map/all_to_all | solution.py:82
  59.8 14.7 %collective-permute-start.7 = (bf16[768,384]{1,0:T(8,128)(2,1)S(1)}, bf16[768,384]{1,0:T(8,128)(2,1)S(1)}, u32[]{:S(2)}, u32[]{:S(2)}) collective-permute-start(bf16[768,384]{1,0:T(8,128)(2,1)S(1)} %slice.76.refs_6_.refs_2_), channel_id=1, source_target_pairs={{0,2},{1,3},{2,0},{3,1},{4,6},{5,7},{6,4},{7,5},{8,10},{9,11},{10,... | collective-permute-start | bytes 1769480 | tf_op jit(solution)/shard_map/ppermute | solution.py:20
  72.0 10.5 %collective-permute-start.10 = (bf16[512,384]{1,0:T(8,128)(2,1)}, bf16[512,384]{1,0:T(8,128)(2,1)S(1)}, u32[]{:S(2)}, u32[]{:S(2)}) collective-permute-start(bf16[512,384]{1,0:T(8,128)(2,1)} %get-tuple-element.139.refs_10_.refs_3_), channel_id=1, source_target_pairs={{0,2},{1,3},{2,0},{3,1},{4,6},{5,7},{6,4},{7,5},{8,10},{9,11},{10,... | collective-permute-start | bytes 1179656 | tf_op jit(solution)/shard_map/ppermute | solution.py:20
  72.6 16.0 %collective-permute-start.6 = (bf16[768,384]{1,0:T(8,128)(2,1)S(1)}, bf16[768,384]{1,0:T(8,128)(2,1)}, u32[]{:S(2)}, u32[]{:S(2)}) collective-permute-start(bf16[768,384]{1,0:T(8,128)(2,1)S(1)} %slice.76.refs_6_.refs_2_), channel_id=1, source_target_pairs={{0,1},{1,0},{2,3},{3,2},{4,5},{5,4},{6,7},{7,6},{8,9},{9,8},{10,11... | collective-permute-start | bytes 1769480 | tf_op jit(solution)/shard_map/ppermute | solution.py:20
  74.5 14.2 %collective-permute-start.8 = (bf16[768,384]{1,0:T(8,128)(2,1)S(1)}, bf16[768,384]{1,0:T(8,128)(2,1)}, u32[]{:S(2)}, u32[]{:S(2)}) collective-permute-start(bf16[768,384]{1,0:T(8,128)(2,1)S(1)} %collective-permute-done.7.refs_8_.refs_4_), channel_id=1, source_target_pairs={{0,1},{1,0},{2,3},{3,2},{4,5},{5,4},{6,7},{7,6},{8,9},{9,8},{10,11... | collective-permute-start | bytes 1769480 | tf_op jit(solution)/shard_map/ppermute | solution.py:20
  74.5 14.1 %collective-permute-start.9 = (bf16[512,384]{1,0:T(8,128)(2,1)}, bf16[512,384]{1,0:T(8,128)(2,1)}, u32[]{:S(2)}, u32[]{:S(2)}) collective-permute-start(bf16[512,384]{1,0:T(8,128)(2,1)} %get-tuple-element.139.refs_10_.refs_3_), channel_id=1, source_target_pairs={{0,1},{1,0},{2,3},{3,2},{4,5},{5,4},{6,7},{7,6},{8,9},{9,8},{10,11... | collective-permute-start | bytes 1179656 | tf_op jit(solution)/shard_map/ppermute | solution.py:20
  100.7 8.1 %collective-permute-start.13 = (bf16[512,384]{1,0:T(8,128)(2,1)}, bf16[512,384]{1,0:T(8,128)(2,1)S(1)}, u32[]{:S(2)}, u32[]{:S(2)}) collective-permute-start(bf16[512,384]{1,0:T(8,128)(2,1)} %get-tuple-element.141.refs_1_.refs_4_), channel_id=1, source_target_pairs={{0,2},{1,3},{2,0},{3,1},{4,6},{5,7},{6,4},{7,5},{8,10},{9,11},{10,... | collective-permute-start | bytes 1179656 | tf_op jit(solution)/shard_map/ppermute | solution.py:20
  138.0 12.4 %collective-permute-start.16 = (bf16[512,384]{1,0:T(8,128)(2,1)S(1)}, bf16[512,384]{1,0:T(8,128)(2,1)}, u32[]{:S(2)}, u32[]{:S(2)}) collective-permute-start(bf16[512,384]{1,0:T(8,128)(2,1)S(1)} %add_convert_fusion.6), channel_id=1, source_target_pairs={{0,2},{1,3},{2,0},{3,1},{4,6},{5,7},{6,4},{7,5},{8,10},{9,11},{10,... | collective-permute-start | bytes 1179656 | tf_op jit(solution)/shard_map/ppermute | solution.py:20
  150.4 63.0 %all-to-all-start.3 = ((bf16[8,96,1536]{2,1,0:T(8,128)(2,1)}), bf16[8,96,1536]{2,1,0:T(8,128)(2,1)S(1)}, u32[]{:S(2)}, u32[]{:S(2)}) async-start(bf16[8,96,1536]{2,1,0:T(8,128)(2,1)} %bitcast.48), calls=%async_computation.3 | async-start | bytes 4718592 | tf_op jit(solution)/shard_map/all_to_all | solution.py:82
  157.9 18.2 %collective-permute-start.21 = (bf16[256,1408]{1,0:T(8,128)(2,1)S(1)}, bf16[256,1408]{1,0:T(8,128)(2,1)S(1)}, u32[]{:S(2)}, u32[]{:S(2)}) collective-permute-start(bf16[256,1408]{1,0:T(8,128)(2,1)S(1)} %add_convert_fusion), channel_id=1, source_target_pairs={{0,2},{1,3},{2,0},{3,1},{4,6},{5,7},{6,4},{7,5},{8,10},{9,11},{10,... | collective-permute-start | bytes 2162696 | tf_op jit(solution)/shard_map/ppermute | solution.py:20
  170.6 8.2 %collective-permute-start.17 = (bf16[256,1408]{1,0:T(8,128)(2,1)}, bf16[256,1408]{1,0:T(8,128)(2,1)}, u32[]{:S(2)}, u32[]{:S(2)}) collective-permute-start(bf16[256,1408]{1,0:T(8,128)(2,1)} %get-tuple-element.159), channel_id=1, source_target_pairs={{0,1},{1,0},{2,3},{3,2},{4,5},{5,4},{6,7},{7,6},{8,9},{9,8},{10,11... | collective-permute-start | bytes 2162696 | tf_op jit(solution)/shard_map/ppermute | solution.py:20
  177.0 11.9 %collective-permute-start.23 = (bf16[512,384]{1,0:T(8,128)(2,1)}, bf16[512,384]{1,0:T(8,128)(2,1)}, u32[]{:S(2)}, u32[]{:S(2)}) collective-permute-start(bf16[512,384]{1,0:T(8,128)(2,1)} %add_convert_fusion.5), channel_id=1, source_target_pairs={{0,2},{1,3},{2,0},{3,1},{4,6},{5,7},{6,4},{7,5},{8,10},{9,11},{10,... | collective-permute-start | bytes 1179656 | tf_op jit(solution)/shard_map/ppermute | solution.py:20
  192.0 20.4 %collective-permute-start.26 = (bf16[4,96,768]{2,1,0:T(8,128)(2,1)}, bf16[4,96,768]{2,1,0:T(8,128)(2,1)S(1)}, u32[]{:S(2)}, u32[]{:S(2)}) collective-permute-start(bf16[4,96,768]{2,1,0:T(8,128)(2,1)} %get-tuple-element.202), channel_id=1, source_target_pairs={{0,4},{4,0},{8,12},{12,8},{16,20},{20,16},{24,28},{28,24},{1,5},{5... | collective-permute-start | bytes 1769480 | tf_op jit(solution)/shard_map/ppermute | solution.py:53
  194.0 19.4 %collective-permute-start.25 = (bf16[256,768]{1,0:T(8,128)(2,1)S(1)}, bf16[256,768]{1,0:T(8,128)(2,1)}, u32[]{:S(2)}, u32[]{:S(2)}) collective-permute-start(bf16[256,768]{1,0:T(8,128)(2,1)S(1)} %add_convert_fusion.4), channel_id=1, source_target_pairs={{0,2},{1,3},{2,0},{3,1},{4,6},{5,7},{6,4},{7,5},{8,10},{9,11},{10,... | collective-permute-start | bytes 1179656 | tf_op jit(solution)/shard_map/ppermute | solution.py:20
  195.5 17.9 %collective-permute-start.27 = (bf16[256,768]{1,0:T(8,128)(2,1)}, bf16[256,768]{1,0:T(8,128)(2,1)}, u32[]{:S(2)}, u32[]{:S(2)}) collective-permute-start(bf16[256,768]{1,0:T(8,128)(2,1)} %get-tuple-element.207), channel_id=1, source_target_pairs={{0,1},{1,0},{2,3},{3,2},{4,5},{5,4},{6,7},{7,6},{8,9},{9,8},{10,11... | collective-permute-start | bytes 1179656 | tf_op jit(solution)/shard_map/ppermute | solution.py:20
  220.7 23.7 %all-to-all-start.4 = ((bf16[4,96,768]{2,1,0:T(8,128)(2,1)}), bf16[4,96,768]{2,1,0:T(8,128)(2,1)S(1)}, u32[]{:S(2)}, u32[]{:S(2)}) async-start(bf16[4,96,768]{2,1,0:T(8,128)(2,1)} %add_convert_fusion.2), calls=%async_computation.4 | async-start | bytes 1179648 | tf_op jit(solution)/shard_map/all_to_all | solution.py:95
  225.6 16.7 %collective-permute-start.28 = (bf16[4,96,768]{2,1,0:T(8,128)(2,1)}, bf16[4,96,768]{2,1,0:T(8,128)(2,1)}, u32[]{:S(2)}, u32[]{:S(2)}) collective-permute-start(bf16[4,96,768]{2,1,0:T(8,128)(2,1)} %get-tuple-element.217), channel_id=1, source_target_pairs={{0,4},{4,0},{8,12},{12,8},{16,20},{20,16},{24,28},{28,24},{1,5},{5... | collective-permute-start | bytes 1769480 | tf_op jit(solution)/shard_map/ppermute | solution.py:53
  233.7 8.7 %collective-permute-start.31 = (bf16[16,768]{1,0:T(8,128)(2,1)S(1)}, bf16[16,768]{1,0:T(8,128)(2,1)S(1)}, u32[]{:S(2)}, u32[]{:S(2)}) collective-permute-start(bf16[16,768]{1,0:T(8,128)(2,1)S(1)} %select_convert_fusion), channel_id=1, source_target_pairs={{0,4},{4,0},{8,12},{12,8},{16,20},{20,16},{24,28},{28,24},{1,5},{5... | collective-permute-start | bytes 73736 | tf_op jit(solution)/shard_map/ppermute | solution.py:53
  247.4 25.6 %all-to-all-start.5 = ((bf16[4,128,768]{2,1,0:T(8,128)(2,1)}), bf16[4,128,768]{2,1,0:T(8,128)(2,1)S(1)}, u32[]{:S(2)}, u32[]{:S(2)}) async-start(bf16[4,128,768]{2,1,0:T(8,128)(2,1)} %pad_maximum_fusion), calls=%async_computation.5 | async-start | bytes 1572864 | tf_op jit(solution)/shard_map/all_to_all | solution.py:95
  254.3 11.4 %collective-permute-start.34 = (bf16[256,768]{1,0:T(8,128)(2,1)S(1)}, bf16[256,768]{1,0:T(8,128)(2,1)S(1)}, u32[]{:S(2)}, u32[]{:S(2)}) collective-permute-start(bf16[256,768]{1,0:T(8,128)(2,1)S(1)} %add_convert_fusion.3), channel_id=1, source_target_pairs={{0,2},{1,3},{2,0},{3,1},{4,6},{5,7},{6,4},{7,5},{8,10},{9,11},{10,... | collective-permute-start | bytes 1179656 | tf_op jit(solution)/shard_map/ppermute | solution.py:20
  274.0 15.2 %collective-permute-start.35 = (bf16[24,1536]{1,0:T(8,128)(2,1)S(1)}, bf16[24,1536]{1,0:T(8,128)(2,1)S(1)}, u32[]{:S(2)}, u32[]{:S(2)}) collective-permute-start(bf16[24,1536]{1,0:T(8,128)(2,1)S(1)} %get-tuple-element.228), channel_id=1, source_target_pairs={{0,1},{1,0},{2,3},{3,2},{4,5},{5,4},{6,7},{7,6},{8,9},{9,8},{10,11... | collective-permute-start | bytes 221192 | tf_op jit(solution)/shard_map/ppermute | solution.py:817
  274.1 15.1 %collective-permute-start.36 = (bf16[24,1536]{1,0:T(8,128)(2,1)S(1)}, bf16[24,1536]{1,0:T(8,128)(2,1)S(1)}, u32[]{:S(2)}, u32[]{:S(2)}) collective-permute-start(bf16[24,1536]{1,0:T(8,128)(2,1)S(1)} %get-tuple-element.229), channel_id=1, source_target_pairs={{0,2},{1,3},{2,0},{3,1},{4,6},{5,7},{6,4},{7,5},{8,10},{9,11},{10,... | collective-permute-start | bytes 221192 | tf_op jit(solution)/shard_map/ppermute | solution.py:817
  274.7 14.4 %collective-permute-start.37 = (bf16[24,1536]{1,0:T(8,128)(2,1)S(1)}, bf16[24,1536]{1,0:T(8,128)(2,1)S(1)}, u32[]{:S(2)}, u32[]{:S(2)}) collective-permute-start(bf16[24,1536]{1,0:T(8,128)(2,1)S(1)} %get-tuple-element.230), channel_id=1, source_target_pairs={{0,3},{1,2},{2,1},{3,0},{4,7},{5,6},{6,5},{7,4},{8,11},{9,10},{10,... | collective-permute-start | bytes 221192 | tf_op jit(solution)/shard_map/ppermute | solution.py:817
  276.9 10.3 %all-to-all-start.6 = ((f32[8,1,96]{2,1,0:T(1,128)}), f32[8,1,96]{2,1,0:T(1,128)S(1)}, u32[]{:S(2)}, u32[]{:S(2)}) async-start(f32[8,1,96]{2,1,0:T(1,128)} %bitcast.12), calls=%async_computation.6 | async-start | bytes 8192 | tf_op jit(solution)/shard_map/all_to_all | solution.py:82
  (40 other events, 393.1 us)
Sparse Core Ops, SparseCore 0:
  10.8 47.8 all-gather.2
  61.5 56.4 all-gather.4

commit v5 on v4

--- a/solution.py
+++ b/solution.py
@@ -38,13 +38,6 @@
     )
 
 
-def head_sum(chunks, swap=swap):
-    a, b = swap(chunks[1], 1), swap(chunks[3], 1)
-    mine = chunks[0].astype(F32) + a.astype(F32)
-    other = (chunks[2].astype(F32) + b.astype(F32)).astype(chunks[0].dtype)
-    return mine + swap(other, 2).astype(F32)
-
-
 def after(values, ready):
     return lax.optimization_barrier((values, ready))[0]
 
@@ -53,46 +46,22 @@
     return lax.ppermute(x, "seq", [(i, i ^ bit) for i in range(lax.axis_size("seq"))])
 
 
-def seq_bits():
-    return [1 << b for b in range(lax.axis_size("seq").bit_length() - 1)]
-
-
-def seq_gather(x):
-    for bit in seq_bits():
-        x = jnp.concatenate([x, seq_swap(x, bit)], axis=0)
-    return x
-
-
-def seq_scatter_sum(x):
-    for bit in reversed(seq_bits()):
-        x = x[:bit] + seq_swap(x[bit:], bit)
-    return x
-
-
-def seq_order(x, s):
-    n = x.shape[0]
-    at = (s ^ jnp.arange(n))[:, None] == jnp.arange(n)[None, :]
-    precision = lax.Precision.HIGHEST if x.dtype == F32 else None
-    return lax.dot_general(
-        at.astype(x.dtype), x, (((1,), (0,)), ((), ())), precision=precision, preferred_element_type=F32
-    )
-
-
 def exchange(x):
     return lax.all_to_all(x, "seq", split_axis=0, concat_axis=0, tiled=True)
 
 
-def alike():
-    n = lax.axis_size("seq")
-    return [list(range(odd, n, 2)) for odd in (0, 1)]
-
-
 def half_reduce(near, far):
     return (near.astype(F32) + seq_swap(far, 1).astype(F32)).astype(BF)
 
 
-def rest_reduce(part):
-    return lax.all_to_all(part, "seq", split_axis=0, concat_axis=0, axis_index_groups=alike(), tiled=True)
+def rest_reduce(x, sent=None):
+    x, bit = x.astype(F32), 2
+    while x.shape[0] > 1:
+        send = x[1::2].astype(BF)
+        if sent is not None:
+            sent.append(send)
+        x, bit = x[0::2] + seq_swap(send, bit).astype(F32), 2 * bit
+    return x[0]
 
 
 def stats(v):
@@ -465,25 +434,51 @@
     )
 
 
-def self_back(a0, a1, a2, sm, inv, qkv, p, grads_ref, ds_ref):
+def self_back(
+    place, a0, a1, a2, sm, inv, qkv, p, n_one, w, mod, vec_c, vec_d, gate, grads_ref, near_ref, far_ref, vec_ref, ds_ref, whole_ref,
+    *, kr,
+):
     hw = qkv.shape[2]
+    width = w.shape[0]
     grads = [sum(unpack(a, b).astype(F32) for a in (a0, a1, a2)) for b in BLOCKS]
     results = [unpack(sm, b) for b in BLOCKS]
     dqs, dk, dv = softmax_back(qkv[1], qkv[2], qkv[0], p, inv, results, grads, ds_ref)
-    for b in BLOCKS:
-        grads_ref[block(b), :hw] = dqs[b]
-    grads_ref[:, hw : 2 * hw] = dk
-    grads_ref[:, 2 * hw :] = dv
-
-
-def first_back(x0, x1, x2, x3, grads, w, mod, gas, gf_ref):
+    joint = jnp.concatenate([jnp.concatenate(dqs, axis=0), dk, dv], axis=1)
+    grads_ref[...] = joint
+    grads_ref.send()
+    product = mm(n_one[...], joint, 0, 0)
+    sums = jnp.sum(joint.astype(F32), axis=0, keepdims=True)
+    weights = w[...].astype(F32)
+    grad = (1.0 + mod[:, width : 2 * width]).T * product + mod[:, :width].T * sums
+    empty = jnp.zeros((width, near_ref.shape[-1] - 3 * hw), BF)
+    whole_ref[...] = jnp.concatenate([grad.astype(BF), empty], axis=1)
+    part_rows(whole_ref, place, near_ref, far_ref, kr)
+    shift_one = jnp.sum(weights * sums, axis=1, keepdims=True).T
+    scale_one = jnp.sum(weights * product, axis=1, keepdims=True).T
+    rows = [shift_one, scale_one, vec_d[0:1], vec_c[0:1], vec_c[1:2], gate[...], vec_d[2:3], vec_d[1:2]]
+    rows += [vec_c[2:3], vec_c[4:5], vec_c[3:4], jnp.zeros((5, width), F32)]
+    vec_ref[...] = jnp.concatenate(rows, axis=0)
+
+
+def out_rows(place, o0, o1, o2, near_ref, far_ref, cap_ref, whole_ref, *, kr):
+    hw = o0.shape[1] // 4
+    rows = o0.shape[0]
+    total = sum(o[...].astype(F32) for o in (o0, o1, o2))
+    cap_ref[0] = total[:, 3 * hw :]
+    low = total[:, : 3 * hw].astype(BF)
+    for k in range(3):
+        whole_ref[block(k, rows), :] = low[:, k * hw : (k + 1) * hw]
+    part_rows(whole_ref, place, near_ref, far_ref, kr, out_third=kr // 3)
+
+
+def first_back(x0, x1, x2, x3, grads, w, mod, gas, *frame_refs):
     width = x0.shape[1]
     weights = w[:, w.shape[1] - grads.shape[1] :]
     gfirsts = [mm(grads[block(b), :], weights, 1, 1) for b in BLOCKS]
     scale = 1.0 + mod[:, width : 2 * width]
     for b, x in enumerate((x0, x1, x2, x3)):
         ga = normback(*stats(x[...].astype(F32)), scale * gfirsts[b])
-        gf_ref[block(b), :] = (gas[block(b), :].astype(F32) + ga).astype(BF)
+        frame_refs[b][...] = (gas[block(b), :].astype(F32) + ga).astype(BF)
 
 
 def own_columns(head, *refs, hw):
@@ -515,21 +510,27 @@
     both_ref[:, gup.shape[1] :] = mm(gfeed[...], hidden[...], 0, 0).astype(BF)
 
 
-def part_rows(value, odd, near_ref, far_ref, kr):
+def part_rows(value, place, near_ref, far_ref, kr, out_third=0):
     if kr % 16:
-        near_ref[...] = value
-        far_ref[...] = value
+        near_ref[...] = value[...]
+        far_ref[...] = value[...]
         return
-    for z in range(value.shape[0] // (2 * kr)):
-        even_rows = value[2 * z * kr : (2 * z + 1) * kr]
-        odd_rows = value[(2 * z + 1) * kr : (2 * z + 2) * kr]
-        near_ref[z] = jnp.where(odd == 1, odd_rows, even_rows)
-        far_ref[z] = jnp.where(odd == 1, even_rows, odd_rows)
+    for j in range(near_ref.shape[0]):
+        first = ((place[1] >> 1) ^ j) * 2
+        for ref, index in ((near_ref, first + (place[1] & 1)), (far_ref, first + 1 - (place[1] & 1))):
+            block_rows = value[pl.ds(pl.multiple_of(index * kr, kr), kr), :]
+            if out_third:
+                hw = block_rows.shape[1]
+                for k in range(3):
+                    ref[j, :, k * hw : (k + 1) * hw] = block_rows[k * out_third : (k + 1) * out_third]
+                ref[j, :, 3 * hw :] = jnp.zeros((out_third, ref.shape[2] - 3 * hw), BF)
+            else:
+                ref[j] = block_rows
 
 
 def mid_weights(
     place, f0, f1, f2, across, cot, mod, dn_bias, sm, gproj, caption, dpair, w_later, second, dq,
-    near_ref, far_ref, c0, c1, c2, c3, output_ref, gate_ref, *, kr,
+    near_ref, far_ref, c0, c1, c2, c3, output_ref, gate_ref, whole_ref, *, kr,
 ):
     hw, width = dq.shape[1], sm.shape[1]
     rows = f0.shape[0]
@@ -547,33 +548,19 @@
     low = total[:, width:].astype(BF)
     cross = jnp.concatenate([low[:, k * hw : (k + 1) * hw] for k in range(3)], axis=0)
     parts = [mm(second[...], dq[...], 0, 0)] + [mm(caption[...], dpair[t], 0, 0) for t in range(2)]
-    part_rows(jnp.concatenate([cross] + [p.astype(BF) for p in parts], axis=1), place[1], near_ref, far_ref, kr)
-
-
-def last_weights(place, n_one, gjoint, mod, w, o0, o1, o2, vec_c, vec_d, gate, near_ref, far_ref, cap_ref, vec_ref, *, kr):
-    hw = gjoint.shape[1] // 3
-    rows, width = o0.shape[0], w.shape[0]
-    product = mm(n_one[...], gjoint[...], 0, 0)
-    sums = jnp.sum(gjoint[...].astype(F32), axis=0, keepdims=True)
-    weights = w[:, 2 * hw :].astype(F32)
-    vec_ref[0:1, :] = jnp.sum(weights * sums, axis=1, keepdims=True).T
-    vec_ref[1:2, :] = jnp.sum(weights * product, axis=1, keepdims=True).T
-    grad = (1.0 + mod[:, width : 2 * width]).T * product + mod[:, :width].T * sums
-    total = sum(o[...].astype(F32) for o in (o0, o1, o2))
-    cap_ref[0] = total[:, 3 * hw :]
-    low = total[:, : 3 * hw].astype(BF)
-    cross = jnp.concatenate([low[:, k * hw : (k + 1) * hw] for k in range(3)], axis=0)
-    part_rows(jnp.concatenate([cross, grad.astype(BF)], axis=1), place[1], near_ref, far_ref, kr)
-    rest = (vec_d[0:1], vec_c[0:1], vec_c[1:2], gate[...], vec_d[2:3], vec_d[1:2], vec_c[2:3], vec_c[4:5], vec_c[3:4])
-    for t, row in enumerate(rest):
-        vec_ref[2 + t : 3 + t, :] = row
-    vec_ref[2 + len(rest) :, :] = jnp.zeros((vec_ref.shape[0] - 2 - len(rest), width), F32)
-
-
-def column_chunks(head, mid, last, *refs):
+    whole_ref[...] = jnp.concatenate([cross] + [p.astype(BF) for p in parts], axis=1)
+    part_rows(whole_ref, place, near_ref, far_ref, kr)
+
+
+def column_chunks(head, mid, last, third_rows, *refs):
     own = refs[0].shape[0]
-    parts = mid[...], last[:, : mid.shape[1], :]
-    value = jnp.concatenate([jnp.sum(v.astype(F32), axis=0) for v in parts], axis=1)
+    hw = mid.shape[1] // 4
+    kr = 4 * own
+
+    outs = third_rows[...]
+    if outs.shape[1] > hw:
+        outs = jnp.concatenate([outs[:, k * hw : (k + 1) * hw] for k in range(3)], axis=0)
+    value = jnp.concatenate([mid[...], outs, last[:kr, : 3 * hw]], axis=1)
     for j, ref in enumerate(refs):
         ref[...] = pick([value[a * own : (a + 1) * own] for a in range(4)], head[0] ^ j).astype(BF)
 
@@ -703,7 +690,7 @@
 
     mine, near, other = near_terms(chunks)
     far = swap(other, 2)
-    place = jnp.stack([h, s & 1]).astype(jnp.int32)
+    place = jnp.stack([h, s]).astype(jnp.int32)
 
     def halves(columns):
         shape = (width, columns) if kr % 16 else (n // 2, kr, columns)
@@ -712,11 +699,11 @@
     def parted(near_rows, far_rows):
         if kr % 16 == 0:
             return near_rows, far_rows
-        near_rows, far_rows = (v.reshape(n // 2, 2, kr, -1) for v in (near_rows, far_rows))
-        return (
-            lax.dynamic_index_in_dim(near_rows, s & 1, 1, keepdims=False),
-            lax.dynamic_index_in_dim(far_rows, 1 - (s & 1), 1, keepdims=False),
-        )
+        v = near_rows.reshape(n, kr, -1)
+        for bit in (1 << b for b in range(n.bit_length() - 1)):
+            pairs = v.reshape(n // (2 * bit), 2, bit, kr, -1)
+            v = jnp.where((s & bit) != 0, pairs[:, ::-1], pairs).reshape(n, kr, -1)
+        return v[0::2], v[1::2]
 
     *feed_chunks, both = call(
         feed_weights,
@@ -748,44 +735,55 @@
         halves(4 * hw)
         + [out((rows, 4 * hw), BF) for _ in range(4)]
         + [out((rows, width), BF), out((1, width), F32)],
+        [pltpu.VMEM((width, 4 * hw), BF)],
     )
     out_mine, out_near, out_other = near_terms(after((out0, out1, out2, out3), far))
     far, mid, out_other = lax.optimization_barrier((far, mid, out_other))
+    out_far = swap(out_other, 2)
     mid = half_reduce(*parted(*mid))
-    out_far = swap(out_other, 2)
-    (g_joint,) = call(
-        self_back,
-        [],
-        [mine, near, far, sm_own, inv, qkv, probs],
-        [out((total, 3 * hw), BF)],
-        [pltpu.VMEM((heads, total, total), BF)],
-    )
-    n_one, out_far, mid, both = after((n_one, out_far, mid, both), g_joint)
-    *last, grad_captions, vec = call(
-        partial(last_weights, kr=kr),
+    g_joint, *last, vec = call(
+        partial(self_back, kr=kr),
         [place],
-        [n_one, g_joint, mod, w_own, out_mine, out_near, out_far, vec_c, vec_d, gv_gate2],
-        halves(4 * hw) + [out((1, slots, hw), F32), out((16, width), F32)],
-    )
-    mid = rest_reduce(after(mid, both))
-    gas, last, vec = lax.optimization_barrier((gas, last, vec))
+        [mine, near, far, sm_own, inv, qkv, probs, n_one, (w_own, (slice(None), slice(2 * hw, 5 * hw)))]
+        + [mod, vec_c, vec_d, gv_gate2],
+        [out((total, 3 * hw), BF)] + halves(3 * hw + pad) + [out((16, width), F32)],
+        [pltpu.VMEM((heads, total, total), BF), pltpu.VMEM((width, 3 * hw + pad), BF)],
+    )
+    vec, mid, both, out_far = lax.optimization_barrier((vec, mid, both, out_far))
+    near_rows, far_rows = parted(*last)
+    last = half_reduce(near_rows, after(far_rows, mid))
+    last_y = last
     shared = vec + swap(vec, 1)
     shared = shared + swap(shared, 2)
     vec = jnp.where(jnp.arange(16)[:, None] == 10, vec, shared).astype(BF)
-    last = half_reduce(*parted(*last))
-    vec = jnp.concatenate([vec, seq_swap(vec, 1)], axis=0)
-    (gf,) = call(first_back, [], [*x, g_joint, w_own, mod, gas], [deep])
-    gf, last, vec, mid = lax.optimization_barrier((gf, last, vec, mid))
-    last = jnp.concatenate([last, jnp.broadcast_to(vec[None], (n // 2, *vec.shape))], axis=1)
-    last = rest_reduce(last)
-    vec = last[:, kr:].reshape(n, 16, width).astype(F32)
+    mid_y = mid
+    mid = rest_reduce(mid)
+    third_shape = (width, hw) if kr % 16 else (n // 2, kr // 3, 3 * hw + pad)
+    *outs, grad_captions = call(
+        partial(out_rows, kr=kr),
+        [place],
+        [out_mine, out_near, out_far],
+        [out(third_shape, BF) for _ in range(2)] + [out((1, slots, hw), F32)],
+        [pltpu.VMEM((width, hw), BF)],
+    )
+    near_rows, far_rows = parted(*outs)
     if kr % 16:
-        last = last[:, :kr]
-    grad_frames = head_sum([gf[j * rows : (j + 1) * rows] for j in range(4)])
-
-    def pairs(v):
-        v = v.reshape(n // 2, 2, -1)
-        return jnp.where((s & 1) == 1, v[:, ::-1], v).reshape(n, -1)
+        near_rows, far_rows = (
+            jnp.pad(
+                v.reshape(n // 2, 3, kr // 3, hw).transpose(0, 2, 1, 3).reshape(n // 2, kr // 3, 3 * hw),
+                ((0, 0), (0, 0), (0, pad)),
+            )
+            for v in (near_rows, far_rows)
+        )
+    outs = half_reduce(near_rows, far_rows)
+    vec = exchange(jnp.broadcast_to(after(vec, last_y)[None], (n, *vec.shape))).astype(F32)
+    sent = []
+    last = rest_reduce(jnp.concatenate([last, outs], axis=1), sent)
+    outs = last[kr:]
+    gf = call(first_back, [], [*x, g_joint, w_own, mod, after(gas, sent[-1])], [out((rows, width), BF)] * 4)
+    if kr % 16:
+        outs = outs[:, : 3 * hw].reshape(own * 4 // 3, 3, hw).transpose(1, 0, 2).reshape(kr, hw)
+    frame_mine, frame_near, frame_other = near_terms(gf)
 
     g_mod = vec[:, :6].reshape(n, 6 * width)
     g_cond = lax.dot_general(
@@ -795,10 +793,10 @@
         precision=lax.Precision.HIGHEST,
         preferred_element_type=F32,
     )
-    g_silu = exchange(pairs(g_cond)).reshape(width)
+    g_silu = exchange(after(g_cond, frame_other)).reshape(width)
     g_cond = jax.vjp(jax.nn.silu, condition[0].astype(F32))[1](g_silu)[0]
     grad_condition = lax.dynamic_slice_in_dim(g_cond, h * hw, hw, 0)[None]
-    cond_rows = pairs(lax.dynamic_slice_in_dim(cond_own, h * own, own, 1).astype(F32))
+    cond_rows = lax.dynamic_slice_in_dim(cond_own, h * own, own, 1).astype(F32)
     grad_mod_weight = lax.dot_general(
         cond_rows, g_mod, (((0,), (0,)), ((), ())), precision=lax.Precision.HIGHEST, preferred_element_type=F32
     )
@@ -812,7 +810,9 @@
 
     both = both.astype(F32).sum(0)
     tiny = dict(small=1 << 20, limit=8)
-    cols = call(column_chunks, [head], [mid, last], [out((own, 8 * hw), BF) for _ in range(4)], **tiny)
+    cols = call(column_chunks, [head], [mid, last, outs], [out((own, 8 * hw), BF) for _ in range(4)], **tiny)
+    frame_far = swap(frame_other, 2)
+    grad_frames = frame_mine.astype(F32) + frame_near.astype(F32) + frame_far.astype(F32)
     cols = [cols[0]] + [
         lax.ppermute(cols[j], "head", [(i, i ^ j) for i in range(4)]) for j in range(1, 4)
     ]

time: 301 us -> 293 us (0.973)
  waiting for transfers between devices: 74 us -> 60.5 us
  starting transfers between devices: 50.3 us -> 54.1 us
    ppermute x32, waiting for transfers between devices: 37.9 us -> 26.9 us  [swap(): return lax.ppermute(x, 'head', [(i, i ^ bit) for i in range(4)])]
    all_to_all x2 -> x0, starting transfers between devices: 9.78 us -> none  [rest_reduce(): lax.all_to_all(part, 'seq', split_axis=0, concat_axis=0, axis_index_group...]
    ppermute x3 -> x7, starting transfers between devices: 4.29 us -> 11.5 us  [seq_swap(): lax.ppermute(x, 'seq', [(i, i ^ bit) for i in range(lax.axis_size('seq'))])]
    all_to_all x2 -> x0, waiting for transfers between devices: 5.28 us -> none  [rest_reduce(): lax.all_to_all(part, 'seq', split_axis=0, concat_axis=0, axis_index_group...]
    all_to_all x4 -> x5, starting transfers between devices: 19.4 us -> 24.6 us  [exchange(): return lax.all_to_all(x, 'seq', split_axis=0, concat_axis=0, tiled=True)]
    ppermute x3, waiting for transfers between devices: 0.01 us -> 4.88 us  [on_device(): lax.ppermute(cols[j], 'head', [(i, i ^ j) for i in range(4)])]
    ppermute x3 -> x7, waiting for transfers between devices: 6.36 us -> 9.49 us  [seq_swap(): lax.ppermute(x, 'seq', [(i, i ^ bit) for i in range(lax.axis_size('seq'))])]
    all_to_all x4 -> x5, waiting for transfers between devices: 13 us -> 10.3 us  [exchange(): return lax.all_to_all(x, 'seq', split_axis=0, concat_axis=0, tiled=True)]
  transfers between devices with their start and end apart: 46 -> 49, of which waited for: 21 -> 19; matrix products, arithmetic and copies ran while one was open for 12% -> 13% of each run, Pallas kernels for 25% -> 29%
where the time goes in v5:
time: 293 us; the launch traced here: 289 us
  Pallas kernels  102 us (35%)
  waiting for transfers between devices  60.5 us (21%)
  starting transfers between devices  54.1 us (18%)
  other arithmetic  22.3 us (8%)
  local copies, waits for them, and re-layouts  18.9 us (6%)
  between operations  15.6 us (5%)
  blocking collectives  13.9 us (5%)
    pallas_call x13, Pallas kernels, call(): pl.pallas_call(body, in_specs=[pl.BlockSpec(memory_space=pltpu.SMEM)] * l...  102 us
    ppermute x32, waiting for transfers between devices, swap(): return lax.ppermute(x, 'head', [(i, i ^ bit) for i in range(4)])  26.9 us
    all_to_all x5, starting transfers between devices, exchange(): return lax.all_to_all(x, 'seq', split_axis=0, concat_axis=0, tiled=True)  24.6 us
    ppermute x32, starting transfers between devices, swap(): return lax.ppermute(x, 'head', [(i, i ^ bit) for i in range(4)])  16 us
    all_to_all x1, blocking collectives, exchange(): return lax.all_to_all(x, 'seq', split_axis=0, concat_axis=0, tiled=True)  13.9 us
    ppermute x7, starting transfers between devices, seq_swap(): lax.ppermute(x, 'seq', [(i, i ^ bit) for i in range(lax.axis_size('seq'))])  11.5 us
    all_to_all x5, waiting for transfers between devices, exchange(): return lax.all_to_all(x, 'seq', split_axis=0, concat_axis=0, tiled=True)  10.3 us
    ppermute x7, waiting for transfers between devices, seq_swap(): lax.ppermute(x, 'seq', [(i, i ^ bit) for i in range(lax.axis_size('seq'))])  9.49 us
  transfers between devices with their start and end apart: 49, of which 19 were waited for; matrix products, arithmetic and copies ran while one was open for 13% of the time, Pallas kernels for 29%

profile of v5, /device:TPU:0, one launch (start us, length us, event | category | flops | bytes accessed | tf_op | source)
XLA Modules:
  0.0 289.1 jit_solution(543269414067450542)
XLA Ops:
  7.3 2.2 shard_map.322
  9.5 3.0 %collective-permute-start.1 = (bf16[256,768]{1,0:T(8,128)(2,1)}, bf16[256,768]{1,0:T(8,128)(2,1)S(1)}, u32[]{:S(2)}, u32[]{:S(2)}) collective-permute-start(bf16[256,768]{1,0:T(8,128)(2,1)} %refs_0_.1), channel_id=1, source_target_pairs={{0,2},{1,3},{2,0},{3,1},{4,6},{5,7},{6,4},{7,5},{8,10},{9,11},{10,... | collective-permute-start | bytes 1179656 | tf_op jit(solution)/shard_map/ppermute | solution.py:20
  16.4 6.1 %all-to-all-start = ((bf16[8,2,240]{2,1,0:T(2,128)(2,1)}), bf16[8,2,240]{2,1,0:T(2,128)(2,1)S(1)}, u32[]{:S(2)}, u32[]{:S(2)}) async-start(bf16[8,2,240]{2,1,0:T(2,128)(2,1)} %reshape.131), calls=%async_computation | async-start | bytes 16384 | tf_op jit(solution)/shard_map/all_to_all | solution.py:50
  23.5 5.6 %all-to-all-done = bf16[8,2,240]{2,1,0:T(2,128)(2,1)S(1)} async-done(((bf16[8,2,240]{2,1,0:T(2,128)(2,1)}), bf16[8,2,240]{2,1,0:T(2,128)(2,1)S(1)}, u32[]{:S(2)}, u32[]{:S(2)}) %all-to-all-start) | async-done | bytes 7712 | tf_op jit(solution)/shard_map/all_to_all | solution.py:50
  30.6 13.9 %all_to_all.45 = f32[8,1,4608]{2,1,0:T(1,128)S(1)} all-to-all(f32[8,1,4608]{2,1,0:T(1,128)S(1)} %copy.44), channel_id=1, replica_groups=mesh['seq'=8,'head'=4] {'seq'}, dimensions={0} | all-to-all | bytes 294912 | tf_op jit(solution)/shard_map/all_to_all | solution.py:50
  48.5 2.3 shard_map.323
  50.8 6.1 %all-to-all-start.2 = ((bf16[8,96,576]{2,1,0:T(8,128)(2,1)}), bf16[8,96,576]{2,1,0:T(8,128)(2,1)S(1)}, u32[]{:S(2)}, u32[]{:S(2)}) async-start(bf16[8,96,576]{2,1,0:T(8,128)(2,1)} %shard_map.323), calls=%async_computation.2 | async-start | bytes 1966080 | tf_op jit(solution)/shard_map/all_to_all | solution.py:50
  61.2 10.6 %shard_map.324 = (bf16[1024,768]{1,0:T(8,128)(2,1)}, bf16[3,1024,192]{2,1,0:T(8,128)(2,1)}, bf16[512,384]{1,0:T(8,128)(2,1)}, bf16[3,1024,1024]{2,1,0:T(8,128)(2,1)}, f32[3,1024]{1,0:T(4,128)}) custom-call(bf16[256,768]{1,0:T(8,128)(2,1)} %refs_0_.1, bf16[256,768]{1,0:T(8,128)(2,1)} %copy-done.4, bf16[256,768]{1,0:T(8,128)(2,1)} %copy-done.3, ...), custom_call_target="tpu_custom_call" | custom-call | tf_op jit(solution)/shard_map/pallas_call | solution.py:146
  72.7 2.6 collective-permute-done.7.refs_8_.refs_4_
  75.8 7.4 %collective-permute-done.10.refs_12_ = bf16[512,384]{1,0:T(8,128)(2,1)S(1)} collective-permute-done((bf16[512,384]{1,0:T(8,128)(2,1)}, bf16[512,384]{1,0:T(8,128)(2,1)S(1)}, u32[]{:S(2)}, u32[]{:S(2)}) %collective-permute-start.10) | collective-permute-done | bytes 393248 | tf_op jit(solution)/shard_map/ppermute | solution.py:20
  85.4 4.8 %all-to-all-done.2 = bf16[8,96,576]{2,1,0:T(8,128)(2,1)S(1)} async-done(((bf16[8,96,576]{2,1,0:T(8,128)(2,1)}), bf16[8,96,576]{2,1,0:T(8,128)(2,1)S(1)}, u32[]{:S(2)}, u32[]{:S(2)}) %all-to-all-start.2) | async-done | bytes 884768 | tf_op jit(solution)/shard_map/all_to_all | solution.py:50
  91.2 11.1 %shard_map.325 = (bf16[1024,768]{1,0:T(8,128)(2,1)}, bf16[768,768]{1,0:T(8,128)(2,1)}, bf16[1024,768]{1,0:T(8,128)(2,1)}, f32[1024,768]{1,0:T(8,128)}, bf16[1024...) custom-call(s32[1]{0:T(128)} %bitcast.refs_0_, ...), custom_call_target="tpu_custom_call" | custom-call | tf_op jit(solution)/shard_map/pallas_call | solution.py:146
  103.8 6.5 %collective-permute-done.13.refs_7_ = bf16[512,384]{1,0:T(8,128)(2,1)S(1)} collective-permute-done((bf16[512,384]{1,0:T(8,128)(2,1)}, bf16[512,384]{1,0:T(8,128)(2,1)S(1)}, u32[]{:S(2)}, u32[]{:S(2)}) %collective-permute-start.13) | collective-permute-done | bytes 393248 | tf_op jit(solution)/shard_map/ppermute | solution.py:20
  112.0 6.9 %all-gather.5.cloned.1.call-done.refs_12_.refs_14_.refs_4_ = bf16[768,1536]{1,0:T(8,128)(2,1)} async-done(((bf16[96,1536]{1,0:T(8,128)(2,1)}), bf16[768,1536]{1,0:T(8,128)(2,1)}) %all-gather.5.cloned.1.call-update) | async-done | bytes 2359312 | tf_op jit(solution)/shard_map/all_gather | solution.py:636
  119.0 16.9 %shard_map.326 = (bf16[1024,768]{1,0:T(8,128)(2,1)}, bf16[768,768]{1,0:T(8,128)(2,1)}, f32[256,768]{1,0:T(8,128)}, bf16[1024,768]{1,0:T(8,128)(2,1)}, bf16[1024,...) custom-call(s32[1]{0:T(128)} %bitcast.refs_0_, ...), custom_call_target="tpu_custom_call" | custom-call | tf_op jit(solution)/shard_map/pallas_call | solution.py:146
  136.0 1.9 collective-permute-done.15
  140.5 10.9 %shard_map.327 = (bf16[256,1408]{1,0:T(8,128)(2,1)}, bf16[256,1408]{1,0:T(8,128)(2,1)}, bf16[256,1408]{1,0:T(8,128)(2,1)}, bf16[256,1408]{1,0:T(8,128)(2,1)}, bf16[768,1536]{1,0:T(8,128)(2,1)}) custom-call(s32[1]{0:T(128)} %bitcast.refs_0_, bf16[1024,768]{1,0:T(8,128)(2,1)} %get-tuple-element.150.refs_1_, ...), custom_call_target="tpu_custom_call" | custom-call | tf_op jit(solution)/shard_map/pallas_call | solution.py:146
  151.4 3.8 %all-to-all-start.3 = ((bf16[8,96,1536]{2,1,0:T(8,128)(2,1)}), bf16[8,96,1536]{2,1,0:T(8,128)(2,1)S(1)}, u32[]{:S(2)}, u32[]{:S(2)}) async-start(bf16[8,96,1536]{2,1,0:T(8,128)(2,1)} %bitcast.41), calls=%async_computation.3 | async-start | bytes 4718592 | tf_op jit(solution)/shard_map/all_to_all | solution.py:50
  160.3 11.2 %shard_map.328 = (bf16[1024,192]{1,0:T(8,128)(2,1)}, bf16[2,256,192]{2,1,0:T(8,128)(2,1)}, bf16[1024,768]{1,0:T(8,128)(2,1)}, bf16[1024,768]{1,0:T(8,128)(2,1)},...) custom-call(s32[1]{0:T(128)} %bitcast.refs_0_, ...), custom_call_target="tpu_custom_call" | custom-call | tf_op jit(solution)/shard_map/pallas_call | solution.py:146
  179.8 10.1 %shard_map.329 = (bf16[4,96,768]{2,1,0:T(8,128)(2,1)}, bf16[4,96,768]{2,1,0:T(8,128)(2,1)}, bf16[256,768]{1,0:T(8,128)(2,1)}, bf16[256,768]{1,0:T(8,128)(2,1)}, ...) custom-call(s32[2]{0:T(128)} %pad_add_fusion.refs_0_, ...), custom_call_target="tpu_custom_call" | custom-call | tf_op jit(solution)/shard_map/pallas_call | solution.py:146
  199.1 15.3 %shard_map.330 = (bf16[1024,576]{1,0:T(8,128)(2,1)}, bf16[4,96,640]{2,1,0:T(8,128)(2,1)}, bf16[4,96,640]{2,1,0:T(8,128)(2,1)}, f32[16,768]{1,0:T(8,128)}) custom-call(s32[2]{0:T(128)} %pad_add_fusion.refs_0_, bf16[512,384]{1,0:T(8,128)(2,1)} %get-tuple-element.186.refs_1_, bf16[512,384]{1,0:T(8,128)(2,1)} %copy-done.18, ...), custom_call_target="tpu_custom_call" | custom-call | tf_op jit(solution)/shard_map/pallas_call | solution.py:146
  214.4 2.0 add_convert_fusion.1
  217.5 3.2 %shard_map.331 = (bf16[4,32,640]{2,1,0:T(8,128)(2,1)}, bf16[4,32,640]{2,1,0:T(8,128)(2,1)}, f32[1,256,192]{2,1,0:T(8,128)}) custom-call(s32[2]{0:T(128)} %pad_add_fusion.refs_0_, bf16[256,768]{1,0:T(8,128)(2,1)} %get-tuple-element.216.refs_1_, bf16[256,768]{1,0:T(8,128)(2,1)} %collective-permute-done.28.refs_2_, bf16[256,768]{1,0:T(8,128)(2,1)} %collective-permute-done.26.refs_3_), custom_call_target="tpu_custom_call" | custom-call | tf_op jit(solution)/shard_map/pallas_call | solution.py:146
  220.7 2.3 collective-permute-start.29
  223.2 1.9 collective-permute-start.27
  234.9 3.9 %collective-permute-done.27 = bf16[4,96,640]{2,1,0:T(8,128)(2,1)} collective-permute-done((bf16[4,96,640]{2,1,0:T(8,128)(2,1)}, bf16[4,96,640]{2,1,0:T(8,128)(2,1)}, u32[]{:S(2)}, u32[]{:S(2)}) %collective-permute-start.27) | collective-permute-done | bytes 491552 | tf_op jit(solution)/shard_map/ppermute | solution.py:46
  242.6 3.9 %all-to-all-start.4 = ((bf16[8,16,768]{2,1,0:T(8,128)(2,1)}), bf16[8,16,768]{2,1,0:T(8,128)(2,1)S(1)}, u32[]{:S(2)}, u32[]{:S(2)}) async-start(bf16[8,16,768]{2,1,0:T(8,128)(2,1)} %broadcast_in_dim.37), calls=%async_computation.4 | async-start | bytes 393216 | tf_op jit(solution)/shard_map/all_to_all | solution.py:50
  246.6 4.1 %collective-permute-done.30 = bf16[2,128,640]{2,1,0:T(8,128)(2,1)S(1)} collective-permute-done((bf16[2,128,640]{2,1,0:T(8,128)(2,1)S(1)}, bf16[2,128,640]{2,1,0:T(8,128)(2,1)S(1)}, u32[]{:S(2)}, u32[]{:S(2)}) %collective-permute-start.30) | collective-permute-done | bytes 327712 | tf_op jit(solution)/shard_map/ppermute | solution.py:46
  252.6 6.7 %shard_map.332 = (bf16[256,768]{1,0:T(8,128)(2,1)}, bf16[256,768]{1,0:T(8,128)(2,1)}, bf16[256,768]{1,0:T(8,128)(2,1)}, bf16[256,768]{1,0:T(8,128)(2,1)}) custom-call(bf16[256,768]{1,0:T(8,128)(2,1)} %refs_0_.1, bf16[256,768]{1,0:T(8,128)(2,1)} %copy-done.4, bf16[256,768]{1,0:T(8,128)(2,1)} %copy-done.3, bf16[256,768]{1,0:T(8,128)(2,1)} %copy-done.5, ...), custom_call_target="tpu_custom_call" | custom-call | tf_op jit(solution)/shard_map/pallas_call | solution.py:146
  266.2 4.7 %all-to-all-start.5 = ((f32[8,1,96]{2,1,0:T(1,128)}), f32[8,1,96]{2,1,0:T(1,128)S(1)}, u32[]{:S(2)}, u32[]{:S(2)}) async-start(f32[8,1,96]{2,1,0:T(1,128)} %bitcast.11), calls=%async_computation.5 | async-start | bytes 8192 | tf_op jit(solution)/shard_map/all_to_all | solution.py:50
  272.0 4.9 %collective-permute-done.40.refs_3_ = bf16[24,1536]{1,0:T(8,128)(2,1)S(1)} collective-permute-done((bf16[24,1536]{1,0:T(8,128)(2,1)S(1)}, bf16[24,1536]{1,0:T(8,128)(2,1)S(1)}, u32[]{:S(2)}, u32[]{:S(2)}) %collective-permute-start.40) | collective-permute-done | bytes 73760 | tf_op jit(solution)/shard_map/ppermute | solution.py:817
  279.8 2.1 convert_add_fusion
  (206 shorter events, 74.6 us)
Async XLA Ops:
  7.2 51.6 %all-gather.3.cloned.1.call-start = ((), (), s32[]{:S(2)}) async-start(), calls=%async_computation.6 | async-start | bytes 1769472 | tf_op jit(solution)/shard_map/all_gather | solution.py:618
  9.5 13.2 %collective-permute-start.1 = (bf16[256,768]{1,0:T(8,128)(2,1)}, bf16[256,768]{1,0:T(8,128)(2,1)S(1)}, u32[]{:S(2)}, u32[]{:S(2)}) collective-permute-start(bf16[256,768]{1,0:T(8,128)(2,1)} %refs_0_.1), channel_id=1, source_target_pairs={{0,2},{1,3},{2,0},{3,1},{4,6},{5,7},{6,4},{7,5},{8,10},{9,11},{10,... | collective-permute-start | bytes 1179656 | tf_op jit(solution)/shard_map/ppermute | solution.py:20
  12.5 18.0 %collective-permute-start = (bf16[256,768]{1,0:T(8,128)(2,1)}, bf16[256,768]{1,0:T(8,128)(2,1)S(1)}, u32[]{:S(2)}, u32[]{:S(2)}) collective-permute-start(bf16[256,768]{1,0:T(8,128)(2,1)} %refs_0_.1), channel_id=1, source_target_pairs={{0,1},{1,0},{2,3},{3,2},{4,5},{5,4},{6,7},{7,6},{8,9},{9,8},{10,11... | collective-permute-start | bytes 1179656 | tf_op jit(solution)/shard_map/ppermute | solution.py:20
  12.5 17.8 %collective-permute-start.4 = (bf16[256,768]{1,0:T(8,128)(2,1)}, bf16[256,768]{1,0:T(8,128)(2,1)S(1)}, u32[]{:S(2)}, u32[]{:S(2)}) collective-permute-start(bf16[256,768]{1,0:T(8,128)(2,1)} %refs_5_.1), channel_id=1, source_target_pairs={{0,2},{1,3},{2,0},{3,1},{4,6},{5,7},{6,4},{7,5},{8,10},{9,11},{10,... | collective-permute-start | bytes 1179656 | tf_op jit(solution)/shard_map/ppermute | solution.py:20
  12.6 34.0 %collective-permute-start.3 = (bf16[256,768]{1,0:T(8,128)(2,1)}, bf16[256,768]{1,0:T(8,128)(2,1)S(1)}, u32[]{:S(2)}, u32[]{:S(2)}) collective-permute-start(bf16[256,768]{1,0:T(8,128)(2,1)} %refs_5_.1), channel_id=1, source_target_pairs={{0,1},{1,0},{2,3},{3,2},{4,5},{5,4},{6,7},{7,6},{8,9},{9,8},{10,11... | collective-permute-start | bytes 1179656 | tf_op jit(solution)/shard_map/ppermute | solution.py:20
  16.4 12.7 %all-to-all-start = ((bf16[8,2,240]{2,1,0:T(2,128)(2,1)}), bf16[8,2,240]{2,1,0:T(2,128)(2,1)S(1)}, u32[]{:S(2)}, u32[]{:S(2)}) async-start(bf16[8,2,240]{2,1,0:T(2,128)(2,1)} %reshape.131), calls=%async_computation | async-start | bytes 16384 | tf_op jit(solution)/shard_map/all_to_all | solution.py:50
  22.5 96.5 %all-gather.5.cloned.1.call-start = ((), (), s32[]{:S(2)}) async-start(), calls=%async_computation.7 | async-start | bytes 2654208 | tf_op jit(solution)/shard_map/all_gather | solution.py:636
  30.2 16.4 %collective-permute-start.5 = (bf16[256,768]{1,0:T(8,128)(2,1)S(1)}, bf16[256,768]{1,0:T(8,128)(2,1)S(1)}, u32[]{:S(2)}, u32[]{:S(2)}) collective-permute-start(bf16[256,768]{1,0:T(8,128)(2,1)S(1)} %collective-permute-done.4.refs_17_), channel_id=1, source_target_pairs={{0,1},{1,0},{2,3},{3,2},{4,5},{5,4},{6,7},{7,6},{8,9},{9,8},{10,11... | collective-permute-start | bytes 1179656 | tf_op jit(solution)/shard_map/ppermute | solution.py:20
  50.8 39.3 %all-to-all-start.2 = ((bf16[8,96,576]{2,1,0:T(8,128)(2,1)}), bf16[8,96,576]{2,1,0:T(8,128)(2,1)S(1)}, u32[]{:S(2)}, u32[]{:S(2)}) async-start(bf16[8,96,576]{2,1,0:T(8,128)(2,1)} %shard_map.323), calls=%async_computation.2 | async-start | bytes 1966080 | tf_op jit(solution)/shard_map/all_to_all | solution.py:50
  60.0 15.3 %collective-permute-start.7 = (bf16[768,384]{1,0:T(8,128)(2,1)S(1)}, bf16[768,384]{1,0:T(8,128)(2,1)S(1)}, u32[]{:S(2)}, u32[]{:S(2)}) collective-permute-start(bf16[768,384]{1,0:T(8,128)(2,1)S(1)} %slice.105.refs_6_.refs_2_), channel_id=1, source_target_pairs={{0,2},{1,3},{2,0},{3,1},{4,6},{5,7},{6,4},{7,5},{8,10},{9,11},{10,... | collective-permute-start | bytes 1769480 | tf_op jit(solution)/shard_map/ppermute | solution.py:20
  71.8 11.4 %collective-permute-start.10 = (bf16[512,384]{1,0:T(8,128)(2,1)}, bf16[512,384]{1,0:T(8,128)(2,1)S(1)}, u32[]{:S(2)}, u32[]{:S(2)}) collective-permute-start(bf16[512,384]{1,0:T(8,128)(2,1)} %get-tuple-element.141.refs_10_.refs_4_), channel_id=1, source_target_pairs={{0,2},{1,3},{2,0},{3,1},{4,6},{5,7},{6,4},{7,5},{8,10},{9,11},{10,... | collective-permute-start | bytes 1179656 | tf_op jit(solution)/shard_map/ppermute | solution.py:20
  72.7 17.4 %collective-permute-start.6 = (bf16[768,384]{1,0:T(8,128)(2,1)S(1)}, bf16[768,384]{1,0:T(8,128)(2,1)}, u32[]{:S(2)}, u32[]{:S(2)}) collective-permute-start(bf16[768,384]{1,0:T(8,128)(2,1)S(1)} %slice.105.refs_6_.refs_2_), channel_id=1, source_target_pairs={{0,1},{1,0},{2,3},{3,2},{4,5},{5,4},{6,7},{7,6},{8,9},{9,8},{10,11... | collective-permute-start | bytes 1769480 | tf_op jit(solution)/shard_map/ppermute | solution.py:20
  75.3 14.9 %collective-permute-start.8 = (bf16[768,384]{1,0:T(8,128)(2,1)S(1)}, bf16[768,384]{1,0:T(8,128)(2,1)}, u32[]{:S(2)}, u32[]{:S(2)}) collective-permute-start(bf16[768,384]{1,0:T(8,128)(2,1)S(1)} %collective-permute-done.7.refs_8_.refs_4_), channel_id=1, source_target_pairs={{0,1},{1,0},{2,3},{3,2},{4,5},{5,4},{6,7},{7,6},{8,9},{9,8},{10,11... | collective-permute-start | bytes 1769480 | tf_op jit(solution)/shard_map/ppermute | solution.py:20
  75.3 14.9 %collective-permute-start.9 = (bf16[512,384]{1,0:T(8,128)(2,1)}, bf16[512,384]{1,0:T(8,128)(2,1)}, u32[]{:S(2)}, u32[]{:S(2)}) collective-permute-start(bf16[512,384]{1,0:T(8,128)(2,1)} %get-tuple-element.141.refs_10_.refs_4_), channel_id=1, source_target_pairs={{0,1},{1,0},{2,3},{3,2},{4,5},{5,4},{6,7},{7,6},{8,9},{9,8},{10,11... | collective-permute-start | bytes 1179656 | tf_op jit(solution)/shard_map/ppermute | solution.py:20
  139.0 12.4 %collective-permute-start.16 = (bf16[512,384]{1,0:T(8,128)(2,1)S(1)}, bf16[512,384]{1,0:T(8,128)(2,1)}, u32[]{:S(2)}, u32[]{:S(2)}) collective-permute-start(bf16[512,384]{1,0:T(8,128)(2,1)S(1)} %add_convert_fusion.6), channel_id=1, source_target_pairs={{0,2},{1,3},{2,0},{3,1},{4,6},{5,7},{6,4},{7,5},{8,10},{9,11},{10,... | collective-permute-start | bytes 1179656 | tf_op jit(solution)/shard_map/ppermute | solution.py:20
  151.4 65.0 %all-to-all-start.3 = ((bf16[8,96,1536]{2,1,0:T(8,128)(2,1)}), bf16[8,96,1536]{2,1,0:T(8,128)(2,1)S(1)}, u32[]{:S(2)}, u32[]{:S(2)}) async-start(bf16[8,96,1536]{2,1,0:T(8,128)(2,1)} %bitcast.41), calls=%async_computation.3 | async-start | bytes 4718592 | tf_op jit(solution)/shard_map/all_to_all | solution.py:50
  159.0 18.2 %collective-permute-start.21 = (bf16[256,1408]{1,0:T(8,128)(2,1)S(1)}, bf16[256,1408]{1,0:T(8,128)(2,1)S(1)}, u32[]{:S(2)}, u32[]{:S(2)}) collective-permute-start(bf16[256,1408]{1,0:T(8,128)(2,1)S(1)} %add_convert_fusion), channel_id=1, source_target_pairs={{0,2},{1,3},{2,0},{3,1},{4,6},{5,7},{6,4},{7,5},{8,10},{9,11},{10,... | collective-permute-start | bytes 2162696 | tf_op jit(solution)/shard_map/ppermute | solution.py:20
  178.0 11.9 %collective-permute-start.23 = (bf16[512,384]{1,0:T(8,128)(2,1)}, bf16[512,384]{1,0:T(8,128)(2,1)}, u32[]{:S(2)}, u32[]{:S(2)}) collective-permute-start(bf16[512,384]{1,0:T(8,128)(2,1)} %add_convert_fusion.5), channel_id=1, source_target_pairs={{0,2},{1,3},{2,0},{3,1},{4,6},{5,7},{6,4},{7,5},{8,10},{9,11},{10,... | collective-permute-start | bytes 1179656 | tf_op jit(solution)/shard_map/ppermute | solution.py:20
  193.8 20.5 %collective-permute-start.25 = (bf16[4,96,768]{2,1,0:T(8,128)(2,1)}, bf16[4,96,768]{2,1,0:T(8,128)(2,1)}, u32[]{:S(2)}, u32[]{:S(2)}) collective-permute-start(bf16[4,96,768]{2,1,0:T(8,128)(2,1)} %get-tuple-element.210), channel_id=1, source_target_pairs={{0,4},{4,0},{8,12},{12,8},{16,20},{20,16},{24,28},{28,24},{1,5},{5... | collective-permute-start | bytes 1769480 | tf_op jit(solution)/shard_map/ppermute | solution.py:46
  196.3 21.2 %collective-permute-start.28 = (bf16[256,768]{1,0:T(8,128)(2,1)}, bf16[256,768]{1,0:T(8,128)(2,1)}, u32[]{:S(2)}, u32[]{:S(2)}) collective-permute-start(bf16[256,768]{1,0:T(8,128)(2,1)} %get-tuple-element.217), channel_id=1, source_target_pairs={{0,1},{1,0},{2,3},{3,2},{4,5},{5,4},{6,7},{7,6},{8,9},{9,8},{10,11... | collective-permute-start | bytes 1179656 | tf_op jit(solution)/shard_map/ppermute | solution.py:20
  196.8 19.6 %collective-permute-start.26 = (bf16[256,768]{1,0:T(8,128)(2,1)}, bf16[256,768]{1,0:T(8,128)(2,1)}, u32[]{:S(2)}, u32[]{:S(2)}) collective-permute-start(bf16[256,768]{1,0:T(8,128)(2,1)} %add_convert_fusion.4), channel_id=1, source_target_pairs={{0,2},{1,3},{2,0},{3,1},{4,6},{5,7},{6,4},{7,5},{8,10},{9,11},{10,... | collective-permute-start | bytes 1179656 | tf_op jit(solution)/shard_map/ppermute | solution.py:20
  217.4 10.7 %collective-permute-start.34 = (f32[16,768]{1,0:T(8,128)}, f32[16,768]{1,0:T(8,128)}, u32[]{:S(2)}, u32[]{:S(2)}) collective-permute-start(f32[16,768]{1,0:T(8,128)} %get-tuple-element.226), channel_id=1, source_target_pairs={{0,1},{1,0},{2,3},{3,2},{4,5},{5,4},{6,7},{7,6},{8,9},{9,8},{10,11... | collective-permute-start | bytes 147464 | tf_op jit(solution)/shard_map/ppermute | solution.py:20
  223.2 15.6 %collective-permute-start.27 = (bf16[4,96,640]{2,1,0:T(8,128)(2,1)}, bf16[4,96,640]{2,1,0:T(8,128)(2,1)}, u32[]{:S(2)}, u32[]{:S(2)}) collective-permute-start(bf16[4,96,640]{2,1,0:T(8,128)(2,1)} %get-tuple-element.215), channel_id=1, source_target_pairs={{0,4},{4,0},{8,12},{12,8},{16,20},{20,16},{24,28},{28,24},{1,5},{5... | collective-permute-start | bytes 1474568 | tf_op jit(solution)/shard_map/ppermute | solution.py:46
  229.0 12.9 %collective-permute-start.35 = (f32[16,768]{1,0:T(8,128)S(1)}, f32[16,768]{1,0:T(8,128)S(1)}, u32[]{:S(2)}, u32[]{:S(2)}) collective-permute-start(f32[16,768]{1,0:T(8,128)S(1)} %add.103), channel_id=1, source_target_pairs={{0,2},{1,3},{2,0},{3,1},{4,6},{5,7},{6,4},{7,5},{8,10},{9,11},{10,... | collective-permute-start | bytes 147464 | tf_op jit(solution)/shard_map/ppermute | solution.py:20
  233.3 13.2 %collective-permute-start.37 = (bf16[1,96,768]{2,1,0:T(8,128)(2,1)S(1)}, bf16[1,96,768]{2,1,0:T(8,128)(2,1)S(1)}, u32[]{:S(2)}, u32[]{:S(2)}) collective-permute-start(bf16[1,96,768]{2,1,0:T(8,128)(2,1)S(1)} %slice.177), channel_id=1, source_target_pairs={{0,16},{4,20},{8,24},{12,28},{16,0},{20,4},{24,8},{28,12},{1,17},{... | collective-permute-start | bytes 442376 | tf_op jit(solution)/shard_map/ppermute | solution.py:46
  242.6 17.3 %all-to-all-start.4 = ((bf16[8,16,768]{2,1,0:T(8,128)(2,1)}), bf16[8,16,768]{2,1,0:T(8,128)(2,1)S(1)}, u32[]{:S(2)}, u32[]{:S(2)}) async-start(bf16[8,16,768]{2,1,0:T(8,128)(2,1)} %broadcast_in_dim.37), calls=%async_computation.4 | async-start | bytes 393216 | tf_op jit(solution)/shard_map/all_to_all | solution.py:50
  250.8 12.4 %collective-permute-start.38 = (bf16[1,128,640]{2,1,0:T(8,128)(2,1)S(1)}, bf16[1,128,640]{2,1,0:T(8,128)(2,1)S(1)}, u32[]{:S(2)}, u32[]{:S(2)}) collective-permute-start(bf16[1,128,640]{2,1,0:T(8,128)(2,1)S(1)} %slice.176), channel_id=1, source_target_pairs={{0,16},{4,20},{8,24},{12,28},{16,0},{20,4},{24,8},{28,12},{1,17},{... | collective-permute-start | bytes 491528 | tf_op jit(solution)/shard_map/ppermute | solution.py:46
  259.4 20.5 %collective-permute-start.31 = (bf16[256,768]{1,0:T(8,128)(2,1)}, bf16[256,768]{1,0:T(8,128)(2,1)}, u32[]{:S(2)}, u32[]{:S(2)}) collective-permute-start(bf16[256,768]{1,0:T(8,128)(2,1)} %get-tuple-element.223), channel_id=1, source_target_pairs={{0,1},{1,0},{2,3},{3,2},{4,5},{5,4},{6,7},{7,6},{8,9},{9,8},{10,11... | collective-permute-start | bytes 1179656 | tf_op jit(solution)/shard_map/ppermute | solution.py:20
  263.4 16.4 %collective-permute-start.33 = (bf16[256,768]{1,0:T(8,128)(2,1)S(1)}, bf16[256,768]{1,0:T(8,128)(2,1)S(1)}, u32[]{:S(2)}, u32[]{:S(2)}) collective-permute-start(bf16[256,768]{1,0:T(8,128)(2,1)S(1)} %add_convert_fusion.3), channel_id=1, source_target_pairs={{0,2},{1,3},{2,0},{3,1},{4,6},{5,7},{6,4},{7,5},{8,10},{9,11},{10,... | collective-permute-start | bytes 1179656 | tf_op jit(solution)/shard_map/ppermute | solution.py:20
  264.3 12.6 %collective-permute-start.40 = (bf16[24,1536]{1,0:T(8,128)(2,1)S(1)}, bf16[24,1536]{1,0:T(8,128)(2,1)S(1)}, u32[]{:S(2)}, u32[]{:S(2)}) collective-permute-start(bf16[24,1536]{1,0:T(8,128)(2,1)S(1)} %get-tuple-element.232), channel_id=1, source_target_pairs={{0,2},{1,3},{2,0},{3,1},{4,6},{5,7},{6,4},{7,5},{8,10},{9,11},{10,... | collective-permute-start | bytes 221192 | tf_op jit(solution)/shard_map/ppermute | solution.py:817
  265.8 11.1 %collective-permute-start.41 = (bf16[24,1536]{1,0:T(8,128)(2,1)S(1)}, bf16[24,1536]{1,0:T(8,128)(2,1)S(1)}, u32[]{:S(2)}, u32[]{:S(2)}) collective-permute-start(bf16[24,1536]{1,0:T(8,128)(2,1)S(1)} %get-tuple-element.233), channel_id=1, source_target_pairs={{0,3},{1,2},{2,1},{3,0},{4,7},{5,6},{6,5},{7,4},{8,11},{9,10},{10,... | collective-permute-start | bytes 221192 | tf_op jit(solution)/shard_map/ppermute | solution.py:817
  266.2 11.7 %all-to-all-start.5 = ((f32[8,1,96]{2,1,0:T(1,128)}), f32[8,1,96]{2,1,0:T(1,128)S(1)}, u32[]{:S(2)}, u32[]{:S(2)}) async-start(f32[8,1,96]{2,1,0:T(1,128)} %bitcast.11), calls=%async_computation.5 | async-start | bytes 8192 | tf_op jit(solution)/shard_map/all_to_all | solution.py:50
  (44 other events, 402.4 us)
Sparse Core Ops, SparseCore 0:
  10.8 47.9 all-gather.2
  61.6 57.3 all-gather.4

commit v6 on v5

--- a/solution.py
+++ b/solution.py
@@ -757,7 +757,8 @@
     shared = shared + swap(shared, 2)
     vec = jnp.where(jnp.arange(16)[:, None] == 10, vec, shared).astype(BF)
     mid_y = mid
-    mid = rest_reduce(mid)
+    sent_mid = []
+    mid = rest_reduce(mid, sent_mid)
     third_shape = (width, hw) if kr % 16 else (n // 2, kr // 3, 3 * hw + pad)
     *outs, grad_captions = call(
         partial(out_rows, kr=kr),
@@ -780,7 +781,7 @@
     sent = []
     last = rest_reduce(jnp.concatenate([last, outs], axis=1), sent)
     outs = last[kr:]
-    gf = call(first_back, [], [*x, g_joint, w_own, mod, after(gas, sent[-1])], [out((rows, width), BF)] * 4)
+    gf = call(first_back, [], [*x, g_joint, w_own, mod, after(gas, sent_mid[-1])], [out((rows, width), BF)] * 4)
     if kr % 16:
         outs = outs[:, : 3 * hw].reshape(own * 4 // 3, 3, hw).transpose(1, 0, 2).reshape(kr, hw)
     frame_mine, frame_near, frame_other = near_terms(gf)

time: 293 us -> 291 us (level)
    all_to_all x5, waiting for transfers between devices: 10.3 us -> 13.7 us  [exchange(): return lax.all_to_all(x, 'seq', split_axis=0, concat_axis=0, tiled=True)]
    unnamed x59 -> x61, local copies, waits for them, and re-layouts: 5.99 us -> 6.69 us
  transfers between devices with their start and end apart: 49 -> 49, of which waited for: 19 -> 25; matrix products, arithmetic and copies ran while one was open for 13% -> 12% of each run, Pallas kernels for 29% -> 29%
where the time goes in v6:
time: 291 us; the launch traced here: 288 us
  Pallas kernels  101 us (35%)
  waiting for transfers between devices  61.4 us (21%)
  starting transfers between devices  52.6 us (18%)
  other arithmetic  22 us (8%)
  local copies, waits for them, and re-layouts  18.6 us (6%)
  between operations  15.6 us (5%)
  blocking collectives  13.9 us (5%)
    pallas_call x13, Pallas kernels, call(): pl.pallas_call(body, in_specs=[pl.BlockSpec(memory_space=pltpu.SMEM)] * l...  101 us
    ppermute x32, waiting for transfers between devices, swap(): return lax.ppermute(x, 'head', [(i, i ^ bit) for i in range(4)])  27.7 us
    all_to_all x5, starting transfers between devices, exchange(): return lax.all_to_all(x, 'seq', split_axis=0, concat_axis=0, tiled=True)  23 us
    ppermute x32, starting transfers between devices, swap(): return lax.ppermute(x, 'head', [(i, i ^ bit) for i in range(4)])  16.8 us
    all_to_all x1, blocking collectives, exchange(): return lax.all_to_all(x, 'seq', split_axis=0, concat_axis=0, tiled=True)  13.9 us
    all_to_all x5, waiting for transfers between devices, exchange(): return lax.all_to_all(x, 'seq', split_axis=0, concat_axis=0, tiled=True)  13.7 us
    ppermute x7, starting transfers between devices, seq_swap(): lax.ppermute(x, 'seq', [(i, i ^ bit) for i in range(lax.axis_size('seq'))])  10.9 us
    ppermute x7, waiting for transfers between devices, seq_swap(): lax.ppermute(x, 'seq', [(i, i ^ bit) for i in range(lax.axis_size('seq'))])  7.51 us
  transfers between devices with their start and end apart: 49, of which 25 were waited for; matrix products, arithmetic and copies ran while one was open for 12% of the time, Pallas kernels for 29%

profile of v6, /device:TPU:0, one launch (start us, length us, event | category | flops | bytes accessed | tf_op | source)
XLA Modules:
  0.0 287.6 jit_solution(2299082732835435541)
XLA Ops:
  7.3 2.2 shard_map.322
  9.5 3.0 %collective-permute-start.1 = (bf16[256,768]{1,0:T(8,128)(2,1)}, bf16[256,768]{1,0:T(8,128)(2,1)S(1)}, u32[]{:S(2)}, u32[]{:S(2)}) collective-permute-start(bf16[256,768]{1,0:T(8,128)(2,1)} %refs_0_.1), channel_id=1, source_target_pairs={{0,2},{1,3},{2,0},{3,1},{4,6},{5,7},{6,4},{7,5},{8,10},{9,11},{10,... | collective-permute-start | bytes 1179656 | tf_op jit(solution)/shard_map/ppermute | solution.py:20
  16.4 6.1 %all-to-all-start = ((bf16[8,2,240]{2,1,0:T(2,128)(2,1)}), bf16[8,2,240]{2,1,0:T(2,128)(2,1)S(1)}, u32[]{:S(2)}, u32[]{:S(2)}) async-start(bf16[8,2,240]{2,1,0:T(2,128)(2,1)} %reshape.131), calls=%async_computation | async-start | bytes 16384 | tf_op jit(solution)/shard_map/all_to_all | solution.py:50
  23.5 5.6 %all-to-all-done = bf16[8,2,240]{2,1,0:T(2,128)(2,1)S(1)} async-done(((bf16[8,2,240]{2,1,0:T(2,128)(2,1)}), bf16[8,2,240]{2,1,0:T(2,128)(2,1)S(1)}, u32[]{:S(2)}, u32[]{:S(2)}) %all-to-all-start) | async-done | bytes 7712 | tf_op jit(solution)/shard_map/all_to_all | solution.py:50
  30.6 13.9 %all_to_all.45 = f32[8,1,4608]{2,1,0:T(1,128)S(1)} all-to-all(f32[8,1,4608]{2,1,0:T(1,128)S(1)} %copy.44), channel_id=1, replica_groups=mesh['seq'=8,'head'=4] {'seq'}, dimensions={0} | all-to-all | bytes 294912 | tf_op jit(solution)/shard_map/all_to_all | solution.py:50
  48.5 2.3 shard_map.323
  50.8 6.1 %all-to-all-start.2 = ((bf16[8,96,576]{2,1,0:T(8,128)(2,1)}), bf16[8,96,576]{2,1,0:T(8,128)(2,1)S(1)}, u32[]{:S(2)}, u32[]{:S(2)}) async-start(bf16[8,96,576]{2,1,0:T(8,128)(2,1)} %shard_map.323), calls=%async_computation.2 | async-start | bytes 1966080 | tf_op jit(solution)/shard_map/all_to_all | solution.py:50
  61.2 10.6 %shard_map.324 = (bf16[1024,768]{1,0:T(8,128)(2,1)}, bf16[3,1024,192]{2,1,0:T(8,128)(2,1)}, bf16[512,384]{1,0:T(8,128)(2,1)}, bf16[3,1024,1024]{2,1,0:T(8,128)(2,1)}, f32[3,1024]{1,0:T(4,128)}) custom-call(bf16[256,768]{1,0:T(8,128)(2,1)} %refs_0_.1, bf16[256,768]{1,0:T(8,128)(2,1)} %copy-done.4, bf16[256,768]{1,0:T(8,128)(2,1)} %copy-done.3, ...), custom_call_target="tpu_custom_call" | custom-call | tf_op jit(solution)/shard_map/pallas_call | solution.py:146
  72.7 2.6 collective-permute-done.7.refs_8_.refs_4_
  75.8 7.4 %collective-permute-done.10.refs_12_ = bf16[512,384]{1,0:T(8,128)(2,1)S(1)} collective-permute-done((bf16[512,384]{1,0:T(8,128)(2,1)}, bf16[512,384]{1,0:T(8,128)(2,1)S(1)}, u32[]{:S(2)}, u32[]{:S(2)}) %collective-permute-start.10) | collective-permute-done | bytes 393248 | tf_op jit(solution)/shard_map/ppermute | solution.py:20
  85.4 4.8 %all-to-all-done.2 = bf16[8,96,576]{2,1,0:T(8,128)(2,1)S(1)} async-done(((bf16[8,96,576]{2,1,0:T(8,128)(2,1)}), bf16[8,96,576]{2,1,0:T(8,128)(2,1)S(1)}, u32[]{:S(2)}, u32[]{:S(2)}) %all-to-all-start.2) | async-done | bytes 884768 | tf_op jit(solution)/shard_map/all_to_all | solution.py:50
  91.2 11.1 %shard_map.325 = (bf16[1024,768]{1,0:T(8,128)(2,1)}, bf16[768,768]{1,0:T(8,128)(2,1)}, bf16[1024,768]{1,0:T(8,128)(2,1)}, f32[1024,768]{1,0:T(8,128)}, bf16[1024...) custom-call(s32[1]{0:T(128)} %bitcast.refs_0_, ...), custom_call_target="tpu_custom_call" | custom-call | tf_op jit(solution)/shard_map/pallas_call | solution.py:146
  103.8 6.5 %collective-permute-done.13.refs_7_ = bf16[512,384]{1,0:T(8,128)(2,1)S(1)} collective-permute-done((bf16[512,384]{1,0:T(8,128)(2,1)}, bf16[512,384]{1,0:T(8,128)(2,1)S(1)}, u32[]{:S(2)}, u32[]{:S(2)}) %collective-permute-start.13) | collective-permute-done | bytes 393248 | tf_op jit(solution)/shard_map/ppermute | solution.py:20
  112.0 6.9 %all-gather.5.cloned.1.call-done.refs_12_.refs_14_.refs_4_ = bf16[768,1536]{1,0:T(8,128)(2,1)} async-done(((bf16[96,1536]{1,0:T(8,128)(2,1)}), bf16[768,1536]{1,0:T(8,128)(2,1)}) %all-gather.5.cloned.1.call-update) | async-done | bytes 2359312 | tf_op jit(solution)/shard_map/all_gather | solution.py:636
  119.0 16.9 %shard_map.326 = (bf16[1024,768]{1,0:T(8,128)(2,1)}, bf16[768,768]{1,0:T(8,128)(2,1)}, f32[256,768]{1,0:T(8,128)}, bf16[1024,768]{1,0:T(8,128)(2,1)}, bf16[1024,...) custom-call(s32[1]{0:T(128)} %bitcast.refs_0_, ...), custom_call_target="tpu_custom_call" | custom-call | tf_op jit(solution)/shard_map/pallas_call | solution.py:146
  140.5 10.9 %shard_map.327 = (bf16[256,1408]{1,0:T(8,128)(2,1)}, bf16[256,1408]{1,0:T(8,128)(2,1)}, bf16[256,1408]{1,0:T(8,128)(2,1)}, bf16[256,1408]{1,0:T(8,128)(2,1)}, bf16[768,1536]{1,0:T(8,128)(2,1)}) custom-call(s32[1]{0:T(128)} %bitcast.refs_0_, bf16[1024,768]{1,0:T(8,128)(2,1)} %get-tuple-element.150.refs_1_, ...), custom_call_target="tpu_custom_call" | custom-call | tf_op jit(solution)/shard_map/pallas_call | solution.py:146
  151.4 3.8 %all-to-all-start.3 = ((bf16[8,96,1536]{2,1,0:T(8,128)(2,1)}), bf16[8,96,1536]{2,1,0:T(8,128)(2,1)S(1)}, u32[]{:S(2)}, u32[]{:S(2)}) async-start(bf16[8,96,1536]{2,1,0:T(8,128)(2,1)} %bitcast.41), calls=%async_computation.3 | async-start | bytes 4718592 | tf_op jit(solution)/shard_map/all_to_all | solution.py:50
  160.3 11.2 %shard_map.328 = (bf16[1024,192]{1,0:T(8,128)(2,1)}, bf16[2,256,192]{2,1,0:T(8,128)(2,1)}, bf16[1024,768]{1,0:T(8,128)(2,1)}, bf16[1024,768]{1,0:T(8,128)(2,1)},...) custom-call(s32[1]{0:T(128)} %bitcast.refs_0_, ...), custom_call_target="tpu_custom_call" | custom-call | tf_op jit(solution)/shard_map/pallas_call | solution.py:146
  179.9 10.1 %shard_map.329 = (bf16[4,96,768]{2,1,0:T(8,128)(2,1)}, bf16[4,96,768]{2,1,0:T(8,128)(2,1)}, bf16[256,768]{1,0:T(8,128)(2,1)}, bf16[256,768]{1,0:T(8,128)(2,1)}, ...) custom-call(s32[2]{0:T(128)} %pad_add_fusion.refs_0_, ...), custom_call_target="tpu_custom_call" | custom-call | tf_op jit(solution)/shard_map/pallas_call | solution.py:146
  198.4 15.3 %shard_map.330 = (bf16[1024,576]{1,0:T(8,128)(2,1)}, bf16[4,96,640]{2,1,0:T(8,128)(2,1)}, bf16[4,96,640]{2,1,0:T(8,128)(2,1)}, f32[16,768]{1,0:T(8,128)}) custom-call(s32[2]{0:T(128)} %pad_add_fusion.refs_0_, bf16[512,384]{1,0:T(8,128)(2,1)} %get-tuple-element.186.refs_1_, bf16[512,384]{1,0:T(8,128)(2,1)} %copy-done.18, ...), custom_call_target="tpu_custom_call" | custom-call | tf_op jit(solution)/shard_map/pallas_call | solution.py:146
  214.2 2.0 add_convert_fusion.1
  219.4 3.0 %shard_map.332 = (bf16[4,32,640]{2,1,0:T(8,128)(2,1)}, bf16[4,32,640]{2,1,0:T(8,128)(2,1)}, f32[1,256,192]{2,1,0:T(8,128)}) custom-call(s32[2]{0:T(128)} %pad_add_fusion.refs_0_, bf16[256,768]{1,0:T(8,128)(2,1)} %get-tuple-element.224.refs_1_, bf16[256,768]{1,0:T(8,128)(2,1)} %collective-permute-done.34.refs_2_, bf16[256,768]{1,0:T(8,128)(2,1)} %collective-permute-done.26.refs_3_), custom_call_target="tpu_custom_call" | custom-call | tf_op jit(solution)/shard_map/pallas_call | solution.py:146
  224.2 2.4 collective-permute-start.36
  226.8 1.9 collective-permute-start.33
  228.8 3.1 %collective-permute-done.36 = bf16[4,32,640]{2,1,0:T(8,128)(2,1)S(1)} collective-permute-done((bf16[4,32,640]{2,1,0:T(8,128)(2,1)}, bf16[4,32,640]{2,1,0:T(8,128)(2,1)S(1)}, u32[]{:S(2)}, u32[]{:S(2)}) %collective-permute-start.36) | collective-permute-done | bytes 163872 | tf_op jit(solution)/shard_map/ppermute | solution.py:46
  232.9 2.3 collective-permute-done.27
  236.4 6.7 %shard_map.331 = (bf16[256,768]{1,0:T(8,128)(2,1)}, bf16[256,768]{1,0:T(8,128)(2,1)}, bf16[256,768]{1,0:T(8,128)(2,1)}, bf16[256,768]{1,0:T(8,128)(2,1)}) custom-call(bf16[256,768]{1,0:T(8,128)(2,1)} %refs_0_.1, bf16[256,768]{1,0:T(8,128)(2,1)} %copy-done.4, bf16[256,768]{1,0:T(8,128)(2,1)} %copy-done.3, bf16[256,768]{1,0:T(8,128)(2,1)} %copy-done.5, ...), custom_call_target="tpu_custom_call" | custom-call | tf_op jit(solution)/shard_map/pallas_call | solution.py:146
  246.5 3.4 %all-to-all-start.4 = ((bf16[8,16,768]{2,1,0:T(8,128)(2,1)}), bf16[8,16,768]{2,1,0:T(8,128)(2,1)S(1)}, u32[]{:S(2)}, u32[]{:S(2)}) async-start(bf16[8,16,768]{2,1,0:T(8,128)(2,1)} %broadcast_in_dim.37), calls=%async_computation.4 | async-start | bytes 393216 | tf_op jit(solution)/shard_map/all_to_all | solution.py:50
  259.0 3.5 %all-to-all-start.5 = ((f32[8,1,96]{2,1,0:T(1,128)}), f32[8,1,96]{2,1,0:T(1,128)S(1)}, u32[]{:S(2)}, u32[]{:S(2)}) async-start(f32[8,1,96]{2,1,0:T(1,128)} %bitcast.11), calls=%async_computation.5 | async-start | bytes 8192 | tf_op jit(solution)/shard_map/all_to_all | solution.py:50
  266.1 2.8 all-to-all-done.5
  273.9 2.3 collective-permute-done.40.refs_3_
  278.5 2.0 convert_add_fusion
  (208 shorter events, 79.2 us)
Async XLA Ops:
  7.2 51.6 %all-gather.3.cloned.1.call-start = ((), (), s32[]{:S(2)}) async-start(), calls=%async_computation.6 | async-start | bytes 1769472 | tf_op jit(solution)/shard_map/all_gather | solution.py:618
  9.5 13.2 %collective-permute-start.1 = (bf16[256,768]{1,0:T(8,128)(2,1)}, bf16[256,768]{1,0:T(8,128)(2,1)S(1)}, u32[]{:S(2)}, u32[]{:S(2)}) collective-permute-start(bf16[256,768]{1,0:T(8,128)(2,1)} %refs_0_.1), channel_id=1, source_target_pairs={{0,2},{1,3},{2,0},{3,1},{4,6},{5,7},{6,4},{7,5},{8,10},{9,11},{10,... | collective-permute-start | bytes 1179656 | tf_op jit(solution)/shard_map/ppermute | solution.py:20
  12.5 18.0 %collective-permute-start = (bf16[256,768]{1,0:T(8,128)(2,1)}, bf16[256,768]{1,0:T(8,128)(2,1)S(1)}, u32[]{:S(2)}, u32[]{:S(2)}) collective-permute-start(bf16[256,768]{1,0:T(8,128)(2,1)} %refs_0_.1), channel_id=1, source_target_pairs={{0,1},{1,0},{2,3},{3,2},{4,5},{5,4},{6,7},{7,6},{8,9},{9,8},{10,11... | collective-permute-start | bytes 1179656 | tf_op jit(solution)/shard_map/ppermute | solution.py:20
  12.5 17.8 %collective-permute-start.4 = (bf16[256,768]{1,0:T(8,128)(2,1)}, bf16[256,768]{1,0:T(8,128)(2,1)S(1)}, u32[]{:S(2)}, u32[]{:S(2)}) collective-permute-start(bf16[256,768]{1,0:T(8,128)(2,1)} %refs_5_.1), channel_id=1, source_target_pairs={{0,2},{1,3},{2,0},{3,1},{4,6},{5,7},{6,4},{7,5},{8,10},{9,11},{10,... | collective-permute-start | bytes 1179656 | tf_op jit(solution)/shard_map/ppermute | solution.py:20
  12.6 34.0 %collective-permute-start.3 = (bf16[256,768]{1,0:T(8,128)(2,1)}, bf16[256,768]{1,0:T(8,128)(2,1)S(1)}, u32[]{:S(2)}, u32[]{:S(2)}) collective-permute-start(bf16[256,768]{1,0:T(8,128)(2,1)} %refs_5_.1), channel_id=1, source_target_pairs={{0,1},{1,0},{2,3},{3,2},{4,5},{5,4},{6,7},{7,6},{8,9},{9,8},{10,11... | collective-permute-start | bytes 1179656 | tf_op jit(solution)/shard_map/ppermute | solution.py:20
  16.4 12.7 %all-to-all-start = ((bf16[8,2,240]{2,1,0:T(2,128)(2,1)}), bf16[8,2,240]{2,1,0:T(2,128)(2,1)S(1)}, u32[]{:S(2)}, u32[]{:S(2)}) async-start(bf16[8,2,240]{2,1,0:T(2,128)(2,1)} %reshape.131), calls=%async_computation | async-start | bytes 16384 | tf_op jit(solution)/shard_map/all_to_all | solution.py:50
  22.5 96.5 %all-gather.5.cloned.1.call-start = ((), (), s32[]{:S(2)}) async-start(), calls=%async_computation.7 | async-start | bytes 2654208 | tf_op jit(solution)/shard_map/all_gather | solution.py:636
  30.2 16.4 %collective-permute-start.5 = (bf16[256,768]{1,0:T(8,128)(2,1)S(1)}, bf16[256,768]{1,0:T(8,128)(2,1)S(1)}, u32[]{:S(2)}, u32[]{:S(2)}) collective-permute-start(bf16[256,768]{1,0:T(8,128)(2,1)S(1)} %collective-permute-done.4.refs_17_), channel_id=1, source_target_pairs={{0,1},{1,0},{2,3},{3,2},{4,5},{5,4},{6,7},{7,6},{8,9},{9,8},{10,11... | collective-permute-start | bytes 1179656 | tf_op jit(solution)/shard_map/ppermute | solution.py:20
  50.8 39.3 %all-to-all-start.2 = ((bf16[8,96,576]{2,1,0:T(8,128)(2,1)}), bf16[8,96,576]{2,1,0:T(8,128)(2,1)S(1)}, u32[]{:S(2)}, u32[]{:S(2)}) async-start(bf16[8,96,576]{2,1,0:T(8,128)(2,1)} %shard_map.323), calls=%async_computation.2 | async-start | bytes 1966080 | tf_op jit(solution)/shard_map/all_to_all | solution.py:50
  60.0 15.3 %collective-permute-start.7 = (bf16[768,384]{1,0:T(8,128)(2,1)S(1)}, bf16[768,384]{1,0:T(8,128)(2,1)S(1)}, u32[]{:S(2)}, u32[]{:S(2)}) collective-permute-start(bf16[768,384]{1,0:T(8,128)(2,1)S(1)} %slice.105.refs_6_.refs_2_), channel_id=1, source_target_pairs={{0,2},{1,3},{2,0},{3,1},{4,6},{5,7},{6,4},{7,5},{8,10},{9,11},{10,... | collective-permute-start | bytes 1769480 | tf_op jit(solution)/shard_map/ppermute | solution.py:20
  71.8 11.4 %collective-permute-start.10 = (bf16[512,384]{1,0:T(8,128)(2,1)}, bf16[512,384]{1,0:T(8,128)(2,1)S(1)}, u32[]{:S(2)}, u32[]{:S(2)}) collective-permute-start(bf16[512,384]{1,0:T(8,128)(2,1)} %get-tuple-element.141.refs_10_.refs_4_), channel_id=1, source_target_pairs={{0,2},{1,3},{2,0},{3,1},{4,6},{5,7},{6,4},{7,5},{8,10},{9,11},{10,... | collective-permute-start | bytes 1179656 | tf_op jit(solution)/shard_map/ppermute | solution.py:20
  72.7 17.4 %collective-permute-start.6 = (bf16[768,384]{1,0:T(8,128)(2,1)S(1)}, bf16[768,384]{1,0:T(8,128)(2,1)}, u32[]{:S(2)}, u32[]{:S(2)}) collective-permute-start(bf16[768,384]{1,0:T(8,128)(2,1)S(1)} %slice.105.refs_6_.refs_2_), channel_id=1, source_target_pairs={{0,1},{1,0},{2,3},{3,2},{4,5},{5,4},{6,7},{7,6},{8,9},{9,8},{10,11... | collective-permute-start | bytes 1769480 | tf_op jit(solution)/shard_map/ppermute | solution.py:20
  75.3 14.9 %collective-permute-start.8 = (bf16[768,384]{1,0:T(8,128)(2,1)S(1)}, bf16[768,384]{1,0:T(8,128)(2,1)}, u32[]{:S(2)}, u32[]{:S(2)}) collective-permute-start(bf16[768,384]{1,0:T(8,128)(2,1)S(1)} %collective-permute-done.7.refs_8_.refs_4_), channel_id=1, source_target_pairs={{0,1},{1,0},{2,3},{3,2},{4,5},{5,4},{6,7},{7,6},{8,9},{9,8},{10,11... | collective-permute-start | bytes 1769480 | tf_op jit(solution)/shard_map/ppermute | solution.py:20
  75.3 14.9 %collective-permute-start.9 = (bf16[512,384]{1,0:T(8,128)(2,1)}, bf16[512,384]{1,0:T(8,128)(2,1)}, u32[]{:S(2)}, u32[]{:S(2)}) collective-permute-start(bf16[512,384]{1,0:T(8,128)(2,1)} %get-tuple-element.141.refs_10_.refs_4_), channel_id=1, source_target_pairs={{0,1},{1,0},{2,3},{3,2},{4,5},{5,4},{6,7},{7,6},{8,9},{9,8},{10,11... | collective-permute-start | bytes 1179656 | tf_op jit(solution)/shard_map/ppermute | solution.py:20
  139.0 12.4 %collective-permute-start.16 = (bf16[512,384]{1,0:T(8,128)(2,1)S(1)}, bf16[512,384]{1,0:T(8,128)(2,1)}, u32[]{:S(2)}, u32[]{:S(2)}) collective-permute-start(bf16[512,384]{1,0:T(8,128)(2,1)S(1)} %add_convert_fusion.6), channel_id=1, source_target_pairs={{0,2},{1,3},{2,0},{3,1},{4,6},{5,7},{6,4},{7,5},{8,10},{9,11},{10,... | collective-permute-start | bytes 1179656 | tf_op jit(solution)/shard_map/ppermute | solution.py:20
  151.4 64.8 %all-to-all-start.3 = ((bf16[8,96,1536]{2,1,0:T(8,128)(2,1)}), bf16[8,96,1536]{2,1,0:T(8,128)(2,1)S(1)}, u32[]{:S(2)}, u32[]{:S(2)}) async-start(bf16[8,96,1536]{2,1,0:T(8,128)(2,1)} %bitcast.41), calls=%async_computation.3 | async-start | bytes 4718592 | tf_op jit(solution)/shard_map/all_to_all | solution.py:50
  158.9 18.2 %collective-permute-start.21 = (bf16[256,1408]{1,0:T(8,128)(2,1)S(1)}, bf16[256,1408]{1,0:T(8,128)(2,1)S(1)}, u32[]{:S(2)}, u32[]{:S(2)}) collective-permute-start(bf16[256,1408]{1,0:T(8,128)(2,1)S(1)} %add_convert_fusion), channel_id=1, source_target_pairs={{0,2},{1,3},{2,0},{3,1},{4,6},{5,7},{6,4},{7,5},{8,10},{9,11},{10,... | collective-permute-start | bytes 2162696 | tf_op jit(solution)/shard_map/ppermute | solution.py:20
  171.6 8.3 %collective-permute-start.17 = (bf16[256,1408]{1,0:T(8,128)(2,1)}, bf16[256,1408]{1,0:T(8,128)(2,1)}, u32[]{:S(2)}, u32[]{:S(2)}) collective-permute-start(bf16[256,1408]{1,0:T(8,128)(2,1)} %get-tuple-element.161), channel_id=1, source_target_pairs={{0,1},{1,0},{2,3},{3,2},{4,5},{5,4},{6,7},{7,6},{8,9},{9,8},{10,11... | collective-permute-start | bytes 2162696 | tf_op jit(solution)/shard_map/ppermute | solution.py:20
  178.0 11.9 %collective-permute-start.23 = (bf16[512,384]{1,0:T(8,128)(2,1)}, bf16[512,384]{1,0:T(8,128)(2,1)}, u32[]{:S(2)}, u32[]{:S(2)}) collective-permute-start(bf16[512,384]{1,0:T(8,128)(2,1)} %add_convert_fusion.5), channel_id=1, source_target_pairs={{0,2},{1,3},{2,0},{3,1},{4,6},{5,7},{6,4},{7,5},{8,10},{9,11},{10,... | collective-permute-start | bytes 1179656 | tf_op jit(solution)/shard_map/ppermute | solution.py:20
  193.8 20.4 %collective-permute-start.25 = (bf16[4,96,768]{2,1,0:T(8,128)(2,1)}, bf16[4,96,768]{2,1,0:T(8,128)(2,1)}, u32[]{:S(2)}, u32[]{:S(2)}) collective-permute-start(bf16[4,96,768]{2,1,0:T(8,128)(2,1)} %get-tuple-element.208), channel_id=1, source_target_pairs={{0,4},{4,0},{8,12},{12,8},{16,20},{20,16},{24,28},{28,24},{1,5},{5... | collective-permute-start | bytes 1769480 | tf_op jit(solution)/shard_map/ppermute | solution.py:46
  195.8 20.4 %collective-permute-start.26 = (bf16[256,768]{1,0:T(8,128)(2,1)}, bf16[256,768]{1,0:T(8,128)(2,1)}, u32[]{:S(2)}, u32[]{:S(2)}) collective-permute-start(bf16[256,768]{1,0:T(8,128)(2,1)} %add_convert_fusion.4), channel_id=1, source_target_pairs={{0,2},{1,3},{2,0},{3,1},{4,6},{5,7},{6,4},{7,5},{8,10},{9,11},{10,... | collective-permute-start | bytes 1179656 | tf_op jit(solution)/shard_map/ppermute | solution.py:20
  197.3 22.2 %collective-permute-start.34 = (bf16[256,768]{1,0:T(8,128)(2,1)}, bf16[256,768]{1,0:T(8,128)(2,1)}, u32[]{:S(2)}, u32[]{:S(2)}) collective-permute-start(bf16[256,768]{1,0:T(8,128)(2,1)} %get-tuple-element.225), channel_id=1, source_target_pairs={{0,1},{1,0},{2,3},{3,2},{4,5},{5,4},{6,7},{7,6},{8,9},{9,8},{10,11... | collective-permute-start | bytes 1179656 | tf_op jit(solution)/shard_map/ppermute | solution.py:20
  217.5 11.2 %collective-permute-start.32 = (f32[16,768]{1,0:T(8,128)S(1)}, f32[16,768]{1,0:T(8,128)S(1)}, u32[]{:S(2)}, u32[]{:S(2)}) collective-permute-start(f32[16,768]{1,0:T(8,128)S(1)} %add.101), channel_id=1, source_target_pairs={{0,2},{1,3},{2,0},{3,1},{4,6},{5,7},{6,4},{7,5},{8,10},{9,11},{10,... | collective-permute-start | bytes 147464 | tf_op jit(solution)/shard_map/ppermute | solution.py:20
  226.7 8.5 %collective-permute-start.27 = (bf16[2,96,768]{2,1,0:T(8,128)(2,1)S(1)}, bf16[2,96,768]{2,1,0:T(8,128)(2,1)S(1)}, u32[]{:S(2)}, u32[]{:S(2)}) collective-permute-start(bf16[2,96,768]{2,1,0:T(8,128)(2,1)S(1)} %slice.117), channel_id=1, source_target_pairs={{0,8},{4,12},{8,0},{12,4},{16,24},{20,28},{24,16},{28,20},{1,9},{5... | collective-permute-start | bytes 884744 | tf_op jit(solution)/shard_map/ppermute | solution.py:46
  226.8 17.0 %collective-permute-start.33 = (bf16[4,96,640]{2,1,0:T(8,128)(2,1)S(1)}, bf16[4,96,640]{2,1,0:T(8,128)(2,1)S(1)}, u32[]{:S(2)}, u32[]{:S(2)}) collective-permute-start(bf16[4,96,640]{2,1,0:T(8,128)(2,1)S(1)} %copy-done.27), channel_id=1, source_target_pairs={{0,4},{4,0},{8,12},{12,8},{16,20},{20,16},{24,28},{28,24},{1,5},{5... | collective-permute-start | bytes 1474568 | tf_op jit(solution)/shard_map/ppermute | solution.py:46
  235.3 10.5 %collective-permute-start.35 = (bf16[1,96,768]{2,1,0:T(8,128)(2,1)S(1)}, bf16[1,96,768]{2,1,0:T(8,128)(2,1)S(1)}, u32[]{:S(2)}, u32[]{:S(2)}) collective-permute-start(bf16[1,96,768]{2,1,0:T(8,128)(2,1)S(1)} %slice.177), channel_id=1, source_target_pairs={{0,16},{4,20},{8,24},{12,28},{16,0},{20,4},{24,8},{28,12},{1,17},{... | collective-permute-start | bytes 442376 | tf_op jit(solution)/shard_map/ppermute | solution.py:46
  243.2 35.3 %collective-permute-start.28 = (bf16[256,768]{1,0:T(8,128)(2,1)}, bf16[256,768]{1,0:T(8,128)(2,1)}, u32[]{:S(2)}, u32[]{:S(2)}) collective-permute-start(bf16[256,768]{1,0:T(8,128)(2,1)} %get-tuple-element.215), channel_id=1, source_target_pairs={{0,1},{1,0},{2,3},{3,2},{4,5},{5,4},{6,7},{7,6},{8,9},{9,8},{10,11... | collective-permute-start | bytes 1179656 | tf_op jit(solution)/shard_map/ppermute | solution.py:20
  244.0 10.9 %collective-permute-start.37 = (bf16[2,128,640]{2,1,0:T(8,128)(2,1)S(1)}, bf16[2,128,640]{2,1,0:T(8,128)(2,1)}, u32[]{:S(2)}, u32[]{:S(2)}) collective-permute-start(bf16[2,128,640]{2,1,0:T(8,128)(2,1)S(1)} %slice.124), channel_id=1, source_target_pairs={{0,8},{4,12},{8,0},{12,4},{16,24},{20,28},{24,16},{28,20},{1,9},{5... | collective-permute-start | bytes 983048 | tf_op jit(solution)/shard_map/ppermute | solution.py:46
  246.5 11.5 %all-to-all-start.4 = ((bf16[8,16,768]{2,1,0:T(8,128)(2,1)}), bf16[8,16,768]{2,1,0:T(8,128)(2,1)S(1)}, u32[]{:S(2)}, u32[]{:S(2)}) async-start(bf16[8,16,768]{2,1,0:T(8,128)(2,1)} %broadcast_in_dim.37), calls=%async_computation.4 | async-start | bytes 393216 | tf_op jit(solution)/shard_map/all_to_all | solution.py:50
  251.8 26.7 %collective-permute-start.30 = (bf16[256,768]{1,0:T(8,128)(2,1)S(1)}, bf16[256,768]{1,0:T(8,128)(2,1)S(1)}, u32[]{:S(2)}, u32[]{:S(2)}) collective-permute-start(bf16[256,768]{1,0:T(8,128)(2,1)S(1)} %add_convert_fusion.3), channel_id=1, source_target_pairs={{0,2},{1,3},{2,0},{3,1},{4,6},{5,7},{6,4},{7,5},{8,10},{9,11},{10,... | collective-permute-start | bytes 1179656 | tf_op jit(solution)/shard_map/ppermute | solution.py:20
  256.0 14.2 %collective-permute-start.38 = (bf16[1,128,640]{2,1,0:T(8,128)(2,1)S(1)}, bf16[1,128,640]{2,1,0:T(8,128)(2,1)}, u32[]{:S(2)}, u32[]{:S(2)}) collective-permute-start(bf16[1,128,640]{2,1,0:T(8,128)(2,1)S(1)} %slice.176), channel_id=1, source_target_pairs={{0,16},{4,20},{8,24},{12,28},{16,0},{20,4},{24,8},{28,12},{1,17},{... | collective-permute-start | bytes 491528 | tf_op jit(solution)/shard_map/ppermute | solution.py:46
  259.0 9.9 %all-to-all-start.5 = ((f32[8,1,96]{2,1,0:T(1,128)}), f32[8,1,96]{2,1,0:T(1,128)S(1)}, u32[]{:S(2)}, u32[]{:S(2)}) async-start(f32[8,1,96]{2,1,0:T(1,128)} %bitcast.11), calls=%async_computation.5 | async-start | bytes 8192 | tf_op jit(solution)/shard_map/all_to_all | solution.py:50
  (45 other events, 400.1 us)
Sparse Core Ops, SparseCore 0:
  10.8 48.0 all-gather.2
  61.6 57.3 all-gather.4

commit v7 on v6

--- a/solution.py
+++ b/solution.py
@@ -763,7 +763,7 @@
     *outs, grad_captions = call(
         partial(out_rows, kr=kr),
         [place],
-        [out_mine, out_near, out_far],
+        [out_mine, out_near, after(out_far, vec)],
         [out(third_shape, BF) for _ in range(2)] + [out((1, slots, hw), F32)],
         [pltpu.VMEM((width, hw), BF)],
     )

time: 291 us -> 298 us (1.024)
  waiting for transfers between devices: 61.4 us -> 65.7 us
    unnamed x61 -> x59, local copies, waits for them, and re-layouts: 6.69 us -> 5.93 us
  transfers between devices with their start and end apart: 49 -> 49, of which waited for: 25 -> 24; matrix products, arithmetic and copies ran while one was open for 12% -> 13% of each run, Pallas kernels for 29% -> 28%
where the time goes in v7:
time: 298 us; the launch traced here: 294 us
  Pallas kernels  101 us (34%)
  waiting for transfers between devices  65.7 us (22%)
  starting transfers between devices  51.6 us (17%)
  other arithmetic  24 us (8%)
  local copies, waits for them, and re-layouts  19.5 us (7%)
  between operations  15.6 us (5%)
  blocking collectives  13.9 us (5%)
    pallas_call x13, Pallas kernels, call(): pl.pallas_call(body, in_specs=[pl.BlockSpec(memory_space=pltpu.SMEM)] * l...  101 us
    ppermute x32, waiting for transfers between devices, swap(): return lax.ppermute(x, 'head', [(i, i ^ bit) for i in range(4)])  29.9 us
    all_to_all x5, starting transfers between devices, exchange(): return lax.all_to_all(x, 'seq', split_axis=0, concat_axis=0, tiled=True)  24.4 us
    ppermute x32, starting transfers between devices, swap(): return lax.ppermute(x, 'head', [(i, i ^ bit) for i in range(4)])  15.9 us
    all_to_all x1, blocking collectives, exchange(): return lax.all_to_all(x, 'seq', split_axis=0, concat_axis=0, tiled=True)  13.9 us
    all_to_all x5, waiting for transfers between devices, exchange(): return lax.all_to_all(x, 'seq', split_axis=0, concat_axis=0, tiled=True)  13.9 us
    ppermute x7, waiting for transfers between devices, seq_swap(): lax.ppermute(x, 'seq', [(i, i ^ bit) for i in range(lax.axis_size('seq'))])  9.86 us
    ppermute x7, starting transfers between devices, seq_swap(): lax.ppermute(x, 'seq', [(i, i ^ bit) for i in range(lax.axis_size('seq'))])  9.27 us
  transfers between devices with their start and end apart: 49, of which 24 were waited for; matrix products, arithmetic and copies ran while one was open for 13% of the time, Pallas kernels for 28%

profile of v7, /device:TPU:0, one launch (start us, length us, event | category | flops | bytes accessed | tf_op | source)
XLA Modules:
  0.0 293.9 jit_solution(12580140700466644211)
XLA Ops:
  7.3 2.2 shard_map.322
  9.5 3.0 %collective-permute-start.1 = (bf16[256,768]{1,0:T(8,128)(2,1)}, bf16[256,768]{1,0:T(8,128)(2,1)S(1)}, u32[]{:S(2)}, u32[]{:S(2)}) collective-permute-start(bf16[256,768]{1,0:T(8,128)(2,1)} %refs_0_.1), channel_id=1, source_target_pairs={{0,2},{1,3},{2,0},{3,1},{4,6},{5,7},{6,4},{7,5},{8,10},{9,11},{10,... | collective-permute-start | bytes 1179656 | tf_op jit(solution)/shard_map/ppermute | solution.py:20
  16.4 6.1 %all-to-all-start = ((bf16[8,2,240]{2,1,0:T(2,128)(2,1)}), bf16[8,2,240]{2,1,0:T(2,128)(2,1)S(1)}, u32[]{:S(2)}, u32[]{:S(2)}) async-start(bf16[8,2,240]{2,1,0:T(2,128)(2,1)} %reshape.131), calls=%async_computation | async-start | bytes 16384 | tf_op jit(solution)/shard_map/all_to_all | solution.py:50
  23.5 5.6 %all-to-all-done = bf16[8,2,240]{2,1,0:T(2,128)(2,1)S(1)} async-done(((bf16[8,2,240]{2,1,0:T(2,128)(2,1)}), bf16[8,2,240]{2,1,0:T(2,128)(2,1)S(1)}, u32[]{:S(2)}, u32[]{:S(2)}) %all-to-all-start) | async-done | bytes 7712 | tf_op jit(solution)/shard_map/all_to_all | solution.py:50
  30.6 13.9 %all_to_all.45 = f32[8,1,4608]{2,1,0:T(1,128)S(1)} all-to-all(f32[8,1,4608]{2,1,0:T(1,128)S(1)} %copy.44), channel_id=1, replica_groups=mesh['seq'=8,'head'=4] {'seq'}, dimensions={0} | all-to-all | bytes 294912 | tf_op jit(solution)/shard_map/all_to_all | solution.py:50
  48.5 2.3 shard_map.323
  50.8 6.1 %all-to-all-start.2 = ((bf16[8,96,576]{2,1,0:T(8,128)(2,1)}), bf16[8,96,576]{2,1,0:T(8,128)(2,1)S(1)}, u32[]{:S(2)}, u32[]{:S(2)}) async-start(bf16[8,96,576]{2,1,0:T(8,128)(2,1)} %shard_map.323), calls=%async_computation.2 | async-start | bytes 1966080 | tf_op jit(solution)/shard_map/all_to_all | solution.py:50
  61.2 10.6 %shard_map.324 = (bf16[1024,768]{1,0:T(8,128)(2,1)}, bf16[3,1024,192]{2,1,0:T(8,128)(2,1)}, bf16[512,384]{1,0:T(8,128)(2,1)}, bf16[3,1024,1024]{2,1,0:T(8,128)(2,1)}, f32[3,1024]{1,0:T(4,128)}) custom-call(bf16[256,768]{1,0:T(8,128)(2,1)} %refs_0_.1, bf16[256,768]{1,0:T(8,128)(2,1)} %copy-done.4, bf16[256,768]{1,0:T(8,128)(2,1)} %copy-done.3, ...), custom_call_target="tpu_custom_call" | custom-call | tf_op jit(solution)/shard_map/pallas_call | solution.py:146
  72.7 2.6 collective-permute-done.7.refs_8_.refs_4_
  75.8 7.4 %collective-permute-done.10.refs_12_ = bf16[512,384]{1,0:T(8,128)(2,1)S(1)} collective-permute-done((bf16[512,384]{1,0:T(8,128)(2,1)}, bf16[512,384]{1,0:T(8,128)(2,1)S(1)}, u32[]{:S(2)}, u32[]{:S(2)}) %collective-permute-start.10) | collective-permute-done | bytes 393248 | tf_op jit(solution)/shard_map/ppermute | solution.py:20
  85.4 4.8 %all-to-all-done.2 = bf16[8,96,576]{2,1,0:T(8,128)(2,1)S(1)} async-done(((bf16[8,96,576]{2,1,0:T(8,128)(2,1)}), bf16[8,96,576]{2,1,0:T(8,128)(2,1)S(1)}, u32[]{:S(2)}, u32[]{:S(2)}) %all-to-all-start.2) | async-done | bytes 884768 | tf_op jit(solution)/shard_map/all_to_all | solution.py:50
  91.2 11.1 %shard_map.325 = (bf16[1024,768]{1,0:T(8,128)(2,1)}, bf16[768,768]{1,0:T(8,128)(2,1)}, bf16[1024,768]{1,0:T(8,128)(2,1)}, f32[1024,768]{1,0:T(8,128)}, bf16[1024...) custom-call(s32[1]{0:T(128)} %bitcast.refs_0_, ...), custom_call_target="tpu_custom_call" | custom-call | tf_op jit(solution)/shard_map/pallas_call | solution.py:146
  103.8 6.5 %collective-permute-done.13.refs_7_ = bf16[512,384]{1,0:T(8,128)(2,1)S(1)} collective-permute-done((bf16[512,384]{1,0:T(8,128)(2,1)}, bf16[512,384]{1,0:T(8,128)(2,1)S(1)}, u32[]{:S(2)}, u32[]{:S(2)}) %collective-permute-start.13) | collective-permute-done | bytes 393248 | tf_op jit(solution)/shard_map/ppermute | solution.py:20
  112.0 6.9 %all-gather.5.cloned.1.call-done.refs_12_.refs_14_.refs_4_ = bf16[768,1536]{1,0:T(8,128)(2,1)} async-done(((bf16[96,1536]{1,0:T(8,128)(2,1)}), bf16[768,1536]{1,0:T(8,128)(2,1)}) %all-gather.5.cloned.1.call-update) | async-done | bytes 2359312 | tf_op jit(solution)/shard_map/all_gather | solution.py:636
  119.0 16.9 %shard_map.326 = (bf16[1024,768]{1,0:T(8,128)(2,1)}, bf16[768,768]{1,0:T(8,128)(2,1)}, f32[256,768]{1,0:T(8,128)}, bf16[1024,768]{1,0:T(8,128)(2,1)}, bf16[1024,...) custom-call(s32[1]{0:T(128)} %bitcast.refs_0_, ...), custom_call_target="tpu_custom_call" | custom-call | tf_op jit(solution)/shard_map/pallas_call | solution.py:146
  140.5 10.9 %shard_map.327 = (bf16[256,1408]{1,0:T(8,128)(2,1)}, bf16[256,1408]{1,0:T(8,128)(2,1)}, bf16[256,1408]{1,0:T(8,128)(2,1)}, bf16[256,1408]{1,0:T(8,128)(2,1)}, bf16[768,1536]{1,0:T(8,128)(2,1)}) custom-call(s32[1]{0:T(128)} %bitcast.refs_0_, bf16[1024,768]{1,0:T(8,128)(2,1)} %get-tuple-element.151.refs_1_, ...), custom_call_target="tpu_custom_call" | custom-call | tf_op jit(solution)/shard_map/pallas_call | solution.py:146
  151.4 3.8 %all-to-all-start.3 = ((bf16[8,96,1536]{2,1,0:T(8,128)(2,1)}), bf16[8,96,1536]{2,1,0:T(8,128)(2,1)S(1)}, u32[]{:S(2)}, u32[]{:S(2)}) async-start(bf16[8,96,1536]{2,1,0:T(8,128)(2,1)} %bitcast.41), calls=%async_computation.3 | async-start | bytes 4718592 | tf_op jit(solution)/shard_map/all_to_all | solution.py:50
  160.3 11.2 %shard_map.328 = (bf16[1024,192]{1,0:T(8,128)(2,1)}, bf16[2,256,192]{2,1,0:T(8,128)(2,1)}, bf16[1024,768]{1,0:T(8,128)(2,1)}, bf16[1024,768]{1,0:T(8,128)(2,1)},...) custom-call(s32[1]{0:T(128)} %bitcast.refs_0_, ...), custom_call_target="tpu_custom_call" | custom-call | tf_op jit(solution)/shard_map/pallas_call | solution.py:146
  179.8 10.1 %shard_map.329 = (bf16[4,96,768]{2,1,0:T(8,128)(2,1)}, bf16[4,96,768]{2,1,0:T(8,128)(2,1)}, bf16[256,768]{1,0:T(8,128)(2,1)}, bf16[256,768]{1,0:T(8,128)(2,1)}, ...) custom-call(s32[2]{0:T(128)} %pad_add_fusion.refs_0_, ...), custom_call_target="tpu_custom_call" | custom-call | tf_op jit(solution)/shard_map/pallas_call | solution.py:146
  197.8 15.3 %shard_map.330 = (bf16[1024,576]{1,0:T(8,128)(2,1)}, bf16[4,96,640]{2,1,0:T(8,128)(2,1)}, bf16[4,96,640]{2,1,0:T(8,128)(2,1)}, f32[16,768]{1,0:T(8,128)}) custom-call(s32[2]{0:T(128)} %pad_add_fusion.refs_0_, bf16[512,384]{1,0:T(8,128)(2,1)} %get-tuple-element.187.refs_1_, bf16[512,384]{1,0:T(8,128)(2,1)} %collective-permute-done.22.refs_2_, ...), custom_call_target="tpu_custom_call" | custom-call | tf_op jit(solution)/shard_map/pallas_call | solution.py:146
  217.7 2.8 collective-permute-start.27
  222.6 2.9 collective-permute-done.32
  227.1 3.0 %shard_map.332 = (bf16[4,32,640]{2,1,0:T(8,128)(2,1)}, bf16[4,32,640]{2,1,0:T(8,128)(2,1)}, f32[1,256,192]{2,1,0:T(8,128)}) custom-call(s32[2]{0:T(128)} %pad_add_fusion.refs_0_, bf16[256,768]{1,0:T(8,128)(2,1)} %get-tuple-element.225.refs_1_, bf16[256,768]{1,0:T(8,128)(2,1)} %copy-done.20, bf16[256,768]{1,0:T(8,128)(2,1)} %collective-permute-done.26.refs_3_), custom_call_target="tpu_custom_call" | custom-call | tf_op jit(solution)/shard_map/pallas_call | solution.py:146
  230.2 2.0 collective-permute-start.36
  234.8 2.4 collective-permute-done.36
  240.1 6.7 %shard_map.331 = (bf16[256,768]{1,0:T(8,128)(2,1)}, bf16[256,768]{1,0:T(8,128)(2,1)}, bf16[256,768]{1,0:T(8,128)(2,1)}, bf16[256,768]{1,0:T(8,128)(2,1)}) custom-call(bf16[256,768]{1,0:T(8,128)(2,1)} %refs_0_.1, bf16[256,768]{1,0:T(8,128)(2,1)} %copy-done.4, bf16[256,768]{1,0:T(8,128)(2,1)} %copy-done.3, bf16[256,768]{1,0:T(8,128)(2,1)} %copy-done.5, ...), custom_call_target="tpu_custom_call" | custom-call | tf_op jit(solution)/shard_map/pallas_call | solution.py:146
  250.7 3.6 %all-to-all-start.4 = ((bf16[8,16,768]{2,1,0:T(8,128)(2,1)}), bf16[8,16,768]{2,1,0:T(8,128)(2,1)S(1)}, u32[]{:S(2)}, u32[]{:S(2)}) async-start(bf16[8,16,768]{2,1,0:T(8,128)(2,1)} %broadcast_in_dim.37), calls=%async_computation.4 | async-start | bytes 393216 | tf_op jit(solution)/shard_map/all_to_all | solution.py:50
  255.1 6.4 %collective-permute-done.37 = bf16[2,128,640]{2,1,0:T(8,128)(2,1)} collective-permute-done((bf16[2,128,640]{2,1,0:T(8,128)(2,1)}, bf16[2,128,640]{2,1,0:T(8,128)(2,1)}, u32[]{:S(2)}, u32[]{:S(2)}) %collective-permute-start.37) | collective-permute-done | bytes 327712 | tf_op jit(solution)/shard_map/ppermute | solution.py:46
  264.3 4.8 %all-to-all-start.5 = ((f32[8,1,96]{2,1,0:T(1,128)}), f32[8,1,96]{2,1,0:T(1,128)S(1)}, u32[]{:S(2)}, u32[]{:S(2)}) async-start(f32[8,1,96]{2,1,0:T(1,128)} %bitcast.11), calls=%async_computation.5 | async-start | bytes 8192 | tf_op jit(solution)/shard_map/all_to_all | solution.py:50
  272.7 2.8 all-to-all-done.5
  280.5 2.6 collective-permute-done.40.refs_3_
  284.8 2.0 convert_add_fusion
  (206 shorter events, 79.0 us)
Async XLA Ops:
  7.2 51.6 %all-gather.3.cloned.1.call-start = ((), (), s32[]{:S(2)}) async-start(), calls=%async_computation.6 | async-start | bytes 1769472 | tf_op jit(solution)/shard_map/all_gather | solution.py:618
  9.5 13.2 %collective-permute-start.1 = (bf16[256,768]{1,0:T(8,128)(2,1)}, bf16[256,768]{1,0:T(8,128)(2,1)S(1)}, u32[]{:S(2)}, u32[]{:S(2)}) collective-permute-start(bf16[256,768]{1,0:T(8,128)(2,1)} %refs_0_.1), channel_id=1, source_target_pairs={{0,2},{1,3},{2,0},{3,1},{4,6},{5,7},{6,4},{7,5},{8,10},{9,11},{10,... | collective-permute-start | bytes 1179656 | tf_op jit(solution)/shard_map/ppermute | solution.py:20
  12.5 18.0 %collective-permute-start = (bf16[256,768]{1,0:T(8,128)(2,1)}, bf16[256,768]{1,0:T(8,128)(2,1)S(1)}, u32[]{:S(2)}, u32[]{:S(2)}) collective-permute-start(bf16[256,768]{1,0:T(8,128)(2,1)} %refs_0_.1), channel_id=1, source_target_pairs={{0,1},{1,0},{2,3},{3,2},{4,5},{5,4},{6,7},{7,6},{8,9},{9,8},{10,11... | collective-permute-start | bytes 1179656 | tf_op jit(solution)/shard_map/ppermute | solution.py:20
  12.5 17.8 %collective-permute-start.4 = (bf16[256,768]{1,0:T(8,128)(2,1)}, bf16[256,768]{1,0:T(8,128)(2,1)S(1)}, u32[]{:S(2)}, u32[]{:S(2)}) collective-permute-start(bf16[256,768]{1,0:T(8,128)(2,1)} %refs_5_.1), channel_id=1, source_target_pairs={{0,2},{1,3},{2,0},{3,1},{4,6},{5,7},{6,4},{7,5},{8,10},{9,11},{10,... | collective-permute-start | bytes 1179656 | tf_op jit(solution)/shard_map/ppermute | solution.py:20
  12.6 34.0 %collective-permute-start.3 = (bf16[256,768]{1,0:T(8,128)(2,1)}, bf16[256,768]{1,0:T(8,128)(2,1)S(1)}, u32[]{:S(2)}, u32[]{:S(2)}) collective-permute-start(bf16[256,768]{1,0:T(8,128)(2,1)} %refs_5_.1), channel_id=1, source_target_pairs={{0,1},{1,0},{2,3},{3,2},{4,5},{5,4},{6,7},{7,6},{8,9},{9,8},{10,11... | collective-permute-start | bytes 1179656 | tf_op jit(solution)/shard_map/ppermute | solution.py:20
  16.4 12.7 %all-to-all-start = ((bf16[8,2,240]{2,1,0:T(2,128)(2,1)}), bf16[8,2,240]{2,1,0:T(2,128)(2,1)S(1)}, u32[]{:S(2)}, u32[]{:S(2)}) async-start(bf16[8,2,240]{2,1,0:T(2,128)(2,1)} %reshape.131), calls=%async_computation | async-start | bytes 16384 | tf_op jit(solution)/shard_map/all_to_all | solution.py:50
  22.5 96.5 %all-gather.5.cloned.1.call-start = ((), (), s32[]{:S(2)}) async-start(), calls=%async_computation.7 | async-start | bytes 2654208 | tf_op jit(solution)/shard_map/all_gather | solution.py:636
  30.2 16.4 %collective-permute-start.5 = (bf16[256,768]{1,0:T(8,128)(2,1)S(1)}, bf16[256,768]{1,0:T(8,128)(2,1)S(1)}, u32[]{:S(2)}, u32[]{:S(2)}) collective-permute-start(bf16[256,768]{1,0:T(8,128)(2,1)S(1)} %collective-permute-done.4.refs_17_), channel_id=1, source_target_pairs={{0,1},{1,0},{2,3},{3,2},{4,5},{5,4},{6,7},{7,6},{8,9},{9,8},{10,11... | collective-permute-start | bytes 1179656 | tf_op jit(solution)/shard_map/ppermute | solution.py:20
  50.8 39.3 %all-to-all-start.2 = ((bf16[8,96,576]{2,1,0:T(8,128)(2,1)}), bf16[8,96,576]{2,1,0:T(8,128)(2,1)S(1)}, u32[]{:S(2)}, u32[]{:S(2)}) async-start(bf16[8,96,576]{2,1,0:T(8,128)(2,1)} %shard_map.323), calls=%async_computation.2 | async-start | bytes 1966080 | tf_op jit(solution)/shard_map/all_to_all | solution.py:50
  60.0 15.3 %collective-permute-start.7 = (bf16[768,384]{1,0:T(8,128)(2,1)S(1)}, bf16[768,384]{1,0:T(8,128)(2,1)S(1)}, u32[]{:S(2)}, u32[]{:S(2)}) collective-permute-start(bf16[768,384]{1,0:T(8,128)(2,1)S(1)} %slice.105.refs_6_.refs_2_), channel_id=1, source_target_pairs={{0,2},{1,3},{2,0},{3,1},{4,6},{5,7},{6,4},{7,5},{8,10},{9,11},{10,... | collective-permute-start | bytes 1769480 | tf_op jit(solution)/shard_map/ppermute | solution.py:20
  71.8 11.4 %collective-permute-start.10 = (bf16[512,384]{1,0:T(8,128)(2,1)}, bf16[512,384]{1,0:T(8,128)(2,1)S(1)}, u32[]{:S(2)}, u32[]{:S(2)}) collective-permute-start(bf16[512,384]{1,0:T(8,128)(2,1)} %get-tuple-element.142.refs_10_.refs_4_), channel_id=1, source_target_pairs={{0,2},{1,3},{2,0},{3,1},{4,6},{5,7},{6,4},{7,5},{8,10},{9,11},{10,... | collective-permute-start | bytes 1179656 | tf_op jit(solution)/shard_map/ppermute | solution.py:20
  72.7 17.4 %collective-permute-start.6 = (bf16[768,384]{1,0:T(8,128)(2,1)S(1)}, bf16[768,384]{1,0:T(8,128)(2,1)}, u32[]{:S(2)}, u32[]{:S(2)}) collective-permute-start(bf16[768,384]{1,0:T(8,128)(2,1)S(1)} %slice.105.refs_6_.refs_2_), channel_id=1, source_target_pairs={{0,1},{1,0},{2,3},{3,2},{4,5},{5,4},{6,7},{7,6},{8,9},{9,8},{10,11... | collective-permute-start | bytes 1769480 | tf_op jit(solution)/shard_map/ppermute | solution.py:20
  75.3 14.9 %collective-permute-start.8 = (bf16[768,384]{1,0:T(8,128)(2,1)S(1)}, bf16[768,384]{1,0:T(8,128)(2,1)}, u32[]{:S(2)}, u32[]{:S(2)}) collective-permute-start(bf16[768,384]{1,0:T(8,128)(2,1)S(1)} %collective-permute-done.7.refs_8_.refs_4_), channel_id=1, source_target_pairs={{0,1},{1,0},{2,3},{3,2},{4,5},{5,4},{6,7},{7,6},{8,9},{9,8},{10,11... | collective-permute-start | bytes 1769480 | tf_op jit(solution)/shard_map/ppermute | solution.py:20
  75.3 14.9 %collective-permute-start.9 = (bf16[512,384]{1,0:T(8,128)(2,1)}, bf16[512,384]{1,0:T(8,128)(2,1)}, u32[]{:S(2)}, u32[]{:S(2)}) collective-permute-start(bf16[512,384]{1,0:T(8,128)(2,1)} %get-tuple-element.142.refs_10_.refs_4_), channel_id=1, source_target_pairs={{0,1},{1,0},{2,3},{3,2},{4,5},{5,4},{6,7},{7,6},{8,9},{9,8},{10,11... | collective-permute-start | bytes 1179656 | tf_op jit(solution)/shard_map/ppermute | solution.py:20
  102.3 8.1 %collective-permute-start.13 = (bf16[512,384]{1,0:T(8,128)(2,1)}, bf16[512,384]{1,0:T(8,128)(2,1)S(1)}, u32[]{:S(2)}, u32[]{:S(2)}) collective-permute-start(bf16[512,384]{1,0:T(8,128)(2,1)} %get-tuple-element.144.refs_1_.refs_4_), channel_id=1, source_target_pairs={{0,2},{1,3},{2,0},{3,1},{4,6},{5,7},{6,4},{7,5},{8,10},{9,11},{10,... | collective-permute-start | bytes 1179656 | tf_op jit(solution)/shard_map/ppermute | solution.py:20
  139.0 12.4 %collective-permute-start.16 = (bf16[512,384]{1,0:T(8,128)(2,1)S(1)}, bf16[512,384]{1,0:T(8,128)(2,1)}, u32[]{:S(2)}, u32[]{:S(2)}) collective-permute-start(bf16[512,384]{1,0:T(8,128)(2,1)S(1)} %add_convert_fusion.6), channel_id=1, source_target_pairs={{0,2},{1,3},{2,0},{3,1},{4,6},{5,7},{6,4},{7,5},{8,10},{9,11},{10,... | collective-permute-start | bytes 1179656 | tf_op jit(solution)/shard_map/ppermute | solution.py:20
  151.4 64.8 %all-to-all-start.3 = ((bf16[8,96,1536]{2,1,0:T(8,128)(2,1)}), bf16[8,96,1536]{2,1,0:T(8,128)(2,1)S(1)}, u32[]{:S(2)}, u32[]{:S(2)}) async-start(bf16[8,96,1536]{2,1,0:T(8,128)(2,1)} %bitcast.41), calls=%async_computation.3 | async-start | bytes 4718592 | tf_op jit(solution)/shard_map/all_to_all | solution.py:50
  159.0 18.2 %collective-permute-start.21 = (bf16[256,1408]{1,0:T(8,128)(2,1)S(1)}, bf16[256,1408]{1,0:T(8,128)(2,1)S(1)}, u32[]{:S(2)}, u32[]{:S(2)}) collective-permute-start(bf16[256,1408]{1,0:T(8,128)(2,1)S(1)} %add_convert_fusion), channel_id=1, source_target_pairs={{0,2},{1,3},{2,0},{3,1},{4,6},{5,7},{6,4},{7,5},{8,10},{9,11},{10,... | collective-permute-start | bytes 2162696 | tf_op jit(solution)/shard_map/ppermute | solution.py:20
  171.6 8.2 %collective-permute-start.17 = (bf16[256,1408]{1,0:T(8,128)(2,1)}, bf16[256,1408]{1,0:T(8,128)(2,1)}, u32[]{:S(2)}, u32[]{:S(2)}) collective-permute-start(bf16[256,1408]{1,0:T(8,128)(2,1)} %get-tuple-element.162), channel_id=1, source_target_pairs={{0,1},{1,0},{2,3},{3,2},{4,5},{5,4},{6,7},{7,6},{8,9},{9,8},{10,11... | collective-permute-start | bytes 2162696 | tf_op jit(solution)/shard_map/ppermute | solution.py:20
  178.0 11.9 %collective-permute-start.23 = (bf16[512,384]{1,0:T(8,128)(2,1)}, bf16[512,384]{1,0:T(8,128)(2,1)}, u32[]{:S(2)}, u32[]{:S(2)}) collective-permute-start(bf16[512,384]{1,0:T(8,128)(2,1)} %add_convert_fusion.5), channel_id=1, source_target_pairs={{0,2},{1,3},{2,0},{3,1},{4,6},{5,7},{6,4},{7,5},{8,10},{9,11},{10,... | collective-permute-start | bytes 1179656 | tf_op jit(solution)/shard_map/ppermute | solution.py:20
  193.8 20.3 %collective-permute-start.25 = (bf16[4,96,768]{2,1,0:T(8,128)(2,1)}, bf16[4,96,768]{2,1,0:T(8,128)(2,1)}, u32[]{:S(2)}, u32[]{:S(2)}) collective-permute-start(bf16[4,96,768]{2,1,0:T(8,128)(2,1)} %get-tuple-element.209), channel_id=1, source_target_pairs={{0,4},{4,0},{8,12},{12,8},{16,20},{20,16},{24,28},{28,24},{1,5},{5... | collective-permute-start | bytes 1769480 | tf_op jit(solution)/shard_map/ppermute | solution.py:46
  195.7 20.5 %collective-permute-start.26 = (bf16[256,768]{1,0:T(8,128)(2,1)}, bf16[256,768]{1,0:T(8,128)(2,1)}, u32[]{:S(2)}, u32[]{:S(2)}) collective-permute-start(bf16[256,768]{1,0:T(8,128)(2,1)} %add_convert_fusion.4), channel_id=1, source_target_pairs={{0,2},{1,3},{2,0},{3,1},{4,6},{5,7},{6,4},{7,5},{8,10},{9,11},{10,... | collective-permute-start | bytes 1179656 | tf_op jit(solution)/shard_map/ppermute | solution.py:20
  216.2 10.2 %collective-permute-start.34 = (bf16[256,768]{1,0:T(8,128)(2,1)}, bf16[256,768]{1,0:T(8,128)(2,1)S(1)}, u32[]{:S(2)}, u32[]{:S(2)}) collective-permute-start(bf16[256,768]{1,0:T(8,128)(2,1)} %get-tuple-element.226), channel_id=1, source_target_pairs={{0,1},{1,0},{2,3},{3,2},{4,5},{5,4},{6,7},{7,6},{8,9},{9,8},{10,11... | collective-permute-start | bytes 1179656 | tf_op jit(solution)/shard_map/ppermute | solution.py:20
  217.7 19.5 %collective-permute-start.27 = (bf16[2,96,768]{2,1,0:T(8,128)(2,1)S(1)}, bf16[2,96,768]{2,1,0:T(8,128)(2,1)}, u32[]{:S(2)}, u32[]{:S(2)}) collective-permute-start(bf16[2,96,768]{2,1,0:T(8,128)(2,1)S(1)} %slice.117), channel_id=1, source_target_pairs={{0,8},{4,12},{8,0},{12,4},{16,24},{20,28},{24,16},{28,20},{1,9},{5... | collective-permute-start | bytes 884744 | tf_op jit(solution)/shard_map/ppermute | solution.py:46
  220.5 26.8 %collective-permute-start.33 = (bf16[4,96,640]{2,1,0:T(8,128)(2,1)}, bf16[4,96,640]{2,1,0:T(8,128)(2,1)}, u32[]{:S(2)}, u32[]{:S(2)}) collective-permute-start(bf16[4,96,640]{2,1,0:T(8,128)(2,1)} %get-tuple-element.222), channel_id=1, source_target_pairs={{0,4},{4,0},{8,12},{12,8},{16,20},{20,16},{24,28},{28,24},{1,5},{5... | collective-permute-start | bytes 1474568 | tf_op jit(solution)/shard_map/ppermute | solution.py:46
  238.3 11.7 %collective-permute-start.35 = (bf16[1,96,768]{2,1,0:T(8,128)(2,1)S(1)}, bf16[1,96,768]{2,1,0:T(8,128)(2,1)S(1)}, u32[]{:S(2)}, u32[]{:S(2)}) collective-permute-start(bf16[1,96,768]{2,1,0:T(8,128)(2,1)S(1)} %slice.177), channel_id=1, source_target_pairs={{0,16},{4,20},{8,24},{12,28},{16,0},{20,4},{24,8},{28,12},{1,17},{... | collective-permute-start | bytes 442376 | tf_op jit(solution)/shard_map/ppermute | solution.py:46
  246.8 37.9 %collective-permute-start.28 = (bf16[256,768]{1,0:T(8,128)(2,1)}, bf16[256,768]{1,0:T(8,128)(2,1)}, u32[]{:S(2)}, u32[]{:S(2)}) collective-permute-start(bf16[256,768]{1,0:T(8,128)(2,1)} %get-tuple-element.216), channel_id=1, source_target_pairs={{0,1},{1,0},{2,3},{3,2},{4,5},{5,4},{6,7},{7,6},{8,9},{9,8},{10,11... | collective-permute-start | bytes 1179656 | tf_op jit(solution)/shard_map/ppermute | solution.py:20
  249.4 12.1 %collective-permute-start.37 = (bf16[2,128,640]{2,1,0:T(8,128)(2,1)}, bf16[2,128,640]{2,1,0:T(8,128)(2,1)}, u32[]{:S(2)}, u32[]{:S(2)}) collective-permute-start(bf16[2,128,640]{2,1,0:T(8,128)(2,1)} %slice.124), channel_id=1, source_target_pairs={{0,8},{4,12},{8,0},{12,4},{16,24},{20,28},{24,16},{28,20},{1,9},{5... | collective-permute-start | bytes 983048 | tf_op jit(solution)/shard_map/ppermute | solution.py:46
  250.7 12.6 %all-to-all-start.4 = ((bf16[8,16,768]{2,1,0:T(8,128)(2,1)}), bf16[8,16,768]{2,1,0:T(8,128)(2,1)S(1)}, u32[]{:S(2)}, u32[]{:S(2)}) async-start(bf16[8,16,768]{2,1,0:T(8,128)(2,1)} %broadcast_in_dim.37), calls=%async_computation.4 | async-start | bytes 393216 | tf_op jit(solution)/shard_map/all_to_all | solution.py:50
  254.4 30.3 %collective-permute-start.30 = (bf16[256,768]{1,0:T(8,128)(2,1)S(1)}, bf16[256,768]{1,0:T(8,128)(2,1)S(1)}, u32[]{:S(2)}, u32[]{:S(2)}) collective-permute-start(bf16[256,768]{1,0:T(8,128)(2,1)S(1)} %add_convert_fusion.3), channel_id=1, source_target_pairs={{0,2},{1,3},{2,0},{3,1},{4,6},{5,7},{6,4},{7,5},{8,10},{9,11},{10,... | collective-permute-start | bytes 1179656 | tf_op jit(solution)/shard_map/ppermute | solution.py:20
  262.6 14.2 %collective-permute-start.38 = (bf16[1,128,640]{2,1,0:T(8,128)(2,1)S(1)}, bf16[1,128,640]{2,1,0:T(8,128)(2,1)}, u32[]{:S(2)}, u32[]{:S(2)}) collective-permute-start(bf16[1,128,640]{2,1,0:T(8,128)(2,1)S(1)} %slice.176), channel_id=1, source_target_pairs={{0,16},{4,20},{8,24},{12,28},{16,0},{20,4},{24,8},{28,12},{1,17},{... | collective-permute-start | bytes 491528 | tf_op jit(solution)/shard_map/ppermute | solution.py:46
  264.3 11.2 %all-to-all-start.5 = ((f32[8,1,96]{2,1,0:T(1,128)}), f32[8,1,96]{2,1,0:T(1,128)S(1)}, u32[]{:S(2)}, u32[]{:S(2)}) async-start(f32[8,1,96]{2,1,0:T(1,128)} %bitcast.11), calls=%async_computation.5 | async-start | bytes 8192 | tf_op jit(solution)/shard_map/all_to_all | solution.py:50
  (44 other events, 408.9 us)
Sparse Core Ops, SparseCore 0:
  10.8 47.9 all-gather.2
  61.6 57.3 all-gather.4
